TPU v7x, 128 devices: a whole 4x4x4 slice. The times are simulated.
128 devices in a mesh: dom: 16 (over y, x_hi, core), cls: 8 (over x_lo, z).
Axes of the slice: x: 4 (x_hi: 2, x_lo: 2; x = x_hi * 2 + x_lo), y: 4, z: 4, core: 2. Of those that a mesh axis runs over, the one named last changes fastest.
Arguments:
- particles: bfloat16 [16384, 9216], P(('dom', 'cls')), may hold values from -6 to 6
- references: bfloat16 [200, 9216], P('cls', 'dom'), may hold values from -0.0625 to 0.0625
- owner: int32 [16384, 1], P(('dom', 'cls')), may hold values from 0 to 7; in each aligned block of 128 rows (0 to 127, 128 to 255, ...) at most 32 rows name the same one
- class_offset: int32 [16384], P(('dom', 'cls')), may hold values from 0 to 24
- rotation: int32 [16384], P(('dom', 'cls')), may hold values from 0 to 71
- shifts: int32 [16384, 2], P(('dom', 'cls')), may hold values from -6 to 6
- ctf_group: int32 [16384], P(('dom', 'cls')), may hold values from 0 to 255, as said below
- ctf_table: float32 [256, 64], replicated, may hold values from -6 to 6
Outputs:
- best_score: float32 [16384], P(('dom', 'cls'))
- new_references: float32 [200, 9216], P('cls', 'dom')
Inputs may be any that keep to these rules, and one draw needn't show every extreme that they name: Among the particles of one device no owner index is named more than 32 times, a bound that some block reaches. `ctf_group`: the particles of device block i (rows i * 128 to (i + 1) * 128 - 1) use only groups i * 2 to (i + 1) * 2 - 1.
All inputs are finite; a program needn't handle non-finite values.
Results may differ from a plain program's by a relative error of at most 0.0029.
Values may be sent and summed in bfloat16 or wider, within the bound.
No kernel may reach another device: no remote copies, remote signals or barrier semaphores. Data moves between devices by JAX's collectives and lax.ppermute only.
A program may use at most 128 MiB of HBM per device.

v0:
```python
import math

import jax
import jax.numpy as jnp
from jax import lax
from jax.sharding import PartitionSpec as P

BOX = 128


tau_reg = 1.0


def angle_tables(angles):
    index_grid = (
        jnp.arange(angles, dtype=jnp.int32)[:, None]
        * jnp.arange(angles, dtype=jnp.int32)[None, :]
        % angles
    )
    turn_grid = 2.0 * math.pi * index_grid.astype(jnp.float32) / angles
    cosine = jnp.cos(turn_grid)
    sine_part = jnp.sin(turn_grid)
    forward = jnp.concatenate([cosine, -sine_part], axis=0).astype(jnp.bfloat16)
    inverse = (jnp.concatenate([cosine, -sine_part], axis=1) / angles).astype(jnp.bfloat16)
    return (forward, inverse)


def prepare(particle_rows, shift_rows, group_rows, ctf_table):
    count_rows = particle_rows.shape[0]
    cycle_count = ctf_table.shape[1]
    angles = particle_rows.shape[1] // (2 * cycle_count)
    values_in = particle_rows.reshape(count_rows, angles, 2, cycle_count).astype(jnp.float32)
    angle_grid = 2.0 * math.pi * jnp.arange(angles, dtype=jnp.float32) / angles
    radius = jnp.arange(1, cycle_count + 1, dtype=jnp.float32)
    freq_x = jnp.cos(angle_grid)[:, None] * radius[None, :]
    freq_y = jnp.sin(angle_grid)[:, None] * radius[None, :]
    move_x = shift_rows[:, 0].astype(jnp.float32)[:, None, None]
    move_y = shift_rows[:, 1].astype(jnp.float32)[:, None, None]
    phase_grid = 2.0 * math.pi * (move_x * freq_x[None] + move_y * freq_y[None]) / BOX
    cosine = jnp.cos(phase_grid)
    sine_part = jnp.sin(phase_grid)
    selector = (
        group_rows[:, None] == jnp.arange(ctf_table.shape[0], dtype=jnp.int32)[None, :]
    ).astype(jnp.float32)
    ctf_rows = jnp.dot(
        selector, ctf_table, precision=lax.Precision.HIGHEST, preferred_element_type=jnp.float32
    )
    real_in = values_in[:, :, 0, :]
    imag_in = values_in[:, :, 1, :]
    real_out = (real_in * cosine - imag_in * sine_part) * ctf_rows[:, None, :]
    imag_out = (real_in * sine_part + imag_in * cosine) * ctf_rows[:, None, :]
    weighted = jnp.stack([real_out, imag_out], axis=2).reshape(count_rows, angles * 2 * cycle_count)
    return (weighted.astype(jnp.bfloat16), ctf_rows)


def spectra_of(flat_rows, forward, cycle_count):
    angles = forward.shape[1]
    shaped = flat_rows.reshape(flat_rows.shape[0], angles, 2 * cycle_count)
    spectra = jnp.einsum("ja,nac->jnc", forward, shaped, preferred_element_type=jnp.float32).astype(
        jnp.bfloat16
    )
    return jnp.concatenate([spectra[:angles], spectra[angles:]], axis=2)


def paired(ref_spectra, cycle_count):
    half_width = 2 * cycle_count
    swapped = jnp.concatenate(
        [-ref_spectra[:, :, half_width:], ref_spectra[:, :, :half_width]], axis=2
    )
    return jnp.concatenate([ref_spectra, swapped], axis=1)


def best_scores(part_spectra, ref_pairs, inverse):
    angles = part_spectra.shape[0]
    count_rows = part_spectra.shape[1]
    classes = ref_pairs.shape[1] // 2
    cross_terms = jnp.einsum(
        "mnc,mkc->mnk", part_spectra, ref_pairs, preferred_element_type=jnp.float32
    ).astype(jnp.bfloat16)
    stacked = jnp.concatenate(
        [
            cross_terms[:, :, :classes].reshape(angles, count_rows * classes),
            cross_terms[:, :, classes:].reshape(angles, count_rows * classes),
        ],
        axis=0,
    )
    correlation = jnp.dot(inverse, stacked, preferred_element_type=jnp.float32)
    return jnp.max(correlation.reshape(angles, count_rows, classes), axis=(0, 2))


def rotate_back(weighted, rotation_rows, cycle_count):
    angles = weighted.shape[1] // (2 * cycle_count)
    shaped = weighted.reshape(weighted.shape[0], angles, 2 * cycle_count)
    doubled = jnp.concatenate([shaped, shaped], axis=1)

    def one_row(row_block, start):
        return lax.dynamic_slice_in_dim(row_block, start, angles, 0)

    turned = jax.vmap(one_row)(doubled, rotation_rows)
    return turned.reshape(weighted.shape)


def per_device(particles, references, owner, class_offset, rotation, shifts, ctf_group, ctf_table):
    cycle_count = ctf_table.shape[1]
    full_width = particles.shape[1]
    angles = full_width // (2 * cycle_count)
    local_classes = references.shape[0]
    forward, inverse = angle_tables(angles)
    weighted, ctf_rows = prepare(particles, shifts, ctf_group, ctf_table)
    columns_all = lax.all_gather(references, "dom", axis=1, tiled=True)
    ref_spectra = spectra_of(
        lax.all_gather(columns_all, "cls", axis=0, tiled=True), forward, cycle_count
    )
    ref_pairs = paired(ref_spectra, cycle_count)
    scores = best_scores(spectra_of(weighted, forward, cycle_count), ref_pairs, inverse)
    total_classes = ref_spectra.shape[1]
    owner_rows = owner[:, 0]
    class_index = owner_rows * local_classes + class_offset
    contrib = rotate_back(weighted, rotation, cycle_count)
    selector = class_index[:, None] == jnp.arange(total_classes, dtype=jnp.int32)[None, :]
    weight_part = jnp.dot(
        selector.astype(jnp.float32).T,
        ctf_rows * ctf_rows,
        precision=lax.Precision.HIGHEST,
        preferred_element_type=jnp.float32,
    )
    weight_sum = lax.psum(weight_part, ("dom", "cls"))
    dom_count = lax.axis_size("dom")
    piece_width = full_width // dom_count
    class_sums = jnp.dot(
        selector.astype(jnp.bfloat16).T, contrib, preferred_element_type=jnp.float32
    )
    narrow = lax.psum_scatter(class_sums, "dom", scatter_dimension=1, tiled=True)
    mine = lax.psum_scatter(narrow, "cls", scatter_dimension=0, tiled=True)
    cls_position = lax.axis_index("cls")
    dom_position = lax.axis_index("dom")
    weight_mine = lax.dynamic_slice_in_dim(
        weight_sum, cls_position * local_classes, local_classes, 0
    )
    weight_wide = jnp.tile(jnp.concatenate([weight_mine, weight_mine], axis=1), (1, angles))
    weight_cols = lax.dynamic_slice_in_dim(weight_wide, dom_position * piece_width, piece_width, 1)
    new_references = mine / (weight_cols + tau_reg)
    return (scores, new_references)


def solution(mesh):
    return jax.shard_map(
        per_device,
        mesh=mesh,
        in_specs=(
            P(("dom", "cls"), None),
            P("cls", "dom"),
            P(("dom", "cls"), None),
            P(("dom", "cls")),
            P(("dom", "cls")),
            P(("dom", "cls"), None),
            P(("dom", "cls")),
            P(),
        ),
        out_specs=(P(("dom", "cls")), P("cls", "dom")),
        check_vma=False,
    )
```

profile of v0, /device:TPU:0, one launch (start us, length us, event | category | flops | bytes accessed | tf_op | source)
XLA Modules:
  0.0 296.7 jit_solution(6683293741572668623)
XLA Ops:
  8.1 27.7 %all-gather = bf16[16,576,25]{1,2,0:T(8,128)(2,1)S(1)} all-gather(bf16[1,576,25]{1,2,0:T(8,128)(2,1)} %bitcast.51), channel_id=1, replica_groups=mesh['dom'=16,'cls'=8] {'dom'}, dimensions={0}, use_global_device_ids=true | all-gather | bytes 489600 | tf_op jit(solution)/shard_map/all_gather | solution.py:110
  35.9 1.3 reshape.148
  37.4 3.0 %copy.24 = bf16[128,9216]{0,1:T(8,128)(2,1)S(1)} copy(bf16[128,9216]{1,0:T(8,128)(2,1)} %param.8) | data formatting | bytes 4718592 | tf_op args[0]
  41.5 10.3 %multiply_convert_fusion.1 = (bf16[128,72,1,64]{0,3,2,1:T(8,128)(2,1)S(1)}, bf16[128,72,1,64]{0,3,2,1:T(8,128)(2,1)S(1)}) fusion(f32[128,72,2,64]{0,3,2,1:T(8,128)S(1)} %convert.17, f32[128,64]{0,1:T(8,128)S(1)} %fusion.16, f32[72,64]{1,0:T(8,128)S(1)} %get-tuple-element.14, f32[128]{0:T(128)S(1)} %get-tuple-element.12, f32[72,64]{1,0:T(8,128)S(1)} %get-tuple-element.13, ...), kind=kLoop, calls=%fused_computation.17 | loop fusion | flops 8257536 | bytes 7148544 | tf_op jit(solution)/shard_map/convert.1
  52.0 2.4 copy.31
  54.5 5.0 %pad_maximum_fusion.1 = bf16[128,144,128]{2,0,1:T(8,128)(2,1)} fusion(bf16[128,72,128]{2,0,1:T(8,128)(2,1)} %copy.31), kind=kLoop, calls=%fused_computation.12 | loop fusion | flops 2359296 | bytes 7077888 | tf_op jit(solution)/shard_map/concatenate | solution.py:94
  59.5 10.8 %gather_fusion = bf16[128,72,128]{2,0,1:T(8,128)(2,1)} fusion(bf16[128,144,128]{2,0,1:T(8,128)(2,1)} %pad_maximum_fusion.1, s32[128]{0:T(128)S(1)} %fusion.40), kind=kCustom, calls=%fused_computation | custom fusion | bytes 4720128 | tf_op jit(solution)/shard_map/vmap()/gather | solution.py:97
  70.3 4.3 %copy.33 = bf16[128,72,128]{0,2,1:T(8,128)(2,1)} copy(bf16[128,72,128]{2,0,1:T(8,128)(2,1)} %gather_fusion) | data formatting | bytes 4718592 | tf_op jit(solution)/shard_map/vmap()/gather | solution.py:97
  74.6 6.7 %convolution_bitcast_fusion = f32[9216,200]{1,0:T(8,128)} fusion(bf16[128,9216]{0,1:T(8,128)(2,1)} %bitcast.46, s32[128]{0:T(128)S(1)} %bitcast_add_fusion), kind=kOutput, calls=%fused_computation.4 | convolution fusion | flops 471910400 | bytes 9732608
  81.3 2.8 copy.25
  84.5 73.9 %psum.7 = f32[200,64]{1,0:T(8,128)S(1)} all-reduce(f32[200,64]{1,0:T(8,128)S(1)} %fusion.18), channel_id=1, replica_groups=mesh['dom'=16,'cls'=8] {'dom','cls'}, use_global_device_ids=true, to_apply=%region_4.5 | all-reduce | flops 12800 | bytes 102400 | tf_op jit(solution)/shard_map/psum | solution.py:127
  158.7 1.3 copy.36
  161.6 1.4 convolution_convert_fusion.1
  162.9 0.8 fusion.50
  163.7 2.7 pad_maximum_fusion
  166.4 7.6 %reshape.131 = bf16[200,72,128]{2,1,0:T(8,128)(2,1)} reshape(bf16[8,25,9216]{2,1,0:T(8,128)(2,1)} %all-gather.4.cloned.1.call-done) | data formatting | bytes 7372800 | tf_op jit(solution)/shard_map/reshape | solution.py:58
  174.0 4.1 %convolution_convert_fusion = bf16[144,200,128]{2,0,1:T(8,128)(2,1)S(1)} fusion(bf16[200,72,128]{2,1,0:T(8,128)(2,1)} %reshape.131, bf16[72,72]{1,0:T(8,128)(2,1)S(1)} %get-tuple-element.16, bf16[72,72]{1,0:T(8,128)(2,1)S(1)} %get-tuple-element.15), kind=kOutput, calls=%fused_computation.10 | convolution fusion | flops 534569472 | bytes 11079936 | tf_op jit(solution)/shard_map/ja,nac->jnc/dot_general | solution.py:59
  178.1 1.0 fusion.49
  179.1 22.2 %maximum_maximum_fusion = bf16[72,400,256]{2,0,1:T(8,128)(2,1)} fusion(bf16[72,200,128]{2,0,1:T(8,128)(2,1)S(1)} %get-tuple-element.6, bf16[72,200,128]{2,0,1:T(8,128)(2,1)S(1)} %get-tuple-element.5, bf16[72,200,128]{2,0,1:T(8,128)(2,1)S(1)} %get-tuple-element.4), kind=kLoop, calls=%fused_computation.1 | loop fusion | flops 58982400 | bytes 25804800 | tf_op jit(solution)/shard_map/concatenate | solution.py:70
  201.4 15.7 %fusion.7 = bf16[72,128,400]{1,2,0:T(8,128)(2,1)S(1)} fusion(bf16[72,400,256]{2,0,1:T(8,128)(2,1)} %maximum_maximum_fusion, bf16[72,128,256]{2,0,1:T(8,128)(2,1)} %pad_maximum_fusion), kind=kOutput, calls=%fused_computation.9 | convolution fusion | flops 1891123200 | bytes 26836992 | tf_op jit(solution)/shard_map/mnc,mkc->mnk/dot_general | solution.py:77
  217.1 4.2 %fusion.48 = (bf16[72,128,200]{1,2,0:T(8,128)(2,1)}, bf16[72,128,200]{1,2,0:T(8,128)(2,1)}) fusion(bf16[72,128,400]{1,2,0:T(8,128)(2,1)S(1)} %fusion.7), kind=kLoop, calls=%fused_computation.70 | loop fusion | bytes 14745600 | tf_op jit(solution)/shard_map/slice | solution.py:82
  221.3 6.3 %copy.30 = bf16[72,128,200]{2,1,0:T(8,128)(2,1)} copy(bf16[72,128,200]{1,2,0:T(8,128)(2,1)} %get-tuple-element.3) | data formatting | bytes 7372800 | tf_op jit(solution)/shard_map/slice | solution.py:83
  227.6 9.6 %reshape.133 = bf16[72,25600]{1,0:T(8,128)(2,1)} reshape(bf16[72,128,200]{2,1,0:T(8,128)(2,1)} %copy.30) | data formatting | bytes 7372800 | tf_op jit(solution)/shard_map/reshape | solution.py:83
  237.2 6.3 %copy.29 = bf16[72,128,200]{2,1,0:T(8,128)(2,1)} copy(bf16[72,128,200]{1,2,0:T(8,128)(2,1)} %get-tuple-element.2) | data formatting | bytes 7372800 | tf_op jit(solution)/shard_map/slice | solution.py:82
  243.4 9.6 %reshape.132 = bf16[72,25600]{1,0:T(8,128)(2,1)} reshape(bf16[72,128,200]{2,1,0:T(8,128)(2,1)} %copy.29) | data formatting | bytes 7372800 | tf_op jit(solution)/shard_map/reshape | solution.py:82
  253.0 1.3 copy.35
  254.3 22.7 %fusion = f32[32,576]{1,0:T(8,128)S(1)} fusion(f32[200,576]{1,0:T(8,128)S(1)} %copy.35), kind=kCustom, calls=%all-reduce-scatter | all-reduce-scatter fusion | flops 147457 | bytes 535040
  277.1 2.8 collective-permute-start
  279.9 2.1 collective-permute-start.1
  282.0 4.4 %fusion.13 = f32[25600]{0:T(1024)S(1)} fusion(bf16[72,25600]{1,0:T(8,128)(2,1)} %reshape.133, bf16[72,25600]{1,0:T(8,128)(2,1)} %reshape.132, f32[72,72]{1,0:T(8,128)S(1)} %get-tuple-element.19, f32[72,72]{1,0:T(8,128)S(1)} %get-tuple-element.20), kind=kOutput, calls=%fused_computation.21 | convolution fusion | flops 547435904 | bytes 7516672 | tf_op jit(solution)/shard_map/dot_general | solution.py:87
  286.6 0.6 reduce_max.18
  287.6 1.6 dynamic-slice_divide_fusion
  (47 shorter events, 3.6 us)
Async XLA Ops:
  8.0 33.2 %copy-start = (f32[256,64]{0,1:T(8,128)S(1)}, f32[256,64]{0,1:T(8,128)}, u32[]{:S(2)}) copy-start(f32[256,64]{0,1:T(8,128)} %param.15) | copy-start | bytes 196612
  8.0 158.4 %all-gather.4.cloned.1.call-start = ((), (), s32[]{:S(2)}) async-start(), calls=%async_computation.1 | async-start | bytes 5308416 | tf_op jit(solution)/shard_map/all_gather | solution.py:112
  37.3 215.7 %reduce-scatter.6.cloned.1.call-start = ((), (), s32[]{:S(2)}) async-start(), calls=%async_computation.2 | async-start | bytes 10027008
  40.4 0.7 copy-start.3
  40.4 0.8 copy-start.4
  51.8 2.7 copy-start.6
  70.3 4.3 %copy-start.7 = (s32[128]{0:T(128)S(1)}, s32[128]{0:T(128)}, u32[]{:S(2)}) copy-start(s32[128]{0:T(128)} %param.11) | copy-start | bytes 1540
  70.3 4.3 %copy-start.8 = (s32[128,1]{0,1:T(1,128)S(1)}, s32[128,1]{0,1:T(1,128)}, u32[]{:S(2)}) copy-start(s32[128,1]{0,1:T(1,128)} %param.10) | copy-start | bytes 1540
  84.1 75.9 %copy-start.5 = (u32[128]{0:T(128)S(1)}, u32[128]{0:T(128)}, u32[]{:S(2)}) copy-start(u32[128]{0:T(128)} %constant.83) | copy-start | bytes 1540
  84.1 77.5 %copy-start.2 = (bf16[128,72,128]{2,1,0:T(8,128)(2,1)S(1)}, bf16[128,72,128]{2,1,0:T(8,128)(2,1)}, u32[]{:S(2)}) copy-start(bf16[128,72,128]{2,1,0:T(8,128)(2,1)} %copy.25) | copy-start | bytes 7077892
  277.1 10.2 %collective-permute-start = (f32[32,576]{1,0:T(8,128)S(1)}, f32[32,576]{1,0:T(8,128)S(1)}, u32[]{:S(2)}, u32[]{:S(2)}) collective-permute-start(f32[32,576]{1,0:T(8,128)S(1)} %fusion), channel_id=1, source_target_pairs={{0,1},{1,2},{2,3},{3,4},{4,5},{5,6},{6,7},{8,9},{9,10},{10,11},{11... | collective-permute-start | bytes 221192
  279.9 7.3 %collective-permute-start.1 = (f32[17,576]{1,0:T(8,128)S(1)}, f32[17,576]{1,0:T(8,128)S(1)}, u32[]{:S(2)}, u32[]{:S(2)}) collective-permute-start(f32[17,576]{1,0:T(8,128)S(1)} %slice.53), channel_id=1, source_target_pairs={{0,2},{1,3},{2,4},{3,5},{4,6},{5,7},{8,10},{9,11},{10,12},{11,13},... | collective-permute-start | bytes 117512
  282.0 7.2 %copy-start.1 = (f32[256,64]{0,1:T(8,128)S(1)}, f32[256,64]{0,1:T(8,128)}, u32[]{:S(2)}) copy-start(f32[256,64]{0,1:T(8,128)} %param.15) | copy-start | bytes 196612
Sparse Core Ops, SparseCore 0:
  37.4 55.0 all-gather.3
Sparse Core Ops, SparseCore 1:
  81.4 104.7 reduce-scatter.5
where the time goes:
time: 299 us; the launch traced here: 297 us
  blocking collectives  124 us (41%)
  local copies, waits for them, and re-layouts  73.1 us (24%)
  other arithmetic  44.8 us (15%)
  matrix products  32.9 us (11%)
  between operations  16.4 us (5%)
  starting transfers between devices  4.99 us (2%)
    psum x1, blocking collectives, per_device(): weight_sum = lax.psum(weight_part, ('dom', 'cls'))  73.9 us
    all_gather x1, blocking collectives, per_device(): columns_all = lax.all_gather(references, 'dom', axis=1, tiled=True)  27.7 us
    unnamed x1, blocking collectives  22.7 us
    concatenate x1, other arithmetic, paired(): return jnp.concatenate([ref_spectra, swapped], axis=1)  22.2 us
    dot_general x1, matrix products, best_scores(): jnp.einsum('mnc,mkc->mnk', part_spectra, ref_pairs, preferred_element_typ...  15.7 us
    gather x2, local copies, waits for them, and re-layouts, one_row(): return lax.dynamic_slice_in_dim(row_block, start, angles, 0)  15.1 us
    slice x2, local copies, waits for them, and re-layouts, best_scores(): cross_terms[:, :, :classes].reshape(angles, count_rows * classes)  10.5 us
    another operation x2, other arithmetic  10.4 us
  transfers between devices with their start and end apart: 4, of which 0 were waited for; matrix products, arithmetic and copies ran while one was open for 49% of the time, Pallas kernels for 0%

commit v1 on v0

v1 whole, which is shorter than its diff:
```python
import math

import jax
import jax.numpy as jnp
import numpy as np
from jax import lax
from jax.experimental import pallas as pl
from jax.experimental.pallas import tpu as pltpu
from jax.sharding import PartitionSpec as P

A = 72
M = 37
R = 64
BOX = 128
TAU = 1.0
AXES = ("dom", "cls")
BF = jnp.bfloat16
F32 = jnp.float32
VMEM_LIMIT = 56 * 1024 * 1024
K_INV = 640


def tables():
    m = np.arange(M)[:, None]
    a = np.arange(A)[None, :]
    turn = 2.0 * np.pi * ((m * a) % A) / A
    fwd = np.stack([np.cos(turn), -np.sin(turn)], axis=1).reshape(2 * M, A)
    gain = np.where((np.arange(M) == 0) | (np.arange(M) == A // 2), 1.0, 2.0)[:, None]
    inv = np.stack([np.cos(turn) / A, -np.sin(turn) / A], axis=1).astype(BF).astype(np.float32)
    inv = (inv * gain[:, None, :]).reshape(2 * M, A).T
    eye = np.eye(8, dtype=np.float32)
    fwd_k = np.kron(fwd.astype(np.float32), eye).astype(BF)
    inv_k = np.zeros((A * 8, K_INV), np.float32)
    inv_k[:, : 2 * M * 8] = np.kron(inv, eye)
    return fwd_k, inv_k.astype(BF)


def freq_tables():
    angle = 2.0 * np.pi * np.arange(A // 2) / A
    radius = np.tile(np.arange(1, R + 1), 2)
    fx = np.cos(angle)[:, None] * radius[None, :] / BOX
    fy = np.sin(angle)[:, None] * radius[None, :] / BOX
    return fx.astype(np.float32), fy.astype(np.float32)


def cos_poly():
    n = 8
    nodes = (np.cos((np.arange(64) + 0.5) * np.pi / 64) + 1.0) / 8.0
    return [float(c) for c in np.polynomial.chebyshev.Chebyshev.fit(
        nodes, np.cos(2.0 * np.pi * np.sqrt(nodes)), n - 1, domain=[0.0, 0.25]
    ).convert(kind=np.polynomial.Polynomial).coef]


COEF = cos_poly()


def prep_kernel(sc, x_ref, aux_ref, ctf_ref, fx_ref, fy_ref, w_ref, c0, c1, c2, c3, ws, us):
    sx = aux_ref[:, 0:1].astype(F32)
    sy = aux_ref[:, 1:2].astype(F32)
    rot = aux_ref[:, 2:3]
    second = aux_ref[:, 3:4] > 0
    lane = lax.broadcasted_iota(jnp.int32, (16, 128), 1)
    left = lane < R
    shift = jnp.where(left, 0.0, -0.25).astype(F32)
    sxb = jnp.broadcast_to(sx, (16, 128))
    syb = jnp.broadcast_to(sy, (16, 128))
    ctf = jnp.where(second, ctf_ref[1:2, :], ctf_ref[0:1, :])
    ctf_s = jnp.where(left, -ctf, ctf)
    for b in range(A // 4):
        done = []
        for a in (2 * b, 2 * b + 1):
            u = sxb * fx_ref[a : a + 1, :] + syb * fy_ref[a : a + 1, :]
            v = (u - jnp.round(u)) + shift
            v = v - jnp.round(v)
            q = v * v
            e = jnp.full_like(q, COEF[-1])
            for k in COEF[-2::-1]:
                e = e * q + k
            er = pltpu.roll(e, R, 1)
            cc = jnp.where(left, e, er) * ctf
            ss = jnp.where(left, er, e) * ctf_s
            x0 = x_ref[:, a * 128 : (a + 1) * 128].astype(F32)
            h = a + A // 2
            x1 = x_ref[:, h * 128 : (h + 1) * 128].astype(F32)
            w0 = x0 * cc + pltpu.roll(x0, R, 1) * ss
            w1 = x1 * cc - pltpu.roll(x1, R, 1) * ss
            ws[:, a * 128 : (a + 1) * 128] = w0
            ws[:, h * 128 : (h + 1) * 128] = w1
            done.append((w0, w1))
        for half in (0, 1):
            row = (2 * b + half * (A // 2)) * 8
            for g in (0, 1):
                w_ref[g, row : row + 16, :] = jnp.concatenate(
                    [done[0][half][8 * g : 8 * g + 8], done[1][half][8 * g : 8 * g + 8]], axis=0
                ).astype(BF)
    rotb = jnp.broadcast_to(rot, (16, 128))
    bit = [(rotb & (1 << k)) != 0 for k in range(7)]
    for r in range(8):
        t = [ws[:, (r + 8 * n) * 128 : (r + 8 * n + 1) * 128] for n in range(9)]
        for k in range(4):
            t = [jnp.where(bit[3 + k], t[(n + (1 << k)) % 9], t[n]) for n in range(9)]
        for n in range(9):
            us[:, (r + 8 * n) * 128 : (r + 8 * n + 1) * 128] = t[n]
    for j0 in range(0, A, 8):
        t = [us[:, ((j0 + i) % A) * 128 : ((j0 + i) % A + 1) * 128] for i in range(15)]
        t = [jnp.where(bit[0], t[i + 1], t[i]) for i in range(14)]
        t = [jnp.where(bit[1], t[i + 2], t[i]) for i in range(12)]
        for i in range(8):
            ws[:, (j0 + i) * 128 : (j0 + i + 1) * 128] = jnp.where(bit[2], t[i + 4], t[i])
    meta = jnp.where(lane == 0, aux_ref[:, 4:5], jnp.where(lane == 1, aux_ref[:, 5:6], 0))
    meta = meta.astype(F32).astype(BF)
    width = 18 * 128
    for dy, c_ref in enumerate((c0, c1, c2, c3)):
        dest = lax.rem(sc[0] + dy, 4)
        start = pl.multiple_of(dest * width, 128)
        c_ref[:, 0:width] = ws[:, pl.ds(start, width)].astype(BF)
        c_ref[:, width : width + 128] = meta


def prep(sc, particles, aux, ctf2, fx, fy):
    n = particles.shape[0]
    full = lambda i, s: (0, 0)
    block = lambda i, s: (i, 0)
    return pl.pallas_call(
        prep_kernel,
        grid_spec=pltpu.PrefetchScalarGridSpec(
            num_scalar_prefetch=1,
            grid=(n // 16,),
            in_specs=[
                pl.BlockSpec((16, A * 128), block),
                pl.BlockSpec((16, 8), block),
                pl.BlockSpec((2, 128), full),
                pl.BlockSpec((A // 2, 128), full),
                pl.BlockSpec((A // 2, 128), full),
            ],
            out_specs=[pl.BlockSpec((2, A * 8, 128), lambda i, s: (i, 0, 0))]
            + [pl.BlockSpec((16, 19 * 128), block)] * 4,
            scratch_shapes=[pltpu.VMEM((16, A * 128), F32), pltpu.VMEM((16, A * 128), F32)],
        ),
        out_shape=[jax.ShapeDtypeStruct((n // 8, A * 8, 128), BF)]
        + [jax.ShapeDtypeStruct((n, 19 * 128), BF)] * 4,
        compiler_params=pltpu.CompilerParams(vmem_limit_bytes=VMEM_LIMIT),
        cost_estimate=pl.CostEstimate(flops=40_000_000, bytes_accessed=8_000_000, transcendentals=0),
        name="prep",
    )(sc, particles, aux, ctf2, fx, fy)


def spread(out, dst, rows):
    for m in range(M):
        for i in range(2):
            r = 16 * m + 8 * i
            dst[m, rows, 128 * i : 128 * i + 128] = jnp.concatenate(
                [out[r : r + 8, 0:128], out[r : r + 8, 128:256]], axis=0
            ).astype(BF)


def spectra_kernel(w_ref, f_ref, p_ref):
    g = pl.program_id(0)
    y = jnp.concatenate([w_ref[0], w_ref[1]], axis=1)
    out = jnp.dot(f_ref[...], y, preferred_element_type=F32)
    spread(out, p_ref, pl.ds(0, 16))


def spectra(w, fwd_k):
    n = w.shape[0] * 8
    return pl.pallas_call(
        spectra_kernel,
        grid=(n // 16,),
        in_specs=[
            pl.BlockSpec((2, A * 8, 128), lambda i: (i, 0, 0)),
            pl.BlockSpec((2 * M * 8, A * 8), lambda i: (0, 0)),
        ],
        out_specs=pl.BlockSpec((M, 16, 256), lambda i: (0, i, 0)),
        out_shape=jax.ShapeDtypeStruct((M, n, 256), BF),
        compiler_params=pltpu.CompilerParams(vmem_limit_bytes=VMEM_LIMIT),
        cost_estimate=pl.CostEstimate(flops=2_000_000_000, bytes_accessed=5_000_000, transcendentals=0),
        name="spectra",
    )(w, fwd_k)


def ref_kernel(sc, b0, b1, b2, b3, f_ref, r_ref, s):
    for dy, b in enumerate((b0, b1, b2, b3)):
        src = lax.rem(sc[0] + 4 - dy, 4)
        for xh in range(2):
            for t in range(9):
                v = b[xh, :, t * 128 : (t + 1) * 128].astype(F32)
                row = pl.multiple_of((src * 2 + xh) * 72 + 8 * t, 8)
                s[pl.ds(row, 8), 0:128] = v[0:8]
                s[pl.ds(row, 8), 128:256] = v[8:16]
    out = jnp.dot(f_ref[...], s[...].astype(BF), preferred_element_type=F32)
    spread(out, r_ref, pl.ds(0, 16))


def ref_spectra(sc, blocks, fwd_k):
    v = pl.BlockSpec(memory_space=pltpu.VMEM)
    return pl.pallas_call(
        ref_kernel,
        in_specs=[pl.BlockSpec(memory_space=pltpu.SMEM)] + [v] * 5,
        out_specs=v,
        out_shape=jax.ShapeDtypeStruct((M, 16, 256), BF),
        scratch_shapes=[pltpu.VMEM((A * 8, 256), F32)],
        compiler_params=pltpu.CompilerParams(vmem_limit_bytes=VMEM_LIMIT),
        cost_estimate=pl.CostEstimate(flops=200_000_000, bytes_accessed=1_500_000, transcendentals=0),
        name="ref_spectra",
    )(sc, *blocks, fwd_k)


def score_kernel(p_ref, r0, r1, r2, r3, r4, r5, r6, r7, inv_ref, o_ref, xs, mx):
    blocks = (r0, r1, r2, r3, r4, r5, r6, r7)
    xs[:, 2 * M * 8 :, :] = jnp.zeros((16, K_INV - 2 * M * 8, 256), BF)

    @pl.loop(0, M)
    def _(m):
        p = p_ref[m]
        re, im = p[:, 0:128], p[:, 128:256]
        lhs = jnp.concatenate([p, jnp.concatenate([im, -re], axis=1)], axis=0)
        rhs = jnp.concatenate([b[i, m] for b in blocks for i in range(2)], axis=0)
        x = lax.dot_general(lhs, rhs, (((1,), (1,)), ((), ())), preferred_element_type=F32)
        row = pl.multiple_of(m * 16, 16)
        for g in range(16):
            xs[g, pl.ds(row, 16), :] = jnp.concatenate(
                [x[8 * g : 8 * g + 8], x[128 + 8 * g : 136 + 8 * g]], axis=0
            ).astype(BF)

    @pl.loop(0, 16)
    def _(g):
        y = jnp.dot(inv_ref[...], xs[g], preferred_element_type=F32)
        best = y[0:8]
        for t in range(1, A):
            best = jnp.maximum(best, y[8 * t : 8 * t + 8])
        mx[pl.ds(pl.multiple_of(g * 8, 8), 8), :] = best

    o_ref[...] = jnp.max(mx[...], axis=1, keepdims=True)


def scores_of(p, blocks, inv_k):
    n = p.shape[1]
    v = pl.BlockSpec(memory_space=pltpu.VMEM)
    return pl.pallas_call(
        score_kernel,
        in_specs=[v] * 10,
        out_specs=v,
        out_shape=jax.ShapeDtypeStruct((n, 1), F32),
        scratch_shapes=[pltpu.VMEM((16, K_INV, 256), BF), pltpu.VMEM((n, 256), F32)],
        compiler_params=pltpu.CompilerParams(vmem_limit_bytes=VMEM_LIMIT),
        cost_estimate=pl.CostEstimate(flops=6_000_000_000, bytes_accessed=8_000_000, transcendentals=0),
        name="scores",
    )(p, *blocks, inv_k)


def sums_kernel(sc, c0, c1, c2, c3, tab_ref, mine, other, acc):
    width = 18 * 128
    lane = lax.broadcasted_iota(jnp.int32, (128, 256), 1).astype(F32)
    picks, groups = [], []
    for c in (c0, c1, c2, c3):
        meta = c[:, width : width + 128].astype(F32)
        picks.append(jnp.where(lane == meta[:, 0:1], 1.0, 0.0).astype(F32).T.astype(BF))
        groups.append(jnp.where(lane == meta[:, 1:2], 1.0, 0.0).astype(BF))
    pick = jnp.concatenate(picks, axis=1)
    group = jnp.concatenate(groups, axis=0)
    count = jnp.dot(pick, group, preferred_element_type=F32)
    tab = tab_ref[...]
    wsum = jnp.dot(count, tab * tab, precision=lax.Precision.HIGHEST, preferred_element_type=F32)
    for t in range(9):
        cols = slice(256 * t, 256 * t + 256)
        x = jnp.concatenate([c[:, cols] for c in (c0, c1, c2, c3)], axis=0)
        acc[:, cols] = jnp.dot(pick, x, preferred_element_type=F32)
    left = lax.broadcasted_iota(jnp.int32, (256, 128), 1) < R
    for ref, core in ((mine, sc[2]), (other, 1 - sc[2])):
        for xh in range(2):
            start = pl.multiple_of((9 * xh + 4 * core) * 128, 128)
            ref[xh] = acc[:, pl.ds(start, 640)]
            mid = acc[:, (9 * xh + 4) * 128 : (9 * xh + 5) * 128]
            keep = jnp.logical_xor(left, core == 1)
            ref[xh, :, pl.ds(pl.multiple_of((1 - core) * 512, 128), 128)] = jnp.where(keep, mid, wsum)


def class_sums(sc, cs, tab):
    v = pl.BlockSpec(memory_space=pltpu.VMEM)
    shape = jax.ShapeDtypeStruct((2, 256, 640), F32)
    return pl.pallas_call(
        sums_kernel,
        in_specs=[pl.BlockSpec(memory_space=pltpu.SMEM)] + [v] * 5,
        out_specs=[v, v],
        out_shape=[shape, shape],
        scratch_shapes=[pltpu.VMEM((256, 18 * 128), F32)],
        compiler_params=pltpu.CompilerParams(vmem_limit_bytes=VMEM_LIMIT),
        cost_estimate=pl.CostEstimate(flops=700_000_000, bytes_accessed=5_000_000, transcendentals=0),
        name="class_sums",
    )(sc, *cs, tab)


def cut_x_kernel(sc, a_ref, b_ref, o0, o1, o2, o3):
    for dx, o in enumerate((o0, o1, o2, o3)):
        x = lax.rem(sc[1] + dx, 4)
        xh, xl = x // 2, lax.rem(x, 2)
        rows = pl.ds(pl.multiple_of(xl * 128, 128), 128)
        o[...] = a_ref[xh, rows, :] + b_ref[xh, rows, :]


def cut_x(sc, a, b):
    v = pl.BlockSpec(memory_space=pltpu.VMEM)
    return pl.pallas_call(
        cut_x_kernel,
        in_specs=[pl.BlockSpec(memory_space=pltpu.SMEM), v, v],
        out_specs=[v] * 4,
        out_shape=[jax.ShapeDtypeStruct((128, 640), F32)] * 4,
        compiler_params=pltpu.CompilerParams(vmem_limit_bytes=VMEM_LIMIT),
        cost_estimate=pl.CostEstimate(flops=400_000, bytes_accessed=3_900_000, transcendentals=0),
        name="cut_x",
    )(sc, a, b)


def cut_z_kernel(sc, a0, a1, a2, a3, o0, o1, o2, o3):
    for dz, o in enumerate((o0, o1, o2, o3)):
        z = lax.rem(sc[3] + dz, 4)
        rows = pl.ds(pl.multiple_of(z * 32, 32), 32)
        o[...] = (a0[rows, :] + a1[rows, :]) + (a2[rows, :] + a3[rows, :])


def cut_z(sc, parts):
    v = pl.BlockSpec(memory_space=pltpu.VMEM)
    return pl.pallas_call(
        cut_z_kernel,
        in_specs=[pl.BlockSpec(memory_space=pltpu.SMEM)] + [v] * 4,
        out_specs=[v] * 4,
        out_shape=[jax.ShapeDtypeStruct((32, 640), F32)] * 4,
        compiler_params=pltpu.CompilerParams(vmem_limit_bytes=VMEM_LIMIT),
        cost_estimate=pl.CostEstimate(flops=400_000, bytes_accessed=1_700_000, transcendentals=0),
        name="cut_z",
    )(sc, *parts)


def final_kernel(sc, a0, a1, a2, a3, o_ref):
    s = (a0[...] + a1[...]) + (a2[...] + a3[...])
    odd = sc[2] == 1
    left = lax.broadcasted_iota(jnp.int32, (32, 128), 1) < R
    tile = [s[:, 128 * t : 128 * t + 128] for t in range(5)]
    held = jnp.where(odd, tile[0], tile[4])
    turned = pltpu.roll(held, R, 1)
    weight = jnp.where(jnp.logical_xor(left, odd), turned, held)
    tile = [t / (weight + TAU) for t in tile]
    rolled = [pltpu.roll(t, R, 1) for t in tile]
    later = [jnp.where(left, rolled[t], rolled[t + 1]) for t in range(4)] + [rolled[4]]
    for t in range(4):
        o_ref[:, 128 * t : 128 * t + 128] = jnp.where(odd, later[t], tile[t])[0:25]
    o_ref[:, 512:576] = jnp.where(odd, later[4], tile[4])[0:25, 0:R]


def final(sc, parts):
    v = pl.BlockSpec(memory_space=pltpu.VMEM)
    return pl.pallas_call(
        final_kernel,
        in_specs=[pl.BlockSpec(memory_space=pltpu.SMEM)] + [v] * 4,
        out_specs=v,
        out_shape=jax.ShapeDtypeStruct((25, 576), F32),
        name="final",
    )(sc, *parts)


def place(y, x, z, core):
    return ((y % 4) * 4 + (x % 4) // 2 * 2 + core % 2) * 8 + (x % 2) * 4 + z % 4


def permutation(move):
    return [
        (place(y, x, z, c), place(*move(y, x, z, c)))
        for y in range(4)
        for x in range(4)
        for z in range(4)
        for c in range(2)
    ]


CORE = permutation(lambda y, x, z, c: (y, x, z, c + 1))
HIGH = permutation(lambda y, x, z, c: (y, x + 2, z, c))
LOW = permutation(lambda y, x, z, c: (y, x ^ 1, z, c))
YS = [permutation(lambda y, x, z, c, d=d: (y + d, x, z, c)) for d in range(4)]
XS = [permutation(lambda y, x, z, c, d=d: (y, x + d, z, c)) for d in range(4)]
ZS = [permutation(lambda y, x, z, c, d=d: (y, x, z + d, c)) for d in range(4)]


def move(value, pairs):
    return lax.ppermute(value, AXES, pairs)


def per_device(particles, references, owner, class_offset, rotation, shifts, ctf_group, ctf_table):
    fwd_np, inv_np = tables()
    fwd_k, inv_k = jnp.asarray(fwd_np), jnp.asarray(inv_np)
    fx, fy = (jnp.asarray(t) for t in freq_tables())
    dom, cls = lax.axis_index("dom"), lax.axis_index("cls")
    y, xh, core = dom // 4, dom // 2 % 2, dom % 2
    xl, z = cls // 4, cls % 4
    sc = jnp.stack([y, xh * 2 + xl, core, z]).astype(jnp.int32)

    low, high = references[0:16], references[9:25]
    first = core == 0
    keep = jnp.where(first, low, high)
    give = jnp.where(first, high, low)
    got = move(give, CORE)
    block = jnp.where(
        first, jnp.concatenate([keep, got], axis=1), jnp.concatenate([got, keep], axis=1)
    )
    far = move(block, HIGH)
    lower = xh == 0
    pair = jnp.stack([jnp.where(lower, block, far), jnp.where(lower, far, block)])
    blocks = [pair] + [move(pair, YS[d]) for d in (1, 2, 3)]

    first_group = 2 * (dom * 8 + cls)
    rows = lax.dynamic_slice_in_dim(ctf_table, first_group, 2, 0)
    ctf2 = jnp.concatenate([rows, rows], axis=1)
    zero = jnp.zeros_like(rotation)
    aux = jnp.stack(
        [
            shifts[:, 0],
            shifts[:, 1],
            rotation,
            ctf_group - first_group,
            owner[:, 0] * 32 + class_offset,
            ctf_group,
            zero,
            zero,
        ],
        axis=1,
    )
    weighted, *sent = prep(sc, particles, aux, ctf2, fx, fy)
    held = [sent[0]] + [move(sent[d], YS[d]) for d in (1, 2, 3)]
    part = spectra(weighted, fwd_k)

    own = ref_spectra(sc, blocks, fwd_k)
    both = jnp.stack([own, move(own, LOW)])
    line = [both] + [move(both, ZS[d]) for d in (1, 2, 3)]
    line = line + [move(b, CORE) for b in line]
    scores = scores_of(part, line, inv_k)[:, 0]

    tab = jnp.concatenate([ctf_table, ctf_table], axis=1)
    mine, other = class_sums(sc, held, tab)
    cut = cut_x(sc, mine, move(other, CORE))
    cut = [cut[0]] + [move(cut[d], XS[d]) for d in (1, 2, 3)]
    cut = cut_z(sc, cut)
    cut = [cut[0]] + [move(cut[d], ZS[d]) for d in (1, 2, 3)]
    return scores, final(sc, cut)


def solution(mesh):
    return jax.shard_map(
        per_device,
        mesh=mesh,
        in_specs=(
            P(("dom", "cls"), None),
            P("cls", "dom"),
            P(("dom", "cls"), None),
            P(("dom", "cls")),
            P(("dom", "cls")),
            P(("dom", "cls"), None),
            P(("dom", "cls")),
            P(),
        ),
        out_specs=(P(("dom", "cls")), P("cls", "dom")),
        check_vma=False,
    )
```

time: 299 us -> 149 us (0.50)
  blocking collectives: 124 us -> 0 us
  local copies, waits for them, and re-layouts: 73.1 us -> 8.57 us
  Pallas kernels: 0 us -> 49.4 us
  waiting for transfers between devices: 0.04 us -> 48.8 us
  other arithmetic: 44.8 us -> 5.37 us
  matrix products: 32.9 us -> 0 us
  starting transfers between devices: 4.99 us -> 34.3 us
  between operations: 16.4 us -> 0.89 us
    psum x1 -> x0, blocking collectives: 73.9 us -> none  [per_device(): weight_sum = lax.psum(weight_part, ('dom', 'cls'))]
    pallas_call x0 -> x8, Pallas kernels: none -> 49.4 us  [the longest x1 18.7 us: scores_of(): pl.pallas_call(score_kernel, in_specs=[v] * 10, out_specs=v, out_shape=ja...]
    ppermute x0 -> x23, waiting for transfers between devices: none -> 48.8 us  [move(): return lax.ppermute(value, AXES, pairs)]
    ppermute x0 -> x23, starting transfers between devices: none -> 34.3 us  [move(): return lax.ppermute(value, AXES, pairs)]
    concatenate x4 -> x2, other arithmetic: 30 us -> 1.41 us  [the longest x1 0.75 us: per_device(): tab = jnp.concatenate([ctf_table, ctf_table], axis=1)]
    all_gather x1 -> x0, blocking collectives: 27.7 us -> none  [per_device(): columns_all = lax.all_gather(references, 'dom', axis=1, tiled=True)]
    reshape x3 -> x0, local copies, waits for them, and re-layouts: 26.7 us -> none  [the longest x1 9.59 us: best_scores(): cross_terms[:, :, classes:].reshape(angles, count_rows * classes)]
    dot_general x6 -> x0, matrix products: 26.3 us -> none  [the longest x1 15.7 us: best_scores(): jnp.einsum('mnc,mkc->mnk', part_spectra, ref_pairs, preferred_element_typ...]
  transfers between devices with their start and end apart: 4 -> 23, of which waited for: 0 -> 10; matrix products, arithmetic and copies ran while one was open for 49% -> 2% of each run, Pallas kernels for 0% -> 26%
where the time goes in v1:
time: 149 us; the launch traced here: 147 us
  Pallas kernels  49.4 us (33%)
  waiting for transfers between devices  48.8 us (33%)
  starting transfers between devices  34.3 us (23%)
  local copies, waits for them, and re-layouts  8.57 us (6%)
  other arithmetic  5.37 us (4%)
    ppermute x23, waiting for transfers between devices, move(): return lax.ppermute(value, AXES, pairs)  48.8 us
    ppermute x23, starting transfers between devices, move(): return lax.ppermute(value, AXES, pairs)  34.3 us
    pallas_call x1, Pallas kernels, scores_of(): pl.pallas_call(score_kernel, in_specs=[v] * 10, out_specs=v, out_shape=ja...  18.7 us
    pallas_call x1, Pallas kernels, prep(): pl.pallas_call(prep_kernel, grid_spec=pltpu.PrefetchScalarGridSpec(num_sc...  9.17 us
    pallas_call x1, Pallas kernels, spectra(): pl.pallas_call(spectra_kernel, grid=(n // 16,), in_specs=[pl.BlockSpec((2...  7.6 us
    unnamed x47, local copies, waits for them, and re-layouts  7.11 us
    pallas_call x1, Pallas kernels, class_sums(): pl.pallas_call(sums_kernel, in_specs=[pl.BlockSpec(memory_space=pltpu.SME...  4.54 us
    pallas_call x1, Pallas kernels, cut_x(): pl.pallas_call(cut_x_kernel, in_specs=[pl.BlockSpec(memory_space=pltpu.SM...  3.01 us
  transfers between devices with their start and end apart: 23, of which 10 were waited for; matrix products, arithmetic and copies ran while one was open for 2% of the time, Pallas kernels for 26%

profile of v1, /device:TPU:0, one launch (start us, length us, event | category | flops | bytes accessed | tf_op | source)
XLA Modules:
  0.0 147.3 jit_solution(15613216833776998611)
XLA Ops:
  5.1 9.2 %prep.1 = (bf16[16,576,128]{2,1,0:T(8,128)(2,1)}, bf16[128,2432]{1,0:T(8,128)(2,1)}, bf16[128,2432]{1,0:T(8,128)(2,1)}, bf16[128,2432]{1,0:T(8,128)(2,1)}, bf16[128,2432]{1,0:T(8,128)(2,1)}) custom-call(s32[4]{0:T(128)} %pad_add_fusion.sc, bf16[128,9216]{1,0:T(8,128)(2,1)} %x_ref.1, s32[128,8]{1,0:T(8,128)} %copy.31.aux_ref, ...), custom_call_target="tpu_custom_call" | custom-call | flops 40000000 | bytes 8000000 | tf_op jit(solution)/shard_map/prep/pallas_call | solution.py:124
  14.3 1.7 %collective-permute-start.13 = (bf16[128,2432]{1,0:T(8,128)(2,1)}, bf16[128,2432]{1,0:T(8,128)(2,1)S(1)}, u32[]{:S(2)}, u32[]{:S(2)}) collective-permute-start(bf16[128,2432]{1,0:T(8,128)(2,1)} %get-tuple-element.19), channel_id=1, source_target_pairs={{0,32},{8,40},{1,33},{9,41},{2,34},{10,42},{3,35},{11,43},{4,36},{... | collective-permute-start | bytes 1867784 | tf_op jit(solution)/shard_map/ppermute | solution.py:384
  15.9 2.9 %collective-permute-start.14 = (bf16[128,2432]{1,0:T(8,128)(2,1)}, bf16[128,2432]{1,0:T(8,128)(2,1)S(1)}, u32[]{:S(2)}, u32[]{:S(2)}) collective-permute-start(bf16[128,2432]{1,0:T(8,128)(2,1)} %get-tuple-element.20), channel_id=1, source_target_pairs={{0,64},{8,72},{1,65},{9,73},{2,66},{10,74},{3,67},{11,75},{4,68},{... | collective-permute-start | bytes 1867784 | tf_op jit(solution)/shard_map/ppermute | solution.py:384
  18.9 1.4 collective-permute-start.15
  21.6 3.1 %collective-permute-start.1 = (bf16[16,1152]{1,0:T(8,128)(2,1)S(1)}, bf16[16,1152]{1,0:T(8,128)(2,1)S(1)}, u32[]{:S(2)}, u32[]{:S(2)}) collective-permute-start(bf16[16,1152]{1,0:T(8,128)(2,1)S(1)} %maximum_select_fusion), channel_id=1, source_target_pairs={{0,16},{8,24},{1,17},{9,25},{2,18},{10,26},{3,19},{11,27},{4,20},{... | collective-permute-start | bytes 110600 | tf_op jit(solution)/shard_map/ppermute | solution.py:384
  24.7 6.9 %collective-permute-done.13.c1 = bf16[128,2432]{1,0:T(8,128)(2,1)S(1)} collective-permute-done((bf16[128,2432]{1,0:T(8,128)(2,1)}, bf16[128,2432]{1,0:T(8,128)(2,1)S(1)}, u32[]{:S(2)}, u32[]{:S(2)}) %collective-permute-start.13) | collective-permute-done | bytes 622624 | tf_op jit(solution)/shard_map/ppermute | solution.py:384
  31.6 14.5 %collective-permute-done.14.c2 = bf16[128,2432]{1,0:T(8,128)(2,1)S(1)} collective-permute-done((bf16[128,2432]{1,0:T(8,128)(2,1)}, bf16[128,2432]{1,0:T(8,128)(2,1)S(1)}, u32[]{:S(2)}, u32[]{:S(2)}) %collective-permute-start.14) | collective-permute-done | bytes 622624 | tf_op jit(solution)/shard_map/ppermute | solution.py:384
  47.3 4.5 %class_sums.1 = (f32[2,256,640]{2,1,0:T(8,128)}, f32[2,256,640]{2,1,0:T(8,128)}) custom-call(s32[4]{0:T(128)} %pad_add_fusion.sc, bf16[128,2432]{1,0:T(8,128)(2,1)} %get-tuple-element.18.c0, bf16[128,2432]{1,0:T(8,128)(2,1)} %copy-done.1, bf16[128,2432]{1,0:T(8,128)(2,1)} %copy-done.2, bf16[128,2432]{1,0:T(8,128)(2,1)} %copy-done.3, ...), custom_call_target="tpu_custom_call" | custom-call | flops 700000000 | bytes 5000000 | tf_op jit(solution)/shard_map/class_sums/pallas_call | solution.py:281
  51.9 1.0 collective-permute-start.2
  52.9 2.4 %collective-permute-start.3 = (bf16[2,16,1152]{2,1,0:T(8,128)(2,1)S(1)}, bf16[2,16,1152]{2,1,0:T(8,128)(2,1)S(1)}, u32[]{:S(2)}, u32[]{:S(2)}) collective-permute-start(bf16[2,16,1152]{2,1,0:T(8,128)(2,1)S(1)} %pad_maximum_fusion.2.b0), channel_id=1, source_target_pairs={{0,64},{8,72},{1,65},{9,73},{2,66},{10,74},{3,67},{11,75},{4,68},{... | collective-permute-start | bytes 221192 | tf_op jit(solution)/shard_map/ppermute | solution.py:384
  55.3 1.6 %collective-permute-start.4 = (bf16[2,16,1152]{2,1,0:T(8,128)(2,1)S(1)}, bf16[2,16,1152]{2,1,0:T(8,128)(2,1)S(1)}, u32[]{:S(2)}, u32[]{:S(2)}) collective-permute-start(bf16[2,16,1152]{2,1,0:T(8,128)(2,1)S(1)} %pad_maximum_fusion.2.b0), channel_id=1, source_target_pairs={{0,96},{8,104},{1,97},{9,105},{2,98},{10,106},{3,99},{11,107},{4,1... | collective-permute-start | bytes 221192 | tf_op jit(solution)/shard_map/ppermute | solution.py:384
  56.9 1.2 collective-permute-done.2.b1
  58.1 1.4 collective-permute-done.3.b2
  60.8 2.5 %ref_spectra.1 = bf16[37,16,256]{2,1,0:T(8,128)(2,1)} custom-call(s32[4]{0:T(128)} %pad_add_fusion.sc, bf16[2,16,1152]{2,1,0:T(8,128)(2,1)} %copy-done.8, bf16[2,16,1152]{2,1,0:T(8,128)(2,1)} %copy-done.12, bf16[2,16,1152]{2,1,0:T(8,128)(2,1)} %copy-done.13, bf16[2,16,1152]{2,1,0:T(8,128)(2,1)} %copy-done.14, bf16[592,576]{1,0:T(8,128)(2,1)} %constant.78.clone.f_ref), custom_call_target="tpu_custom_call" | custom-call | flops 200000000 | bytes 1500000 | tf_op jit(solution)/shard_map/ref_spectra/pallas_call | solution.py:196
  63.3 1.5 %collective-permute-start.5 = (bf16[37,16,256]{2,1,0:T(8,128)(2,1)}, bf16[37,16,256]{2,1,0:T(8,128)(2,1)S(1)}, u32[]{:S(2)}, u32[]{:S(2)}) collective-permute-start(bf16[37,16,256]{2,1,0:T(8,128)(2,1)} %ref_spectra.1), channel_id=1, source_target_pairs={{0,4},{8,12},{1,5},{9,13},{2,6},{10,14},{3,7},{11,15},{4,0},{12,8}... | collective-permute-start | bytes 909320 | tf_op jit(solution)/shard_map/ppermute | solution.py:384
  64.8 7.5 %collective-permute-done.5 = bf16[37,16,256]{2,1,0:T(8,128)(2,1)S(1)} collective-permute-done((bf16[37,16,256]{2,1,0:T(8,128)(2,1)}, bf16[37,16,256]{2,1,0:T(8,128)(2,1)S(1)}, u32[]{:S(2)}, u32[]{:S(2)}) %collective-permute-start.5) | collective-permute-done | bytes 303136 | tf_op jit(solution)/shard_map/ppermute | solution.py:384
  73.4 2.0 %collective-permute-start.6 = (bf16[2,37,16,256]{3,2,1,0:T(8,128)(2,1)S(1)}, bf16[2,37,16,256]{3,2,1,0:T(8,128)(2,1)S(1)}, u32[]{:S(2)}, u32[]{:S(2)}) collective-permute-start(bf16[2,37,16,256]{3,2,1,0:T(8,128)(2,1)S(1)} %pad_maximum_fusion.r0), channel_id=1, source_target_pairs={{0,1},{8,9},{1,2},{9,10},{2,3},{10,11},{3,0},{11,8},{4,5},{12,13},... | collective-permute-start | bytes 1818632 | tf_op jit(solution)/shard_map/ppermute | solution.py:384
  75.3 3.6 %collective-permute-start.7 = (bf16[2,37,16,256]{3,2,1,0:T(8,128)(2,1)S(1)}, bf16[2,37,16,256]{3,2,1,0:T(8,128)(2,1)S(1)}, u32[]{:S(2)}, u32[]{:S(2)}) collective-permute-start(bf16[2,37,16,256]{3,2,1,0:T(8,128)(2,1)S(1)} %pad_maximum_fusion.r0), channel_id=1, source_target_pairs={{0,2},{8,10},{1,3},{9,11},{2,0},{10,8},{3,1},{11,9},{4,6},{12,14},... | collective-permute-start | bytes 1818632 | tf_op jit(solution)/shard_map/ppermute | solution.py:384
  79.9 1.1 copy-done
  81.0 3.0 %cut_x.1 = (f32[128,640]{1,0:T(8,128)}, f32[128,640]{1,0:T(8,128)}, f32[128,640]{1,0:T(8,128)}, f32[128,640]{1,0:T(8,128)}) custom-call(s32[4]{0:T(128)} %pad_add_fusion.sc, f32[2,256,640]{2,1,0:T(8,128)} %get-tuple-element.22.a_ref, f32[2,256,640]{2,1,0:T(8,128)} %copy-done), custom_call_target="tpu_custom_call" | custom-call | flops 400000 | bytes 3900000 | tf_op jit(solution)/shard_map/cut_x/pallas_call | solution.py:303
  84.0 1.5 %collective-permute-start.17 = (f32[128,640]{1,0:T(8,128)}, f32[128,640]{1,0:T(8,128)S(1)}, u32[]{:S(2)}, u32[]{:S(2)}) collective-permute-start(f32[128,640]{1,0:T(8,128)} %get-tuple-element.25), channel_id=1, source_target_pairs={{0,4},{8,12},{1,5},{9,13},{2,6},{10,14},{3,7},{11,15},{4,16},{12,2... | collective-permute-start | bytes 983048 | tf_op jit(solution)/shard_map/ppermute | solution.py:384
  85.5 2.7 %collective-permute-start.18 = (f32[128,640]{1,0:T(8,128)}, f32[128,640]{1,0:T(8,128)S(1)}, u32[]{:S(2)}, u32[]{:S(2)}) collective-permute-start(f32[128,640]{1,0:T(8,128)} %get-tuple-element.26), channel_id=1, source_target_pairs={{0,16},{8,24},{1,17},{9,25},{2,18},{10,26},{3,19},{11,27},{4,20},{... | collective-permute-start | bytes 983048 | tf_op jit(solution)/shard_map/ppermute | solution.py:384
  88.3 2.9 %collective-permute-done.6.r1 = bf16[2,37,16,256]{3,2,1,0:T(8,128)(2,1)S(1)} collective-permute-done((bf16[2,37,16,256]{3,2,1,0:T(8,128)(2,1)S(1)}, bf16[2,37,16,256]{3,2,1,0:T(8,128)(2,1)S(1)}, u32[]{:S(2)}, u32[]{:S(2)}) %collective-permute-start.6) | collective-permute-done | bytes 606240 | tf_op jit(solution)/shard_map/ppermute | solution.py:384
  91.2 13.1 %collective-permute-done.7.r2 = bf16[2,37,16,256]{3,2,1,0:T(8,128)(2,1)S(1)} collective-permute-done((bf16[2,37,16,256]{3,2,1,0:T(8,128)(2,1)S(1)}, bf16[2,37,16,256]{3,2,1,0:T(8,128)(2,1)S(1)}, u32[]{:S(2)}, u32[]{:S(2)}) %collective-permute-start.7) | collective-permute-done | bytes 606240 | tf_op jit(solution)/shard_map/ppermute | solution.py:384
  104.9 2.8 %collective-permute-start.19 = (f32[128,640]{1,0:T(8,128)}, f32[128,640]{1,0:T(8,128)S(1)}, u32[]{:S(2)}, u32[]{:S(2)}) collective-permute-start(f32[128,640]{1,0:T(8,128)} %get-tuple-element.27), channel_id=1, source_target_pairs={{0,20},{8,28},{1,21},{9,29},{2,22},{10,30},{3,23},{11,31},{4,0},{1... | collective-permute-start | bytes 983048 | tf_op jit(solution)/shard_map/ppermute | solution.py:384
  107.7 7.6 %spectra.1.p_ref = bf16[37,128,256]{2,1,0:T(8,128)(2,1)} custom-call(bf16[16,576,128]{2,1,0:T(8,128)(2,1)} %get-tuple-element.17.w_ref, bf16[592,576]{1,0:T(8,128)(2,1)} %constant.78.clone.f_ref), custom_call_target="tpu_custom_call" | custom-call | flops 2000000000 | bytes 5000000 | tf_op jit(solution)/shard_map/spectra/pallas_call | solution.py:166
  116.3 2.1 %cut_z.1 = (f32[32,640]{1,0:T(8,128)}, f32[32,640]{1,0:T(8,128)}, f32[32,640]{1,0:T(8,128)}, f32[32,640]{1,0:T(8,128)}) custom-call(s32[4]{0:T(128)} %pad_add_fusion.sc, f32[128,640]{1,0:T(8,128)} %get-tuple-element.24.a0, f32[128,640]{1,0:T(8,128)} %copy-done.5, f32[128,640]{1,0:T(8,128)} %copy-done.6, f32[128,640]{1,0:T(8,128)} %copy-done.7), custom_call_target="tpu_custom_call" | custom-call | flops 400000 | bytes 1700000 | tf_op jit(solution)/shard_map/cut_z/pallas_call | solution.py:323
  119.3 2.4 %collective-permute-start.21 = (f32[32,640]{1,0:T(8,128)}, f32[32,640]{1,0:T(8,128)S(1)}, u32[]{:S(2)}, u32[]{:S(2)}) collective-permute-start(f32[32,640]{1,0:T(8,128)} %get-tuple-element.30), channel_id=1, source_target_pairs={{0,2},{8,10},{1,3},{9,11},{2,0},{10,8},{3,1},{11,9},{4,6},{12,14},... | collective-permute-start | bytes 245768 | tf_op jit(solution)/shard_map/ppermute | solution.py:384
  121.7 1.3 collective-permute-start.22
  124.7 18.7 %scores.1 = f32[128,1]{1,0:T(8,128)} custom-call(bf16[37,128,256]{2,1,0:T(8,128)(2,1)} %spectra.1.p_ref, bf16[2,37,16,256]{3,2,1,0:T(8,128)(2,1)} %copy-done.4, bf16[2,37,16,256]{3,2,1,0:T(8,128)(2,1)} %copy-done.16, bf16[2,37,16,256]{3,2,1,0:T(8,128)(2,1)} %copy-done.17, bf16[2,37,16,256]{3,2,1,0:T(8,128)(2,1)} %copy-done.18, ...), custom_call_target="tpu_custom_call" | custom-call | flops 6000000000 | bytes 8000000 | tf_op jit(solution)/shard_map/scores/pallas_call | solution.py:239
  143.3 1.5 reduce
  145.5 1.8 %final.1 = f32[25,576]{1,0:T(8,128)} custom-call(s32[4]{0:T(128)} %pad_add_fusion.sc, f32[32,640]{1,0:T(8,128)} %get-tuple-element.28.a0, f32[32,640]{1,0:T(8,128)} %copy-done.9, f32[32,640]{1,0:T(8,128)} %copy-done.10, f32[32,640]{1,0:T(8,128)} %copy-done.11), custom_call_target="tpu_custom_call" | custom-call | tf_op jit(solution)/shard_map/final/pallas_call | solution.py:352
  (83 shorter events, 15.1 us)
Async XLA Ops:
  0.6 19.6 %copy-start.15 = (bf16[25,576]{1,0:T(8,128)(2,1)S(1)}, bf16[25,576]{1,0:T(8,128)(2,1)}, u32[]{:S(2)}) copy-start(bf16[25,576]{1,0:T(8,128)(2,1)} %param.13) | copy-start | bytes 86404
  14.3 17.3 %collective-permute-start.13 = (bf16[128,2432]{1,0:T(8,128)(2,1)}, bf16[128,2432]{1,0:T(8,128)(2,1)S(1)}, u32[]{:S(2)}, u32[]{:S(2)}) collective-permute-start(bf16[128,2432]{1,0:T(8,128)(2,1)} %get-tuple-element.19), channel_id=1, source_target_pairs={{0,32},{8,40},{1,33},{9,41},{2,34},{10,42},{3,35},{11,43},{4,36},{... | collective-permute-start | bytes 1867784 | tf_op jit(solution)/shard_map/ppermute | solution.py:384
  15.9 30.2 %collective-permute-start.14 = (bf16[128,2432]{1,0:T(8,128)(2,1)}, bf16[128,2432]{1,0:T(8,128)(2,1)S(1)}, u32[]{:S(2)}, u32[]{:S(2)}) collective-permute-start(bf16[128,2432]{1,0:T(8,128)(2,1)} %get-tuple-element.20), channel_id=1, source_target_pairs={{0,64},{8,72},{1,65},{9,73},{2,66},{10,74},{3,67},{11,75},{4,68},{... | collective-permute-start | bytes 1867784 | tf_op jit(solution)/shard_map/ppermute | solution.py:384
  18.9 27.3 %collective-permute-start.15 = (bf16[128,2432]{1,0:T(8,128)(2,1)}, bf16[128,2432]{1,0:T(8,128)(2,1)S(1)}, u32[]{:S(2)}, u32[]{:S(2)}) collective-permute-start(bf16[128,2432]{1,0:T(8,128)(2,1)} %get-tuple-element.21), channel_id=1, source_target_pairs={{0,96},{8,104},{1,97},{9,105},{2,98},{10,106},{3,99},{11,107},{4,1... | collective-permute-start | bytes 1867784 | tf_op jit(solution)/shard_map/ppermute | solution.py:384
  20.2 1.3 collective-permute-start
  21.6 30.2 %collective-permute-start.1 = (bf16[16,1152]{1,0:T(8,128)(2,1)S(1)}, bf16[16,1152]{1,0:T(8,128)(2,1)S(1)}, u32[]{:S(2)}, u32[]{:S(2)}) collective-permute-start(bf16[16,1152]{1,0:T(8,128)(2,1)S(1)} %maximum_select_fusion), channel_id=1, source_target_pairs={{0,16},{8,24},{1,17},{9,25},{2,18},{10,26},{3,19},{11,27},{4,20},{... | collective-permute-start | bytes 110600 | tf_op jit(solution)/shard_map/ppermute | solution.py:384
  31.6 14.5 %copy-start.1 = (bf16[128,2432]{1,0:T(8,128)(2,1)}, bf16[128,2432]{1,0:T(8,128)(2,1)S(1)}, u32[]{:S(2)}) copy-start(bf16[128,2432]{1,0:T(8,128)(2,1)S(1)} %collective-permute-done.13.c1) | copy-start | bytes 1867780
  51.8 28.1 %collective-permute-start.16 = (f32[2,256,640]{2,1,0:T(8,128)}, f32[2,256,640]{2,1,0:T(8,128)S(1)}, u32[]{:S(2)}, u32[]{:S(2)}) collective-permute-start(f32[2,256,640]{2,1,0:T(8,128)} %get-tuple-element.23), channel_id=1, source_target_pairs={{0,8},{8,0},{1,9},{9,1},{2,10},{10,2},{3,11},{11,3},{4,12},{12,4},... | collective-permute-start | bytes 3932168 | tf_op jit(solution)/shard_map/ppermute | solution.py:384
  51.9 8.1 %copy-start.8 = (bf16[2,16,1152]{2,1,0:T(8,128)(2,1)}, bf16[2,16,1152]{2,1,0:T(8,128)(2,1)S(1)}, u32[]{:S(2)}) copy-start(bf16[2,16,1152]{2,1,0:T(8,128)(2,1)S(1)} %pad_maximum_fusion.2.b0) | copy-start | bytes 221188
  51.9 6.2 %collective-permute-start.2 = (bf16[2,16,1152]{2,1,0:T(8,128)(2,1)S(1)}, bf16[2,16,1152]{2,1,0:T(8,128)(2,1)S(1)}, u32[]{:S(2)}, u32[]{:S(2)}) collective-permute-start(bf16[2,16,1152]{2,1,0:T(8,128)(2,1)S(1)} %pad_maximum_fusion.2.b0), channel_id=1, source_target_pairs={{0,32},{8,40},{1,33},{9,41},{2,34},{10,42},{3,35},{11,43},{4,36},{... | collective-permute-start | bytes 221192 | tf_op jit(solution)/shard_map/ppermute | solution.py:384
  52.9 6.6 %collective-permute-start.3 = (bf16[2,16,1152]{2,1,0:T(8,128)(2,1)S(1)}, bf16[2,16,1152]{2,1,0:T(8,128)(2,1)S(1)}, u32[]{:S(2)}, u32[]{:S(2)}) collective-permute-start(bf16[2,16,1152]{2,1,0:T(8,128)(2,1)S(1)} %pad_maximum_fusion.2.b0), channel_id=1, source_target_pairs={{0,64},{8,72},{1,65},{9,73},{2,66},{10,74},{3,67},{11,75},{4,68},{... | collective-permute-start | bytes 221192 | tf_op jit(solution)/shard_map/ppermute | solution.py:384
  55.3 4.7 %collective-permute-start.4 = (bf16[2,16,1152]{2,1,0:T(8,128)(2,1)S(1)}, bf16[2,16,1152]{2,1,0:T(8,128)(2,1)S(1)}, u32[]{:S(2)}, u32[]{:S(2)}) collective-permute-start(bf16[2,16,1152]{2,1,0:T(8,128)(2,1)S(1)} %pad_maximum_fusion.2.b0), channel_id=1, source_target_pairs={{0,96},{8,104},{1,97},{9,105},{2,98},{10,106},{3,99},{11,107},{4,1... | collective-permute-start | bytes 221192 | tf_op jit(solution)/shard_map/ppermute | solution.py:384
  63.3 9.0 %collective-permute-start.5 = (bf16[37,16,256]{2,1,0:T(8,128)(2,1)}, bf16[37,16,256]{2,1,0:T(8,128)(2,1)S(1)}, u32[]{:S(2)}, u32[]{:S(2)}) collective-permute-start(bf16[37,16,256]{2,1,0:T(8,128)(2,1)} %ref_spectra.1), channel_id=1, source_target_pairs={{0,4},{8,12},{1,5},{9,13},{2,6},{10,14},{3,7},{11,15},{4,0},{12,8}... | collective-permute-start | bytes 909320 | tf_op jit(solution)/shard_map/ppermute | solution.py:384
  73.3 49.6 %copy-start.4 = (bf16[2,37,16,256]{3,2,1,0:T(8,128)(2,1)}, bf16[2,37,16,256]{3,2,1,0:T(8,128)(2,1)S(1)}, u32[]{:S(2)}) copy-start(bf16[2,37,16,256]{3,2,1,0:T(8,128)(2,1)S(1)} %pad_maximum_fusion.r0) | copy-start | bytes 1818628
  73.4 17.8 %collective-permute-start.6 = (bf16[2,37,16,256]{3,2,1,0:T(8,128)(2,1)S(1)}, bf16[2,37,16,256]{3,2,1,0:T(8,128)(2,1)S(1)}, u32[]{:S(2)}, u32[]{:S(2)}) collective-permute-start(bf16[2,37,16,256]{3,2,1,0:T(8,128)(2,1)S(1)} %pad_maximum_fusion.r0), channel_id=1, source_target_pairs={{0,1},{8,9},{1,2},{9,10},{2,3},{10,11},{3,0},{11,8},{4,5},{12,13},... | collective-permute-start | bytes 1818632 | tf_op jit(solution)/shard_map/ppermute | solution.py:384
  75.3 28.9 %collective-permute-start.7 = (bf16[2,37,16,256]{3,2,1,0:T(8,128)(2,1)S(1)}, bf16[2,37,16,256]{3,2,1,0:T(8,128)(2,1)S(1)}, u32[]{:S(2)}, u32[]{:S(2)}) collective-permute-start(bf16[2,37,16,256]{3,2,1,0:T(8,128)(2,1)S(1)} %pad_maximum_fusion.r0), channel_id=1, source_target_pairs={{0,2},{8,10},{1,3},{9,11},{2,0},{10,8},{3,1},{11,9},{4,6},{12,14},... | collective-permute-start | bytes 1818632 | tf_op jit(solution)/shard_map/ppermute | solution.py:384
  78.9 25.4 %collective-permute-start.8 = (bf16[2,37,16,256]{3,2,1,0:T(8,128)(2,1)S(1)}, bf16[2,37,16,256]{3,2,1,0:T(8,128)(2,1)S(1)}, u32[]{:S(2)}, u32[]{:S(2)}) collective-permute-start(bf16[2,37,16,256]{3,2,1,0:T(8,128)(2,1)S(1)} %pad_maximum_fusion.r0), channel_id=1, source_target_pairs={{0,3},{8,11},{1,0},{9,8},{2,1},{10,9},{3,2},{11,10},{4,7},{12,15},... | collective-permute-start | bytes 1818632 | tf_op jit(solution)/shard_map/ppermute | solution.py:384
  84.0 20.8 %collective-permute-start.17 = (f32[128,640]{1,0:T(8,128)}, f32[128,640]{1,0:T(8,128)S(1)}, u32[]{:S(2)}, u32[]{:S(2)}) collective-permute-start(f32[128,640]{1,0:T(8,128)} %get-tuple-element.25), channel_id=1, source_target_pairs={{0,4},{8,12},{1,5},{9,13},{2,6},{10,14},{3,7},{11,15},{4,16},{12,2... | collective-permute-start | bytes 983048 | tf_op jit(solution)/shard_map/ppermute | solution.py:384
  85.5 19.4 %collective-permute-start.18 = (f32[128,640]{1,0:T(8,128)}, f32[128,640]{1,0:T(8,128)S(1)}, u32[]{:S(2)}, u32[]{:S(2)}) collective-permute-start(f32[128,640]{1,0:T(8,128)} %get-tuple-element.26), channel_id=1, source_target_pairs={{0,16},{8,24},{1,17},{9,25},{2,18},{10,26},{3,19},{11,27},{4,20},{... | collective-permute-start | bytes 983048 | tf_op jit(solution)/shard_map/ppermute | solution.py:384
  91.2 24.1 %copy-start.16 = (bf16[2,37,16,256]{3,2,1,0:T(8,128)(2,1)}, bf16[2,37,16,256]{3,2,1,0:T(8,128)(2,1)S(1)}, u32[]{:S(2)}) copy-start(bf16[2,37,16,256]{3,2,1,0:T(8,128)(2,1)S(1)} %collective-permute-done.6.r1) | copy-start | bytes 1818628
  91.2 28.1 %collective-permute-start.9 = (bf16[2,37,16,256]{3,2,1,0:T(8,128)(2,1)S(1)}, bf16[2,37,16,256]{3,2,1,0:T(8,128)(2,1)S(1)}, u32[]{:S(2)}, u32[]{:S(2)}) collective-permute-start(bf16[2,37,16,256]{3,2,1,0:T(8,128)(2,1)S(1)} %pad_maximum_fusion.r0), channel_id=1, source_target_pairs={{0,8},{8,0},{1,9},{9,1},{2,10},{10,2},{3,11},{11,3},{4,12},{12,4},... | collective-permute-start | bytes 1818632 | tf_op jit(solution)/shard_map/ppermute | solution.py:384
  104.3 11.0 %copy-start.17 = (bf16[2,37,16,256]{3,2,1,0:T(8,128)(2,1)}, bf16[2,37,16,256]{3,2,1,0:T(8,128)(2,1)S(1)}, u32[]{:S(2)}) copy-start(bf16[2,37,16,256]{3,2,1,0:T(8,128)(2,1)S(1)} %collective-permute-done.7.r2) | copy-start | bytes 1818628
  104.3 17.4 %collective-permute-start.10 = (bf16[2,37,16,256]{3,2,1,0:T(8,128)(2,1)S(1)}, bf16[2,37,16,256]{3,2,1,0:T(8,128)(2,1)S(1)}, u32[]{:S(2)}, u32[]{:S(2)}) collective-permute-start(bf16[2,37,16,256]{3,2,1,0:T(8,128)(2,1)S(1)} %collective-permute-done.6.r1), channel_id=1, source_target_pairs={{0,8},{8,0},{1,9},{9,1},{2,10},{10,2},{3,11},{11,3},{4,12},{12,4},... | collective-permute-start | bytes 1818632 | tf_op jit(solution)/shard_map/ppermute | solution.py:384
  104.3 11.0 %copy-start.18 = (bf16[2,37,16,256]{3,2,1,0:T(8,128)(2,1)}, bf16[2,37,16,256]{3,2,1,0:T(8,128)(2,1)S(1)}, u32[]{:S(2)}) copy-start(bf16[2,37,16,256]{3,2,1,0:T(8,128)(2,1)S(1)} %collective-permute-done.8.r3) | copy-start | bytes 1818628
  104.3 18.6 %collective-permute-start.11 = (bf16[2,37,16,256]{3,2,1,0:T(8,128)(2,1)S(1)}, bf16[2,37,16,256]{3,2,1,0:T(8,128)(2,1)S(1)}, u32[]{:S(2)}, u32[]{:S(2)}) collective-permute-start(bf16[2,37,16,256]{3,2,1,0:T(8,128)(2,1)S(1)} %collective-permute-done.7.r2), channel_id=1, source_target_pairs={{0,8},{8,0},{1,9},{9,1},{2,10},{10,2},{3,11},{11,3},{4,12},{12,4},... | collective-permute-start | bytes 1818632 | tf_op jit(solution)/shard_map/ppermute | solution.py:384
  104.8 10.5 %copy-start.5 = (f32[128,640]{1,0:T(8,128)}, f32[128,640]{1,0:T(8,128)S(1)}, u32[]{:S(2)}) copy-start(f32[128,640]{1,0:T(8,128)S(1)} %collective-permute-done.17.a1) | copy-start | bytes 983044
  104.8 18.1 %collective-permute-start.12 = (bf16[2,37,16,256]{3,2,1,0:T(8,128)(2,1)S(1)}, bf16[2,37,16,256]{3,2,1,0:T(8,128)(2,1)S(1)}, u32[]{:S(2)}, u32[]{:S(2)}) collective-permute-start(bf16[2,37,16,256]{3,2,1,0:T(8,128)(2,1)S(1)} %collective-permute-done.8.r3), channel_id=1, source_target_pairs={{0,8},{8,0},{1,9},{9,1},{2,10},{10,2},{3,11},{11,3},{4,12},{12,4},... | collective-permute-start | bytes 1818632 | tf_op jit(solution)/shard_map/ppermute | solution.py:384
  104.9 10.4 %copy-start.6 = (f32[128,640]{1,0:T(8,128)}, f32[128,640]{1,0:T(8,128)S(1)}, u32[]{:S(2)}) copy-start(f32[128,640]{1,0:T(8,128)S(1)} %collective-permute-done.18.a2) | copy-start | bytes 983044
  104.9 10.6 %collective-permute-start.19 = (f32[128,640]{1,0:T(8,128)}, f32[128,640]{1,0:T(8,128)S(1)}, u32[]{:S(2)}, u32[]{:S(2)}) collective-permute-start(f32[128,640]{1,0:T(8,128)} %get-tuple-element.27), channel_id=1, source_target_pairs={{0,20},{8,28},{1,21},{9,29},{2,22},{10,30},{3,23},{11,31},{4,0},{1... | collective-permute-start | bytes 983048 | tf_op jit(solution)/shard_map/ppermute | solution.py:384
  118.4 26.4 %collective-permute-start.20 = (f32[32,640]{1,0:T(8,128)}, f32[32,640]{1,0:T(8,128)S(1)}, u32[]{:S(2)}, u32[]{:S(2)}) collective-permute-start(f32[32,640]{1,0:T(8,128)} %get-tuple-element.29), channel_id=1, source_target_pairs={{0,1},{8,9},{1,2},{9,10},{2,3},{10,11},{3,0},{11,8},{4,5},{12,13},... | collective-permute-start | bytes 245768 | tf_op jit(solution)/shard_map/ppermute | solution.py:384
  119.3 25.5 %collective-permute-start.21 = (f32[32,640]{1,0:T(8,128)}, f32[32,640]{1,0:T(8,128)S(1)}, u32[]{:S(2)}, u32[]{:S(2)}) collective-permute-start(f32[32,640]{1,0:T(8,128)} %get-tuple-element.30), channel_id=1, source_target_pairs={{0,2},{8,10},{1,3},{9,11},{2,0},{10,8},{3,1},{11,9},{4,6},{12,14},... | collective-permute-start | bytes 245768 | tf_op jit(solution)/shard_map/ppermute | solution.py:384
  121.7 23.1 %collective-permute-start.22 = (f32[32,640]{1,0:T(8,128)}, f32[32,640]{1,0:T(8,128)S(1)}, u32[]{:S(2)}, u32[]{:S(2)}) collective-permute-start(f32[32,640]{1,0:T(8,128)} %get-tuple-element.31), channel_id=1, source_target_pairs={{0,3},{8,11},{1,0},{9,8},{2,1},{10,9},{3,2},{11,10},{4,7},{12,15},... | collective-permute-start | bytes 245768 | tf_op jit(solution)/shard_map/ppermute | solution.py:384
  (14 other events, 15.6 us)

commit v2 on v1

--- a/solution.py
+++ b/solution.py
@@ -1,4 +1,4 @@
-import math
+import functools
 
 import jax
 import jax.numpy as jnp
@@ -16,7 +16,8 @@
 AXES = ("dom", "cls")
 BF = jnp.bfloat16
 F32 = jnp.float32
-VMEM_LIMIT = 56 * 1024 * 1024
+MIB = 1024 * 1024
+VMEM_LIMIT = 16 * MIB
 K_INV = 640
 
 
@@ -44,7 +45,7 @@
 
 
 def cos_poly():
-    n = 8
+    n = 7
     nodes = (np.cos((np.arange(64) + 0.5) * np.pi / 64) + 1.0) / 8.0
     return [float(c) for c in np.polynomial.chebyshev.Chebyshev.fit(
         nodes, np.cos(2.0 * np.pi * np.sqrt(nodes)), n - 1, domain=[0.0, 0.25]
@@ -54,23 +55,40 @@
 COEF = cos_poly()
 
 
-def prep_kernel(sc, x_ref, aux_ref, ctf_ref, fx_ref, fy_ref, w_ref, c0, c1, c2, c3, ws, us):
-    sx = aux_ref[:, 0:1].astype(F32)
-    sy = aux_ref[:, 1:2].astype(F32)
-    rot = aux_ref[:, 2:3]
-    second = aux_ref[:, 3:4] > 0
+def prep_kernel(first, x_ref, shift_ref, rot_ref, own_ref, off_ref, grp_ref, tab_ref, fx_ref, fy_ref, *refs):
+    w_ref, c0, c1, c2, c3, ws, us, aux, tab = refs[-9:]
+    dom, cls = lax.axis_index("dom"), lax.axis_index("cls")
+    mine = 2 * (dom * 8 + cls)
+    step = pl.program_id(0)
+
+    @pl.when(step == 0)
+    def _():
+        shift_rows = shift_ref[...].astype(F32)
+        group = grp_ref[...]
+        rows = [
+            shift_rows,
+            rot_ref[...].astype(F32),
+            (group - mine).astype(F32),
+            (own_ref[...] * 32 + off_ref[...]).astype(F32),
+            group.astype(F32),
+            jnp.zeros((122, 128), F32),
+        ]
+        aux[...] = jnp.concatenate(rows, axis=0).T
+        flipped = tab_ref[...].T
+        tab[...] = jnp.concatenate([flipped, flipped], axis=1)
+
+    here = aux[pl.ds(pl.multiple_of((step + first) * 16, 16), 16), :]
     lane = lax.broadcasted_iota(jnp.int32, (16, 128), 1)
     left = lane < R
     shift = jnp.where(left, 0.0, -0.25).astype(F32)
-    sxb = jnp.broadcast_to(sx, (16, 128))
-    syb = jnp.broadcast_to(sy, (16, 128))
-    ctf = jnp.where(second, ctf_ref[1:2, :], ctf_ref[0:1, :])
+    sxb = jnp.broadcast_to(here[:, 0:1], (16, 128))
+    syb = jnp.broadcast_to(here[:, 1:2], (16, 128))
+    ctf = jnp.where(here[:, 3:4] > 0.5, tab[pl.ds(mine + 1, 1), :], tab[pl.ds(mine, 1), :])
     ctf_s = jnp.where(left, -ctf, ctf)
     for b in range(A // 4):
         done = []
         for a in (2 * b, 2 * b + 1):
-            u = sxb * fx_ref[a : a + 1, :] + syb * fy_ref[a : a + 1, :]
-            v = (u - jnp.round(u)) + shift
+            v = (sxb * fx_ref[a : a + 1, :] + syb * fy_ref[a : a + 1, :]) + shift
             v = v - jnp.round(v)
             q = v * v
             e = jnp.full_like(q, COEF[-1])
@@ -93,7 +111,7 @@
                 w_ref[g, row : row + 16, :] = jnp.concatenate(
                     [done[0][half][8 * g : 8 * g + 8], done[1][half][8 * g : 8 * g + 8]], axis=0
                 ).astype(BF)
-    rotb = jnp.broadcast_to(rot, (16, 128))
+    rotb = jnp.broadcast_to(here[:, 2:3], (16, 128)).astype(jnp.int32)
     bit = [(rotb & (1 << k)) != 0 for k in range(7)]
     for r in range(8):
         t = [ws[:, (r + 8 * n) * 128 : (r + 8 * n + 1) * 128] for n in range(9)]
@@ -107,142 +125,146 @@
         t = [jnp.where(bit[1], t[i + 2], t[i]) for i in range(12)]
         for i in range(8):
             ws[:, (j0 + i) * 128 : (j0 + i + 1) * 128] = jnp.where(bit[2], t[i + 4], t[i])
-    meta = jnp.where(lane == 0, aux_ref[:, 4:5], jnp.where(lane == 1, aux_ref[:, 5:6], 0))
-    meta = meta.astype(F32).astype(BF)
+    meta = jnp.where(lane == 0, here[:, 4:5], jnp.where(lane == 1, here[:, 5:6], 0.0)).astype(BF)
     width = 18 * 128
     for dy, c_ref in enumerate((c0, c1, c2, c3)):
-        dest = lax.rem(sc[0] + dy, 4)
+        dest = lax.rem(dom // 4 + dy, 4)
         start = pl.multiple_of(dest * width, 128)
         c_ref[:, 0:width] = ws[:, pl.ds(start, width)].astype(BF)
         c_ref[:, width : width + 128] = meta
 
 
-def prep(sc, particles, aux, ctf2, fx, fy):
+def prep(particles, rows, table, fx, fy, first, steps, held=None):
     n = particles.shape[0]
-    full = lambda i, s: (0, 0)
-    block = lambda i, s: (i, 0)
-    return pl.pallas_call(
-        prep_kernel,
-        grid_spec=pltpu.PrefetchScalarGridSpec(
-            num_scalar_prefetch=1,
-            grid=(n // 16,),
-            in_specs=[
-                pl.BlockSpec((16, A * 128), block),
-                pl.BlockSpec((16, 8), block),
-                pl.BlockSpec((2, 128), full),
-                pl.BlockSpec((A // 2, 128), full),
-                pl.BlockSpec((A // 2, 128), full),
-            ],
-            out_specs=[pl.BlockSpec((2, A * 8, 128), lambda i, s: (i, 0, 0))]
-            + [pl.BlockSpec((16, 19 * 128), block)] * 4,
-            scratch_shapes=[pltpu.VMEM((16, A * 128), F32), pltpu.VMEM((16, A * 128), F32)],
-        ),
+    whole = lambda a: pl.BlockSpec(a.shape, lambda i: (0,) * a.ndim)
+    block = lambda i: (i + first, 0)
+    args = [particles, *rows, table, fx, fy]
+    specs = [pl.BlockSpec((16, A * 128), block)] + [whole(a) for a in args[1:]]
+    alias = {}
+    if held is not None:
+        alias = {len(args) + i: i for i in range(5)}
+        args += held
+        specs += [pl.BlockSpec(memory_space=pl.ANY)] * 5
+    return pl.pallas_call(
+        functools.partial(prep_kernel, first),
+        grid=(steps,),
+        in_specs=specs,
+        out_specs=[pl.BlockSpec((2, A * 8, 128), lambda i: (i + first, 0, 0))]
+        + [pl.BlockSpec((16, 19 * 128), block)] * 4,
+        scratch_shapes=[
+            pltpu.VMEM((16, A * 128), F32),
+            pltpu.VMEM((16, A * 128), F32),
+            pltpu.VMEM((128, 128), F32),
+            pltpu.VMEM((256, 128), F32),
+        ],
         out_shape=[jax.ShapeDtypeStruct((n // 8, A * 8, 128), BF)]
         + [jax.ShapeDtypeStruct((n, 19 * 128), BF)] * 4,
-        compiler_params=pltpu.CompilerParams(vmem_limit_bytes=VMEM_LIMIT),
-        cost_estimate=pl.CostEstimate(flops=40_000_000, bytes_accessed=8_000_000, transcendentals=0),
+        input_output_aliases=alias,
+        compiler_params=pltpu.CompilerParams(vmem_limit_bytes=8 * MIB),
+        cost_estimate=pl.CostEstimate(
+            flops=5_000_000 * steps, bytes_accessed=1_000_000 * steps, transcendentals=0
+        ),
         name="prep",
-    )(sc, particles, aux, ctf2, fx, fy)
-
-
-def spread(out, dst, rows):
+    )(*args)
+
+
+def spectra_kernel(w_ref, f_ref, p_ref, s):
+    for g in range(8):
+        y = jnp.concatenate([w_ref[2 * g], w_ref[2 * g + 1]], axis=1)
+        s[:, 256 * g : 256 * g + 256] = jnp.dot(f_ref[...], y, preferred_element_type=F32)
+
+    @pl.loop(0, M)
+    def _(m):
+        for i in range(2):
+            row = pl.multiple_of(m * 16 + 8 * i, 8)
+            v = jnp.concatenate([s[pl.ds(row, 8), 128 * g : 128 * g + 128] for g in range(16)], axis=0)
+            p_ref[m, :, 128 * i : 128 * i + 128] = v.T.astype(BF)
+
+
+def spectra(w, fwd_k):
+    v = pl.BlockSpec(memory_space=pltpu.VMEM)
+    return pl.pallas_call(
+        spectra_kernel,
+        in_specs=[v, v],
+        out_specs=v,
+        out_shape=jax.ShapeDtypeStruct((M, 128, 256), BF),
+        scratch_shapes=[pltpu.VMEM((2 * M * 8, 2048), F32)],
+        compiler_params=pltpu.CompilerParams(vmem_limit_bytes=16 * MIB),
+        cost_estimate=pl.CostEstimate(flops=4_000_000_000, bytes_accessed=5_000_000, transcendentals=0),
+        name="spectra",
+    )(w, fwd_k)
+
+
+def ref_kernel(b_ref, f_ref, r_ref, s):
+    for y in range(4):
+        for xh in range(2):
+            for t in range(9):
+                v = b_ref[y, xh, :, t * 128 : (t + 1) * 128].astype(F32)
+                row = (y * 2 + xh) * 72 + 8 * t
+                s[row : row + 8, 0:128] = v[0:8]
+                s[row : row + 8, 128:256] = v[8:16]
+    out = jnp.dot(f_ref[...], s[...].astype(BF), preferred_element_type=F32)
     for m in range(M):
         for i in range(2):
             r = 16 * m + 8 * i
-            dst[m, rows, 128 * i : 128 * i + 128] = jnp.concatenate(
+            r_ref[m, :, 128 * i : 128 * i + 128] = jnp.concatenate(
                 [out[r : r + 8, 0:128], out[r : r + 8, 128:256]], axis=0
             ).astype(BF)
 
 
-def spectra_kernel(w_ref, f_ref, p_ref):
-    g = pl.program_id(0)
-    y = jnp.concatenate([w_ref[0], w_ref[1]], axis=1)
-    out = jnp.dot(f_ref[...], y, preferred_element_type=F32)
-    spread(out, p_ref, pl.ds(0, 16))
-
-
-def spectra(w, fwd_k):
-    n = w.shape[0] * 8
-    return pl.pallas_call(
-        spectra_kernel,
-        grid=(n // 16,),
-        in_specs=[
-            pl.BlockSpec((2, A * 8, 128), lambda i: (i, 0, 0)),
-            pl.BlockSpec((2 * M * 8, A * 8), lambda i: (0, 0)),
-        ],
-        out_specs=pl.BlockSpec((M, 16, 256), lambda i: (0, i, 0)),
-        out_shape=jax.ShapeDtypeStruct((M, n, 256), BF),
-        compiler_params=pltpu.CompilerParams(vmem_limit_bytes=VMEM_LIMIT),
-        cost_estimate=pl.CostEstimate(flops=2_000_000_000, bytes_accessed=5_000_000, transcendentals=0),
-        name="spectra",
-    )(w, fwd_k)
-
-
-def ref_kernel(sc, b0, b1, b2, b3, f_ref, r_ref, s):
-    for dy, b in enumerate((b0, b1, b2, b3)):
-        src = lax.rem(sc[0] + 4 - dy, 4)
-        for xh in range(2):
-            for t in range(9):
-                v = b[xh, :, t * 128 : (t + 1) * 128].astype(F32)
-                row = pl.multiple_of((src * 2 + xh) * 72 + 8 * t, 8)
-                s[pl.ds(row, 8), 0:128] = v[0:8]
-                s[pl.ds(row, 8), 128:256] = v[8:16]
-    out = jnp.dot(f_ref[...], s[...].astype(BF), preferred_element_type=F32)
-    spread(out, r_ref, pl.ds(0, 16))
-
-
-def ref_spectra(sc, blocks, fwd_k):
+def ref_spectra(blocks, fwd_k):
     v = pl.BlockSpec(memory_space=pltpu.VMEM)
     return pl.pallas_call(
         ref_kernel,
-        in_specs=[pl.BlockSpec(memory_space=pltpu.SMEM)] + [v] * 5,
+        in_specs=[v, v],
         out_specs=v,
         out_shape=jax.ShapeDtypeStruct((M, 16, 256), BF),
         scratch_shapes=[pltpu.VMEM((A * 8, 256), F32)],
-        compiler_params=pltpu.CompilerParams(vmem_limit_bytes=VMEM_LIMIT),
+        compiler_params=pltpu.CompilerParams(vmem_limit_bytes=8 * MIB),
         cost_estimate=pl.CostEstimate(flops=200_000_000, bytes_accessed=1_500_000, transcendentals=0),
         name="ref_spectra",
-    )(sc, *blocks, fwd_k)
-
-
-def score_kernel(p_ref, r0, r1, r2, r3, r4, r5, r6, r7, inv_ref, o_ref, xs, mx):
-    blocks = (r0, r1, r2, r3, r4, r5, r6, r7)
+    )(blocks, fwd_k)
+
+
+def score_kernel(*refs):
+    p_ref, blocks, inv_ref, o_ref, xs = refs[0], refs[1:17], refs[17], refs[18], refs[19]
     xs[:, 2 * M * 8 :, :] = jnp.zeros((16, K_INV - 2 * M * 8, 256), BF)
 
     @pl.loop(0, M)
     def _(m):
-        p = p_ref[m]
-        re, im = p[:, 0:128], p[:, 128:256]
-        lhs = jnp.concatenate([p, jnp.concatenate([im, -re], axis=1)], axis=0)
-        rhs = jnp.concatenate([b[i, m] for b in blocks for i in range(2)], axis=0)
-        x = lax.dot_general(lhs, rhs, (((1,), (1,)), ((), ())), preferred_element_type=F32)
+        upper = p_ref[m]
+        re, im = upper[:, 0:128], upper[:, 128:256]
+        rhs = jnp.concatenate([upper, jnp.concatenate([im, -re], axis=1)], axis=0)
+        lhs = jnp.concatenate([b[m] for b in blocks], axis=0)
+        x = jnp.dot(lhs, rhs, preferred_element_type=F32)
         row = pl.multiple_of(m * 16, 16)
         for g in range(16):
-            xs[g, pl.ds(row, 16), :] = jnp.concatenate(
-                [x[8 * g : 8 * g + 8], x[128 + 8 * g : 136 + 8 * g]], axis=0
-            ).astype(BF)
-
-    @pl.loop(0, 16)
-    def _(g):
+            for h in range(2):
+                k = 16 * g + 8 * h
+                xs[g, pl.ds(row, 16), 128 * h : 128 * h + 128] = jnp.concatenate(
+                    [x[k : k + 8, 0:128], x[k : k + 8, 128:256]], axis=0
+                ).astype(BF)
+
+    def one(g, best):
         y = jnp.dot(inv_ref[...], xs[g], preferred_element_type=F32)
-        best = y[0:8]
-        for t in range(1, A):
+        for t in range(A):
             best = jnp.maximum(best, y[8 * t : 8 * t + 8])
-        mx[pl.ds(pl.multiple_of(g * 8, 8), 8), :] = best
-
-    o_ref[...] = jnp.max(mx[...], axis=1, keepdims=True)
+        return best
+
+    best = lax.fori_loop(0, 16, one, jnp.full((8, 256), -jnp.inf, F32))
+    best = jnp.max(best, axis=0, keepdims=True)
+    o_ref[...] = jnp.maximum(best[:, 0:128], best[:, 128:256])
 
 
 def scores_of(p, blocks, inv_k):
-    n = p.shape[1]
     v = pl.BlockSpec(memory_space=pltpu.VMEM)
     return pl.pallas_call(
         score_kernel,
-        in_specs=[v] * 10,
+        in_specs=[v] * 18,
         out_specs=v,
-        out_shape=jax.ShapeDtypeStruct((n, 1), F32),
-        scratch_shapes=[pltpu.VMEM((16, K_INV, 256), BF), pltpu.VMEM((n, 256), F32)],
-        compiler_params=pltpu.CompilerParams(vmem_limit_bytes=VMEM_LIMIT),
+        out_shape=jax.ShapeDtypeStruct((1, 128), F32),
+        scratch_shapes=[pltpu.VMEM((16, K_INV, 256), BF)],
+        compiler_params=pltpu.CompilerParams(vmem_limit_bytes=20 * MIB),
         cost_estimate=pl.CostEstimate(flops=6_000_000_000, bytes_accessed=8_000_000, transcendentals=0),
         name="scores",
     )(p, *blocks, inv_k)
@@ -259,7 +281,8 @@
     pick = jnp.concatenate(picks, axis=1)
     group = jnp.concatenate(groups, axis=0)
     count = jnp.dot(pick, group, preferred_element_type=F32)
-    tab = tab_ref[...]
+    flipped = tab_ref[...].T
+    tab = jnp.concatenate([flipped, flipped], axis=1)
     wsum = jnp.dot(count, tab * tab, precision=lax.Precision.HIGHEST, preferred_element_type=F32)
     for t in range(9):
         cols = slice(256 * t, 256 * t + 256)
@@ -375,6 +398,8 @@
 CORE = permutation(lambda y, x, z, c: (y, x, z, c + 1))
 HIGH = permutation(lambda y, x, z, c: (y, x + 2, z, c))
 LOW = permutation(lambda y, x, z, c: (y, x ^ 1, z, c))
+Y_NEAR = permutation(lambda y, x, z, c: (y ^ 1, x, z, c))
+Y_FAR = permutation(lambda y, x, z, c: (y + 2, x, z, c))
 YS = [permutation(lambda y, x, z, c, d=d: (y + d, x, z, c)) for d in range(4)]
 XS = [permutation(lambda y, x, z, c, d=d: (y, x + d, z, c)) for d in range(4)]
 ZS = [permutation(lambda y, x, z, c, d=d: (y, x, z + d, c)) for d in range(4)]
@@ -382,6 +407,11 @@
 
 def move(value, pairs):
     return lax.ppermute(value, AXES, pairs)
+
+
+def join(own, other, upper):
+    lower = upper == 0
+    return jnp.stack([jnp.where(lower, own, other), jnp.where(lower, other, own)])
 
 
 def per_device(particles, references, owner, class_offset, rotation, shifts, ctf_group, ctf_table):
@@ -401,40 +431,33 @@
     block = jnp.where(
         first, jnp.concatenate([keep, got], axis=1), jnp.concatenate([got, keep], axis=1)
     )
+    rows = [shifts.T, rotation[None], owner.T, class_offset[None], ctf_group[None]]
+    table = ctf_table.T
+    block, rows[1] = lax.optimization_barrier((block, rows[1]))
+    held = prep(particles, rows, table, fx, fy, 0, 4)
     far = move(block, HIGH)
-    lower = xh == 0
-    pair = jnp.stack([jnp.where(lower, block, far), jnp.where(lower, far, block)])
-    blocks = [pair] + [move(pair, YS[d]) for d in (1, 2, 3)]
-
-    first_group = 2 * (dom * 8 + cls)
-    rows = lax.dynamic_slice_in_dim(ctf_table, first_group, 2, 0)
-    ctf2 = jnp.concatenate([rows, rows], axis=1)
-    zero = jnp.zeros_like(rotation)
-    aux = jnp.stack(
-        [
-            shifts[:, 0],
-            shifts[:, 1],
-            rotation,
-            ctf_group - first_group,
-            owner[:, 0] * 32 + class_offset,
-            ctf_group,
-            zero,
-            zero,
-        ],
-        axis=1,
-    )
-    weighted, *sent = prep(sc, particles, aux, ctf2, fx, fy)
+    far, *held = lax.optimization_barrier((far, *held))
+    pair = join(block, far, xh)
+    pair, rows[1] = lax.optimization_barrier((pair, rows[1]))
+    weighted, *sent = prep(particles, rows, table, fx, fy, 4, 4, held)
+    near = move(pair, Y_NEAR)
+    near, weighted, *sent = lax.optimization_barrier((near, weighted, *sent))
+    quad = join(pair, near, y % 2)
+    octet = join(quad, move(quad, Y_FAR), y // 2).reshape(4, 2, 16, 1152)
+
     held = [sent[0]] + [move(sent[d], YS[d]) for d in (1, 2, 3)]
     part = spectra(weighted, fwd_k)
 
-    own = ref_spectra(sc, blocks, fwd_k)
-    both = jnp.stack([own, move(own, LOW)])
-    line = [both] + [move(both, ZS[d]) for d in (1, 2, 3)]
+    own = ref_spectra(octet, fwd_k)
+    up, down = move(own, ZS[1]), move(own, ZS[3])
+    side = move(own, LOW)
+    *held, up, down, side, part = lax.optimization_barrier((*held, up, down, side, part))
+    side_up, side_down = move(side, ZS[1]), move(side, ZS[3])
+    line = [own, side, up, down, side_up, side_down, move(up, ZS[1]), move(side_down, ZS[3])]
     line = line + [move(b, CORE) for b in line]
-    scores = scores_of(part, line, inv_k)[:, 0]
-
-    tab = jnp.concatenate([ctf_table, ctf_table], axis=1)
-    mine, other = class_sums(sc, held, tab)
+    scores = scores_of(part, line, inv_k)[0]
+
+    mine, other = class_sums(sc, held, table)
     cut = cut_x(sc, mine, move(other, CORE))
     cut = [cut[0]] + [move(cut[d], XS[d]) for d in (1, 2, 3)]
     cut = cut_z(sc, cut)

time: 149 us -> 122 us (0.82)
  waiting for transfers between devices: 48.8 us -> 29.2 us
  Pallas kernels: 49.4 us -> 34.7 us
  local copies, waits for them, and re-layouts: 8.57 us -> 15.9 us
  starting transfers between devices: 34.3 us -> 37.7 us
  other arithmetic: 5.37 us -> 2.05 us
    ppermute x23 -> x29, waiting for transfers between devices: 48.8 us -> 29.2 us  [move(): return lax.ppermute(value, AXES, pairs)]
    pallas_call x4 -> x5, Pallas kernels: 37.9 us -> 28.5 us  [the longest x1 15.1 us: scores_of(): pl.pallas_call(score_kernel, in_specs=[v] * 18, out_specs=v, out_shape=ja...]
    unnamed x47 -> x66, local copies, waits for them, and re-layouts: 7.11 us -> 15.9 us
    ppermute x23 -> x29, starting transfers between devices: 34.3 us -> 37.7 us  [move(): return lax.ppermute(value, AXES, pairs)]
    pallas_call x1, Pallas kernels: 3.01 us -> 0.69 us  [cut_x(): pl.pallas_call(cut_x_kernel, in_specs=[pl.BlockSpec(memory_space=pltpu.SM...]
    pallas_call x1, Pallas kernels: 4.54 us -> 3 us  [class_sums(): pl.pallas_call(sums_kernel, in_specs=[pl.BlockSpec(memory_space=pltpu.SME...]
  transfers between devices with their start and end apart: 23 -> 29, of which waited for: 10 -> 12; matrix products, arithmetic and copies ran while one was open for 2% -> 0% of each run, Pallas kernels for 26% -> 24%
where the time goes in v2:
time: 122 us; the launch traced here: 120 us
  starting transfers between devices  37.7 us (31%)
  Pallas kernels  34.7 us (28%)
  waiting for transfers between devices  29.2 us (24%)
  local copies, waits for them, and re-layouts  15.9 us (13%)
  other arithmetic  2.05 us (2%)
    ppermute x29, starting transfers between devices, move(): return lax.ppermute(value, AXES, pairs)  37.7 us
    ppermute x29, waiting for transfers between devices, move(): return lax.ppermute(value, AXES, pairs)  29.2 us
    unnamed x66, local copies, waits for them, and re-layouts  15.9 us
    pallas_call x1, Pallas kernels, scores_of(): pl.pallas_call(score_kernel, in_specs=[v] * 18, out_specs=v, out_shape=ja...  15.1 us
    pallas_call x2, Pallas kernels, prep(): pl.pallas_call(functools.partial(prep_kernel, first), grid=(steps,), in_s...  7.19 us
    pallas_call x1, Pallas kernels, spectra(): pl.pallas_call(spectra_kernel, in_specs=[v, v], out_specs=v, out_shape=ja...  5.88 us
    pallas_call x1, Pallas kernels, class_sums(): pl.pallas_call(sums_kernel, in_specs=[pl.BlockSpec(memory_space=pltpu.SME...  3 us
  transfers between devices with their start and end apart: 29, of which 12 were waited for; matrix products, arithmetic and copies ran while one was open for 0% of the time, Pallas kernels for 24%

profile of v2, /device:TPU:0, one launch (start us, length us, event | category | flops | bytes accessed | tf_op | source)
XLA Modules:
  0.0 120.5 jit_solution(4697573944508622644)
XLA Ops:
  1.7 1.2 collective-permute-done
  2.9 3.2 %collective-permute-start.1 = (bf16[16,1152]{1,0:T(8,128)(2,1)S(1)}, bf16[16,1152]{1,0:T(8,128)(2,1)S(1)}, u32[]{:S(2)}, u32[]{:S(2)}) collective-permute-start(bf16[16,1152]{1,0:T(8,128)(2,1)S(1)} %maximum_select_fusion), channel_id=1, source_target_pairs={{0,16},{8,24},{1,17},{9,25},{2,18},{10,26},{3,19},{11,27},{4,20},{... | collective-permute-start | bytes 110600 | tf_op jit(solution)/shard_map/ppermute | solution.py:409
  6.1 1.7 %copy-done = bf16[128,9216]{1,0:T(8,128)(2,1)S(1)} copy-done((bf16[128,9216]{1,0:T(8,128)(2,1)S(1)}, bf16[128,9216]{1,0:T(8,128)(2,1)}, u32[]{:S(2)}) %copy-start) | copy-done | bytes 2359320
  13.4 3.6 %prep.2 = (bf16[16,576,128]{2,1,0:T(8,128)(2,1)S(1)}, bf16[128,2432]{1,0:T(8,128)(2,1)S(1)}, bf16[128,2432]{1,0:T(8,128)(2,1)}, bf16[128,2432]{1,0:T(8,128)(2,1)}, bf16[128,2432]{1,0:T(8,128)(2,1)}) custom-call(bf16[128,9216]{1,0:T(8,128)(2,1)S(1)} %copy-done, s32[2,128]{1,0:T(2,128)S(1)} %bitcast.28, s32[1,128]{1,0:T(1,128)S(1)} %bitcast.30, ...), custom_call_target="tpu_custom_call" | custom-call | flops 20000000 | bytes 4000000 | tf_op jit(solution)/shard_map/prep/pallas_call | solution.py:148
  17.0 1.4 %copy-done.2 = bf16[16,576,128]{2,1,0:T(8,128)(2,1)} copy-done((bf16[16,576,128]{2,1,0:T(8,128)(2,1)}, bf16[16,576,128]{2,1,0:T(8,128)(2,1)S(1)}, u32[]{:S(2)}) %copy-start.2) | copy-done | bytes 2359320
  19.3 1.7 %collective-permute-start.2 = (bf16[2,16,1152]{2,1,0:T(8,128)(2,1)S(1)}, bf16[2,16,1152]{2,1,0:T(8,128)(2,1)S(1)}, u32[]{:S(2)}, u32[]{:S(2)}) collective-permute-start(bf16[2,16,1152]{2,1,0:T(8,128)(2,1)S(1)} %pad_maximum_fusion.2), channel_id=1, source_target_pairs={{0,32},{8,40},{1,33},{9,41},{2,34},{10,42},{3,35},{11,43},{4,36},{... | collective-permute-start | bytes 221192 | tf_op jit(solution)/shard_map/ppermute | solution.py:409
  21.0 1.7 %copy-done.3 = bf16[16,576,128]{2,1,0:T(8,128)(2,1)S(1)} copy-done((bf16[16,576,128]{2,1,0:T(8,128)(2,1)S(1)}, bf16[16,576,128]{2,1,0:T(8,128)(2,1)}, u32[]{:S(2)}) %copy-start.3) | copy-done | bytes 2359320
  22.7 1.1 copy-done.8
  23.8 3.6 %prep.3 = (bf16[16,576,128]{2,1,0:T(8,128)(2,1)S(1)}, bf16[128,2432]{1,0:T(8,128)(2,1)S(1)}, bf16[128,2432]{1,0:T(8,128)(2,1)}, bf16[128,2432]{1,0:T(8,128)(2,1)}, bf16[128,2432]{1,0:T(8,128)(2,1)}) custom-call(bf16[128,9216]{1,0:T(8,128)(2,1)S(1)} %copy-done.1, ...), custom_call_target="tpu_custom_call", output_to_operand_aliasing={{0}: (9, {}), {1}: (10, {}), {2}: (11, {}), {3}: (12, {}), ... | custom-call | flops 20000000 | bytes 4000000 | tf_op jit(solution)/shard_map/prep/pallas_call | solution.py:148
  27.4 1.4 %copy-done.4 = bf16[16,576,128]{2,1,0:T(8,128)(2,1)} copy-done((bf16[16,576,128]{2,1,0:T(8,128)(2,1)}, bf16[16,576,128]{2,1,0:T(8,128)(2,1)S(1)}, u32[]{:S(2)}) %copy-start.4) | copy-done | bytes 2359320
  29.7 3.0 %collective-permute-start.6 = (bf16[2,2,16,1152]{3,2,1,0:T(8,128)(2,1)S(1)}, bf16[2,2,16,1152]{3,2,1,0:T(8,128)(2,1)}, u32[]{:S(2)}, u32[]{:S(2)}) collective-permute-start(bf16[2,2,16,1152]{3,2,1,0:T(8,128)(2,1)S(1)} %pad_maximum_fusion.1), channel_id=1, source_target_pairs={{0,64},{8,72},{1,65},{9,73},{2,66},{10,74},{3,67},{11,75},{4,68},{... | collective-permute-start | bytes 442376 | tf_op jit(solution)/shard_map/ppermute | solution.py:409
  32.6 4.1 %collective-permute-done.6 = bf16[2,2,16,1152]{3,2,1,0:T(8,128)(2,1)} collective-permute-done((bf16[2,2,16,1152]{3,2,1,0:T(8,128)(2,1)S(1)}, bf16[2,2,16,1152]{3,2,1,0:T(8,128)(2,1)}, u32[]{:S(2)}, u32[]{:S(2)}) %collective-permute-start.6) | collective-permute-done | bytes 147488 | tf_op jit(solution)/shard_map/ppermute | solution.py:409
  36.7 0.9 select_bitcast_fusion.1
  39.2 3.2 %collective-permute-start.4 = (bf16[128,2432]{1,0:T(8,128)(2,1)}, bf16[128,2432]{1,0:T(8,128)(2,1)}, u32[]{:S(2)}, u32[]{:S(2)}) collective-permute-start(bf16[128,2432]{1,0:T(8,128)(2,1)} %get-tuple-element.68), channel_id=1, source_target_pairs={{0,64},{8,72},{1,65},{9,73},{2,66},{10,74},{3,67},{11,75},{4,68},{... | collective-permute-start | bytes 1867784 | tf_op jit(solution)/shard_map/ppermute | solution.py:409
  42.4 1.9 %collective-permute-start.5 = (bf16[128,2432]{1,0:T(8,128)(2,1)}, bf16[128,2432]{1,0:T(8,128)(2,1)}, u32[]{:S(2)}, u32[]{:S(2)}) collective-permute-start(bf16[128,2432]{1,0:T(8,128)(2,1)} %get-tuple-element.69), channel_id=1, source_target_pairs={{0,96},{8,104},{1,97},{9,105},{2,98},{10,106},{3,99},{11,107},{4,1... | collective-permute-start | bytes 1867784 | tf_op jit(solution)/shard_map/ppermute | solution.py:409
  44.4 4.1 %collective-permute-start.8 = (bf16[37,16,256]{2,1,0:T(8,128)(2,1)S(1)}, bf16[37,16,256]{2,1,0:T(8,128)(2,1)S(1)}, u32[]{:S(2)}, u32[]{:S(2)}) collective-permute-start(bf16[37,16,256]{2,1,0:T(8,128)(2,1)S(1)} %ref_spectra.1.refs_1_), channel_id=1, source_target_pairs={{0,3},{8,11},{1,0},{9,8},{2,1},{10,9},{3,2},{11,10},{4,7},{12,15},... | collective-permute-start | bytes 909320 | tf_op jit(solution)/shard_map/ppermute | solution.py:409
  48.5 5.9 %spectra.1.refs_0_ = bf16[37,128,256]{2,1,0:T(8,128)(2,1)S(1)} custom-call(bf16[16,576,128]{2,1,0:T(8,128)(2,1)S(1)} %copy-done.5, bf16[592,576]{1,0:T(8,128)(2,1)S(1)} %copy-done.6), custom_call_target="tpu_custom_call" | custom-call | flops 4000000000 | bytes 5000000 | tf_op jit(solution)/shard_map/spectra/pallas_call | solution.py:186
  54.4 2.1 %collective-permute-done.7.refs_3_ = bf16[37,16,256]{2,1,0:T(8,128)(2,1)S(1)} collective-permute-done((bf16[37,16,256]{2,1,0:T(8,128)(2,1)S(1)}, bf16[37,16,256]{2,1,0:T(8,128)(2,1)S(1)}, u32[]{:S(2)}, u32[]{:S(2)}) %collective-permute-start.7) | collective-permute-done | bytes 303136 | tf_op jit(solution)/shard_map/ppermute | solution.py:409
  56.9 11.5 %collective-permute-done.4.c2 = bf16[128,2432]{1,0:T(8,128)(2,1)} collective-permute-done((bf16[128,2432]{1,0:T(8,128)(2,1)}, bf16[128,2432]{1,0:T(8,128)(2,1)}, u32[]{:S(2)}, u32[]{:S(2)}) %collective-permute-start.4) | collective-permute-done | bytes 622624 | tf_op jit(solution)/shard_map/ppermute | solution.py:409
  68.6 3.0 %class_sums.1 = (f32[2,256,640]{2,1,0:T(8,128)S(1)}, f32[2,256,640]{2,1,0:T(8,128)S(1)}) custom-call(s32[4]{0:T(128)S(1)} %pad_add_fusion.sc, bf16[128,2432]{1,0:T(8,128)(2,1)S(1)} %copy-done.10, bf16[128,2432]{1,0:T(8,128)(2,1)} %collective-permute-done.3.c1, bf16[128,2432]{1,0:T(8,128)(2,1)} %collective-permute-done.4.c2, ...), custom_call_target="tpu_custom_call" | custom-call | flops 700000000 | bytes 5000000 | tf_op jit(solution)/shard_map/class_sums/pallas_call | solution.py:304
  72.8 1.9 %collective-permute-start.12 = (bf16[37,16,256]{2,1,0:T(8,128)(2,1)S(1)}, bf16[37,16,256]{2,1,0:T(8,128)(2,1)S(1)}, u32[]{:S(2)}, u32[]{:S(2)}) collective-permute-start(bf16[37,16,256]{2,1,0:T(8,128)(2,1)S(1)} %collective-permute-done.7.refs_3_), channel_id=1, source_target_pairs={{0,1},{8,9},{1,2},{9,10},{2,3},{10,11},{3,0},{11,8},{4,5},{12,13},... | collective-permute-start | bytes 909320 | tf_op jit(solution)/shard_map/ppermute | solution.py:409
  74.8 4.0 %collective-permute-start.11 = (bf16[37,16,256]{2,1,0:T(8,128)(2,1)}, bf16[37,16,256]{2,1,0:T(8,128)(2,1)S(1)}, u32[]{:S(2)}, u32[]{:S(2)}) collective-permute-start(bf16[37,16,256]{2,1,0:T(8,128)(2,1)} %collective-permute-done.9.refs_2_), channel_id=1, source_target_pairs={{0,3},{8,11},{1,0},{9,8},{2,1},{10,9},{3,2},{11,10},{4,7},{12,15},... | collective-permute-start | bytes 909320 | tf_op jit(solution)/shard_map/ppermute | solution.py:409
  79.5 1.5 %collective-permute-start.23 = (f32[128,640]{1,0:T(8,128)S(1)}, f32[128,640]{1,0:T(8,128)S(1)}, u32[]{:S(2)}, u32[]{:S(2)}) collective-permute-start(f32[128,640]{1,0:T(8,128)S(1)} %get-tuple-element.83), channel_id=1, source_target_pairs={{0,4},{8,12},{1,5},{9,13},{2,6},{10,14},{3,7},{11,15},{4,16},{12,2... | collective-permute-start | bytes 983048 | tf_op jit(solution)/shard_map/ppermute | solution.py:409
  82.0 2.3 %collective-permute-start.25 = (f32[128,640]{1,0:T(8,128)S(1)}, f32[128,640]{1,0:T(8,128)S(1)}, u32[]{:S(2)}, u32[]{:S(2)}) collective-permute-start(f32[128,640]{1,0:T(8,128)S(1)} %get-tuple-element.85), channel_id=1, source_target_pairs={{0,20},{8,28},{1,21},{9,29},{2,22},{10,30},{3,23},{11,31},{4,0},{1... | collective-permute-start | bytes 983048 | tf_op jit(solution)/shard_map/ppermute | solution.py:409
  84.2 1.6 %collective-permute-done.11.refs_6_ = bf16[37,16,256]{2,1,0:T(8,128)(2,1)S(1)} collective-permute-done((bf16[37,16,256]{2,1,0:T(8,128)(2,1)}, bf16[37,16,256]{2,1,0:T(8,128)(2,1)S(1)}, u32[]{:S(2)}, u32[]{:S(2)}) %collective-permute-start.11) | collective-permute-done | bytes 303136 | tf_op jit(solution)/shard_map/ppermute | solution.py:409
  85.9 3.6 %collective-permute-start.13 = (bf16[37,16,256]{2,1,0:T(8,128)(2,1)S(1)}, bf16[37,16,256]{2,1,0:T(8,128)(2,1)S(1)}, u32[]{:S(2)}, u32[]{:S(2)}) collective-permute-start(bf16[37,16,256]{2,1,0:T(8,128)(2,1)S(1)} %collective-permute-done.11.refs_6_), channel_id=1, source_target_pairs={{0,3},{8,11},{1,0},{9,8},{2,1},{10,9},{3,2},{11,10},{4,7},{12,15},... | collective-permute-start | bytes 909320 | tf_op jit(solution)/shard_map/ppermute | solution.py:409
  89.5 4.9 %collective-permute-done.10.refs_5_ = bf16[37,16,256]{2,1,0:T(8,128)(2,1)S(1)} collective-permute-done((bf16[37,16,256]{2,1,0:T(8,128)(2,1)}, bf16[37,16,256]{2,1,0:T(8,128)(2,1)S(1)}, u32[]{:S(2)}, u32[]{:S(2)}) %collective-permute-start.10) | collective-permute-done | bytes 303136 | tf_op jit(solution)/shard_map/ppermute | solution.py:409
  94.3 1.0 collective-permute-done.13.refs_8_
  95.4 1.9 %collective-permute-done.23.a1 = f32[128,640]{1,0:T(8,128)S(1)} collective-permute-done((f32[128,640]{1,0:T(8,128)S(1)}, f32[128,640]{1,0:T(8,128)S(1)}, u32[]{:S(2)}, u32[]{:S(2)}) %collective-permute-start.23) | collective-permute-done | bytes 327712 | tf_op jit(solution)/shard_map/ppermute | solution.py:409
  99.2 3.6 %collective-permute-start.27 = (f32[32,640]{1,0:T(8,128)S(1)}, f32[32,640]{1,0:T(8,128)S(1)}, u32[]{:S(2)}, u32[]{:S(2)}) collective-permute-start(f32[32,640]{1,0:T(8,128)S(1)} %get-tuple-element.88), channel_id=1, source_target_pairs={{0,2},{8,10},{1,3},{9,11},{2,0},{10,8},{3,1},{11,9},{4,6},{12,14},... | collective-permute-start | bytes 245768 | tf_op jit(solution)/shard_map/ppermute | solution.py:409
  102.9 15.1 %scores.1 = f32[1,128]{1,0:T(1,128)} custom-call(bf16[37,128,256]{2,1,0:T(8,128)(2,1)S(1)} %spectra.1.refs_0_, bf16[37,16,256]{2,1,0:T(8,128)(2,1)S(1)} %ref_spectra.1.refs_1_, bf16[37,16,256]{2,1,0:T(8,128)(2,1)} %collective-permute-done.9.refs_2_, bf16[37,16,256]{2,1,0:T(8,128)(2,1)S(1)} %collective-permute-done.7.refs_3_, ...), custom_call_target="tpu_custom_call" | custom-call | flops 6000000000 | bytes 8000000 | tf_op jit(solution)/shard_map/scores/pallas_call | solution.py:261
  118.6 1.8 %final.1 = f32[25,576]{1,0:T(8,128)} custom-call(s32[4]{0:T(128)} %copy-done.18, f32[32,640]{1,0:T(8,128)} %copy-done.17, f32[32,640]{1,0:T(8,128)} %copy-done.30, f32[32,640]{1,0:T(8,128)} %copy-done.31, f32[32,640]{1,0:T(8,128)} %copy-done.32), custom_call_target="tpu_custom_call" | custom-call | tf_op jit(solution)/shard_map/final/pallas_call | solution.py:375
  (110 shorter events, 16.1 us)
Async XLA Ops:
  1.6 1.3 %collective-permute-start = (bf16[16,576]{1,0:T(8,128)(2,1)S(1)}, bf16[16,576]{1,0:T(8,128)(2,1)S(1)}, u32[]{:S(2)}, u32[]{:S(2)}) collective-permute-start(bf16[16,576]{1,0:T(8,128)(2,1)S(1)} %get-tuple-element.97), channel_id=1, source_target_pairs={{0,8},{8,0},{1,9},{9,1},{2,10},{10,2},{3,11},{11,3},{4,12},{12,4},... | collective-permute-start | bytes 55304 | tf_op jit(solution)/shard_map/ppermute | solution.py:409
  2.9 16.3 %collective-permute-start.1 = (bf16[16,1152]{1,0:T(8,128)(2,1)S(1)}, bf16[16,1152]{1,0:T(8,128)(2,1)S(1)}, u32[]{:S(2)}, u32[]{:S(2)}) collective-permute-start(bf16[16,1152]{1,0:T(8,128)(2,1)S(1)} %maximum_select_fusion), channel_id=1, source_target_pairs={{0,16},{8,24},{1,17},{9,25},{2,18},{10,26},{3,19},{11,27},{4,20},{... | collective-permute-start | bytes 110600 | tf_op jit(solution)/shard_map/ppermute | solution.py:409
  19.3 10.3 %collective-permute-start.2 = (bf16[2,16,1152]{2,1,0:T(8,128)(2,1)S(1)}, bf16[2,16,1152]{2,1,0:T(8,128)(2,1)S(1)}, u32[]{:S(2)}, u32[]{:S(2)}) collective-permute-start(bf16[2,16,1152]{2,1,0:T(8,128)(2,1)S(1)} %pad_maximum_fusion.2), channel_id=1, source_target_pairs={{0,32},{8,40},{1,33},{9,41},{2,34},{10,42},{3,35},{11,43},{4,36},{... | collective-permute-start | bytes 221192 | tf_op jit(solution)/shard_map/ppermute | solution.py:409
  29.7 7.0 %collective-permute-start.6 = (bf16[2,2,16,1152]{3,2,1,0:T(8,128)(2,1)S(1)}, bf16[2,2,16,1152]{3,2,1,0:T(8,128)(2,1)}, u32[]{:S(2)}, u32[]{:S(2)}) collective-permute-start(bf16[2,2,16,1152]{3,2,1,0:T(8,128)(2,1)S(1)} %pad_maximum_fusion.1), channel_id=1, source_target_pairs={{0,64},{8,72},{1,65},{9,73},{2,66},{10,74},{3,67},{11,75},{4,68},{... | collective-permute-start | bytes 442376 | tf_op jit(solution)/shard_map/ppermute | solution.py:409
  38.1 10.3 %collective-permute-start.9 = (bf16[37,16,256]{2,1,0:T(8,128)(2,1)S(1)}, bf16[37,16,256]{2,1,0:T(8,128)(2,1)}, u32[]{:S(2)}, u32[]{:S(2)}) collective-permute-start(bf16[37,16,256]{2,1,0:T(8,128)(2,1)S(1)} %ref_spectra.1.refs_1_), channel_id=1, source_target_pairs={{0,4},{8,12},{1,5},{9,13},{2,6},{10,14},{3,7},{11,15},{4,0},{12,8}... | collective-permute-start | bytes 909320 | tf_op jit(solution)/shard_map/ppermute | solution.py:409
  38.8 18.1 %collective-permute-start.3 = (bf16[128,2432]{1,0:T(8,128)(2,1)}, bf16[128,2432]{1,0:T(8,128)(2,1)}, u32[]{:S(2)}, u32[]{:S(2)}) collective-permute-start(bf16[128,2432]{1,0:T(8,128)(2,1)} %get-tuple-element.67), channel_id=1, source_target_pairs={{0,32},{8,40},{1,33},{9,41},{2,34},{10,42},{3,35},{11,43},{4,36},{... | collective-permute-start | bytes 1867784 | tf_op jit(solution)/shard_map/ppermute | solution.py:409
  39.2 29.2 %collective-permute-start.4 = (bf16[128,2432]{1,0:T(8,128)(2,1)}, bf16[128,2432]{1,0:T(8,128)(2,1)}, u32[]{:S(2)}, u32[]{:S(2)}) collective-permute-start(bf16[128,2432]{1,0:T(8,128)(2,1)} %get-tuple-element.68), channel_id=1, source_target_pairs={{0,64},{8,72},{1,65},{9,73},{2,66},{10,74},{3,67},{11,75},{4,68},{... | collective-permute-start | bytes 1867784 | tf_op jit(solution)/shard_map/ppermute | solution.py:409
  42.4 26.2 %collective-permute-start.5 = (bf16[128,2432]{1,0:T(8,128)(2,1)}, bf16[128,2432]{1,0:T(8,128)(2,1)}, u32[]{:S(2)}, u32[]{:S(2)}) collective-permute-start(bf16[128,2432]{1,0:T(8,128)(2,1)} %get-tuple-element.69), channel_id=1, source_target_pairs={{0,96},{8,104},{1,97},{9,105},{2,98},{10,106},{3,99},{11,107},{4,1... | collective-permute-start | bytes 1867784 | tf_op jit(solution)/shard_map/ppermute | solution.py:409
  44.4 53.5 %copy-start.18 = (s32[4]{0:T(128)}, s32[4]{0:T(128)S(1)}, u32[]{:S(2)}) copy-start(s32[4]{0:T(128)S(1)} %pad_add_fusion.sc) | copy-start | bytes 52
  44.4 24.2 %copy-start.10 = (bf16[128,2432]{1,0:T(8,128)(2,1)S(1)}, bf16[128,2432]{1,0:T(8,128)(2,1)}, u32[]{:S(2)}) copy-start(bf16[128,2432]{1,0:T(8,128)(2,1)} %copy-done.9) | copy-start | bytes 1867780
  44.4 10.0 %collective-permute-start.8 = (bf16[37,16,256]{2,1,0:T(8,128)(2,1)S(1)}, bf16[37,16,256]{2,1,0:T(8,128)(2,1)S(1)}, u32[]{:S(2)}, u32[]{:S(2)}) collective-permute-start(bf16[37,16,256]{2,1,0:T(8,128)(2,1)S(1)} %ref_spectra.1.refs_1_), channel_id=1, source_target_pairs={{0,3},{8,11},{1,0},{9,8},{2,1},{10,9},{3,2},{11,10},{4,7},{12,15},... | collective-permute-start | bytes 909320 | tf_op jit(solution)/shard_map/ppermute | solution.py:409
  48.5 8.0 %collective-permute-start.7 = (bf16[37,16,256]{2,1,0:T(8,128)(2,1)S(1)}, bf16[37,16,256]{2,1,0:T(8,128)(2,1)S(1)}, u32[]{:S(2)}, u32[]{:S(2)}) collective-permute-start(bf16[37,16,256]{2,1,0:T(8,128)(2,1)S(1)} %ref_spectra.1.refs_1_), channel_id=1, source_target_pairs={{0,1},{8,9},{1,2},{9,10},{2,3},{10,11},{3,0},{11,8},{4,5},{12,13},... | collective-permute-start | bytes 909320 | tf_op jit(solution)/shard_map/ppermute | solution.py:409
  71.6 31.2 %copy-start.29 = (bf16[576,640]{1,0:T(8,128)(2,1)S(1)}, bf16[576,640]{1,0:T(8,128)(2,1)}, u32[]{:S(2)}) copy-start(bf16[576,640]{1,0:T(8,128)(2,1)} %constant.83.clone.refs_17_) | copy-start | bytes 2211844
  71.7 3.1 %collective-permute-start.22 = (f32[2,256,640]{2,1,0:T(8,128)S(1)}, f32[2,256,640]{2,1,0:T(8,128)S(1)}, u32[]{:S(2)}, u32[]{:S(2)}) collective-permute-start(f32[2,256,640]{2,1,0:T(8,128)S(1)} %get-tuple-element.81), channel_id=1, source_target_pairs={{0,8},{8,0},{1,9},{9,1},{2,10},{10,2},{3,11},{11,3},{4,12},{12,4},... | collective-permute-start | bytes 3932168 | tf_op jit(solution)/shard_map/ppermute | solution.py:409
  71.8 7.8 %collective-permute-start.14 = (bf16[37,16,256]{2,1,0:T(8,128)(2,1)S(1)}, bf16[37,16,256]{2,1,0:T(8,128)(2,1)S(1)}, u32[]{:S(2)}, u32[]{:S(2)}) collective-permute-start(bf16[37,16,256]{2,1,0:T(8,128)(2,1)S(1)} %ref_spectra.1.refs_1_), channel_id=1, source_target_pairs={{0,8},{8,0},{1,9},{9,1},{2,10},{10,2},{3,11},{11,3},{4,12},{12,4},... | collective-permute-start | bytes 909320 | tf_op jit(solution)/shard_map/ppermute | solution.py:409
  72.2 8.8 %collective-permute-start.17 = (bf16[37,16,256]{2,1,0:T(8,128)(2,1)S(1)}, bf16[37,16,256]{2,1,0:T(8,128)(2,1)S(1)}, u32[]{:S(2)}, u32[]{:S(2)}) collective-permute-start(bf16[37,16,256]{2,1,0:T(8,128)(2,1)S(1)} %collective-permute-done.8.refs_4_), channel_id=1, source_target_pairs={{0,8},{8,0},{1,9},{9,1},{2,10},{10,2},{3,11},{11,3},{4,12},{12,4},... | collective-permute-start | bytes 909320 | tf_op jit(solution)/shard_map/ppermute | solution.py:409
  72.3 9.6 %collective-permute-start.16 = (bf16[37,16,256]{2,1,0:T(8,128)(2,1)S(1)}, bf16[37,16,256]{2,1,0:T(8,128)(2,1)S(1)}, u32[]{:S(2)}, u32[]{:S(2)}) collective-permute-start(bf16[37,16,256]{2,1,0:T(8,128)(2,1)S(1)} %collective-permute-done.7.refs_3_), channel_id=1, source_target_pairs={{0,8},{8,0},{1,9},{9,1},{2,10},{10,2},{3,11},{11,3},{4,12},{12,4},... | collective-permute-start | bytes 909320 | tf_op jit(solution)/shard_map/ppermute | solution.py:409
  72.8 11.5 %collective-permute-start.12 = (bf16[37,16,256]{2,1,0:T(8,128)(2,1)S(1)}, bf16[37,16,256]{2,1,0:T(8,128)(2,1)S(1)}, u32[]{:S(2)}, u32[]{:S(2)}) collective-permute-start(bf16[37,16,256]{2,1,0:T(8,128)(2,1)S(1)} %collective-permute-done.7.refs_3_), channel_id=1, source_target_pairs={{0,1},{8,9},{1,2},{9,10},{2,3},{10,11},{3,0},{11,8},{4,5},{12,13},... | collective-permute-start | bytes 909320 | tf_op jit(solution)/shard_map/ppermute | solution.py:409
  74.8 11.1 %collective-permute-start.11 = (bf16[37,16,256]{2,1,0:T(8,128)(2,1)}, bf16[37,16,256]{2,1,0:T(8,128)(2,1)S(1)}, u32[]{:S(2)}, u32[]{:S(2)}) collective-permute-start(bf16[37,16,256]{2,1,0:T(8,128)(2,1)} %collective-permute-done.9.refs_2_), channel_id=1, source_target_pairs={{0,3},{8,11},{1,0},{9,8},{2,1},{10,9},{3,2},{11,10},{4,7},{12,15},... | collective-permute-start | bytes 909320 | tf_op jit(solution)/shard_map/ppermute | solution.py:409
  79.5 17.8 %collective-permute-start.23 = (f32[128,640]{1,0:T(8,128)S(1)}, f32[128,640]{1,0:T(8,128)S(1)}, u32[]{:S(2)}, u32[]{:S(2)}) collective-permute-start(f32[128,640]{1,0:T(8,128)S(1)} %get-tuple-element.83), channel_id=1, source_target_pairs={{0,4},{8,12},{1,5},{9,13},{2,6},{10,14},{3,7},{11,15},{4,16},{12,2... | collective-permute-start | bytes 983048 | tf_op jit(solution)/shard_map/ppermute | solution.py:409
  81.0 16.3 %collective-permute-start.24 = (f32[128,640]{1,0:T(8,128)S(1)}, f32[128,640]{1,0:T(8,128)S(1)}, u32[]{:S(2)}, u32[]{:S(2)}) collective-permute-start(f32[128,640]{1,0:T(8,128)S(1)} %get-tuple-element.84), channel_id=1, source_target_pairs={{0,16},{8,24},{1,17},{9,25},{2,18},{10,26},{3,19},{11,27},{4,20},{... | collective-permute-start | bytes 983048 | tf_op jit(solution)/shard_map/ppermute | solution.py:409
  82.0 15.9 %collective-permute-start.25 = (f32[128,640]{1,0:T(8,128)S(1)}, f32[128,640]{1,0:T(8,128)S(1)}, u32[]{:S(2)}, u32[]{:S(2)}) collective-permute-start(f32[128,640]{1,0:T(8,128)S(1)} %get-tuple-element.85), channel_id=1, source_target_pairs={{0,20},{8,28},{1,21},{9,29},{2,22},{10,30},{3,23},{11,31},{4,0},{1... | collective-permute-start | bytes 983048 | tf_op jit(solution)/shard_map/ppermute | solution.py:409
  84.2 10.1 %collective-permute-start.10 = (bf16[37,16,256]{2,1,0:T(8,128)(2,1)}, bf16[37,16,256]{2,1,0:T(8,128)(2,1)S(1)}, u32[]{:S(2)}, u32[]{:S(2)}) collective-permute-start(bf16[37,16,256]{2,1,0:T(8,128)(2,1)} %collective-permute-done.9.refs_2_), channel_id=1, source_target_pairs={{0,1},{8,9},{1,2},{9,10},{2,3},{10,11},{3,0},{11,8},{4,5},{12,13},... | collective-permute-start | bytes 909320 | tf_op jit(solution)/shard_map/ppermute | solution.py:409
  85.9 9.5 %collective-permute-start.13 = (bf16[37,16,256]{2,1,0:T(8,128)(2,1)S(1)}, bf16[37,16,256]{2,1,0:T(8,128)(2,1)S(1)}, u32[]{:S(2)}, u32[]{:S(2)}) collective-permute-start(bf16[37,16,256]{2,1,0:T(8,128)(2,1)S(1)} %collective-permute-done.11.refs_6_), channel_id=1, source_target_pairs={{0,3},{8,11},{1,0},{9,8},{2,1},{10,9},{3,2},{11,10},{4,7},{12,15},... | collective-permute-start | bytes 909320 | tf_op jit(solution)/shard_map/ppermute | solution.py:409
  94.3 4.9 %collective-permute-start.15 = (bf16[37,16,256]{2,1,0:T(8,128)(2,1)}, bf16[37,16,256]{2,1,0:T(8,128)(2,1)S(1)}, u32[]{:S(2)}, u32[]{:S(2)}) collective-permute-start(bf16[37,16,256]{2,1,0:T(8,128)(2,1)} %collective-permute-done.9.refs_2_), channel_id=1, source_target_pairs={{0,8},{8,0},{1,9},{9,1},{2,10},{10,2},{3,11},{11,3},{4,12},{12,4},... | collective-permute-start | bytes 909320 | tf_op jit(solution)/shard_map/ppermute | solution.py:409
  95.4 3.8 %collective-permute-start.20 = (bf16[37,16,256]{2,1,0:T(8,128)(2,1)S(1)}, bf16[37,16,256]{2,1,0:T(8,128)(2,1)S(1)}, u32[]{:S(2)}, u32[]{:S(2)}) collective-permute-start(bf16[37,16,256]{2,1,0:T(8,128)(2,1)S(1)} %collective-permute-done.12.refs_7_), channel_id=1, source_target_pairs={{0,8},{8,0},{1,9},{9,1},{2,10},{10,2},{3,11},{11,3},{4,12},{12,4},... | collective-permute-start | bytes 909320 | tf_op jit(solution)/shard_map/ppermute | solution.py:409
  97.3 5.5 %collective-permute-start.19 = (bf16[37,16,256]{2,1,0:T(8,128)(2,1)S(1)}, bf16[37,16,256]{2,1,0:T(8,128)(2,1)S(1)}, u32[]{:S(2)}, u32[]{:S(2)}) collective-permute-start(bf16[37,16,256]{2,1,0:T(8,128)(2,1)S(1)} %collective-permute-done.11.refs_6_), channel_id=1, source_target_pairs={{0,8},{8,0},{1,9},{9,1},{2,10},{10,2},{3,11},{11,3},{4,12},{12,4},... | collective-permute-start | bytes 909320 | tf_op jit(solution)/shard_map/ppermute | solution.py:409
  97.3 5.5 %collective-permute-start.18 = (bf16[37,16,256]{2,1,0:T(8,128)(2,1)S(1)}, bf16[37,16,256]{2,1,0:T(8,128)(2,1)S(1)}, u32[]{:S(2)}, u32[]{:S(2)}) collective-permute-start(bf16[37,16,256]{2,1,0:T(8,128)(2,1)S(1)} %collective-permute-done.10.refs_5_), channel_id=1, source_target_pairs={{0,8},{8,0},{1,9},{9,1},{2,10},{10,2},{3,11},{11,3},{4,12},{12,4},... | collective-permute-start | bytes 909320 | tf_op jit(solution)/shard_map/ppermute | solution.py:409
  97.9 4.9 %collective-permute-start.21 = (bf16[37,16,256]{2,1,0:T(8,128)(2,1)S(1)}, bf16[37,16,256]{2,1,0:T(8,128)(2,1)S(1)}, u32[]{:S(2)}, u32[]{:S(2)}) collective-permute-start(bf16[37,16,256]{2,1,0:T(8,128)(2,1)S(1)} %collective-permute-done.13.refs_8_), channel_id=1, source_target_pairs={{0,8},{8,0},{1,9},{9,1},{2,10},{10,2},{3,11},{11,3},{4,12},{12,4},... | collective-permute-start | bytes 909320 | tf_op jit(solution)/shard_map/ppermute | solution.py:409
  99.2 18.8 %collective-permute-start.26 = (f32[32,640]{1,0:T(8,128)S(1)}, f32[32,640]{1,0:T(8,128)S(1)}, u32[]{:S(2)}, u32[]{:S(2)}) collective-permute-start(f32[32,640]{1,0:T(8,128)S(1)} %get-tuple-element.87), channel_id=1, source_target_pairs={{0,1},{8,9},{1,2},{9,10},{2,3},{10,11},{3,0},{11,8},{4,5},{12,13},... | collective-permute-start | bytes 245768 | tf_op jit(solution)/shard_map/ppermute | solution.py:409
  99.2 18.7 %collective-permute-start.27 = (f32[32,640]{1,0:T(8,128)S(1)}, f32[32,640]{1,0:T(8,128)S(1)}, u32[]{:S(2)}, u32[]{:S(2)}) collective-permute-start(f32[32,640]{1,0:T(8,128)S(1)} %get-tuple-element.88), channel_id=1, source_target_pairs={{0,2},{8,10},{1,3},{9,11},{2,0},{10,8},{3,1},{11,9},{4,6},{12,14},... | collective-permute-start | bytes 245768 | tf_op jit(solution)/shard_map/ppermute | solution.py:409
  102.8 15.1 %collective-permute-start.28 = (f32[32,640]{1,0:T(8,128)S(1)}, f32[32,640]{1,0:T(8,128)S(1)}, u32[]{:S(2)}, u32[]{:S(2)}) collective-permute-start(f32[32,640]{1,0:T(8,128)S(1)} %get-tuple-element.89), channel_id=1, source_target_pairs={{0,3},{8,11},{1,0},{9,8},{2,1},{10,9},{3,2},{11,10},{4,7},{12,15},... | collective-permute-start | bytes 245768 | tf_op jit(solution)/shard_map/ppermute | solution.py:409
  (30 other events, 219.8 us)

commit v3 on v2

--- a/solution.py
+++ b/solution.py
@@ -1,5 +1,3 @@
-import functools
-
 import jax
 import jax.numpy as jnp
 import numpy as np
@@ -18,6 +16,7 @@
 F32 = jnp.float32
 MIB = 1024 * 1024
 VMEM_LIMIT = 16 * MIB
+PREP_MIB = 56
 K_INV = 640
 
 
@@ -55,8 +54,10 @@
 COEF = cos_poly()
 
 
-def prep_kernel(first, x_ref, shift_ref, rot_ref, own_ref, off_ref, grp_ref, tab_ref, fx_ref, fy_ref, *refs):
-    w_ref, c0, c1, c2, c3, ws, us, aux, tab = refs[-9:]
+def prep_kernel(
+    x_ref, shift_ref, rot_ref, own_ref, off_ref, grp_ref, tab_ref, fx_ref, fy_ref,
+    w_ref, c0, c1, c2, c3, ws, us, aux, tab,
+):
     dom, cls = lax.axis_index("dom"), lax.axis_index("cls")
     mine = 2 * (dom * 8 + cls)
     step = pl.program_id(0)
@@ -77,7 +78,7 @@
         flipped = tab_ref[...].T
         tab[...] = jnp.concatenate([flipped, flipped], axis=1)
 
-    here = aux[pl.ds(pl.multiple_of((step + first) * 16, 16), 16), :]
+    here = aux[pl.ds(pl.multiple_of(step * 16, 16), 16), :]
     lane = lax.broadcasted_iota(jnp.int32, (16, 128), 1)
     left = lane < R
     shift = jnp.where(left, 0.0, -0.25).astype(F32)
@@ -134,22 +135,16 @@
         c_ref[:, width : width + 128] = meta
 
 
-def prep(particles, rows, table, fx, fy, first, steps, held=None):
+def prep(particles, rows, table, fx, fy):
     n = particles.shape[0]
     whole = lambda a: pl.BlockSpec(a.shape, lambda i: (0,) * a.ndim)
-    block = lambda i: (i + first, 0)
+    block = lambda i: (i, 0)
     args = [particles, *rows, table, fx, fy]
-    specs = [pl.BlockSpec((16, A * 128), block)] + [whole(a) for a in args[1:]]
-    alias = {}
-    if held is not None:
-        alias = {len(args) + i: i for i in range(5)}
-        args += held
-        specs += [pl.BlockSpec(memory_space=pl.ANY)] * 5
-    return pl.pallas_call(
-        functools.partial(prep_kernel, first),
-        grid=(steps,),
-        in_specs=specs,
-        out_specs=[pl.BlockSpec((2, A * 8, 128), lambda i: (i + first, 0, 0))]
+    return pl.pallas_call(
+        prep_kernel,
+        grid=(n // 16,),
+        in_specs=[pl.BlockSpec((16, A * 128), block)] + [whole(a) for a in args[1:]],
+        out_specs=[pl.BlockSpec((2, A * 8, 128), lambda i: (i, 0, 0))]
         + [pl.BlockSpec((16, 19 * 128), block)] * 4,
         scratch_shapes=[
             pltpu.VMEM((16, A * 128), F32),
@@ -159,10 +154,9 @@
         ],
         out_shape=[jax.ShapeDtypeStruct((n // 8, A * 8, 128), BF)]
         + [jax.ShapeDtypeStruct((n, 19 * 128), BF)] * 4,
-        input_output_aliases=alias,
-        compiler_params=pltpu.CompilerParams(vmem_limit_bytes=8 * MIB),
+        compiler_params=pltpu.CompilerParams(vmem_limit_bytes=PREP_MIB * MIB),
         cost_estimate=pl.CostEstimate(
-            flops=5_000_000 * steps, bytes_accessed=1_000_000 * steps, transcendentals=0
+            flops=40_000_000, bytes_accessed=8_000_000, transcendentals=0
         ),
         name="prep",
     )(*args)
@@ -190,7 +184,7 @@
         out_shape=jax.ShapeDtypeStruct((M, 128, 256), BF),
         scratch_shapes=[pltpu.VMEM((2 * M * 8, 2048), F32)],
         compiler_params=pltpu.CompilerParams(vmem_limit_bytes=16 * MIB),
-        cost_estimate=pl.CostEstimate(flops=4_000_000_000, bytes_accessed=5_000_000, transcendentals=0),
+        cost_estimate=pl.CostEstimate(flops=1000, bytes_accessed=1000, transcendentals=0),
         name="spectra",
     )(w, fwd_k)
 
@@ -221,13 +215,13 @@
         out_shape=jax.ShapeDtypeStruct((M, 16, 256), BF),
         scratch_shapes=[pltpu.VMEM((A * 8, 256), F32)],
         compiler_params=pltpu.CompilerParams(vmem_limit_bytes=8 * MIB),
-        cost_estimate=pl.CostEstimate(flops=200_000_000, bytes_accessed=1_500_000, transcendentals=0),
+        cost_estimate=pl.CostEstimate(flops=1000, bytes_accessed=1000, transcendentals=0),
         name="ref_spectra",
     )(blocks, fwd_k)
 
 
 def score_kernel(*refs):
-    p_ref, blocks, inv_ref, o_ref, xs = refs[0], refs[1:17], refs[17], refs[18], refs[19]
+    p_ref, blocks, inv_ref, o_ref, xs = refs[0], refs[1:5], refs[5], refs[6], refs[7]
     xs[:, 2 * M * 8 :, :] = jnp.zeros((16, K_INV - 2 * M * 8, 256), BF)
 
     @pl.loop(0, M)
@@ -235,7 +229,7 @@
         upper = p_ref[m]
         re, im = upper[:, 0:128], upper[:, 128:256]
         rhs = jnp.concatenate([upper, jnp.concatenate([im, -re], axis=1)], axis=0)
-        lhs = jnp.concatenate([b[m] for b in blocks], axis=0)
+        lhs = jnp.concatenate([b[i, m] for b in blocks for i in range(4)], axis=0)
         x = jnp.dot(lhs, rhs, preferred_element_type=F32)
         row = pl.multiple_of(m * 16, 16)
         for g in range(16):
@@ -260,7 +254,7 @@
     v = pl.BlockSpec(memory_space=pltpu.VMEM)
     return pl.pallas_call(
         score_kernel,
-        in_specs=[v] * 18,
+        in_specs=[v] * 6,
         out_specs=v,
         out_shape=jax.ShapeDtypeStruct((1, 128), F32),
         scratch_shapes=[pltpu.VMEM((16, K_INV, 256), BF)],
@@ -434,14 +428,11 @@
     rows = [shifts.T, rotation[None], owner.T, class_offset[None], ctf_group[None]]
     table = ctf_table.T
     block, rows[1] = lax.optimization_barrier((block, rows[1]))
-    held = prep(particles, rows, table, fx, fy, 0, 4)
+    weighted, *sent = prep(particles, rows, table, fx, fy)
     far = move(block, HIGH)
-    far, *held = lax.optimization_barrier((far, *held))
+    far, weighted, *sent = lax.optimization_barrier((far, weighted, *sent))
     pair = join(block, far, xh)
-    pair, rows[1] = lax.optimization_barrier((pair, rows[1]))
-    weighted, *sent = prep(particles, rows, table, fx, fy, 4, 4, held)
     near = move(pair, Y_NEAR)
-    near, weighted, *sent = lax.optimization_barrier((near, weighted, *sent))
     quad = join(pair, near, y % 2)
     octet = join(quad, move(quad, Y_FAR), y // 2).reshape(4, 2, 16, 1152)
 
@@ -451,18 +442,21 @@
     own = ref_spectra(octet, fwd_k)
     up, down = move(own, ZS[1]), move(own, ZS[3])
     side = move(own, LOW)
-    *held, up, down, side, part = lax.optimization_barrier((*held, up, down, side, part))
     side_up, side_down = move(side, ZS[1]), move(side, ZS[3])
-    line = [own, side, up, down, side_up, side_down, move(up, ZS[1]), move(side_down, ZS[3])]
-    line = line + [move(b, CORE) for b in line]
-    scores = scores_of(part, line, inv_k)[0]
-
+    *held, side, up, down, part = lax.optimization_barrier((*held, side, up, down, part))
+    on_up, on_down = move(up, ZS[1]), move(side_down, ZS[3])
+    early, late = jnp.stack([own, side, up, down]), jnp.stack([side_up, side_down, on_up, on_down])
+    early_twin, late_twin = move(early, CORE), move(late, CORE)
+    *held, late_twin, early_twin = lax.optimization_barrier((*held, late_twin, early_twin))
     mine, other = class_sums(sc, held, table)
-    cut = cut_x(sc, mine, move(other, CORE))
+    other = move(other, CORE)
+    cut = cut_x(sc, mine, other)
     cut = [cut[0]] + [move(cut[d], XS[d]) for d in (1, 2, 3)]
+    scores = scores_of(part, [early, early_twin, late, late_twin], inv_k)
+    *cut, scores = lax.optimization_barrier((*cut, scores))
     cut = cut_z(sc, cut)
     cut = [cut[0]] + [move(cut[d], ZS[d]) for d in (1, 2, 3)]
-    return scores, final(sc, cut)
+    return scores[0], final(sc, cut)
 
 
 def solution(mesh):

time: 122 us -> 110 us (0.902)
  local copies, waits for them, and re-layouts: 15.9 us -> 4.5 us
  starting transfers between devices: 37.7 us -> 31.8 us
  waiting for transfers between devices: 29.2 us -> 32.3 us
  Pallas kernels: 34.7 us -> 36.5 us
  other arithmetic: 2.05 us -> 3.54 us
    unnamed x66 -> x32, local copies, waits for them, and re-layouts: 15.9 us -> 4.5 us
    ppermute x29 -> x23, starting transfers between devices: 37.7 us -> 31.8 us  [move(): return lax.ppermute(value, AXES, pairs)]
    ppermute x29 -> x23, waiting for transfers between devices: 29.2 us -> 32.3 us  [move(): return lax.ppermute(value, AXES, pairs)]
    pallas_call x3 -> x2, Pallas kernels: 22.3 us -> 24.9 us  [the longest x1 16.4 us: scores_of(): pl.pallas_call(score_kernel, in_specs=[v] * 6, out_specs=v, out_shape=jax...]
    another operation x0 -> x2, other arithmetic: none -> 2.4 us  [the longest x1 1.2 us: per_device(): jnp.stack([own, side, up, down])]
  transfers between devices with their start and end apart: 29 -> 23, of which waited for: 12 -> 13; matrix products, arithmetic and copies ran while one was open for 0% -> 2% of each run, Pallas kernels for 24% -> 29%
where the time goes in v3:
time: 110 us; the launch traced here: 109 us
  Pallas kernels  36.5 us (33%)
  waiting for transfers between devices  32.3 us (29%)
  starting transfers between devices  31.8 us (29%)
  local copies, waits for them, and re-layouts  4.5 us (4%)
  other arithmetic  3.54 us (3%)
    ppermute x23, waiting for transfers between devices, move(): return lax.ppermute(value, AXES, pairs)  32.3 us
    ppermute x23, starting transfers between devices, move(): return lax.ppermute(value, AXES, pairs)  31.8 us
    pallas_call x1, Pallas kernels, scores_of(): pl.pallas_call(score_kernel, in_specs=[v] * 6, out_specs=v, out_shape=jax...  16.4 us
    pallas_call x1, Pallas kernels, prep(): pl.pallas_call(prep_kernel, grid=(n // 16,), in_specs=[pl.BlockSpec((16,...  8.52 us
    pallas_call x1, Pallas kernels, spectra(): pl.pallas_call(spectra_kernel, in_specs=[v, v], out_specs=v, out_shape=ja...  5.88 us
    unnamed x32, local copies, waits for them, and re-layouts  4.5 us
  transfers between devices with their start and end apart: 23, of which 13 were waited for; matrix products, arithmetic and copies ran while one was open for 2% of the time, Pallas kernels for 29%

profile of v3, /device:TPU:0, one launch (start us, length us, event | category | flops | bytes accessed | tf_op | source)
XLA Modules:
  0.0 109.4 jit_solution(12620090066577069519)
XLA Ops:
  1.6 1.2 %collective-permute-done = bf16[16,576]{1,0:T(8,128)(2,1)S(1)} collective-permute-done((bf16[16,576]{1,0:T(8,128)(2,1)S(1)}, bf16[16,576]{1,0:T(8,128)(2,1)S(1)}, u32[]{:S(2)}, u32[]{:S(2)}) %collective-permute-start) | collective-permute-done | bytes 18464 | tf_op jit(solution)/shard_map/ppermute | solution.py:403
  2.9 3.2 %collective-permute-start.1 = (bf16[16,1152]{1,0:T(8,128)(2,1)S(1)}, bf16[16,1152]{1,0:T(8,128)(2,1)S(1)}, u32[]{:S(2)}, u32[]{:S(2)}) collective-permute-start(bf16[16,1152]{1,0:T(8,128)(2,1)S(1)} %maximum_select_fusion), channel_id=1, source_target_pairs={{0,16},{8,24},{1,17},{9,25},{2,18},{10,26},{3,19},{11,27},{4,20},{... | collective-permute-start | bytes 110600 | tf_op jit(solution)/shard_map/ppermute | solution.py:403
  6.0 8.5 %prep.1 = (bf16[16,576,128]{2,1,0:T(8,128)(2,1)}, bf16[128,2432]{1,0:T(8,128)(2,1)}, bf16[128,2432]{1,0:T(8,128)(2,1)}, bf16[128,2432]{1,0:T(8,128)(2,1)}, bf16[128,2432]{1,0:T(8,128)(2,1)}) custom-call(bf16[128,9216]{1,0:T(8,128)(2,1)} %x_ref.1, s32[2,128]{1,0:T(2,128)} %bitcast.43, s32[1,128]{1,0:T(1,128)} %bitcast.44, s32[1,128]{1,0:T(1,128)} %bitcast.45, ...), custom_call_target="tpu_custom_call" | custom-call | flops 40000000 | bytes 8000000 | tf_op jit(solution)/shard_map/prep/pallas_call | solution.py:143
  14.6 1.7 %collective-permute-start.5 = (bf16[2,16,1152]{2,1,0:T(8,128)(2,1)S(1)}, bf16[2,16,1152]{2,1,0:T(8,128)(2,1)S(1)}, u32[]{:S(2)}, u32[]{:S(2)}) collective-permute-start(bf16[2,16,1152]{2,1,0:T(8,128)(2,1)S(1)} %pad_maximum_fusion.4), channel_id=1, source_target_pairs={{0,32},{8,40},{1,33},{9,41},{2,34},{10,42},{3,35},{11,43},{4,36},{... | collective-permute-start | bytes 221192 | tf_op jit(solution)/shard_map/ppermute | solution.py:403
  16.3 2.8 %collective-permute-done.5 = bf16[2,16,1152]{2,1,0:T(8,128)(2,1)S(1)} collective-permute-done((bf16[2,16,1152]{2,1,0:T(8,128)(2,1)S(1)}, bf16[2,16,1152]{2,1,0:T(8,128)(2,1)S(1)}, u32[]{:S(2)}, u32[]{:S(2)}) %collective-permute-start.5) | collective-permute-done | bytes 73760 | tf_op jit(solution)/shard_map/ppermute | solution.py:403
  19.1 3.3 %collective-permute-start.6 = (bf16[2,2,16,1152]{3,2,1,0:T(8,128)(2,1)S(1)}, bf16[2,2,16,1152]{3,2,1,0:T(8,128)(2,1)S(1)}, u32[]{:S(2)}, u32[]{:S(2)}) collective-permute-start(bf16[2,2,16,1152]{3,2,1,0:T(8,128)(2,1)S(1)} %pad_maximum_fusion.3), channel_id=1, source_target_pairs={{0,64},{8,72},{1,65},{9,73},{2,66},{10,74},{3,67},{11,75},{4,68},{... | collective-permute-start | bytes 442376 | tf_op jit(solution)/shard_map/ppermute | solution.py:403
  23.1 1.8 %collective-permute-start.3 = (bf16[128,2432]{1,0:T(8,128)(2,1)}, bf16[128,2432]{1,0:T(8,128)(2,1)S(1)}, u32[]{:S(2)}, u32[]{:S(2)}) collective-permute-start(bf16[128,2432]{1,0:T(8,128)(2,1)} %get-tuple-element.53), channel_id=1, source_target_pairs={{0,64},{8,72},{1,65},{9,73},{2,66},{10,74},{3,67},{11,75},{4,68},{... | collective-permute-start | bytes 1867784 | tf_op jit(solution)/shard_map/ppermute | solution.py:403
  25.7 1.7 %collective-permute-done.6 = bf16[2,2,16,1152]{3,2,1,0:T(8,128)(2,1)S(1)} collective-permute-done((bf16[2,2,16,1152]{3,2,1,0:T(8,128)(2,1)S(1)}, bf16[2,2,16,1152]{3,2,1,0:T(8,128)(2,1)S(1)}, u32[]{:S(2)}, u32[]{:S(2)}) %collective-permute-start.6) | collective-permute-done | bytes 147488 | tf_op jit(solution)/shard_map/ppermute | solution.py:403
  27.9 4.1 %collective-permute-start.9 = (bf16[37,16,256]{2,1,0:T(8,128)(2,1)S(1)}, bf16[37,16,256]{2,1,0:T(8,128)(2,1)S(1)}, u32[]{:S(2)}, u32[]{:S(2)}) collective-permute-start(bf16[37,16,256]{2,1,0:T(8,128)(2,1)S(1)} %ref_spectra.1), channel_id=1, source_target_pairs={{0,3},{8,11},{1,0},{9,8},{2,1},{10,9},{3,2},{11,10},{4,7},{12,15},... | collective-permute-start | bytes 909320 | tf_op jit(solution)/shard_map/ppermute | solution.py:403
  32.6 4.5 %collective-permute-done.9 = bf16[37,16,256]{2,1,0:T(8,128)(2,1)S(1)} collective-permute-done((bf16[37,16,256]{2,1,0:T(8,128)(2,1)S(1)}, bf16[37,16,256]{2,1,0:T(8,128)(2,1)S(1)}, u32[]{:S(2)}, u32[]{:S(2)}) %collective-permute-start.9) | collective-permute-done | bytes 303136 | tf_op jit(solution)/shard_map/ppermute | solution.py:403
  37.1 1.7 %collective-permute-done.7 = bf16[37,16,256]{2,1,0:T(8,128)(2,1)S(1)} collective-permute-done((bf16[37,16,256]{2,1,0:T(8,128)(2,1)S(1)}, bf16[37,16,256]{2,1,0:T(8,128)(2,1)S(1)}, u32[]{:S(2)}, u32[]{:S(2)}) %collective-permute-start.7) | collective-permute-done | bytes 303136 | tf_op jit(solution)/shard_map/ppermute | solution.py:403
  38.8 2.0 %collective-permute-start.11 = (bf16[37,16,256]{2,1,0:T(8,128)(2,1)S(1)}, bf16[37,16,256]{2,1,0:T(8,128)(2,1)S(1)}, u32[]{:S(2)}, u32[]{:S(2)}) collective-permute-start(bf16[37,16,256]{2,1,0:T(8,128)(2,1)S(1)} %collective-permute-done.7), channel_id=1, source_target_pairs={{0,3},{8,11},{1,0},{9,8},{2,1},{10,9},{3,2},{11,10},{4,7},{12,15},... | collective-permute-start | bytes 909320 | tf_op jit(solution)/shard_map/ppermute | solution.py:403
  40.8 5.9 %spectra.1.refs_0_ = bf16[37,128,256]{2,1,0:T(8,128)(2,1)S(1)} custom-call(bf16[16,576,128]{2,1,0:T(8,128)(2,1)S(1)} %copy-done.1, bf16[592,576]{1,0:T(8,128)(2,1)S(1)} %copy-done), custom_call_target="tpu_custom_call" | custom-call | flops 1000 | bytes 1000 | tf_op jit(solution)/shard_map/spectra/pallas_call | solution.py:180
  46.8 6.0 %collective-permute-done.2.c1 = bf16[128,2432]{1,0:T(8,128)(2,1)S(1)} collective-permute-done((bf16[128,2432]{1,0:T(8,128)(2,1)}, bf16[128,2432]{1,0:T(8,128)(2,1)S(1)}, u32[]{:S(2)}, u32[]{:S(2)}) %collective-permute-start.2) | collective-permute-done | bytes 622624 | tf_op jit(solution)/shard_map/ppermute | solution.py:403
  52.9 1.9 %collective-permute-start.12 = (bf16[37,16,256]{2,1,0:T(8,128)(2,1)S(1)}, bf16[37,16,256]{2,1,0:T(8,128)(2,1)S(1)}, u32[]{:S(2)}, u32[]{:S(2)}) collective-permute-start(bf16[37,16,256]{2,1,0:T(8,128)(2,1)S(1)} %collective-permute-done.8), channel_id=1, source_target_pairs={{0,1},{8,9},{1,2},{9,10},{2,3},{10,11},{3,0},{11,8},{4,5},{12,13},... | collective-permute-start | bytes 909320 | tf_op jit(solution)/shard_map/ppermute | solution.py:403
  54.8 2.2 %collective-permute-start.13 = (bf16[37,16,256]{2,1,0:T(8,128)(2,1)S(1)}, bf16[37,16,256]{2,1,0:T(8,128)(2,1)S(1)}, u32[]{:S(2)}, u32[]{:S(2)}) collective-permute-start(bf16[37,16,256]{2,1,0:T(8,128)(2,1)S(1)} %collective-permute-done.11), channel_id=1, source_target_pairs={{0,3},{8,11},{1,0},{9,8},{2,1},{10,9},{3,2},{11,10},{4,7},{12,15},... | collective-permute-start | bytes 909320 | tf_op jit(solution)/shard_map/ppermute | solution.py:403
  57.0 1.2 %pad_maximum_fusion.1.refs_1_ = bf16[4,37,16,256]{3,2,1,0:T(8,128)(2,1)} fusion(bf16[1,37,16,256]{3,2,1,0:T(8,128)(2,1)S(1)} %bitcast.37, bf16[1,37,16,256]{3,2,1,0:T(8,128)(2,1)S(1)} %bitcast.39, bf16[1,37,16,256]{3,2,1,0:T(8,128)(2,1)S(1)} %bitcast.36, bf16[1,37,16,256]{3,2,1,0:T(8,128)(2,1)S(1)} %bitcast.32), kind=kLoop, calls=%fused_computation.1 | loop fusion | flops 1818624 | bytes 2424832 | tf_op jit(solution)/shard_map/stack | solution.py:448
  58.3 5.0 %collective-permute-done.12 = bf16[37,16,256]{2,1,0:T(8,128)(2,1)S(1)} collective-permute-done((bf16[37,16,256]{2,1,0:T(8,128)(2,1)S(1)}, bf16[37,16,256]{2,1,0:T(8,128)(2,1)S(1)}, u32[]{:S(2)}, u32[]{:S(2)}) %collective-permute-start.12) | collective-permute-done | bytes 303136 | tf_op jit(solution)/shard_map/ppermute | solution.py:403
  63.4 1.2 %pad_maximum_fusion.refs_3_ = bf16[4,37,16,256]{3,2,1,0:T(8,128)(2,1)} fusion(bf16[1,37,16,256]{3,2,1,0:T(8,128)(2,1)S(1)} %bitcast.42, bf16[1,37,16,256]{3,2,1,0:T(8,128)(2,1)S(1)} %bitcast.41, bf16[1,37,16,256]{3,2,1,0:T(8,128)(2,1)S(1)} %bitcast.38, bf16[1,37,16,256]{3,2,1,0:T(8,128)(2,1)S(1)} %bitcast.40), kind=kLoop, calls=%fused_computation | loop fusion | flops 1818624 | bytes 2424832 | tf_op jit(solution)/shard_map/stack | solution.py:448
  64.6 3.2 %collective-permute-done.14.refs_4_ = bf16[4,37,16,256]{3,2,1,0:T(8,128)(2,1)} collective-permute-done((bf16[4,37,16,256]{3,2,1,0:T(8,128)(2,1)}, bf16[4,37,16,256]{3,2,1,0:T(8,128)(2,1)}, u32[]{:S(2)}, u32[]{:S(2)}) %collective-permute-start.14) | collective-permute-done | bytes 1212448 | tf_op jit(solution)/shard_map/ppermute | solution.py:403
  67.8 1.1 copy-done.7
  68.9 1.1 copy-done.9
  70.0 1.1 copy-done.11
  71.0 2.1 %class_sums.1 = (f32[2,256,640]{2,1,0:T(8,128)S(1)}, f32[2,256,640]{2,1,0:T(8,128)S(1)}) custom-call(s32[4]{0:T(128)S(1)} %pad_add_fusion.sc, bf16[128,2432]{1,0:T(8,128)(2,1)S(1)} %copy-done.5, bf16[128,2432]{1,0:T(8,128)(2,1)S(1)} %copy-done.7, bf16[128,2432]{1,0:T(8,128)(2,1)S(1)} %copy-done.9, bf16[128,2432]{1,0:T(8,128)(2,1)S(1)} %copy-done.11, ...), custom_call_target="tpu_custom_call" | custom-call | flops 700000000 | bytes 5000000 | tf_op jit(solution)/shard_map/class_sums/pallas_call | solution.py:298
  73.4 2.9 %collective-permute-done.16.b_ref = f32[2,256,640]{2,1,0:T(8,128)S(1)} collective-permute-done((f32[2,256,640]{2,1,0:T(8,128)S(1)}, f32[2,256,640]{2,1,0:T(8,128)S(1)}, u32[]{:S(2)}, u32[]{:S(2)}) %collective-permute-start.16) | collective-permute-done | bytes 1310752 | tf_op jit(solution)/shard_map/ppermute | solution.py:403
  77.6 2.0 %collective-permute-start.18 = (f32[128,640]{1,0:T(8,128)S(1)}, f32[128,640]{1,0:T(8,128)S(1)}, u32[]{:S(2)}, u32[]{:S(2)}) collective-permute-start(f32[128,640]{1,0:T(8,128)S(1)} %get-tuple-element.72), channel_id=1, source_target_pairs={{0,16},{8,24},{1,17},{9,25},{2,18},{10,26},{3,19},{11,27},{4,20},{... | collective-permute-start | bytes 983048 | tf_op jit(solution)/shard_map/ppermute | solution.py:403
  80.4 16.4 %scores.1 = f32[1,128]{1,0:T(1,128)} custom-call(bf16[37,128,256]{2,1,0:T(8,128)(2,1)S(1)} %spectra.1.refs_0_, bf16[4,37,16,256]{3,2,1,0:T(8,128)(2,1)} %pad_maximum_fusion.1.refs_1_, bf16[4,37,16,256]{3,2,1,0:T(8,128)(2,1)} %collective-permute-done.15.refs_2_, bf16[4,37,16,256]{3,2,1,0:T(8,128)(2,1)} %pad_maximum_fusion.refs_3_, ...), custom_call_target="tpu_custom_call" | custom-call | flops 6000000000 | bytes 8000000 | tf_op jit(solution)/shard_map/scores/pallas_call | solution.py:255
  98.1 1.3 %collective-permute-start.20 = (f32[32,640]{1,0:T(8,128)S(1)}, f32[32,640]{1,0:T(8,128)S(1)}, u32[]{:S(2)}, u32[]{:S(2)}) collective-permute-start(f32[32,640]{1,0:T(8,128)S(1)} %get-tuple-element.83), channel_id=1, source_target_pairs={{0,1},{8,9},{1,2},{9,10},{2,3},{10,11},{3,0},{11,8},{4,5},{12,13},... | collective-permute-start | bytes 245768 | tf_op jit(solution)/shard_map/ppermute | solution.py:403
  99.3 3.2 %collective-permute-start.21 = (f32[32,640]{1,0:T(8,128)S(1)}, f32[32,640]{1,0:T(8,128)S(1)}, u32[]{:S(2)}, u32[]{:S(2)}) collective-permute-start(f32[32,640]{1,0:T(8,128)S(1)} %get-tuple-element.84), channel_id=1, source_target_pairs={{0,2},{8,10},{1,3},{9,11},{2,0},{10,8},{3,1},{11,9},{4,6},{12,14},... | collective-permute-start | bytes 245768 | tf_op jit(solution)/shard_map/ppermute | solution.py:403
  102.6 1.1 collective-permute-start.22
  104.4 1.8 %collective-permute-done.21.a2 = f32[32,640]{1,0:T(8,128)S(1)} collective-permute-done((f32[32,640]{1,0:T(8,128)S(1)}, f32[32,640]{1,0:T(8,128)S(1)}, u32[]{:S(2)}, u32[]{:S(2)}) %collective-permute-start.21) | collective-permute-done | bytes 81952 | tf_op jit(solution)/shard_map/ppermute | solution.py:403
  107.6 1.8 %final.1 = f32[25,576]{1,0:T(8,128)} custom-call(s32[4]{0:T(128)} %copy-done.4, f32[32,640]{1,0:T(8,128)} %copy-done.2, f32[32,640]{1,0:T(8,128)} %copy-done.13, f32[32,640]{1,0:T(8,128)} %copy-done.14, f32[32,640]{1,0:T(8,128)} %copy-done.15), custom_call_target="tpu_custom_call" | custom-call | tf_op jit(solution)/shard_map/final/pallas_call | solution.py:369
  (65 shorter events, 9.9 us)
Async XLA Ops:
  1.5 1.3 %collective-permute-start = (bf16[16,576]{1,0:T(8,128)(2,1)S(1)}, bf16[16,576]{1,0:T(8,128)(2,1)S(1)}, u32[]{:S(2)}, u32[]{:S(2)}) collective-permute-start(bf16[16,576]{1,0:T(8,128)(2,1)S(1)} %get-tuple-element.93), channel_id=1, source_target_pairs={{0,8},{8,0},{1,9},{9,1},{2,10},{10,2},{3,11},{11,3},{4,12},{12,4},... | collective-permute-start | bytes 55304 | tf_op jit(solution)/shard_map/ppermute | solution.py:403
  2.9 11.7 %collective-permute-start.1 = (bf16[16,1152]{1,0:T(8,128)(2,1)S(1)}, bf16[16,1152]{1,0:T(8,128)(2,1)S(1)}, u32[]{:S(2)}, u32[]{:S(2)}) collective-permute-start(bf16[16,1152]{1,0:T(8,128)(2,1)S(1)} %maximum_select_fusion), channel_id=1, source_target_pairs={{0,16},{8,24},{1,17},{9,25},{2,18},{10,26},{3,19},{11,27},{4,20},{... | collective-permute-start | bytes 110600 | tf_op jit(solution)/shard_map/ppermute | solution.py:403
  14.6 12.9 %copy-start = (bf16[592,576]{1,0:T(8,128)(2,1)S(1)}, bf16[592,576]{1,0:T(8,128)(2,1)}, u32[]{:S(2)}) copy-start(bf16[592,576]{1,0:T(8,128)(2,1)} %constant.82.clone.f_ref) | copy-start | bytes 2045956
  14.6 4.4 %collective-permute-start.5 = (bf16[2,16,1152]{2,1,0:T(8,128)(2,1)S(1)}, bf16[2,16,1152]{2,1,0:T(8,128)(2,1)S(1)}, u32[]{:S(2)}, u32[]{:S(2)}) collective-permute-start(bf16[2,16,1152]{2,1,0:T(8,128)(2,1)S(1)} %pad_maximum_fusion.4), channel_id=1, source_target_pairs={{0,32},{8,40},{1,33},{9,41},{2,34},{10,42},{3,35},{11,43},{4,36},{... | collective-permute-start | bytes 221192 | tf_op jit(solution)/shard_map/ppermute | solution.py:403
  19.1 8.3 %collective-permute-start.6 = (bf16[2,2,16,1152]{3,2,1,0:T(8,128)(2,1)S(1)}, bf16[2,2,16,1152]{3,2,1,0:T(8,128)(2,1)S(1)}, u32[]{:S(2)}, u32[]{:S(2)}) collective-permute-start(bf16[2,2,16,1152]{3,2,1,0:T(8,128)(2,1)S(1)} %pad_maximum_fusion.3), channel_id=1, source_target_pairs={{0,64},{8,72},{1,65},{9,73},{2,66},{10,74},{3,67},{11,75},{4,68},{... | collective-permute-start | bytes 442376 | tf_op jit(solution)/shard_map/ppermute | solution.py:403
  22.4 18.4 %copy-start.1 = (bf16[16,576,128]{2,1,0:T(8,128)(2,1)S(1)}, bf16[16,576,128]{2,1,0:T(8,128)(2,1)}, u32[]{:S(2)}) copy-start(bf16[16,576,128]{2,1,0:T(8,128)(2,1)} %get-tuple-element.56.w_ref) | copy-start | bytes 7077892
  22.4 30.4 %collective-permute-start.2 = (bf16[128,2432]{1,0:T(8,128)(2,1)}, bf16[128,2432]{1,0:T(8,128)(2,1)S(1)}, u32[]{:S(2)}, u32[]{:S(2)}) collective-permute-start(bf16[128,2432]{1,0:T(8,128)(2,1)} %get-tuple-element.52), channel_id=1, source_target_pairs={{0,32},{8,40},{1,33},{9,41},{2,34},{10,42},{3,35},{11,43},{4,36},{... | collective-permute-start | bytes 1867784 | tf_op jit(solution)/shard_map/ppermute | solution.py:403
  23.1 29.8 %collective-permute-start.3 = (bf16[128,2432]{1,0:T(8,128)(2,1)}, bf16[128,2432]{1,0:T(8,128)(2,1)S(1)}, u32[]{:S(2)}, u32[]{:S(2)}) collective-permute-start(bf16[128,2432]{1,0:T(8,128)(2,1)} %get-tuple-element.53), channel_id=1, source_target_pairs={{0,64},{8,72},{1,65},{9,73},{2,66},{10,74},{3,67},{11,75},{4,68},{... | collective-permute-start | bytes 1867784 | tf_op jit(solution)/shard_map/ppermute | solution.py:403
  24.9 28.0 %collective-permute-start.4 = (bf16[128,2432]{1,0:T(8,128)(2,1)}, bf16[128,2432]{1,0:T(8,128)(2,1)S(1)}, u32[]{:S(2)}, u32[]{:S(2)}) collective-permute-start(bf16[128,2432]{1,0:T(8,128)(2,1)} %get-tuple-element.54), channel_id=1, source_target_pairs={{0,96},{8,104},{1,97},{9,105},{2,98},{10,106},{3,99},{11,107},{4,1... | collective-permute-start | bytes 1867784 | tf_op jit(solution)/shard_map/ppermute | solution.py:403
  27.9 9.2 %collective-permute-start.9 = (bf16[37,16,256]{2,1,0:T(8,128)(2,1)S(1)}, bf16[37,16,256]{2,1,0:T(8,128)(2,1)S(1)}, u32[]{:S(2)}, u32[]{:S(2)}) collective-permute-start(bf16[37,16,256]{2,1,0:T(8,128)(2,1)S(1)} %ref_spectra.1), channel_id=1, source_target_pairs={{0,3},{8,11},{1,0},{9,8},{2,1},{10,9},{3,2},{11,10},{4,7},{12,15},... | collective-permute-start | bytes 909320 | tf_op jit(solution)/shard_map/ppermute | solution.py:403
  32.0 6.8 %collective-permute-start.7 = (bf16[37,16,256]{2,1,0:T(8,128)(2,1)S(1)}, bf16[37,16,256]{2,1,0:T(8,128)(2,1)S(1)}, u32[]{:S(2)}, u32[]{:S(2)}) collective-permute-start(bf16[37,16,256]{2,1,0:T(8,128)(2,1)S(1)} %ref_spectra.1), channel_id=1, source_target_pairs={{0,4},{8,12},{1,5},{9,13},{2,6},{10,14},{3,7},{11,15},{4,0},{12,8}... | collective-permute-start | bytes 909320 | tf_op jit(solution)/shard_map/ppermute | solution.py:403
  37.1 9.6 %collective-permute-start.8 = (bf16[37,16,256]{2,1,0:T(8,128)(2,1)S(1)}, bf16[37,16,256]{2,1,0:T(8,128)(2,1)S(1)}, u32[]{:S(2)}, u32[]{:S(2)}) collective-permute-start(bf16[37,16,256]{2,1,0:T(8,128)(2,1)S(1)} %ref_spectra.1), channel_id=1, source_target_pairs={{0,1},{8,9},{1,2},{9,10},{2,3},{10,11},{3,0},{11,8},{4,5},{12,13},... | collective-permute-start | bytes 909320 | tf_op jit(solution)/shard_map/ppermute | solution.py:403
  38.8 16.0 %collective-permute-start.11 = (bf16[37,16,256]{2,1,0:T(8,128)(2,1)S(1)}, bf16[37,16,256]{2,1,0:T(8,128)(2,1)S(1)}, u32[]{:S(2)}, u32[]{:S(2)}) collective-permute-start(bf16[37,16,256]{2,1,0:T(8,128)(2,1)S(1)} %collective-permute-done.7), channel_id=1, source_target_pairs={{0,3},{8,11},{1,0},{9,8},{2,1},{10,9},{3,2},{11,10},{4,7},{12,15},... | collective-permute-start | bytes 909320 | tf_op jit(solution)/shard_map/ppermute | solution.py:403
  46.7 11.6 %collective-permute-start.10 = (bf16[37,16,256]{2,1,0:T(8,128)(2,1)S(1)}, bf16[37,16,256]{2,1,0:T(8,128)(2,1)S(1)}, u32[]{:S(2)}, u32[]{:S(2)}) collective-permute-start(bf16[37,16,256]{2,1,0:T(8,128)(2,1)S(1)} %collective-permute-done.7), channel_id=1, source_target_pairs={{0,1},{8,9},{1,2},{9,10},{2,3},{10,11},{3,0},{11,8},{4,5},{12,13},... | collective-permute-start | bytes 909320 | tf_op jit(solution)/shard_map/ppermute | solution.py:403
  52.8 5.4 %copy-start.6 = (bf16[128,2432]{1,0:T(8,128)(2,1)}, bf16[128,2432]{1,0:T(8,128)(2,1)S(1)}, u32[]{:S(2)}) copy-start(bf16[128,2432]{1,0:T(8,128)(2,1)S(1)} %collective-permute-done.2.c1) | copy-start | bytes 1867780
  52.8 5.4 %copy-start.8 = (bf16[128,2432]{1,0:T(8,128)(2,1)}, bf16[128,2432]{1,0:T(8,128)(2,1)S(1)}, u32[]{:S(2)}) copy-start(bf16[128,2432]{1,0:T(8,128)(2,1)S(1)} %collective-permute-done.3.c2) | copy-start | bytes 1867780
  52.9 5.3 %copy-start.10 = (bf16[128,2432]{1,0:T(8,128)(2,1)}, bf16[128,2432]{1,0:T(8,128)(2,1)S(1)}, u32[]{:S(2)}) copy-start(bf16[128,2432]{1,0:T(8,128)(2,1)S(1)} %collective-permute-done.4.c3) | copy-start | bytes 1867780
  52.9 10.4 %collective-permute-start.12 = (bf16[37,16,256]{2,1,0:T(8,128)(2,1)S(1)}, bf16[37,16,256]{2,1,0:T(8,128)(2,1)S(1)}, u32[]{:S(2)}, u32[]{:S(2)}) collective-permute-start(bf16[37,16,256]{2,1,0:T(8,128)(2,1)S(1)} %collective-permute-done.8), channel_id=1, source_target_pairs={{0,1},{8,9},{1,2},{9,10},{2,3},{10,11},{3,0},{11,8},{4,5},{12,13},... | collective-permute-start | bytes 909320 | tf_op jit(solution)/shard_map/ppermute | solution.py:403
  54.8 8.5 %collective-permute-start.13 = (bf16[37,16,256]{2,1,0:T(8,128)(2,1)S(1)}, bf16[37,16,256]{2,1,0:T(8,128)(2,1)S(1)}, u32[]{:S(2)}, u32[]{:S(2)}) collective-permute-start(bf16[37,16,256]{2,1,0:T(8,128)(2,1)S(1)} %collective-permute-done.11), channel_id=1, source_target_pairs={{0,3},{8,11},{1,0},{9,8},{2,1},{10,9},{3,2},{11,10},{4,7},{12,15},... | collective-permute-start | bytes 909320 | tf_op jit(solution)/shard_map/ppermute | solution.py:403
  58.2 6.4 %collective-permute-start.15 = (bf16[4,37,16,256]{3,2,1,0:T(8,128)(2,1)}, bf16[4,37,16,256]{3,2,1,0:T(8,128)(2,1)}, u32[]{:S(2)}, u32[]{:S(2)}) collective-permute-start(bf16[4,37,16,256]{3,2,1,0:T(8,128)(2,1)} %pad_maximum_fusion.1.refs_1_), channel_id=1, source_target_pairs={{0,8},{8,0},{1,9},{9,1},{2,10},{10,2},{3,11},{11,3},{4,12},{12,4},... | collective-permute-start | bytes 3637256 | tf_op jit(solution)/shard_map/ppermute | solution.py:403
  63.4 4.4 %copy-start.3 = (f32[256,64]{0,1:T(8,128)S(1)}, f32[256,64]{0,1:T(8,128)}, u32[]{:S(2)}) copy-start(f32[256,64]{0,1:T(8,128)} %param.19) | copy-start | bytes 196612
  63.4 4.4 %copy-start.5 = (bf16[128,2432]{1,0:T(8,128)(2,1)S(1)}, bf16[128,2432]{1,0:T(8,128)(2,1)}, u32[]{:S(2)}) copy-start(bf16[128,2432]{1,0:T(8,128)(2,1)} %get-tuple-element.64.c0) | copy-start | bytes 1867780
  64.6 3.2 %collective-permute-start.14 = (bf16[4,37,16,256]{3,2,1,0:T(8,128)(2,1)}, bf16[4,37,16,256]{3,2,1,0:T(8,128)(2,1)}, u32[]{:S(2)}, u32[]{:S(2)}) collective-permute-start(bf16[4,37,16,256]{3,2,1,0:T(8,128)(2,1)} %pad_maximum_fusion.refs_3_), channel_id=1, source_target_pairs={{0,8},{8,0},{1,9},{9,1},{2,10},{10,2},{3,11},{11,3},{4,12},{12,4},... | collective-permute-start | bytes 3637256 | tf_op jit(solution)/shard_map/ppermute | solution.py:403
  64.6 32.2 %copy-start.4 = (s32[4]{0:T(128)}, s32[4]{0:T(128)S(1)}, u32[]{:S(2)}) copy-start(s32[4]{0:T(128)S(1)} %pad_add_fusion.sc) | copy-start | bytes 52
  73.1 3.1 %collective-permute-start.16 = (f32[2,256,640]{2,1,0:T(8,128)S(1)}, f32[2,256,640]{2,1,0:T(8,128)S(1)}, u32[]{:S(2)}, u32[]{:S(2)}) collective-permute-start(f32[2,256,640]{2,1,0:T(8,128)S(1)} %get-tuple-element.69), channel_id=1, source_target_pairs={{0,8},{8,0},{1,9},{9,1},{2,10},{10,2},{3,11},{11,3},{4,12},{12,4},... | collective-permute-start | bytes 3932168 | tf_op jit(solution)/shard_map/ppermute | solution.py:403
  76.3 4.1 %copy-start.12 = (bf16[576,640]{1,0:T(8,128)(2,1)S(1)}, bf16[576,640]{1,0:T(8,128)(2,1)}, u32[]{:S(2)}) copy-start(bf16[576,640]{1,0:T(8,128)(2,1)} %constant.83.clone.refs_5_) | copy-start | bytes 2211844
  76.9 19.9 %collective-permute-start.17 = (f32[128,640]{1,0:T(8,128)S(1)}, f32[128,640]{1,0:T(8,128)S(1)}, u32[]{:S(2)}, u32[]{:S(2)}) collective-permute-start(f32[128,640]{1,0:T(8,128)S(1)} %get-tuple-element.71), channel_id=1, source_target_pairs={{0,4},{8,12},{1,5},{9,13},{2,6},{10,14},{3,7},{11,15},{4,16},{12,2... | collective-permute-start | bytes 983048 | tf_op jit(solution)/shard_map/ppermute | solution.py:403
  77.6 19.2 %collective-permute-start.18 = (f32[128,640]{1,0:T(8,128)S(1)}, f32[128,640]{1,0:T(8,128)S(1)}, u32[]{:S(2)}, u32[]{:S(2)}) collective-permute-start(f32[128,640]{1,0:T(8,128)S(1)} %get-tuple-element.72), channel_id=1, source_target_pairs={{0,16},{8,24},{1,17},{9,25},{2,18},{10,26},{3,19},{11,27},{4,20},{... | collective-permute-start | bytes 983048 | tf_op jit(solution)/shard_map/ppermute | solution.py:403
  79.6 17.2 %collective-permute-start.19 = (f32[128,640]{1,0:T(8,128)S(1)}, f32[128,640]{1,0:T(8,128)S(1)}, u32[]{:S(2)}, u32[]{:S(2)}) collective-permute-start(f32[128,640]{1,0:T(8,128)S(1)} %get-tuple-element.73), channel_id=1, source_target_pairs={{0,20},{8,28},{1,21},{9,29},{2,22},{10,30},{3,23},{11,31},{4,0},{1... | collective-permute-start | bytes 983048 | tf_op jit(solution)/shard_map/ppermute | solution.py:403
  98.1 6.4 %collective-permute-start.20 = (f32[32,640]{1,0:T(8,128)S(1)}, f32[32,640]{1,0:T(8,128)S(1)}, u32[]{:S(2)}, u32[]{:S(2)}) collective-permute-start(f32[32,640]{1,0:T(8,128)S(1)} %get-tuple-element.83), channel_id=1, source_target_pairs={{0,1},{8,9},{1,2},{9,10},{2,3},{10,11},{3,0},{11,8},{4,5},{12,13},... | collective-permute-start | bytes 245768 | tf_op jit(solution)/shard_map/ppermute | solution.py:403
  99.3 6.9 %collective-permute-start.21 = (f32[32,640]{1,0:T(8,128)S(1)}, f32[32,640]{1,0:T(8,128)S(1)}, u32[]{:S(2)}, u32[]{:S(2)}) collective-permute-start(f32[32,640]{1,0:T(8,128)S(1)} %get-tuple-element.84), channel_id=1, source_target_pairs={{0,2},{8,10},{1,3},{9,11},{2,0},{10,8},{3,1},{11,9},{4,6},{12,14},... | collective-permute-start | bytes 245768 | tf_op jit(solution)/shard_map/ppermute | solution.py:403
  102.6 4.4 %collective-permute-start.22 = (f32[32,640]{1,0:T(8,128)S(1)}, f32[32,640]{1,0:T(8,128)S(1)}, u32[]{:S(2)}, u32[]{:S(2)}) collective-permute-start(f32[32,640]{1,0:T(8,128)S(1)} %get-tuple-element.85), channel_id=1, source_target_pairs={{0,3},{8,11},{1,0},{9,8},{2,1},{10,9},{3,2},{11,10},{4,7},{12,15},... | collective-permute-start | bytes 245768 | tf_op jit(solution)/shard_map/ppermute | solution.py:403
  (7 other events, 7.8 us)

commit v4 on v3

--- a/solution.py
+++ b/solution.py
@@ -1,3 +1,5 @@
+import functools
+
 import jax
 import jax.numpy as jnp
 import numpy as np
@@ -54,10 +56,8 @@
 COEF = cos_poly()
 
 
-def prep_kernel(
-    x_ref, shift_ref, rot_ref, own_ref, off_ref, grp_ref, tab_ref, fx_ref, fy_ref,
-    w_ref, c0, c1, c2, c3, ws, us, aux, tab,
-):
+def prep_kernel(first, x_ref, shift_ref, rot_ref, own_ref, off_ref, grp_ref, tab_ref, fx_ref, fy_ref, *refs):
+    w_ref, c0, c1, c2, c3, ws, us, aux, tab = refs[-9:]
     dom, cls = lax.axis_index("dom"), lax.axis_index("cls")
     mine = 2 * (dom * 8 + cls)
     step = pl.program_id(0)
@@ -78,7 +78,7 @@
         flipped = tab_ref[...].T
         tab[...] = jnp.concatenate([flipped, flipped], axis=1)
 
-    here = aux[pl.ds(pl.multiple_of(step * 16, 16), 16), :]
+    here = aux[pl.ds(pl.multiple_of((step + first) * 16, 16), 16), :]
     lane = lax.broadcasted_iota(jnp.int32, (16, 128), 1)
     left = lane < R
     shift = jnp.where(left, 0.0, -0.25).astype(F32)
@@ -135,16 +135,19 @@
         c_ref[:, width : width + 128] = meta
 
 
-def prep(particles, rows, table, fx, fy):
+def prep(particles, rows, table, fx, fy, first, held=()):
     n = particles.shape[0]
     whole = lambda a: pl.BlockSpec(a.shape, lambda i: (0,) * a.ndim)
-    block = lambda i: (i, 0)
+    block = lambda i: (i + first, 0)
     args = [particles, *rows, table, fx, fy]
-    return pl.pallas_call(
-        prep_kernel,
-        grid=(n // 16,),
-        in_specs=[pl.BlockSpec((16, A * 128), block)] + [whole(a) for a in args[1:]],
-        out_specs=[pl.BlockSpec((2, A * 8, 128), lambda i: (i, 0, 0))]
+    given = len(args)
+    return pl.pallas_call(
+        functools.partial(prep_kernel, first),
+        grid=(n // 32,),
+        in_specs=[pl.BlockSpec((16, A * 128), block)]
+        + [whole(a) for a in args[1:]]
+        + [pl.BlockSpec(memory_space=pltpu.HBM)] * len(held),
+        out_specs=[pl.BlockSpec((2, A * 8, 128), lambda i: (i + first, 0, 0))]
         + [pl.BlockSpec((16, 19 * 128), block)] * 4,
         scratch_shapes=[
             pltpu.VMEM((16, A * 128), F32),
@@ -154,12 +157,22 @@
         ],
         out_shape=[jax.ShapeDtypeStruct((n // 8, A * 8, 128), BF)]
         + [jax.ShapeDtypeStruct((n, 19 * 128), BF)] * 4,
+        input_output_aliases={given + i: i for i in range(len(held))},
         compiler_params=pltpu.CompilerParams(vmem_limit_bytes=PREP_MIB * MIB),
         cost_estimate=pl.CostEstimate(
-            flops=40_000_000, bytes_accessed=8_000_000, transcendentals=0
+            flops=20_000_000, bytes_accessed=4_000_000, transcendentals=0
         ),
         name="prep",
-    )(*args)
+    )(*args, *held)
+
+
+def repeat(step):
+    @pl.loop(0, M // 4)
+    def _(i):
+        for u in range(4):
+            step(4 * i + u)
+
+    step(M - 1)
 
 
 def spectra_kernel(w_ref, f_ref, p_ref, s):
@@ -167,12 +180,13 @@
         y = jnp.concatenate([w_ref[2 * g], w_ref[2 * g + 1]], axis=1)
         s[:, 256 * g : 256 * g + 256] = jnp.dot(f_ref[...], y, preferred_element_type=F32)
 
-    @pl.loop(0, M)
-    def _(m):
+    def turn(m):
         for i in range(2):
             row = pl.multiple_of(m * 16 + 8 * i, 8)
             v = jnp.concatenate([s[pl.ds(row, 8), 128 * g : 128 * g + 128] for g in range(16)], axis=0)
             p_ref[m, :, 128 * i : 128 * i + 128] = v.T.astype(BF)
+
+    repeat(turn)
 
 
 def spectra(w, fwd_k):
@@ -224,8 +238,7 @@
     p_ref, blocks, inv_ref, o_ref, xs = refs[0], refs[1:5], refs[5], refs[6], refs[7]
     xs[:, 2 * M * 8 :, :] = jnp.zeros((16, K_INV - 2 * M * 8, 256), BF)
 
-    @pl.loop(0, M)
-    def _(m):
+    def cross(m):
         upper = p_ref[m]
         re, im = upper[:, 0:128], upper[:, 128:256]
         rhs = jnp.concatenate([upper, jnp.concatenate([im, -re], axis=1)], axis=0)
@@ -239,13 +252,16 @@
                     [x[k : k + 8, 0:128], x[k : k + 8, 128:256]], axis=0
                 ).astype(BF)
 
-    def one(g, best):
-        y = jnp.dot(inv_ref[...], xs[g], preferred_element_type=F32)
-        for t in range(A):
-            best = jnp.maximum(best, y[8 * t : 8 * t + 8])
+    repeat(cross)
+
+    def four(i, best):
+        for u in range(4):
+            y = jnp.dot(inv_ref[...], xs[4 * i + u], preferred_element_type=F32)
+            for t in range(A):
+                best = jnp.maximum(best, y[8 * t : 8 * t + 8])
         return best
 
-    best = lax.fori_loop(0, 16, one, jnp.full((8, 256), -jnp.inf, F32))
+    best = lax.fori_loop(0, 4, four, jnp.full((8, 256), -jnp.inf, F32))
     best = jnp.max(best, axis=0, keepdims=True)
     o_ref[...] = jnp.maximum(best[:, 0:128], best[:, 128:256])
 
@@ -264,12 +280,20 @@
     )(p, *blocks, inv_k)
 
 
-def sums_kernel(sc, c0, c1, c2, c3, tab_ref, mine, other, acc):
+def sums_kernel(sc, h0, h1, h2, h3, tab_ref, mine, other, acc, rows, sems):
+    copies = [
+        pltpu.make_async_copy(h, rows.at[pl.ds(128 * i, 128)], sems.at[i])
+        for i, h in enumerate((h0, h1, h2, h3))
+    ]
+    for c in copies:
+        c.start()
+    for c in copies:
+        c.wait()
     width = 18 * 128
     lane = lax.broadcasted_iota(jnp.int32, (128, 256), 1).astype(F32)
     picks, groups = [], []
-    for c in (c0, c1, c2, c3):
-        meta = c[:, width : width + 128].astype(F32)
+    for i in range(4):
+        meta = rows[128 * i : 128 * i + 128, width : width + 128].astype(F32)
         picks.append(jnp.where(lane == meta[:, 0:1], 1.0, 0.0).astype(F32).T.astype(BF))
         groups.append(jnp.where(lane == meta[:, 1:2], 1.0, 0.0).astype(BF))
     pick = jnp.concatenate(picks, axis=1)
@@ -280,8 +304,7 @@
     wsum = jnp.dot(count, tab * tab, precision=lax.Precision.HIGHEST, preferred_element_type=F32)
     for t in range(9):
         cols = slice(256 * t, 256 * t + 256)
-        x = jnp.concatenate([c[:, cols] for c in (c0, c1, c2, c3)], axis=0)
-        acc[:, cols] = jnp.dot(pick, x, preferred_element_type=F32)
+        acc[:, cols] = jnp.dot(pick, rows[:, cols], preferred_element_type=F32)
     left = lax.broadcasted_iota(jnp.int32, (256, 128), 1) < R
     for ref, core in ((mine, sc[2]), (other, 1 - sc[2])):
         for xh in range(2):
@@ -294,14 +317,19 @@
 
 def class_sums(sc, cs, tab):
     v = pl.BlockSpec(memory_space=pltpu.VMEM)
+    hbm = pl.BlockSpec(memory_space=pltpu.HBM)
     shape = jax.ShapeDtypeStruct((2, 256, 640), F32)
     return pl.pallas_call(
         sums_kernel,
-        in_specs=[pl.BlockSpec(memory_space=pltpu.SMEM)] + [v] * 5,
+        in_specs=[pl.BlockSpec(memory_space=pltpu.SMEM)] + [hbm] * 4 + [v],
         out_specs=[v, v],
         out_shape=[shape, shape],
-        scratch_shapes=[pltpu.VMEM((256, 18 * 128), F32)],
-        compiler_params=pltpu.CompilerParams(vmem_limit_bytes=VMEM_LIMIT),
+        scratch_shapes=[
+            pltpu.VMEM((256, 18 * 128), F32),
+            pltpu.VMEM((512, 19 * 128), BF),
+            pltpu.SemaphoreType.DMA((4,)),
+        ],
+        compiler_params=pltpu.CompilerParams(vmem_limit_bytes=56 * MIB),
         cost_estimate=pl.CostEstimate(flops=700_000_000, bytes_accessed=5_000_000, transcendentals=0),
         name="class_sums",
     )(sc, *cs, tab)
@@ -428,11 +456,14 @@
     rows = [shifts.T, rotation[None], owner.T, class_offset[None], ctf_group[None]]
     table = ctf_table.T
     block, rows[1] = lax.optimization_barrier((block, rows[1]))
-    weighted, *sent = prep(particles, rows, table, fx, fy)
+    half = prep(particles, rows, table, fx, fy, 0)
     far = move(block, HIGH)
-    far, weighted, *sent = lax.optimization_barrier((far, weighted, *sent))
+    far, *half = lax.optimization_barrier((far, *half))
     pair = join(block, far, xh)
+    pair, rows[1] = lax.optimization_barrier((pair, rows[1]))
+    weighted, *sent = prep(particles, rows, table, fx, fy, 4, half)
     near = move(pair, Y_NEAR)
+    near, weighted, *sent = lax.optimization_barrier((near, weighted, *sent))
     quad = join(pair, near, y % 2)
     octet = join(quad, move(quad, Y_FAR), y // 2).reshape(4, 2, 16, 1152)
 
@@ -447,7 +478,7 @@
     on_up, on_down = move(up, ZS[1]), move(side_down, ZS[3])
     early, late = jnp.stack([own, side, up, down]), jnp.stack([side_up, side_down, on_up, on_down])
     early_twin, late_twin = move(early, CORE), move(late, CORE)
-    *held, late_twin, early_twin = lax.optimization_barrier((*held, late_twin, early_twin))
+    *held, side_up, side_down, early_twin = lax.optimization_barrier((*held, side_up, side_down, early_twin))
     mine, other = class_sums(sc, held, table)
     other = move(other, CORE)
     cut = cut_x(sc, mine, other)

time: 110 us -> 111 us (level)
  waiting for transfers between devices: 32.3 us -> 37.2 us
  Pallas kernels: 36.5 us -> 32 us
  local copies, waits for them, and re-layouts: 4.5 us -> 1.3 us
  other arithmetic: 3.54 us -> 5.39 us
  starting transfers between devices: 31.8 us -> 33.6 us
    pallas_call x1, Pallas kernels: 16.4 us -> 9.56 us  [scores_of(): pl.pallas_call(score_kernel, in_specs=[v] * 6, out_specs=v, out_shape=jax...]
    ppermute x23, waiting for transfers between devices: 32.3 us -> 37.2 us  [move(): return lax.ppermute(value, AXES, pairs)]
    pallas_call x1, Pallas kernels: 2.1 us -> 5.43 us  [class_sums(): pl.pallas_call(sums_kernel, in_specs=[pl.BlockSpec(memory_space=pltpu.SME...]
    unnamed x32 -> x24, local copies, waits for them, and re-layouts: 4.5 us -> 1.3 us
    pallas_call x1, Pallas kernels: 5.88 us -> 3.39 us  [spectra(): pl.pallas_call(spectra_kernel, in_specs=[v, v], out_specs=v, out_shape=ja...]
    ppermute x23, starting transfers between devices: 31.8 us -> 33.6 us  [move(): return lax.ppermute(value, AXES, pairs)]
    pallas_call x1 -> x2, Pallas kernels: 8.52 us -> 10.1 us  [prep(): pl.pallas_call(functools.partial(prep_kernel, first), grid=(n // 32,), in...]
    another operation x1, other arithmetic: 1.2 us -> 2.39 us  [per_device(): jnp.stack([own, side, up, down])]
  transfers between devices with their start and end apart: 23 -> 23, of which waited for: 13 -> 13; matrix products, arithmetic and copies ran while one was open for 2% -> 2% of each run, Pallas kernels for 29% -> 27%
where the time goes in v4:
time: 111 us; the launch traced here: 110 us
  waiting for transfers between devices  37.2 us (34%)
  starting transfers between devices  33.6 us (30%)
  Pallas kernels  32 us (29%)
  other arithmetic  5.39 us (5%)
  local copies, waits for them, and re-layouts  1.3 us (1%)
    ppermute x23, waiting for transfers between devices, move(): return lax.ppermute(value, AXES, pairs)  37.2 us
    ppermute x23, starting transfers between devices, move(): return lax.ppermute(value, AXES, pairs)  33.6 us
    pallas_call x2, Pallas kernels, prep(): pl.pallas_call(functools.partial(prep_kernel, first), grid=(n // 32,), in...  10.1 us
    pallas_call x1, Pallas kernels, scores_of(): pl.pallas_call(score_kernel, in_specs=[v] * 6, out_specs=v, out_shape=jax...  9.56 us
    pallas_call x1, Pallas kernels, class_sums(): pl.pallas_call(sums_kernel, in_specs=[pl.BlockSpec(memory_space=pltpu.SME...  5.43 us
    pallas_call x1, Pallas kernels, spectra(): pl.pallas_call(spectra_kernel, in_specs=[v, v], out_specs=v, out_shape=ja...  3.39 us
    another operation x1, other arithmetic, per_device(): jnp.stack([own, side, up, down])  2.39 us
  transfers between devices with their start and end apart: 23, of which 13 were waited for; matrix products, arithmetic and copies ran while one was open for 2% of the time, Pallas kernels for 27%

profile of v4, /device:TPU:0, one launch (start us, length us, event | category | flops | bytes accessed | tf_op | source)
XLA Modules:
  0.0 110.4 jit_solution(1735349335123094102)
XLA Ops:
  0.6 0.8 broadcast_select_fusion.1
  1.6 1.2 %collective-permute-done = bf16[16,576]{1,0:T(8,128)(2,1)S(1)} collective-permute-done((bf16[16,576]{1,0:T(8,128)(2,1)S(1)}, bf16[16,576]{1,0:T(8,128)(2,1)S(1)}, u32[]{:S(2)}, u32[]{:S(2)}) %collective-permute-start) | collective-permute-done | bytes 18464 | tf_op jit(solution)/shard_map/ppermute | solution.py:431
  2.9 3.2 %collective-permute-start.1 = (bf16[16,1152]{1,0:T(8,128)(2,1)S(1)}, bf16[16,1152]{1,0:T(8,128)(2,1)S(1)}, u32[]{:S(2)}, u32[]{:S(2)}) collective-permute-start(bf16[16,1152]{1,0:T(8,128)(2,1)S(1)} %maximum_select_fusion), channel_id=1, source_target_pairs={{0,16},{8,24},{1,17},{9,25},{2,18},{10,26},{3,19},{11,27},{4,20},{... | collective-permute-start | bytes 110600 | tf_op jit(solution)/shard_map/ppermute | solution.py:431
  6.0 5.1 %prep.2 = (bf16[16,576,128]{2,1,0:T(8,128)(2,1)}, bf16[128,2432]{1,0:T(8,128)(2,1)}, bf16[128,2432]{1,0:T(8,128)(2,1)}, bf16[128,2432]{1,0:T(8,128)(2,1)}, bf16[128,2432]{1,0:T(8,128)(2,1)}) custom-call(bf16[128,9216]{1,0:T(8,128)(2,1)} %x_ref.3, s32[2,128]{1,0:T(2,128)} %bitcast.41, s32[1,128]{1,0:T(1,128)} %bitcast.43, s32[1,128]{1,0:T(1,128)} %bitcast.45, ...), custom_call_target="tpu_custom_call" | custom-call | flops 20000000 | bytes 4000000 | tf_op jit(solution)/shard_map/prep/pallas_call | solution.py:144
  11.2 1.7 %collective-permute-start.2 = (bf16[2,16,1152]{2,1,0:T(8,128)(2,1)S(1)}, bf16[2,16,1152]{2,1,0:T(8,128)(2,1)S(1)}, u32[]{:S(2)}, u32[]{:S(2)}) collective-permute-start(bf16[2,16,1152]{2,1,0:T(8,128)(2,1)S(1)} %pad_maximum_fusion.4), channel_id=1, source_target_pairs={{0,32},{8,40},{1,33},{9,41},{2,34},{10,42},{3,35},{11,43},{4,36},{... | collective-permute-start | bytes 221192 | tf_op jit(solution)/shard_map/ppermute | solution.py:431
  12.8 5.0 %prep.3 = (bf16[16,576,128]{2,1,0:T(8,128)(2,1)}, bf16[128,2432]{1,0:T(8,128)(2,1)}, bf16[128,2432]{1,0:T(8,128)(2,1)}, bf16[128,2432]{1,0:T(8,128)(2,1)}, bf16[128,2432]{1,0:T(8,128)(2,1)}) custom-call(bf16[128,9216]{1,0:T(8,128)(2,1)} %x_ref.3, s32[2,128]{1,0:T(2,128)} %bitcast.42, ...), custom_call_target="tpu_custom_call", output_to_operand_aliasing={{0}: (9, {}), {1}: (10, {}), {2}: (11, {}), {3}: (12, {}), ... | custom-call | flops 20000000 | bytes 4000000 | tf_op jit(solution)/shard_map/prep/pallas_call | solution.py:144
  17.9 3.0 %collective-permute-start.6 = (bf16[2,2,16,1152]{3,2,1,0:T(8,128)(2,1)S(1)}, bf16[2,2,16,1152]{3,2,1,0:T(8,128)(2,1)S(1)}, u32[]{:S(2)}, u32[]{:S(2)}) collective-permute-start(bf16[2,2,16,1152]{3,2,1,0:T(8,128)(2,1)S(1)} %pad_maximum_fusion.3), channel_id=1, source_target_pairs={{0,64},{8,72},{1,65},{9,73},{2,66},{10,74},{3,67},{11,75},{4,68},{... | collective-permute-start | bytes 442376 | tf_op jit(solution)/shard_map/ppermute | solution.py:431
  21.0 1.5 %collective-permute-start.4 = (bf16[128,2432]{1,0:T(8,128)(2,1)}, bf16[128,2432]{1,0:T(8,128)(2,1)S(1)}, u32[]{:S(2)}, u32[]{:S(2)}) collective-permute-start(bf16[128,2432]{1,0:T(8,128)(2,1)} %get-tuple-element.78), channel_id=1, source_target_pairs={{0,64},{8,72},{1,65},{9,73},{2,66},{10,74},{3,67},{11,75},{4,68},{... | collective-permute-start | bytes 1867784 | tf_op jit(solution)/shard_map/ppermute | solution.py:431
  22.6 1.6 %collective-permute-start.5 = (bf16[128,2432]{1,0:T(8,128)(2,1)}, bf16[128,2432]{1,0:T(8,128)(2,1)S(1)}, u32[]{:S(2)}, u32[]{:S(2)}) collective-permute-start(bf16[128,2432]{1,0:T(8,128)(2,1)} %get-tuple-element.79), channel_id=1, source_target_pairs={{0,96},{8,104},{1,97},{9,105},{2,98},{10,106},{3,99},{11,107},{4,1... | collective-permute-start | bytes 1867784 | tf_op jit(solution)/shard_map/ppermute | solution.py:431
  24.2 2.1 %collective-permute-done.6 = bf16[2,2,16,1152]{3,2,1,0:T(8,128)(2,1)S(1)} collective-permute-done((bf16[2,2,16,1152]{3,2,1,0:T(8,128)(2,1)S(1)}, bf16[2,2,16,1152]{3,2,1,0:T(8,128)(2,1)S(1)}, u32[]{:S(2)}, u32[]{:S(2)}) %collective-permute-start.6) | collective-permute-done | bytes 147488 | tf_op jit(solution)/shard_map/ppermute | solution.py:431
  27.4 1.9 %collective-permute-start.8 = (bf16[37,16,256]{2,1,0:T(8,128)(2,1)S(1)}, bf16[37,16,256]{2,1,0:T(8,128)(2,1)S(1)}, u32[]{:S(2)}, u32[]{:S(2)}) collective-permute-start(bf16[37,16,256]{2,1,0:T(8,128)(2,1)S(1)} %ref_spectra.1), channel_id=1, source_target_pairs={{0,1},{8,9},{1,2},{9,10},{2,3},{10,11},{3,0},{11,8},{4,5},{12,13},... | collective-permute-start | bytes 909320 | tf_op jit(solution)/shard_map/ppermute | solution.py:431
  29.4 4.4 %collective-permute-done.7 = bf16[37,16,256]{2,1,0:T(8,128)(2,1)} collective-permute-done((bf16[37,16,256]{2,1,0:T(8,128)(2,1)S(1)}, bf16[37,16,256]{2,1,0:T(8,128)(2,1)}, u32[]{:S(2)}, u32[]{:S(2)}) %collective-permute-start.7) | collective-permute-done | bytes 303136 | tf_op jit(solution)/shard_map/ppermute | solution.py:431
  33.8 4.0 %collective-permute-start.9 = (bf16[37,16,256]{2,1,0:T(8,128)(2,1)S(1)}, bf16[37,16,256]{2,1,0:T(8,128)(2,1)S(1)}, u32[]{:S(2)}, u32[]{:S(2)}) collective-permute-start(bf16[37,16,256]{2,1,0:T(8,128)(2,1)S(1)} %ref_spectra.1), channel_id=1, source_target_pairs={{0,3},{8,11},{1,0},{9,8},{2,1},{10,9},{3,2},{11,10},{4,7},{12,15},... | collective-permute-start | bytes 909320 | tf_op jit(solution)/shard_map/ppermute | solution.py:431
  37.8 3.4 %spectra.1.refs_0_ = bf16[37,128,256]{2,1,0:T(8,128)(2,1)S(1)} custom-call(bf16[16,576,128]{2,1,0:T(8,128)(2,1)S(1)} %copy-done, bf16[592,576]{1,0:T(8,128)(2,1)S(1)} %copy-done.1), custom_call_target="tpu_custom_call" | custom-call | flops 1000 | bytes 1000 | tf_op jit(solution)/shard_map/spectra/pallas_call | solution.py:194
  41.2 0.9 collective-permute-done.9
  42.1 9.8 %collective-permute-done.3.h1 = bf16[128,2432]{1,0:T(8,128)(2,1)S(1)} collective-permute-done((bf16[128,2432]{1,0:T(8,128)(2,1)}, bf16[128,2432]{1,0:T(8,128)(2,1)S(1)}, u32[]{:S(2)}, u32[]{:S(2)}) %collective-permute-start.3) | collective-permute-done | bytes 622624 | tf_op jit(solution)/shard_map/ppermute | solution.py:431
  52.0 2.4 %pad_maximum_fusion.refs_1_ = bf16[4,37,16,256]{3,2,1,0:T(8,128)(2,1)} fusion(bf16[1,37,16,256]{3,2,1,0:T(8,128)(2,1)S(1)} %bitcast.37, bf16[1,37,16,256]{3,2,1,0:T(8,128)(2,1)S(1)} %bitcast.34, bf16[1,37,16,256]{3,2,1,0:T(8,128)(2,1)} %bitcast.18, bf16[1,37,16,256]{3,2,1,0:T(8,128)(2,1)S(1)} %bitcast.32), kind=kLoop, calls=%fused_computation | loop fusion | flops 1818624 | bytes 2424832 | tf_op jit(solution)/shard_map/stack | solution.py:479
  54.4 4.1 %collective-permute-start.11 = (bf16[37,16,256]{2,1,0:T(8,128)(2,1)}, bf16[37,16,256]{2,1,0:T(8,128)(2,1)S(1)}, u32[]{:S(2)}, u32[]{:S(2)}) collective-permute-start(bf16[37,16,256]{2,1,0:T(8,128)(2,1)} %collective-permute-done.7), channel_id=1, source_target_pairs={{0,3},{8,11},{1,0},{9,8},{2,1},{10,9},{3,2},{11,10},{4,7},{12,15},... | collective-permute-start | bytes 909320 | tf_op jit(solution)/shard_map/ppermute | solution.py:431
  58.6 7.4 %collective-permute-done.11 = bf16[37,16,256]{2,1,0:T(8,128)(2,1)S(1)} collective-permute-done((bf16[37,16,256]{2,1,0:T(8,128)(2,1)}, bf16[37,16,256]{2,1,0:T(8,128)(2,1)S(1)}, u32[]{:S(2)}, u32[]{:S(2)}) %collective-permute-start.11) | collective-permute-done | bytes 303136 | tf_op jit(solution)/shard_map/ppermute | solution.py:431
  65.9 3.6 %collective-permute-start.18 = (bf16[37,16,256]{2,1,0:T(8,128)(2,1)S(1)}, bf16[37,16,256]{2,1,0:T(8,128)(2,1)}, u32[]{:S(2)}, u32[]{:S(2)}) collective-permute-start(bf16[37,16,256]{2,1,0:T(8,128)(2,1)S(1)} %collective-permute-done.11), channel_id=1, source_target_pairs={{0,3},{8,11},{1,0},{9,8},{2,1},{10,9},{3,2},{11,10},{4,7},{12,15},... | collective-permute-start | bytes 909320 | tf_op jit(solution)/shard_map/ppermute | solution.py:431
  70.1 5.4 %class_sums.1 = (f32[2,256,640]{2,1,0:T(8,128)}, f32[2,256,640]{2,1,0:T(8,128)}) custom-call(s32[4]{0:T(128)} %pad_add_fusion.sc, bf16[128,2432]{1,0:T(8,128)(2,1)} %get-tuple-element.89.h0, bf16[128,2432]{1,0:T(8,128)(2,1)} %copy-done.9, bf16[128,2432]{1,0:T(8,128)(2,1)} %copy-done.10, bf16[128,2432]{1,0:T(8,128)(2,1)} %copy-done.11, f32[64,256]{1,0:T(8,128)} %bitcast.40), custom_call_target="tpu_custom_call" | custom-call | flops 700000000 | bytes 5000000 | tf_op jit(solution)/shard_map/class_sums/pallas_call | solution.py:322
  75.8 1.3 %pad_maximum_fusion.1.refs_3_ = bf16[4,37,16,256]{3,2,1,0:T(8,128)(2,1)S(1)} fusion(bf16[1,37,16,256]{3,2,1,0:T(8,128)(2,1)} %bitcast.24, bf16[1,37,16,256]{3,2,1,0:T(8,128)(2,1)} %bitcast.23, bf16[1,37,16,256]{3,2,1,0:T(8,128)(2,1)S(1)} %bitcast.35, bf16[1,37,16,256]{3,2,1,0:T(8,128)(2,1)S(1)} %bitcast.36), kind=kLoop, calls=%fused_computation.1 | loop fusion | flops 1818624 | bytes 2424832 | tf_op jit(solution)/shard_map/stack | solution.py:479
  77.6 1.3 %collective-permute-done.13.b_ref = f32[2,256,640]{2,1,0:T(8,128)S(1)} collective-permute-done((f32[2,256,640]{2,1,0:T(8,128)}, f32[2,256,640]{2,1,0:T(8,128)S(1)}, u32[]{:S(2)}, u32[]{:S(2)}) %collective-permute-start.13) | collective-permute-done | bytes 1310752 | tf_op jit(solution)/shard_map/ppermute | solution.py:431
  80.3 2.0 %collective-permute-start.15 = (f32[128,640]{1,0:T(8,128)S(1)}, f32[128,640]{1,0:T(8,128)S(1)}, u32[]{:S(2)}, u32[]{:S(2)}) collective-permute-start(f32[128,640]{1,0:T(8,128)S(1)} %get-tuple-element.97), channel_id=1, source_target_pairs={{0,16},{8,24},{1,17},{9,25},{2,18},{10,26},{3,19},{11,27},{4,20},{... | collective-permute-start | bytes 983048 | tf_op jit(solution)/shard_map/ppermute | solution.py:431
  82.3 0.9 collective-permute-start.16
  83.2 9.6 %scores.1 = f32[1,128]{1,0:T(1,128)} custom-call(bf16[37,128,256]{2,1,0:T(8,128)(2,1)S(1)} %spectra.1.refs_0_, bf16[4,37,16,256]{3,2,1,0:T(8,128)(2,1)} %pad_maximum_fusion.refs_1_, bf16[4,37,16,256]{3,2,1,0:T(8,128)(2,1)} %collective-permute-done.12.refs_2_, bf16[4,37,16,256]{3,2,1,0:T(8,128)(2,1)S(1)} %pad_maximum_fusion.1.refs_3_, ...), custom_call_target="tpu_custom_call" | custom-call | flops 6000000000 | bytes 8000000 | tf_op jit(solution)/shard_map/scores/pallas_call | solution.py:271
  92.8 4.9 %collective-permute-done.14.a1 = f32[128,640]{1,0:T(8,128)S(1)} collective-permute-done((f32[128,640]{1,0:T(8,128)S(1)}, f32[128,640]{1,0:T(8,128)S(1)}, u32[]{:S(2)}, u32[]{:S(2)}) %collective-permute-start.14) | collective-permute-done | bytes 327712 | tf_op jit(solution)/shard_map/ppermute | solution.py:431
  99.5 3.9 %collective-permute-start.21 = (f32[32,640]{1,0:T(8,128)S(1)}, f32[32,640]{1,0:T(8,128)S(1)}, u32[]{:S(2)}, u32[]{:S(2)}) collective-permute-start(f32[32,640]{1,0:T(8,128)S(1)} %get-tuple-element.108), channel_id=1, source_target_pairs={{0,2},{8,10},{1,3},{9,11},{2,0},{10,8},{3,1},{11,9},{4,6},{12,14},... | collective-permute-start | bytes 245768 | tf_op jit(solution)/shard_map/ppermute | solution.py:431
  103.5 2.5 %collective-permute-done.20.a1 = f32[32,640]{1,0:T(8,128)S(1)} collective-permute-done((f32[32,640]{1,0:T(8,128)S(1)}, f32[32,640]{1,0:T(8,128)S(1)}, u32[]{:S(2)}, u32[]{:S(2)}) %collective-permute-start.20) | collective-permute-done | bytes 81952 | tf_op jit(solution)/shard_map/ppermute | solution.py:431
  106.0 0.9 collective-permute-done.21.a2
  106.9 1.0 collective-permute-done.22.a3
  108.5 1.8 %final.1 = f32[25,576]{1,0:T(8,128)} custom-call(s32[4]{0:T(128)} %pad_add_fusion.sc, f32[32,640]{1,0:T(8,128)} %copy-done.3, f32[32,640]{1,0:T(8,128)} %copy-done.6, f32[32,640]{1,0:T(8,128)} %copy-done.7, f32[32,640]{1,0:T(8,128)} %copy-done.8), custom_call_target="tpu_custom_call" | custom-call | tf_op jit(solution)/shard_map/final/pallas_call | solution.py:397
  (58 shorter events, 6.8 us)
Async XLA Ops:
  1.5 1.3 %collective-permute-start = (bf16[16,576]{1,0:T(8,128)(2,1)S(1)}, bf16[16,576]{1,0:T(8,128)(2,1)S(1)}, u32[]{:S(2)}, u32[]{:S(2)}) collective-permute-start(bf16[16,576]{1,0:T(8,128)(2,1)S(1)} %get-tuple-element.117), channel_id=1, source_target_pairs={{0,8},{8,0},{1,9},{9,1},{2,10},{10,2},{3,11},{11,3},{4,12},{12,4},... | collective-permute-start | bytes 55304 | tf_op jit(solution)/shard_map/ppermute | solution.py:431
  2.9 8.3 %collective-permute-start.1 = (bf16[16,1152]{1,0:T(8,128)(2,1)S(1)}, bf16[16,1152]{1,0:T(8,128)(2,1)S(1)}, u32[]{:S(2)}, u32[]{:S(2)}) collective-permute-start(bf16[16,1152]{1,0:T(8,128)(2,1)S(1)} %maximum_select_fusion), channel_id=1, source_target_pairs={{0,16},{8,24},{1,17},{9,25},{2,18},{10,26},{3,19},{11,27},{4,20},{... | collective-permute-start | bytes 110600 | tf_op jit(solution)/shard_map/ppermute | solution.py:431
  11.2 6.7 %collective-permute-start.2 = (bf16[2,16,1152]{2,1,0:T(8,128)(2,1)S(1)}, bf16[2,16,1152]{2,1,0:T(8,128)(2,1)S(1)}, u32[]{:S(2)}, u32[]{:S(2)}) collective-permute-start(bf16[2,16,1152]{2,1,0:T(8,128)(2,1)S(1)} %pad_maximum_fusion.4), channel_id=1, source_target_pairs={{0,32},{8,40},{1,33},{9,41},{2,34},{10,42},{3,35},{11,43},{4,36},{... | collective-permute-start | bytes 221192 | tf_op jit(solution)/shard_map/ppermute | solution.py:431
  17.8 8.5 %copy-start.1 = (bf16[592,576]{1,0:T(8,128)(2,1)S(1)}, bf16[592,576]{1,0:T(8,128)(2,1)}, u32[]{:S(2)}) copy-start(bf16[592,576]{1,0:T(8,128)(2,1)} %constant.82.clone.f_ref) | copy-start | bytes 2045956
  17.9 8.4 %collective-permute-start.6 = (bf16[2,2,16,1152]{3,2,1,0:T(8,128)(2,1)S(1)}, bf16[2,2,16,1152]{3,2,1,0:T(8,128)(2,1)S(1)}, u32[]{:S(2)}, u32[]{:S(2)}) collective-permute-start(bf16[2,2,16,1152]{3,2,1,0:T(8,128)(2,1)S(1)} %pad_maximum_fusion.3), channel_id=1, source_target_pairs={{0,64},{8,72},{1,65},{9,73},{2,66},{10,74},{3,67},{11,75},{4,68},{... | collective-permute-start | bytes 442376 | tf_op jit(solution)/shard_map/ppermute | solution.py:431
  20.9 16.9 %copy-start = (bf16[16,576,128]{2,1,0:T(8,128)(2,1)S(1)}, bf16[16,576,128]{2,1,0:T(8,128)(2,1)}, u32[]{:S(2)}) copy-start(bf16[16,576,128]{2,1,0:T(8,128)(2,1)} %get-tuple-element.81.w_ref) | copy-start | bytes 7077892
  20.9 31.0 %collective-permute-start.3 = (bf16[128,2432]{1,0:T(8,128)(2,1)}, bf16[128,2432]{1,0:T(8,128)(2,1)S(1)}, u32[]{:S(2)}, u32[]{:S(2)}) collective-permute-start(bf16[128,2432]{1,0:T(8,128)(2,1)} %get-tuple-element.77), channel_id=1, source_target_pairs={{0,32},{8,40},{1,33},{9,41},{2,34},{10,42},{3,35},{11,43},{4,36},{... | collective-permute-start | bytes 1867784 | tf_op jit(solution)/shard_map/ppermute | solution.py:431
  21.0 30.9 %collective-permute-start.4 = (bf16[128,2432]{1,0:T(8,128)(2,1)}, bf16[128,2432]{1,0:T(8,128)(2,1)S(1)}, u32[]{:S(2)}, u32[]{:S(2)}) collective-permute-start(bf16[128,2432]{1,0:T(8,128)(2,1)} %get-tuple-element.78), channel_id=1, source_target_pairs={{0,64},{8,72},{1,65},{9,73},{2,66},{10,74},{3,67},{11,75},{4,68},{... | collective-permute-start | bytes 1867784 | tf_op jit(solution)/shard_map/ppermute | solution.py:431
  22.6 29.4 %collective-permute-start.5 = (bf16[128,2432]{1,0:T(8,128)(2,1)}, bf16[128,2432]{1,0:T(8,128)(2,1)S(1)}, u32[]{:S(2)}, u32[]{:S(2)}) collective-permute-start(bf16[128,2432]{1,0:T(8,128)(2,1)} %get-tuple-element.79), channel_id=1, source_target_pairs={{0,96},{8,104},{1,97},{9,105},{2,98},{10,106},{3,99},{11,107},{4,1... | collective-permute-start | bytes 1867784 | tf_op jit(solution)/shard_map/ppermute | solution.py:431
  26.8 7.0 %collective-permute-start.7 = (bf16[37,16,256]{2,1,0:T(8,128)(2,1)S(1)}, bf16[37,16,256]{2,1,0:T(8,128)(2,1)}, u32[]{:S(2)}, u32[]{:S(2)}) collective-permute-start(bf16[37,16,256]{2,1,0:T(8,128)(2,1)S(1)} %ref_spectra.1), channel_id=1, source_target_pairs={{0,4},{8,12},{1,5},{9,13},{2,6},{10,14},{3,7},{11,15},{4,0},{12,8}... | collective-permute-start | bytes 909320 | tf_op jit(solution)/shard_map/ppermute | solution.py:431
  27.4 13.8 %collective-permute-start.8 = (bf16[37,16,256]{2,1,0:T(8,128)(2,1)S(1)}, bf16[37,16,256]{2,1,0:T(8,128)(2,1)S(1)}, u32[]{:S(2)}, u32[]{:S(2)}) collective-permute-start(bf16[37,16,256]{2,1,0:T(8,128)(2,1)S(1)} %ref_spectra.1), channel_id=1, source_target_pairs={{0,1},{8,9},{1,2},{9,10},{2,3},{10,11},{3,0},{11,8},{4,5},{12,13},... | collective-permute-start | bytes 909320 | tf_op jit(solution)/shard_map/ppermute | solution.py:431
  33.8 8.4 %collective-permute-start.9 = (bf16[37,16,256]{2,1,0:T(8,128)(2,1)S(1)}, bf16[37,16,256]{2,1,0:T(8,128)(2,1)S(1)}, u32[]{:S(2)}, u32[]{:S(2)}) collective-permute-start(bf16[37,16,256]{2,1,0:T(8,128)(2,1)S(1)} %ref_spectra.1), channel_id=1, source_target_pairs={{0,3},{8,11},{1,0},{9,8},{2,1},{10,9},{3,2},{11,10},{4,7},{12,15},... | collective-permute-start | bytes 909320 | tf_op jit(solution)/shard_map/ppermute | solution.py:431
  51.9 2.4 %copy-start.9 = (bf16[128,2432]{1,0:T(8,128)(2,1)}, bf16[128,2432]{1,0:T(8,128)(2,1)S(1)}, u32[]{:S(2)}) copy-start(bf16[128,2432]{1,0:T(8,128)(2,1)S(1)} %collective-permute-done.3.h1) | copy-start | bytes 1867780
  51.9 2.4 %copy-start.10 = (bf16[128,2432]{1,0:T(8,128)(2,1)}, bf16[128,2432]{1,0:T(8,128)(2,1)S(1)}, u32[]{:S(2)}) copy-start(bf16[128,2432]{1,0:T(8,128)(2,1)S(1)} %collective-permute-done.4.h2) | copy-start | bytes 1867780
  51.9 2.4 %copy-start.11 = (bf16[128,2432]{1,0:T(8,128)(2,1)}, bf16[128,2432]{1,0:T(8,128)(2,1)S(1)}, u32[]{:S(2)}) copy-start(bf16[128,2432]{1,0:T(8,128)(2,1)S(1)} %collective-permute-done.5.h3) | copy-start | bytes 1867780
  54.3 15.8 %collective-permute-start.12 = (bf16[4,37,16,256]{3,2,1,0:T(8,128)(2,1)}, bf16[4,37,16,256]{3,2,1,0:T(8,128)(2,1)}, u32[]{:S(2)}, u32[]{:S(2)}) collective-permute-start(bf16[4,37,16,256]{3,2,1,0:T(8,128)(2,1)} %pad_maximum_fusion.refs_1_), channel_id=1, source_target_pairs={{0,8},{8,0},{1,9},{9,1},{2,10},{10,2},{3,11},{11,3},{4,12},{12,4},... | collective-permute-start | bytes 3637256 | tf_op jit(solution)/shard_map/ppermute | solution.py:431
  54.4 11.5 %collective-permute-start.11 = (bf16[37,16,256]{2,1,0:T(8,128)(2,1)}, bf16[37,16,256]{2,1,0:T(8,128)(2,1)S(1)}, u32[]{:S(2)}, u32[]{:S(2)}) collective-permute-start(bf16[37,16,256]{2,1,0:T(8,128)(2,1)} %collective-permute-done.7), channel_id=1, source_target_pairs={{0,3},{8,11},{1,0},{9,8},{2,1},{10,9},{3,2},{11,10},{4,7},{12,15},... | collective-permute-start | bytes 909320 | tf_op jit(solution)/shard_map/ppermute | solution.py:431
  58.5 11.6 %collective-permute-start.10 = (bf16[37,16,256]{2,1,0:T(8,128)(2,1)}, bf16[37,16,256]{2,1,0:T(8,128)(2,1)S(1)}, u32[]{:S(2)}, u32[]{:S(2)}) collective-permute-start(bf16[37,16,256]{2,1,0:T(8,128)(2,1)} %collective-permute-done.7), channel_id=1, source_target_pairs={{0,1},{8,9},{1,2},{9,10},{2,3},{10,11},{3,0},{11,8},{4,5},{12,13},... | collective-permute-start | bytes 909320 | tf_op jit(solution)/shard_map/ppermute | solution.py:431
  58.6 17.3 %collective-permute-start.17 = (bf16[37,16,256]{2,1,0:T(8,128)(2,1)S(1)}, bf16[37,16,256]{2,1,0:T(8,128)(2,1)}, u32[]{:S(2)}, u32[]{:S(2)}) collective-permute-start(bf16[37,16,256]{2,1,0:T(8,128)(2,1)S(1)} %collective-permute-done.8), channel_id=1, source_target_pairs={{0,1},{8,9},{1,2},{9,10},{2,3},{10,11},{3,0},{11,8},{4,5},{12,13},... | collective-permute-start | bytes 909320 | tf_op jit(solution)/shard_map/ppermute | solution.py:431
  65.9 9.9 %collective-permute-start.18 = (bf16[37,16,256]{2,1,0:T(8,128)(2,1)S(1)}, bf16[37,16,256]{2,1,0:T(8,128)(2,1)}, u32[]{:S(2)}, u32[]{:S(2)}) collective-permute-start(bf16[37,16,256]{2,1,0:T(8,128)(2,1)S(1)} %collective-permute-done.11), channel_id=1, source_target_pairs={{0,3},{8,11},{1,0},{9,8},{2,1},{10,9},{3,2},{11,10},{4,7},{12,15},... | collective-permute-start | bytes 909320 | tf_op jit(solution)/shard_map/ppermute | solution.py:431
  75.6 3.3 %collective-permute-start.13 = (f32[2,256,640]{2,1,0:T(8,128)}, f32[2,256,640]{2,1,0:T(8,128)S(1)}, u32[]{:S(2)}, u32[]{:S(2)}) collective-permute-start(f32[2,256,640]{2,1,0:T(8,128)} %get-tuple-element.94), channel_id=1, source_target_pairs={{0,8},{8,0},{1,9},{9,1},{2,10},{10,2},{3,11},{11,3},{4,12},{12,4},... | collective-permute-start | bytes 3932168 | tf_op jit(solution)/shard_map/ppermute | solution.py:431
  75.8 3.1 %copy-start.2 = (f32[2,256,640]{2,1,0:T(8,128)S(1)}, f32[2,256,640]{2,1,0:T(8,128)}, u32[]{:S(2)}) copy-start(f32[2,256,640]{2,1,0:T(8,128)} %get-tuple-element.93.a_ref) | copy-start | bytes 3932164
  75.8 3.1 %copy-start.4 = (s32[4]{0:T(128)S(1)}, s32[4]{0:T(128)}, u32[]{:S(2)}) copy-start(s32[4]{0:T(128)} %pad_add_fusion.sc) | copy-start | bytes 52
  77.1 6.1 %collective-permute-start.19 = (bf16[4,37,16,256]{3,2,1,0:T(8,128)(2,1)S(1)}, bf16[4,37,16,256]{3,2,1,0:T(8,128)(2,1)S(1)}, u32[]{:S(2)}, u32[]{:S(2)}) collective-permute-start(bf16[4,37,16,256]{3,2,1,0:T(8,128)(2,1)S(1)} %pad_maximum_fusion.1.refs_3_), channel_id=1, source_target_pairs={{0,8},{8,0},{1,9},{9,1},{2,10},{10,2},{3,11},{11,3},{4,12},{12,4},... | collective-permute-start | bytes 3637256 | tf_op jit(solution)/shard_map/ppermute | solution.py:431
  78.9 4.3 %copy-start.5 = (bf16[576,640]{1,0:T(8,128)(2,1)S(1)}, bf16[576,640]{1,0:T(8,128)(2,1)}, u32[]{:S(2)}) copy-start(bf16[576,640]{1,0:T(8,128)(2,1)} %constant.83.clone.refs_5_) | copy-start | bytes 2211844
  79.6 18.1 %collective-permute-start.14 = (f32[128,640]{1,0:T(8,128)S(1)}, f32[128,640]{1,0:T(8,128)S(1)}, u32[]{:S(2)}, u32[]{:S(2)}) collective-permute-start(f32[128,640]{1,0:T(8,128)S(1)} %get-tuple-element.96), channel_id=1, source_target_pairs={{0,4},{8,12},{1,5},{9,13},{2,6},{10,14},{3,7},{11,15},{4,16},{12,2... | collective-permute-start | bytes 983048 | tf_op jit(solution)/shard_map/ppermute | solution.py:431
  80.3 17.4 %collective-permute-start.15 = (f32[128,640]{1,0:T(8,128)S(1)}, f32[128,640]{1,0:T(8,128)S(1)}, u32[]{:S(2)}, u32[]{:S(2)}) collective-permute-start(f32[128,640]{1,0:T(8,128)S(1)} %get-tuple-element.97), channel_id=1, source_target_pairs={{0,16},{8,24},{1,17},{9,25},{2,18},{10,26},{3,19},{11,27},{4,20},{... | collective-permute-start | bytes 983048 | tf_op jit(solution)/shard_map/ppermute | solution.py:431
  82.3 16.0 %collective-permute-start.16 = (f32[128,640]{1,0:T(8,128)S(1)}, f32[128,640]{1,0:T(8,128)S(1)}, u32[]{:S(2)}, u32[]{:S(2)}) collective-permute-start(f32[128,640]{1,0:T(8,128)S(1)} %get-tuple-element.98), channel_id=1, source_target_pairs={{0,20},{8,28},{1,21},{9,29},{2,22},{10,30},{3,23},{11,31},{4,0},{1... | collective-permute-start | bytes 983048 | tf_op jit(solution)/shard_map/ppermute | solution.py:431
  99.5 6.5 %collective-permute-start.20 = (f32[32,640]{1,0:T(8,128)S(1)}, f32[32,640]{1,0:T(8,128)S(1)}, u32[]{:S(2)}, u32[]{:S(2)}) collective-permute-start(f32[32,640]{1,0:T(8,128)S(1)} %get-tuple-element.107), channel_id=1, source_target_pairs={{0,1},{8,9},{1,2},{9,10},{2,3},{10,11},{3,0},{11,8},{4,5},{12,13},... | collective-permute-start | bytes 245768 | tf_op jit(solution)/shard_map/ppermute | solution.py:431
  99.5 7.3 %collective-permute-start.21 = (f32[32,640]{1,0:T(8,128)S(1)}, f32[32,640]{1,0:T(8,128)S(1)}, u32[]{:S(2)}, u32[]{:S(2)}) collective-permute-start(f32[32,640]{1,0:T(8,128)S(1)} %get-tuple-element.108), channel_id=1, source_target_pairs={{0,2},{8,10},{1,3},{9,11},{2,0},{10,8},{3,1},{11,9},{4,6},{12,14},... | collective-permute-start | bytes 245768 | tf_op jit(solution)/shard_map/ppermute | solution.py:431
  103.4 4.4 %collective-permute-start.22 = (f32[32,640]{1,0:T(8,128)S(1)}, f32[32,640]{1,0:T(8,128)S(1)}, u32[]{:S(2)}, u32[]{:S(2)}) collective-permute-start(f32[32,640]{1,0:T(8,128)S(1)} %get-tuple-element.109), channel_id=1, source_target_pairs={{0,3},{8,11},{1,0},{9,8},{2,1},{10,9},{3,2},{11,10},{4,7},{12,15},... | collective-permute-start | bytes 245768 | tf_op jit(solution)/shard_map/ppermute | solution.py:431
  106.0 1.9 %copy-start.6 = (f32[32,640]{1,0:T(8,128)}, f32[32,640]{1,0:T(8,128)S(1)}, u32[]{:S(2)}) copy-start(f32[32,640]{1,0:T(8,128)S(1)} %collective-permute-done.20.a1) | copy-start | bytes 245764
  (3 other events, 2.3 us)

commit v5 on v4

--- a/solution.py
+++ b/solution.py
@@ -17,7 +17,7 @@
 BF = jnp.bfloat16
 F32 = jnp.float32
 MIB = 1024 * 1024
-VMEM_LIMIT = 16 * MIB
+VMEM_LIMIT = 8 * MIB
 PREP_MIB = 56
 K_INV = 640
 
@@ -280,20 +280,12 @@
     )(p, *blocks, inv_k)
 
 
-def sums_kernel(sc, h0, h1, h2, h3, tab_ref, mine, other, acc, rows, sems):
-    copies = [
-        pltpu.make_async_copy(h, rows.at[pl.ds(128 * i, 128)], sems.at[i])
-        for i, h in enumerate((h0, h1, h2, h3))
-    ]
-    for c in copies:
-        c.start()
-    for c in copies:
-        c.wait()
+def sums_kernel(sc, c0, c1, c2, c3, tab_ref, mine, other, acc):
     width = 18 * 128
     lane = lax.broadcasted_iota(jnp.int32, (128, 256), 1).astype(F32)
     picks, groups = [], []
-    for i in range(4):
-        meta = rows[128 * i : 128 * i + 128, width : width + 128].astype(F32)
+    for c in (c0, c1, c2, c3):
+        meta = c[:, width : width + 128].astype(F32)
         picks.append(jnp.where(lane == meta[:, 0:1], 1.0, 0.0).astype(F32).T.astype(BF))
         groups.append(jnp.where(lane == meta[:, 1:2], 1.0, 0.0).astype(BF))
     pick = jnp.concatenate(picks, axis=1)
@@ -304,7 +296,8 @@
     wsum = jnp.dot(count, tab * tab, precision=lax.Precision.HIGHEST, preferred_element_type=F32)
     for t in range(9):
         cols = slice(256 * t, 256 * t + 256)
-        acc[:, cols] = jnp.dot(pick, rows[:, cols], preferred_element_type=F32)
+        x = jnp.concatenate([c[:, cols] for c in (c0, c1, c2, c3)], axis=0)
+        acc[:, cols] = jnp.dot(pick, x, preferred_element_type=F32)
     left = lax.broadcasted_iota(jnp.int32, (256, 128), 1) < R
     for ref, core in ((mine, sc[2]), (other, 1 - sc[2])):
         for xh in range(2):
@@ -317,19 +310,14 @@
 
 def class_sums(sc, cs, tab):
     v = pl.BlockSpec(memory_space=pltpu.VMEM)
-    hbm = pl.BlockSpec(memory_space=pltpu.HBM)
     shape = jax.ShapeDtypeStruct((2, 256, 640), F32)
     return pl.pallas_call(
         sums_kernel,
-        in_specs=[pl.BlockSpec(memory_space=pltpu.SMEM)] + [hbm] * 4 + [v],
+        in_specs=[pl.BlockSpec(memory_space=pltpu.SMEM)] + [v] * 5,
         out_specs=[v, v],
         out_shape=[shape, shape],
-        scratch_shapes=[
-            pltpu.VMEM((256, 18 * 128), F32),
-            pltpu.VMEM((512, 19 * 128), BF),
-            pltpu.SemaphoreType.DMA((4,)),
-        ],
-        compiler_params=pltpu.CompilerParams(vmem_limit_bytes=56 * MIB),
+        scratch_shapes=[pltpu.VMEM((256, 18 * 128), F32)],
+        compiler_params=pltpu.CompilerParams(vmem_limit_bytes=VMEM_LIMIT),
         cost_estimate=pl.CostEstimate(flops=700_000_000, bytes_accessed=5_000_000, transcendentals=0),
         name="class_sums",
     )(sc, *cs, tab)
@@ -399,6 +387,7 @@
         in_specs=[pl.BlockSpec(memory_space=pltpu.SMEM)] + [v] * 4,
         out_specs=v,
         out_shape=jax.ShapeDtypeStruct((25, 576), F32),
+        compiler_params=pltpu.CompilerParams(vmem_limit_bytes=2 * MIB),
         name="final",
     )(sc, *parts)
 
@@ -429,6 +418,10 @@
 
 def move(value, pairs):
     return lax.ppermute(value, AXES, pairs)
+
+
+def after(values, *others):
+    return lax.optimization_barrier((*values, *others))[: len(values)]
 
 
 def join(own, other, upper):
@@ -474,14 +467,15 @@
     up, down = move(own, ZS[1]), move(own, ZS[3])
     side = move(own, LOW)
     side_up, side_down = move(side, ZS[1]), move(side, ZS[3])
-    *held, side, up, down, part = lax.optimization_barrier((*held, side, up, down, part))
     on_up, on_down = move(up, ZS[1]), move(side_down, ZS[3])
-    early, late = jnp.stack([own, side, up, down]), jnp.stack([side_up, side_down, on_up, on_down])
-    early_twin, late_twin = move(early, CORE), move(late, CORE)
-    *held, side_up, side_down, early_twin = lax.optimization_barrier((*held, side_up, side_down, early_twin))
+    early = jnp.stack([own, side, up, down])
+    early_twin = move(early, CORE)
+    held = after(held, side, up, down, side_up, side_down, part)
+    held = after(held, on_up, on_down)
     mine, other = class_sums(sc, held, table)
-    other = move(other, CORE)
-    cut = cut_x(sc, mine, other)
+    cut = cut_x(sc, mine, move(other, CORE))
+    late = jnp.stack([side_up, side_down, on_up, on_down])
+    late_twin = move(late, CORE)
     cut = [cut[0]] + [move(cut[d], XS[d]) for d in (1, 2, 3)]
     scores = scores_of(part, [early, early_twin, late, late_twin], inv_k)
     *cut, scores = lax.optimization_barrier((*cut, scores))

time: 111 us -> 98.9 us (0.89)
  Pallas kernels: 32 us -> 27.3 us
  waiting for transfers between devices: 37.2 us -> 33.1 us
  starting transfers between devices: 33.6 us -> 31.6 us
    ppermute x23, waiting for transfers between devices: 37.2 us -> 33.1 us  [move(): return lax.ppermute(value, AXES, pairs)]
    pallas_call x1, Pallas kernels: 5.43 us -> 2.83 us  [class_sums(): pl.pallas_call(sums_kernel, in_specs=[pl.BlockSpec(memory_space=pltpu.SME...]
    ppermute x23, starting transfers between devices: 33.6 us -> 31.6 us  [move(): return lax.ppermute(value, AXES, pairs)]
    pallas_call x1, Pallas kernels: 9.56 us -> 7.92 us  [scores_of(): pl.pallas_call(score_kernel, in_specs=[v] * 6, out_specs=v, out_shape=jax...]
  transfers between devices with their start and end apart: 23 -> 23, of which waited for: 13 -> 13; matrix products, arithmetic and copies ran while one was open for 2% -> 4% of each run, Pallas kernels for 27% -> 26%
where the time goes in v5:
time: 98.9 us; the launch traced here: 98.4 us
  waiting for transfers between devices  33.1 us (33%)
  starting transfers between devices  31.6 us (32%)
  Pallas kernels  27.3 us (28%)
  other arithmetic  4.75 us (5%)
    ppermute x23, waiting for transfers between devices, move(): return lax.ppermute(value, AXES, pairs)  33.1 us
    ppermute x23, starting transfers between devices, move(): return lax.ppermute(value, AXES, pairs)  31.6 us
    pallas_call x2, Pallas kernels, prep(): pl.pallas_call(functools.partial(prep_kernel, first), grid=(n // 32,), in...  10.1 us
    pallas_call x1, Pallas kernels, scores_of(): pl.pallas_call(score_kernel, in_specs=[v] * 6, out_specs=v, out_shape=jax...  7.92 us
    pallas_call x1, Pallas kernels, spectra(): pl.pallas_call(spectra_kernel, in_specs=[v, v], out_specs=v, out_shape=ja...  3.4 us
    pallas_call x1, Pallas kernels, class_sums(): pl.pallas_call(sums_kernel, in_specs=[pl.BlockSpec(memory_space=pltpu.SME...  2.83 us
  transfers between devices with their start and end apart: 23, of which 13 were waited for; matrix products, arithmetic and copies ran while one was open for 4% of the time, Pallas kernels for 26%

profile of v5, /device:TPU:0, one launch (start us, length us, event | category | flops | bytes accessed | tf_op | source)
XLA Modules:
  0.0 98.4 jit_solution(151020959964756392)
XLA Ops:
  0.6 0.8 broadcast_select_fusion.1
  1.6 1.2 %collective-permute-done = bf16[16,576]{1,0:T(8,128)(2,1)S(1)} collective-permute-done((bf16[16,576]{1,0:T(8,128)(2,1)S(1)}, bf16[16,576]{1,0:T(8,128)(2,1)S(1)}, u32[]{:S(2)}, u32[]{:S(2)}) %collective-permute-start) | collective-permute-done | bytes 18464 | tf_op jit(solution)/shard_map/ppermute | solution.py:420
  2.9 3.2 %collective-permute-start.1 = (bf16[16,1152]{1,0:T(8,128)(2,1)S(1)}, bf16[16,1152]{1,0:T(8,128)(2,1)S(1)}, u32[]{:S(2)}, u32[]{:S(2)}) collective-permute-start(bf16[16,1152]{1,0:T(8,128)(2,1)S(1)} %maximum_select_fusion), channel_id=1, source_target_pairs={{0,16},{8,24},{1,17},{9,25},{2,18},{10,26},{3,19},{11,27},{4,20},{... | collective-permute-start | bytes 110600 | tf_op jit(solution)/shard_map/ppermute | solution.py:420
  6.0 5.0 %prep.2 = (bf16[16,576,128]{2,1,0:T(8,128)(2,1)}, bf16[128,2432]{1,0:T(8,128)(2,1)}, bf16[128,2432]{1,0:T(8,128)(2,1)}, bf16[128,2432]{1,0:T(8,128)(2,1)}, bf16[128,2432]{1,0:T(8,128)(2,1)}) custom-call(bf16[128,9216]{1,0:T(8,128)(2,1)} %x_ref.3, s32[2,128]{1,0:T(2,128)} %bitcast.38, s32[1,128]{1,0:T(1,128)} %bitcast.40, s32[1,128]{1,0:T(1,128)} %bitcast.42, ...), custom_call_target="tpu_custom_call" | custom-call | flops 20000000 | bytes 4000000 | tf_op jit(solution)/shard_map/prep/pallas_call | solution.py:144
  11.1 1.7 %collective-permute-start.2 = (bf16[2,16,1152]{2,1,0:T(8,128)(2,1)S(1)}, bf16[2,16,1152]{2,1,0:T(8,128)(2,1)S(1)}, u32[]{:S(2)}, u32[]{:S(2)}) collective-permute-start(bf16[2,16,1152]{2,1,0:T(8,128)(2,1)S(1)} %pad_maximum_fusion.4), channel_id=1, source_target_pairs={{0,32},{8,40},{1,33},{9,41},{2,34},{10,42},{3,35},{11,43},{4,36},{... | collective-permute-start | bytes 221192 | tf_op jit(solution)/shard_map/ppermute | solution.py:420
  12.8 5.1 %prep.3 = (bf16[16,576,128]{2,1,0:T(8,128)(2,1)}, bf16[128,2432]{1,0:T(8,128)(2,1)}, bf16[128,2432]{1,0:T(8,128)(2,1)}, bf16[128,2432]{1,0:T(8,128)(2,1)}, bf16[128,2432]{1,0:T(8,128)(2,1)}) custom-call(bf16[128,9216]{1,0:T(8,128)(2,1)} %x_ref.3, s32[2,128]{1,0:T(2,128)} %bitcast.39, ...), custom_call_target="tpu_custom_call", output_to_operand_aliasing={{0}: (9, {}), {1}: (10, {}), {2}: (11, {}), {3}: (12, {}), ... | custom-call | flops 20000000 | bytes 4000000 | tf_op jit(solution)/shard_map/prep/pallas_call | solution.py:144
  17.9 3.0 %collective-permute-start.6 = (bf16[2,2,16,1152]{3,2,1,0:T(8,128)(2,1)S(1)}, bf16[2,2,16,1152]{3,2,1,0:T(8,128)(2,1)}, u32[]{:S(2)}, u32[]{:S(2)}) collective-permute-start(bf16[2,2,16,1152]{3,2,1,0:T(8,128)(2,1)S(1)} %pad_maximum_fusion.3), channel_id=1, source_target_pairs={{0,64},{8,72},{1,65},{9,73},{2,66},{10,74},{3,67},{11,75},{4,68},{... | collective-permute-start | bytes 442376 | tf_op jit(solution)/shard_map/ppermute | solution.py:420
  21.1 5.3 %collective-permute-done.6 = bf16[2,2,16,1152]{3,2,1,0:T(8,128)(2,1)} collective-permute-done((bf16[2,2,16,1152]{3,2,1,0:T(8,128)(2,1)S(1)}, bf16[2,2,16,1152]{3,2,1,0:T(8,128)(2,1)}, u32[]{:S(2)}, u32[]{:S(2)}) %collective-permute-start.6) | collective-permute-done | bytes 147488 | tf_op jit(solution)/shard_map/ppermute | solution.py:420
  26.4 0.9 select_bitcast_fusion.1
  27.8 4.1 %collective-permute-start.9 = (bf16[37,16,256]{2,1,0:T(8,128)(2,1)S(1)}, bf16[37,16,256]{2,1,0:T(8,128)(2,1)S(1)}, u32[]{:S(2)}, u32[]{:S(2)}) collective-permute-start(bf16[37,16,256]{2,1,0:T(8,128)(2,1)S(1)} %ref_spectra.1), channel_id=1, source_target_pairs={{0,3},{8,11},{1,0},{9,8},{2,1},{10,9},{3,2},{11,10},{4,7},{12,15},... | collective-permute-start | bytes 909320 | tf_op jit(solution)/shard_map/ppermute | solution.py:420
  32.5 2.9 %collective-permute-start.4 = (bf16[128,2432]{1,0:T(8,128)(2,1)}, bf16[128,2432]{1,0:T(8,128)(2,1)}, u32[]{:S(2)}, u32[]{:S(2)}) collective-permute-start(bf16[128,2432]{1,0:T(8,128)(2,1)} %get-tuple-element.73), channel_id=1, source_target_pairs={{0,64},{8,72},{1,65},{9,73},{2,66},{10,74},{3,67},{11,75},{4,68},{... | collective-permute-start | bytes 1867784 | tf_op jit(solution)/shard_map/ppermute | solution.py:420
  36.6 2.2 %collective-permute-done.7 = bf16[37,16,256]{2,1,0:T(8,128)(2,1)} collective-permute-done((bf16[37,16,256]{2,1,0:T(8,128)(2,1)S(1)}, bf16[37,16,256]{2,1,0:T(8,128)(2,1)}, u32[]{:S(2)}, u32[]{:S(2)}) %collective-permute-start.7) | collective-permute-done | bytes 303136 | tf_op jit(solution)/shard_map/ppermute | solution.py:420
  38.8 1.2 %collective-permute-start.11 = (bf16[37,16,256]{2,1,0:T(8,128)(2,1)}, bf16[37,16,256]{2,1,0:T(8,128)(2,1)}, u32[]{:S(2)}, u32[]{:S(2)}) collective-permute-start(bf16[37,16,256]{2,1,0:T(8,128)(2,1)} %collective-permute-done.7), channel_id=1, source_target_pairs={{0,3},{8,11},{1,0},{9,8},{2,1},{10,9},{3,2},{11,10},{4,7},{12,15},... | collective-permute-start | bytes 909320 | tf_op jit(solution)/shard_map/ppermute | solution.py:420
  40.0 4.8 %collective-permute-done.8 = bf16[37,16,256]{2,1,0:T(8,128)(2,1)} collective-permute-done((bf16[37,16,256]{2,1,0:T(8,128)(2,1)S(1)}, bf16[37,16,256]{2,1,0:T(8,128)(2,1)}, u32[]{:S(2)}, u32[]{:S(2)}) %collective-permute-start.8) | collective-permute-done | bytes 303136 | tf_op jit(solution)/shard_map/ppermute | solution.py:420
  44.8 7.1 %collective-permute-done.3.c1 = bf16[128,2432]{1,0:T(8,128)(2,1)S(1)} collective-permute-done((bf16[128,2432]{1,0:T(8,128)(2,1)}, bf16[128,2432]{1,0:T(8,128)(2,1)S(1)}, u32[]{:S(2)}, u32[]{:S(2)}) %collective-permute-start.3) | collective-permute-done | bytes 622624 | tf_op jit(solution)/shard_map/ppermute | solution.py:420
  52.8 1.9 %collective-permute-start.12 = (bf16[37,16,256]{2,1,0:T(8,128)(2,1)}, bf16[37,16,256]{2,1,0:T(8,128)(2,1)}, u32[]{:S(2)}, u32[]{:S(2)}) collective-permute-start(bf16[37,16,256]{2,1,0:T(8,128)(2,1)} %collective-permute-done.8), channel_id=1, source_target_pairs={{0,1},{8,9},{1,2},{9,10},{2,3},{10,11},{3,0},{11,8},{4,5},{12,13},... | collective-permute-start | bytes 909320 | tf_op jit(solution)/shard_map/ppermute | solution.py:420
  54.7 2.1 %collective-permute-start.13 = (bf16[37,16,256]{2,1,0:T(8,128)(2,1)}, bf16[37,16,256]{2,1,0:T(8,128)(2,1)}, u32[]{:S(2)}, u32[]{:S(2)}) collective-permute-start(bf16[37,16,256]{2,1,0:T(8,128)(2,1)} %collective-permute-done.11), channel_id=1, source_target_pairs={{0,3},{8,11},{1,0},{9,8},{2,1},{10,9},{3,2},{11,10},{4,7},{12,15},... | collective-permute-start | bytes 909320 | tf_op jit(solution)/shard_map/ppermute | solution.py:420
  56.9 3.4 %spectra.1.refs_0_ = bf16[37,128,256]{2,1,0:T(8,128)(2,1)S(1)} custom-call(bf16[16,576,128]{2,1,0:T(8,128)(2,1)S(1)} %copy-done, bf16[592,576]{1,0:T(8,128)(2,1)S(1)} %copy-done.1), custom_call_target="tpu_custom_call" | custom-call | flops 1000 | bytes 1000 | tf_op jit(solution)/shard_map/spectra/pallas_call | solution.py:194
  60.4 1.3 %pad_maximum_fusion.refs_1_ = bf16[4,37,16,256]{3,2,1,0:T(8,128)(2,1)S(1)} fusion(bf16[1,37,16,256]{3,2,1,0:T(8,128)(2,1)S(1)} %bitcast.37, bf16[1,37,16,256]{3,2,1,0:T(8,128)(2,1)} %bitcast.19, bf16[1,37,16,256]{3,2,1,0:T(8,128)(2,1)} %bitcast.18, bf16[1,37,16,256]{3,2,1,0:T(8,128)(2,1)S(1)} %bitcast.32), kind=kLoop, calls=%fused_computation | loop fusion | flops 1818624 | bytes 2424832 | tf_op jit(solution)/shard_map/stack | solution.py:471
  62.0 2.8 %class_sums.1 = (f32[2,256,640]{2,1,0:T(8,128)S(1)}, f32[2,256,640]{2,1,0:T(8,128)S(1)}) custom-call(s32[4]{0:T(128)S(1)} %pad_add_fusion.sc, bf16[128,2432]{1,0:T(8,128)(2,1)S(1)} %copy-done.2, bf16[128,2432]{1,0:T(8,128)(2,1)S(1)} %copy-done.5, bf16[128,2432]{1,0:T(8,128)(2,1)} %collective-permute-done.4.c2, bf16[128,2432]{1,0:T(8,128)(2,1)} %collective-permute-done.5.c3, ...), custom_call_target="tpu_custom_call" | custom-call | flops 700000000 | bytes 5000000 | tf_op jit(solution)/shard_map/class_sums/pallas_call | solution.py:314
  65.2 1.4 %pad_maximum_fusion.1.refs_3_ = bf16[4,37,16,256]{3,2,1,0:T(8,128)(2,1)S(1)} fusion(bf16[1,37,16,256]{3,2,1,0:T(8,128)(2,1)} %bitcast.24, bf16[1,37,16,256]{3,2,1,0:T(8,128)(2,1)} %bitcast.23, bf16[1,37,16,256]{3,2,1,0:T(8,128)(2,1)} %bitcast.22, bf16[1,37,16,256]{3,2,1,0:T(8,128)(2,1)} %bitcast.21), kind=kLoop, calls=%fused_computation.1 | loop fusion | flops 1818624 | bytes 2424832 | tf_op jit(solution)/shard_map/stack | solution.py:477
  66.9 1.1 %collective-permute-done.14.b_ref = f32[2,256,640]{2,1,0:T(8,128)S(1)} collective-permute-done((f32[2,256,640]{2,1,0:T(8,128)S(1)}, f32[2,256,640]{2,1,0:T(8,128)S(1)}, u32[]{:S(2)}, u32[]{:S(2)}) %collective-permute-start.14) | collective-permute-done | bytes 1310752 | tf_op jit(solution)/shard_map/ppermute | solution.py:420
  69.3 2.0 %collective-permute-start.16 = (f32[128,640]{1,0:T(8,128)S(1)}, f32[128,640]{1,0:T(8,128)S(1)}, u32[]{:S(2)}, u32[]{:S(2)}) collective-permute-start(f32[128,640]{1,0:T(8,128)S(1)} %get-tuple-element.89), channel_id=1, source_target_pairs={{0,16},{8,24},{1,17},{9,25},{2,18},{10,26},{3,19},{11,27},{4,20},{... | collective-permute-start | bytes 983048 | tf_op jit(solution)/shard_map/ppermute | solution.py:420
  71.3 0.9 collective-permute-start.17
  72.2 7.9 %scores.1 = f32[1,128]{1,0:T(1,128)} custom-call(bf16[37,128,256]{2,1,0:T(8,128)(2,1)S(1)} %spectra.1.refs_0_, bf16[4,37,16,256]{3,2,1,0:T(8,128)(2,1)S(1)} %pad_maximum_fusion.refs_1_, bf16[4,37,16,256]{3,2,1,0:T(8,128)(2,1)S(1)} %collective-permute-done.18.refs_2_, bf16[4,37,16,256]{3,2,1,0:T(8,128)(2,1)S(1)} %pad_maximum_fusion.1.refs_3_, ...), custom_call_target="tpu_custom_call" | custom-call | flops 6000000000 | bytes 8000000 | tf_op jit(solution)/shard_map/scores/pallas_call | solution.py:271
  80.2 6.7 %collective-permute-done.15.a1 = f32[128,640]{1,0:T(8,128)S(1)} collective-permute-done((f32[128,640]{1,0:T(8,128)S(1)}, f32[128,640]{1,0:T(8,128)S(1)}, u32[]{:S(2)}, u32[]{:S(2)}) %collective-permute-start.15) | collective-permute-done | bytes 327712 | tf_op jit(solution)/shard_map/ppermute | solution.py:420
  88.1 1.6 %collective-permute-start.20 = (f32[32,640]{1,0:T(8,128)S(1)}, f32[32,640]{1,0:T(8,128)S(1)}, u32[]{:S(2)}, u32[]{:S(2)}) collective-permute-start(f32[32,640]{1,0:T(8,128)S(1)} %get-tuple-element.97), channel_id=1, source_target_pairs={{0,1},{8,9},{1,2},{9,10},{2,3},{10,11},{3,0},{11,8},{4,5},{12,13},... | collective-permute-start | bytes 245768 | tf_op jit(solution)/shard_map/ppermute | solution.py:420
  89.8 2.9 %collective-permute-start.21 = (f32[32,640]{1,0:T(8,128)S(1)}, f32[32,640]{1,0:T(8,128)S(1)}, u32[]{:S(2)}, u32[]{:S(2)}) collective-permute-start(f32[32,640]{1,0:T(8,128)S(1)} %get-tuple-element.98), channel_id=1, source_target_pairs={{0,2},{8,10},{1,3},{9,11},{2,0},{10,8},{3,1},{11,9},{4,6},{12,14},... | collective-permute-start | bytes 245768 | tf_op jit(solution)/shard_map/ppermute | solution.py:420
  92.7 1.4 %collective-permute-start.22 = (f32[32,640]{1,0:T(8,128)S(1)}, f32[32,640]{1,0:T(8,128)S(1)}, u32[]{:S(2)}, u32[]{:S(2)}) collective-permute-start(f32[32,640]{1,0:T(8,128)S(1)} %get-tuple-element.99), channel_id=1, source_target_pairs={{0,3},{8,11},{1,0},{9,8},{2,1},{10,9},{3,2},{11,10},{4,7},{12,15},... | collective-permute-start | bytes 245768 | tf_op jit(solution)/shard_map/ppermute | solution.py:420
  94.7 1.2 %collective-permute-done.21.a2 = f32[32,640]{1,0:T(8,128)S(1)} collective-permute-done((f32[32,640]{1,0:T(8,128)S(1)}, f32[32,640]{1,0:T(8,128)S(1)}, u32[]{:S(2)}, u32[]{:S(2)}) %collective-permute-start.21) | collective-permute-done | bytes 81952 | tf_op jit(solution)/shard_map/ppermute | solution.py:420
  96.0 1.1 %collective-permute-done.22.a3 = f32[32,640]{1,0:T(8,128)S(1)} collective-permute-done((f32[32,640]{1,0:T(8,128)S(1)}, f32[32,640]{1,0:T(8,128)S(1)}, u32[]{:S(2)}, u32[]{:S(2)}) %collective-permute-start.22) | collective-permute-done | bytes 81952 | tf_op jit(solution)/shard_map/ppermute | solution.py:420
  97.1 1.3 %final.1 = f32[25,576]{1,0:T(8,128)} custom-call(s32[4]{0:T(128)S(1)} %pad_add_fusion.sc, f32[32,640]{1,0:T(8,128)S(1)} %get-tuple-element.96.a0, f32[32,640]{1,0:T(8,128)S(1)} %collective-permute-done.20.a1, f32[32,640]{1,0:T(8,128)S(1)} %collective-permute-done.21.a2, f32[32,640]{1,0:T(8,128)S(1)} %collective-permute-done.22.a3), custom_call_target="tpu_custom_call" | custom-call | tf_op jit(solution)/shard_map/final/pallas_call | solution.py:385
  (52 shorter events, 7.7 us)
Async XLA Ops:
  1.5 1.3 %collective-permute-start = (bf16[16,576]{1,0:T(8,128)(2,1)S(1)}, bf16[16,576]{1,0:T(8,128)(2,1)S(1)}, u32[]{:S(2)}, u32[]{:S(2)}) collective-permute-start(bf16[16,576]{1,0:T(8,128)(2,1)S(1)} %get-tuple-element.107), channel_id=1, source_target_pairs={{0,8},{8,0},{1,9},{9,1},{2,10},{10,2},{3,11},{11,3},{4,12},{12,4},... | collective-permute-start | bytes 55304 | tf_op jit(solution)/shard_map/ppermute | solution.py:420
  2.9 8.2 %collective-permute-start.1 = (bf16[16,1152]{1,0:T(8,128)(2,1)S(1)}, bf16[16,1152]{1,0:T(8,128)(2,1)S(1)}, u32[]{:S(2)}, u32[]{:S(2)}) collective-permute-start(bf16[16,1152]{1,0:T(8,128)(2,1)S(1)} %maximum_select_fusion), channel_id=1, source_target_pairs={{0,16},{8,24},{1,17},{9,25},{2,18},{10,26},{3,19},{11,27},{4,20},{... | collective-permute-start | bytes 110600 | tf_op jit(solution)/shard_map/ppermute | solution.py:420
  11.1 6.7 %collective-permute-start.2 = (bf16[2,16,1152]{2,1,0:T(8,128)(2,1)S(1)}, bf16[2,16,1152]{2,1,0:T(8,128)(2,1)S(1)}, u32[]{:S(2)}, u32[]{:S(2)}) collective-permute-start(bf16[2,16,1152]{2,1,0:T(8,128)(2,1)S(1)} %pad_maximum_fusion.4), channel_id=1, source_target_pairs={{0,32},{8,40},{1,33},{9,41},{2,34},{10,42},{3,35},{11,43},{4,36},{... | collective-permute-start | bytes 221192 | tf_op jit(solution)/shard_map/ppermute | solution.py:420
  17.9 9.5 %copy-start.1 = (bf16[592,576]{1,0:T(8,128)(2,1)S(1)}, bf16[592,576]{1,0:T(8,128)(2,1)}, u32[]{:S(2)}) copy-start(bf16[592,576]{1,0:T(8,128)(2,1)} %constant.82.clone.f_ref) | copy-start | bytes 2045956
  17.9 8.5 %collective-permute-start.6 = (bf16[2,2,16,1152]{3,2,1,0:T(8,128)(2,1)S(1)}, bf16[2,2,16,1152]{3,2,1,0:T(8,128)(2,1)}, u32[]{:S(2)}, u32[]{:S(2)}) collective-permute-start(bf16[2,2,16,1152]{3,2,1,0:T(8,128)(2,1)S(1)} %pad_maximum_fusion.3), channel_id=1, source_target_pairs={{0,64},{8,72},{1,65},{9,73},{2,66},{10,74},{3,67},{11,75},{4,68},{... | collective-permute-start | bytes 442376 | tf_op jit(solution)/shard_map/ppermute | solution.py:420
  20.9 36.0 %copy-start = (bf16[16,576,128]{2,1,0:T(8,128)(2,1)S(1)}, bf16[16,576,128]{2,1,0:T(8,128)(2,1)}, u32[]{:S(2)}) copy-start(bf16[16,576,128]{2,1,0:T(8,128)(2,1)} %get-tuple-element.76.w_ref) | copy-start | bytes 7077892
  20.9 31.0 %collective-permute-start.3 = (bf16[128,2432]{1,0:T(8,128)(2,1)}, bf16[128,2432]{1,0:T(8,128)(2,1)S(1)}, u32[]{:S(2)}, u32[]{:S(2)}) collective-permute-start(bf16[128,2432]{1,0:T(8,128)(2,1)} %get-tuple-element.72), channel_id=1, source_target_pairs={{0,32},{8,40},{1,33},{9,41},{2,34},{10,42},{3,35},{11,43},{4,36},{... | collective-permute-start | bytes 1867784 | tf_op jit(solution)/shard_map/ppermute | solution.py:420
  27.8 8.4 %collective-permute-start.9 = (bf16[37,16,256]{2,1,0:T(8,128)(2,1)S(1)}, bf16[37,16,256]{2,1,0:T(8,128)(2,1)S(1)}, u32[]{:S(2)}, u32[]{:S(2)}) collective-permute-start(bf16[37,16,256]{2,1,0:T(8,128)(2,1)S(1)} %ref_spectra.1), channel_id=1, source_target_pairs={{0,3},{8,11},{1,0},{9,8},{2,1},{10,9},{3,2},{11,10},{4,7},{12,15},... | collective-permute-start | bytes 909320 | tf_op jit(solution)/shard_map/ppermute | solution.py:420
  31.9 6.9 %collective-permute-start.7 = (bf16[37,16,256]{2,1,0:T(8,128)(2,1)S(1)}, bf16[37,16,256]{2,1,0:T(8,128)(2,1)}, u32[]{:S(2)}, u32[]{:S(2)}) collective-permute-start(bf16[37,16,256]{2,1,0:T(8,128)(2,1)S(1)} %ref_spectra.1), channel_id=1, source_target_pairs={{0,4},{8,12},{1,5},{9,13},{2,6},{10,14},{3,7},{11,15},{4,0},{12,8}... | collective-permute-start | bytes 909320 | tf_op jit(solution)/shard_map/ppermute | solution.py:420
  32.5 29.2 %collective-permute-start.4 = (bf16[128,2432]{1,0:T(8,128)(2,1)}, bf16[128,2432]{1,0:T(8,128)(2,1)}, u32[]{:S(2)}, u32[]{:S(2)}) collective-permute-start(bf16[128,2432]{1,0:T(8,128)(2,1)} %get-tuple-element.73), channel_id=1, source_target_pairs={{0,64},{8,72},{1,65},{9,73},{2,66},{10,74},{3,67},{11,75},{4,68},{... | collective-permute-start | bytes 1867784 | tf_op jit(solution)/shard_map/ppermute | solution.py:420
  35.4 26.4 %collective-permute-start.5 = (bf16[128,2432]{1,0:T(8,128)(2,1)}, bf16[128,2432]{1,0:T(8,128)(2,1)}, u32[]{:S(2)}, u32[]{:S(2)}) collective-permute-start(bf16[128,2432]{1,0:T(8,128)(2,1)} %get-tuple-element.74), channel_id=1, source_target_pairs={{0,96},{8,104},{1,97},{9,105},{2,98},{10,106},{3,99},{11,107},{4,1... | collective-permute-start | bytes 1867784 | tf_op jit(solution)/shard_map/ppermute | solution.py:420
  36.2 15.7 %copy-start.7 = (bf16[37,16,256]{2,1,0:T(8,128)(2,1)}, bf16[37,16,256]{2,1,0:T(8,128)(2,1)S(1)}, u32[]{:S(2)}) copy-start(bf16[37,16,256]{2,1,0:T(8,128)(2,1)S(1)} %collective-permute-done.9) | copy-start | bytes 909316
  36.2 8.6 %collective-permute-start.8 = (bf16[37,16,256]{2,1,0:T(8,128)(2,1)S(1)}, bf16[37,16,256]{2,1,0:T(8,128)(2,1)}, u32[]{:S(2)}, u32[]{:S(2)}) collective-permute-start(bf16[37,16,256]{2,1,0:T(8,128)(2,1)S(1)} %ref_spectra.1), channel_id=1, source_target_pairs={{0,1},{8,9},{1,2},{9,10},{2,3},{10,11},{3,0},{11,8},{4,5},{12,13},... | collective-permute-start | bytes 909320 | tf_op jit(solution)/shard_map/ppermute | solution.py:420
  38.8 15.9 %collective-permute-start.11 = (bf16[37,16,256]{2,1,0:T(8,128)(2,1)}, bf16[37,16,256]{2,1,0:T(8,128)(2,1)}, u32[]{:S(2)}, u32[]{:S(2)}) collective-permute-start(bf16[37,16,256]{2,1,0:T(8,128)(2,1)} %collective-permute-done.7), channel_id=1, source_target_pairs={{0,3},{8,11},{1,0},{9,8},{2,1},{10,9},{3,2},{11,10},{4,7},{12,15},... | collective-permute-start | bytes 909320 | tf_op jit(solution)/shard_map/ppermute | solution.py:420
  44.8 17.0 %collective-permute-start.10 = (bf16[37,16,256]{2,1,0:T(8,128)(2,1)}, bf16[37,16,256]{2,1,0:T(8,128)(2,1)}, u32[]{:S(2)}, u32[]{:S(2)}) collective-permute-start(bf16[37,16,256]{2,1,0:T(8,128)(2,1)} %collective-permute-done.7), channel_id=1, source_target_pairs={{0,1},{8,9},{1,2},{9,10},{2,3},{10,11},{3,0},{11,8},{4,5},{12,13},... | collective-permute-start | bytes 909320 | tf_op jit(solution)/shard_map/ppermute | solution.py:420
  52.0 0.8 copy-start.4
  52.8 9.1 %collective-permute-start.12 = (bf16[37,16,256]{2,1,0:T(8,128)(2,1)}, bf16[37,16,256]{2,1,0:T(8,128)(2,1)}, u32[]{:S(2)}, u32[]{:S(2)}) collective-permute-start(bf16[37,16,256]{2,1,0:T(8,128)(2,1)} %collective-permute-done.8), channel_id=1, source_target_pairs={{0,1},{8,9},{1,2},{9,10},{2,3},{10,11},{3,0},{11,8},{4,5},{12,13},... | collective-permute-start | bytes 909320 | tf_op jit(solution)/shard_map/ppermute | solution.py:420
  54.7 7.2 %collective-permute-start.13 = (bf16[37,16,256]{2,1,0:T(8,128)(2,1)}, bf16[37,16,256]{2,1,0:T(8,128)(2,1)}, u32[]{:S(2)}, u32[]{:S(2)}) collective-permute-start(bf16[37,16,256]{2,1,0:T(8,128)(2,1)} %collective-permute-done.11), channel_id=1, source_target_pairs={{0,3},{8,11},{1,0},{9,8},{2,1},{10,9},{3,2},{11,10},{4,7},{12,15},... | collective-permute-start | bytes 909320 | tf_op jit(solution)/shard_map/ppermute | solution.py:420
  56.9 3.4 %copy-start.8 = (bf16[37,16,256]{2,1,0:T(8,128)(2,1)S(1)}, bf16[37,16,256]{2,1,0:T(8,128)(2,1)}, u32[]{:S(2)}) copy-start(bf16[37,16,256]{2,1,0:T(8,128)(2,1)} %copy-done.7) | copy-start | bytes 909316
  60.3 1.6 %copy-start.2 = (bf16[128,2432]{1,0:T(8,128)(2,1)S(1)}, bf16[128,2432]{1,0:T(8,128)(2,1)}, u32[]{:S(2)}) copy-start(bf16[128,2432]{1,0:T(8,128)(2,1)} %get-tuple-element.81.c0) | copy-start | bytes 1867780
  60.3 1.6 %copy-start.3 = (f32[256,64]{0,1:T(8,128)S(1)}, f32[256,64]{0,1:T(8,128)}, u32[]{:S(2)}) copy-start(f32[256,64]{0,1:T(8,128)} %param.19) | copy-start | bytes 196612
  60.4 1.6 %copy-start.5 = (bf16[128,2432]{1,0:T(8,128)(2,1)S(1)}, bf16[128,2432]{1,0:T(8,128)(2,1)}, u32[]{:S(2)}) copy-start(bf16[128,2432]{1,0:T(8,128)(2,1)} %copy-done.4) | copy-start | bytes 1867780
  61.7 10.5 %collective-permute-start.18 = (bf16[4,37,16,256]{3,2,1,0:T(8,128)(2,1)S(1)}, bf16[4,37,16,256]{3,2,1,0:T(8,128)(2,1)S(1)}, u32[]{:S(2)}, u32[]{:S(2)}) collective-permute-start(bf16[4,37,16,256]{3,2,1,0:T(8,128)(2,1)S(1)} %pad_maximum_fusion.refs_1_), channel_id=1, source_target_pairs={{0,8},{8,0},{1,9},{9,1},{2,10},{10,2},{3,11},{11,3},{4,12},{12,4},... | collective-permute-start | bytes 3637256 | tf_op jit(solution)/shard_map/ppermute | solution.py:420
  64.8 3.1 %collective-permute-start.14 = (f32[2,256,640]{2,1,0:T(8,128)S(1)}, f32[2,256,640]{2,1,0:T(8,128)S(1)}, u32[]{:S(2)}, u32[]{:S(2)}) collective-permute-start(f32[2,256,640]{2,1,0:T(8,128)S(1)} %get-tuple-element.86), channel_id=1, source_target_pairs={{0,8},{8,0},{1,9},{9,1},{2,10},{10,2},{3,11},{11,3},{4,12},{12,4},... | collective-permute-start | bytes 3932168 | tf_op jit(solution)/shard_map/ppermute | solution.py:420
  66.6 5.6 %collective-permute-start.19 = (bf16[4,37,16,256]{3,2,1,0:T(8,128)(2,1)S(1)}, bf16[4,37,16,256]{3,2,1,0:T(8,128)(2,1)S(1)}, u32[]{:S(2)}, u32[]{:S(2)}) collective-permute-start(bf16[4,37,16,256]{3,2,1,0:T(8,128)(2,1)S(1)} %pad_maximum_fusion.1.refs_3_), channel_id=1, source_target_pairs={{0,8},{8,0},{1,9},{9,1},{2,10},{10,2},{3,11},{11,3},{4,12},{12,4},... | collective-permute-start | bytes 3637256 | tf_op jit(solution)/shard_map/ppermute | solution.py:420
  67.9 4.3 %copy-start.6 = (bf16[576,640]{1,0:T(8,128)(2,1)S(1)}, bf16[576,640]{1,0:T(8,128)(2,1)}, u32[]{:S(2)}) copy-start(bf16[576,640]{1,0:T(8,128)(2,1)} %constant.83.clone.refs_5_) | copy-start | bytes 2211844
  68.6 18.3 %collective-permute-start.15 = (f32[128,640]{1,0:T(8,128)S(1)}, f32[128,640]{1,0:T(8,128)S(1)}, u32[]{:S(2)}, u32[]{:S(2)}) collective-permute-start(f32[128,640]{1,0:T(8,128)S(1)} %get-tuple-element.88), channel_id=1, source_target_pairs={{0,4},{8,12},{1,5},{9,13},{2,6},{10,14},{3,7},{11,15},{4,16},{12,2... | collective-permute-start | bytes 983048 | tf_op jit(solution)/shard_map/ppermute | solution.py:420
  69.3 17.6 %collective-permute-start.16 = (f32[128,640]{1,0:T(8,128)S(1)}, f32[128,640]{1,0:T(8,128)S(1)}, u32[]{:S(2)}, u32[]{:S(2)}) collective-permute-start(f32[128,640]{1,0:T(8,128)S(1)} %get-tuple-element.89), channel_id=1, source_target_pairs={{0,16},{8,24},{1,17},{9,25},{2,18},{10,26},{3,19},{11,27},{4,20},{... | collective-permute-start | bytes 983048 | tf_op jit(solution)/shard_map/ppermute | solution.py:420
  71.3 16.2 %collective-permute-start.17 = (f32[128,640]{1,0:T(8,128)S(1)}, f32[128,640]{1,0:T(8,128)S(1)}, u32[]{:S(2)}, u32[]{:S(2)}) collective-permute-start(f32[128,640]{1,0:T(8,128)S(1)} %get-tuple-element.90), channel_id=1, source_target_pairs={{0,20},{8,28},{1,21},{9,29},{2,22},{10,30},{3,23},{11,31},{4,0},{1... | collective-permute-start | bytes 983048 | tf_op jit(solution)/shard_map/ppermute | solution.py:420
  88.1 6.6 %collective-permute-start.20 = (f32[32,640]{1,0:T(8,128)S(1)}, f32[32,640]{1,0:T(8,128)S(1)}, u32[]{:S(2)}, u32[]{:S(2)}) collective-permute-start(f32[32,640]{1,0:T(8,128)S(1)} %get-tuple-element.97), channel_id=1, source_target_pairs={{0,1},{8,9},{1,2},{9,10},{2,3},{10,11},{3,0},{11,8},{4,5},{12,13},... | collective-permute-start | bytes 245768 | tf_op jit(solution)/shard_map/ppermute | solution.py:420
  89.8 6.2 %collective-permute-start.21 = (f32[32,640]{1,0:T(8,128)S(1)}, f32[32,640]{1,0:T(8,128)S(1)}, u32[]{:S(2)}, u32[]{:S(2)}) collective-permute-start(f32[32,640]{1,0:T(8,128)S(1)} %get-tuple-element.98), channel_id=1, source_target_pairs={{0,2},{8,10},{1,3},{9,11},{2,0},{10,8},{3,1},{11,9},{4,6},{12,14},... | collective-permute-start | bytes 245768 | tf_op jit(solution)/shard_map/ppermute | solution.py:420
  92.7 4.4 %collective-permute-start.22 = (f32[32,640]{1,0:T(8,128)S(1)}, f32[32,640]{1,0:T(8,128)S(1)}, u32[]{:S(2)}, u32[]{:S(2)}) collective-permute-start(f32[32,640]{1,0:T(8,128)S(1)} %get-tuple-element.99), channel_id=1, source_target_pairs={{0,3},{8,11},{1,0},{9,8},{2,1},{10,9},{3,2},{11,10},{4,7},{12,15},... | collective-permute-start | bytes 245768 | tf_op jit(solution)/shard_map/ppermute | solution.py:420

commit v6 on v5

--- a/solution.py
+++ b/solution.py
@@ -328,7 +328,7 @@
         x = lax.rem(sc[1] + dx, 4)
         xh, xl = x // 2, lax.rem(x, 2)
         rows = pl.ds(pl.multiple_of(xl * 128, 128), 128)
-        o[...] = a_ref[xh, rows, :] + b_ref[xh, rows, :]
+        o[...] = (a_ref[xh, rows, :] + b_ref[xh, rows, :]).astype(o.dtype)
 
 
 def cut_x(sc, a, b):
@@ -337,7 +337,7 @@
         cut_x_kernel,
         in_specs=[pl.BlockSpec(memory_space=pltpu.SMEM), v, v],
         out_specs=[v] * 4,
-        out_shape=[jax.ShapeDtypeStruct((128, 640), F32)] * 4,
+        out_shape=[jax.ShapeDtypeStruct((128, 640), F32)] + [jax.ShapeDtypeStruct((128, 640), BF)] * 3,
         compiler_params=pltpu.CompilerParams(vmem_limit_bytes=VMEM_LIMIT),
         cost_estimate=pl.CostEstimate(flops=400_000, bytes_accessed=3_900_000, transcendentals=0),
         name="cut_x",
@@ -348,7 +348,8 @@
     for dz, o in enumerate((o0, o1, o2, o3)):
         z = lax.rem(sc[3] + dz, 4)
         rows = pl.ds(pl.multiple_of(z * 32, 32), 32)
-        o[...] = (a0[rows, :] + a1[rows, :]) + (a2[rows, :] + a3[rows, :])
+        far = a1[rows, :].astype(F32) + a2[rows, :].astype(F32) + a3[rows, :].astype(F32)
+        o[...] = a0[rows, :] + far
 
 
 def cut_z(sc, parts):

time: 98.9 us -> 91.8 us (0.928)
  waiting for transfers between devices: 33.1 us -> 26.1 us
    ppermute x23, waiting for transfers between devices: 33.1 us -> 26.1 us  [move(): return lax.ppermute(value, AXES, pairs)]
  transfers between devices with their start and end apart: 23 -> 23, of which waited for: 13 -> 12; matrix products, arithmetic and copies ran while one was open for 4% -> 4% of each run, Pallas kernels for 26% -> 28%
where the time goes in v6:
time: 91.8 us; the launch traced here: 91.4 us
  starting transfers between devices  31.6 us (34%)
  Pallas kernels  27.3 us (30%)
  waiting for transfers between devices  26.1 us (28%)
  other arithmetic  4.75 us (5%)
    ppermute x23, starting transfers between devices, move(): return lax.ppermute(value, AXES, pairs)  31.6 us
    ppermute x23, waiting for transfers between devices, move(): return lax.ppermute(value, AXES, pairs)  26.1 us
    pallas_call x2, Pallas kernels, prep(): pl.pallas_call(functools.partial(prep_kernel, first), grid=(n // 32,), in...  10.1 us
    pallas_call x1, Pallas kernels, scores_of(): pl.pallas_call(score_kernel, in_specs=[v] * 6, out_specs=v, out_shape=jax...  7.93 us
    pallas_call x1, Pallas kernels, spectra(): pl.pallas_call(spectra_kernel, in_specs=[v, v], out_specs=v, out_shape=ja...  3.4 us
    pallas_call x1, Pallas kernels, class_sums(): pl.pallas_call(sums_kernel, in_specs=[pl.BlockSpec(memory_space=pltpu.SME...  2.83 us
  transfers between devices with their start and end apart: 23, of which 12 were waited for; matrix products, arithmetic and copies ran while one was open for 4% of the time, Pallas kernels for 28%

profile of v6, /device:TPU:0, one launch (start us, length us, event | category | flops | bytes accessed | tf_op | source)
XLA Modules:
  0.0 91.4 jit_solution(1301406286016642614)
XLA Ops:
  0.6 0.8 broadcast_select_fusion.1
  1.6 1.2 %collective-permute-done = bf16[16,576]{1,0:T(8,128)(2,1)S(1)} collective-permute-done((bf16[16,576]{1,0:T(8,128)(2,1)S(1)}, bf16[16,576]{1,0:T(8,128)(2,1)S(1)}, u32[]{:S(2)}, u32[]{:S(2)}) %collective-permute-start) | collective-permute-done | bytes 18464 | tf_op jit(solution)/shard_map/ppermute | solution.py:421
  2.9 3.2 %collective-permute-start.1 = (bf16[16,1152]{1,0:T(8,128)(2,1)S(1)}, bf16[16,1152]{1,0:T(8,128)(2,1)S(1)}, u32[]{:S(2)}, u32[]{:S(2)}) collective-permute-start(bf16[16,1152]{1,0:T(8,128)(2,1)S(1)} %maximum_select_fusion), channel_id=1, source_target_pairs={{0,16},{8,24},{1,17},{9,25},{2,18},{10,26},{3,19},{11,27},{4,20},{... | collective-permute-start | bytes 110600 | tf_op jit(solution)/shard_map/ppermute | solution.py:421
  6.0 5.0 %prep.2 = (bf16[16,576,128]{2,1,0:T(8,128)(2,1)}, bf16[128,2432]{1,0:T(8,128)(2,1)}, bf16[128,2432]{1,0:T(8,128)(2,1)}, bf16[128,2432]{1,0:T(8,128)(2,1)}, bf16[128,2432]{1,0:T(8,128)(2,1)}) custom-call(bf16[128,9216]{1,0:T(8,128)(2,1)} %x_ref.3, s32[2,128]{1,0:T(2,128)} %bitcast.38, s32[1,128]{1,0:T(1,128)} %bitcast.40, s32[1,128]{1,0:T(1,128)} %bitcast.42, ...), custom_call_target="tpu_custom_call" | custom-call | flops 20000000 | bytes 4000000 | tf_op jit(solution)/shard_map/prep/pallas_call | solution.py:144
  11.1 1.7 %collective-permute-start.2 = (bf16[2,16,1152]{2,1,0:T(8,128)(2,1)S(1)}, bf16[2,16,1152]{2,1,0:T(8,128)(2,1)S(1)}, u32[]{:S(2)}, u32[]{:S(2)}) collective-permute-start(bf16[2,16,1152]{2,1,0:T(8,128)(2,1)S(1)} %pad_maximum_fusion.4), channel_id=1, source_target_pairs={{0,32},{8,40},{1,33},{9,41},{2,34},{10,42},{3,35},{11,43},{4,36},{... | collective-permute-start | bytes 221192 | tf_op jit(solution)/shard_map/ppermute | solution.py:421
  12.8 5.1 %prep.3 = (bf16[16,576,128]{2,1,0:T(8,128)(2,1)}, bf16[128,2432]{1,0:T(8,128)(2,1)}, bf16[128,2432]{1,0:T(8,128)(2,1)}, bf16[128,2432]{1,0:T(8,128)(2,1)}, bf16[128,2432]{1,0:T(8,128)(2,1)}) custom-call(bf16[128,9216]{1,0:T(8,128)(2,1)} %x_ref.3, s32[2,128]{1,0:T(2,128)} %bitcast.39, ...), custom_call_target="tpu_custom_call", output_to_operand_aliasing={{0}: (9, {}), {1}: (10, {}), {2}: (11, {}), {3}: (12, {}), ... | custom-call | flops 20000000 | bytes 4000000 | tf_op jit(solution)/shard_map/prep/pallas_call | solution.py:144
  17.9 3.0 %collective-permute-start.6 = (bf16[2,2,16,1152]{3,2,1,0:T(8,128)(2,1)S(1)}, bf16[2,2,16,1152]{3,2,1,0:T(8,128)(2,1)}, u32[]{:S(2)}, u32[]{:S(2)}) collective-permute-start(bf16[2,2,16,1152]{3,2,1,0:T(8,128)(2,1)S(1)} %pad_maximum_fusion.3), channel_id=1, source_target_pairs={{0,64},{8,72},{1,65},{9,73},{2,66},{10,74},{3,67},{11,75},{4,68},{... | collective-permute-start | bytes 442376 | tf_op jit(solution)/shard_map/ppermute | solution.py:421
  21.1 5.3 %collective-permute-done.6 = bf16[2,2,16,1152]{3,2,1,0:T(8,128)(2,1)} collective-permute-done((bf16[2,2,16,1152]{3,2,1,0:T(8,128)(2,1)S(1)}, bf16[2,2,16,1152]{3,2,1,0:T(8,128)(2,1)}, u32[]{:S(2)}, u32[]{:S(2)}) %collective-permute-start.6) | collective-permute-done | bytes 147488 | tf_op jit(solution)/shard_map/ppermute | solution.py:421
  26.4 0.9 %select_bitcast_fusion.1 = (bf16[1,2,2,16,1152]{4,3,2,1,0:T(8,128)(2,1)S(1)}, bf16[1,2,2,16,1152]{4,3,2,1,0:T(8,128)(2,1)S(1)}) fusion(bf16[2,2,16,1152]{3,2,1,0:T(8,128)(2,1)} %collective-permute-done.6, pred[]{:T(512)S(6)} %eq.19, bf16[1,2,16,1152]{3,2,1,0:T(8,128)(2,1)S(1)} %get-tuple-element.103, bf16[1,2,16,1152]{3,2,1,0:T(8,128)(2,1)S(1)} %get-tuple-element.102), kind=kLoop, calls=%fused_computation.5 | loop fusion | flops 221184 | bytes 589825 | tf_op jit(solution)/shard_map/stack | solution.py:430
  27.8 4.1 %collective-permute-start.9 = (bf16[37,16,256]{2,1,0:T(8,128)(2,1)S(1)}, bf16[37,16,256]{2,1,0:T(8,128)(2,1)S(1)}, u32[]{:S(2)}, u32[]{:S(2)}) collective-permute-start(bf16[37,16,256]{2,1,0:T(8,128)(2,1)S(1)} %ref_spectra.1), channel_id=1, source_target_pairs={{0,3},{8,11},{1,0},{9,8},{2,1},{10,9},{3,2},{11,10},{4,7},{12,15},... | collective-permute-start | bytes 909320 | tf_op jit(solution)/shard_map/ppermute | solution.py:421
  32.5 2.9 %collective-permute-start.4 = (bf16[128,2432]{1,0:T(8,128)(2,1)}, bf16[128,2432]{1,0:T(8,128)(2,1)}, u32[]{:S(2)}, u32[]{:S(2)}) collective-permute-start(bf16[128,2432]{1,0:T(8,128)(2,1)} %get-tuple-element.73), channel_id=1, source_target_pairs={{0,64},{8,72},{1,65},{9,73},{2,66},{10,74},{3,67},{11,75},{4,68},{... | collective-permute-start | bytes 1867784 | tf_op jit(solution)/shard_map/ppermute | solution.py:421
  36.6 2.2 %collective-permute-done.7 = bf16[37,16,256]{2,1,0:T(8,128)(2,1)} collective-permute-done((bf16[37,16,256]{2,1,0:T(8,128)(2,1)S(1)}, bf16[37,16,256]{2,1,0:T(8,128)(2,1)}, u32[]{:S(2)}, u32[]{:S(2)}) %collective-permute-start.7) | collective-permute-done | bytes 303136 | tf_op jit(solution)/shard_map/ppermute | solution.py:421
  38.8 1.2 %collective-permute-start.11 = (bf16[37,16,256]{2,1,0:T(8,128)(2,1)}, bf16[37,16,256]{2,1,0:T(8,128)(2,1)}, u32[]{:S(2)}, u32[]{:S(2)}) collective-permute-start(bf16[37,16,256]{2,1,0:T(8,128)(2,1)} %collective-permute-done.7), channel_id=1, source_target_pairs={{0,3},{8,11},{1,0},{9,8},{2,1},{10,9},{3,2},{11,10},{4,7},{12,15},... | collective-permute-start | bytes 909320 | tf_op jit(solution)/shard_map/ppermute | solution.py:421
  40.0 4.8 %collective-permute-done.8 = bf16[37,16,256]{2,1,0:T(8,128)(2,1)} collective-permute-done((bf16[37,16,256]{2,1,0:T(8,128)(2,1)S(1)}, bf16[37,16,256]{2,1,0:T(8,128)(2,1)}, u32[]{:S(2)}, u32[]{:S(2)}) %collective-permute-start.8) | collective-permute-done | bytes 303136 | tf_op jit(solution)/shard_map/ppermute | solution.py:421
  44.8 7.1 %collective-permute-done.3.c1 = bf16[128,2432]{1,0:T(8,128)(2,1)S(1)} collective-permute-done((bf16[128,2432]{1,0:T(8,128)(2,1)}, bf16[128,2432]{1,0:T(8,128)(2,1)S(1)}, u32[]{:S(2)}, u32[]{:S(2)}) %collective-permute-start.3) | collective-permute-done | bytes 622624 | tf_op jit(solution)/shard_map/ppermute | solution.py:421
  52.0 0.8 copy-done.4
  52.8 1.9 %collective-permute-start.12 = (bf16[37,16,256]{2,1,0:T(8,128)(2,1)}, bf16[37,16,256]{2,1,0:T(8,128)(2,1)}, u32[]{:S(2)}, u32[]{:S(2)}) collective-permute-start(bf16[37,16,256]{2,1,0:T(8,128)(2,1)} %collective-permute-done.8), channel_id=1, source_target_pairs={{0,1},{8,9},{1,2},{9,10},{2,3},{10,11},{3,0},{11,8},{4,5},{12,13},... | collective-permute-start | bytes 909320 | tf_op jit(solution)/shard_map/ppermute | solution.py:421
  54.7 2.1 %collective-permute-start.13 = (bf16[37,16,256]{2,1,0:T(8,128)(2,1)}, bf16[37,16,256]{2,1,0:T(8,128)(2,1)}, u32[]{:S(2)}, u32[]{:S(2)}) collective-permute-start(bf16[37,16,256]{2,1,0:T(8,128)(2,1)} %collective-permute-done.11), channel_id=1, source_target_pairs={{0,3},{8,11},{1,0},{9,8},{2,1},{10,9},{3,2},{11,10},{4,7},{12,15},... | collective-permute-start | bytes 909320 | tf_op jit(solution)/shard_map/ppermute | solution.py:421
  56.9 3.4 %spectra.1.refs_0_ = bf16[37,128,256]{2,1,0:T(8,128)(2,1)S(1)} custom-call(bf16[16,576,128]{2,1,0:T(8,128)(2,1)S(1)} %copy-done, bf16[592,576]{1,0:T(8,128)(2,1)S(1)} %copy-done.1), custom_call_target="tpu_custom_call" | custom-call | flops 1000 | bytes 1000 | tf_op jit(solution)/shard_map/spectra/pallas_call | solution.py:194
  60.4 1.3 %pad_maximum_fusion.refs_1_ = bf16[4,37,16,256]{3,2,1,0:T(8,128)(2,1)S(1)} fusion(bf16[1,37,16,256]{3,2,1,0:T(8,128)(2,1)S(1)} %bitcast.37, bf16[1,37,16,256]{3,2,1,0:T(8,128)(2,1)} %bitcast.19, bf16[1,37,16,256]{3,2,1,0:T(8,128)(2,1)} %bitcast.18, bf16[1,37,16,256]{3,2,1,0:T(8,128)(2,1)S(1)} %bitcast.32), kind=kLoop, calls=%fused_computation | loop fusion | flops 1818624 | bytes 2424832 | tf_op jit(solution)/shard_map/stack | solution.py:472
  62.0 2.8 %class_sums.1 = (f32[2,256,640]{2,1,0:T(8,128)S(1)}, f32[2,256,640]{2,1,0:T(8,128)S(1)}) custom-call(s32[4]{0:T(128)S(1)} %pad_add_fusion.sc, bf16[128,2432]{1,0:T(8,128)(2,1)S(1)} %copy-done.2, bf16[128,2432]{1,0:T(8,128)(2,1)S(1)} %copy-done.5, bf16[128,2432]{1,0:T(8,128)(2,1)} %collective-permute-done.4.c2, bf16[128,2432]{1,0:T(8,128)(2,1)} %collective-permute-done.5.c3, ...), custom_call_target="tpu_custom_call" | custom-call | flops 700000000 | bytes 5000000 | tf_op jit(solution)/shard_map/class_sums/pallas_call | solution.py:314
  65.2 1.4 %pad_maximum_fusion.1.refs_3_ = bf16[4,37,16,256]{3,2,1,0:T(8,128)(2,1)S(1)} fusion(bf16[1,37,16,256]{3,2,1,0:T(8,128)(2,1)} %bitcast.24, bf16[1,37,16,256]{3,2,1,0:T(8,128)(2,1)} %bitcast.23, bf16[1,37,16,256]{3,2,1,0:T(8,128)(2,1)} %bitcast.22, bf16[1,37,16,256]{3,2,1,0:T(8,128)(2,1)} %bitcast.21), kind=kLoop, calls=%fused_computation.1 | loop fusion | flops 1818624 | bytes 2424832 | tf_op jit(solution)/shard_map/stack | solution.py:478
  66.9 1.1 %collective-permute-done.14.b_ref = f32[2,256,640]{2,1,0:T(8,128)S(1)} collective-permute-done((f32[2,256,640]{2,1,0:T(8,128)S(1)}, f32[2,256,640]{2,1,0:T(8,128)S(1)}, u32[]{:S(2)}, u32[]{:S(2)}) %collective-permute-start.14) | collective-permute-done | bytes 1310752 | tf_op jit(solution)/shard_map/ppermute | solution.py:421
  69.3 2.0 %collective-permute-start.16 = (bf16[128,640]{1,0:T(8,128)(2,1)S(1)}, bf16[128,640]{1,0:T(8,128)(2,1)S(1)}, u32[]{:S(2)}, u32[]{:S(2)}) collective-permute-start(bf16[128,640]{1,0:T(8,128)(2,1)S(1)} %get-tuple-element.89), channel_id=1, source_target_pairs={{0,16},{8,24},{1,17},{9,25},{2,18},{10,26},{3,19},{11,27},{4,20},{... | collective-permute-start | bytes 491528 | tf_op jit(solution)/shard_map/ppermute | solution.py:421
  71.3 0.9 %collective-permute-start.17 = (bf16[128,640]{1,0:T(8,128)(2,1)S(1)}, bf16[128,640]{1,0:T(8,128)(2,1)S(1)}, u32[]{:S(2)}, u32[]{:S(2)}) collective-permute-start(bf16[128,640]{1,0:T(8,128)(2,1)S(1)} %get-tuple-element.90), channel_id=1, source_target_pairs={{0,20},{8,28},{1,21},{9,29},{2,22},{10,30},{3,23},{11,31},{4,0},{1... | collective-permute-start | bytes 491528 | tf_op jit(solution)/shard_map/ppermute | solution.py:421
  72.2 7.9 %scores.1 = f32[1,128]{1,0:T(1,128)} custom-call(bf16[37,128,256]{2,1,0:T(8,128)(2,1)S(1)} %spectra.1.refs_0_, bf16[4,37,16,256]{3,2,1,0:T(8,128)(2,1)S(1)} %pad_maximum_fusion.refs_1_, bf16[4,37,16,256]{3,2,1,0:T(8,128)(2,1)S(1)} %collective-permute-done.18.refs_2_, bf16[4,37,16,256]{3,2,1,0:T(8,128)(2,1)S(1)} %pad_maximum_fusion.1.refs_3_, ...), custom_call_target="tpu_custom_call" | custom-call | flops 6000000000 | bytes 8000000 | tf_op jit(solution)/shard_map/scores/pallas_call | solution.py:271
  81.1 1.6 %collective-permute-start.20 = (f32[32,640]{1,0:T(8,128)S(1)}, f32[32,640]{1,0:T(8,128)S(1)}, u32[]{:S(2)}, u32[]{:S(2)}) collective-permute-start(f32[32,640]{1,0:T(8,128)S(1)} %get-tuple-element.97), channel_id=1, source_target_pairs={{0,1},{8,9},{1,2},{9,10},{2,3},{10,11},{3,0},{11,8},{4,5},{12,13},... | collective-permute-start | bytes 245768 | tf_op jit(solution)/shard_map/ppermute | solution.py:421
  82.8 2.9 %collective-permute-start.21 = (f32[32,640]{1,0:T(8,128)S(1)}, f32[32,640]{1,0:T(8,128)S(1)}, u32[]{:S(2)}, u32[]{:S(2)}) collective-permute-start(f32[32,640]{1,0:T(8,128)S(1)} %get-tuple-element.98), channel_id=1, source_target_pairs={{0,2},{8,10},{1,3},{9,11},{2,0},{10,8},{3,1},{11,9},{4,6},{12,14},... | collective-permute-start | bytes 245768 | tf_op jit(solution)/shard_map/ppermute | solution.py:421
  85.6 1.4 %collective-permute-start.22 = (f32[32,640]{1,0:T(8,128)S(1)}, f32[32,640]{1,0:T(8,128)S(1)}, u32[]{:S(2)}, u32[]{:S(2)}) collective-permute-start(f32[32,640]{1,0:T(8,128)S(1)} %get-tuple-element.99), channel_id=1, source_target_pairs={{0,3},{8,11},{1,0},{9,8},{2,1},{10,9},{3,2},{11,10},{4,7},{12,15},... | collective-permute-start | bytes 245768 | tf_op jit(solution)/shard_map/ppermute | solution.py:421
  87.7 1.5 %collective-permute-done.21.a2 = f32[32,640]{1,0:T(8,128)S(1)} collective-permute-done((f32[32,640]{1,0:T(8,128)S(1)}, f32[32,640]{1,0:T(8,128)S(1)}, u32[]{:S(2)}, u32[]{:S(2)}) %collective-permute-start.21) | collective-permute-done | bytes 81952 | tf_op jit(solution)/shard_map/ppermute | solution.py:421
  89.2 0.9 collective-permute-done.22.a3
  90.1 1.3 %final.1 = f32[25,576]{1,0:T(8,128)} custom-call(s32[4]{0:T(128)S(1)} %pad_add_fusion.sc, f32[32,640]{1,0:T(8,128)S(1)} %get-tuple-element.96.a0, f32[32,640]{1,0:T(8,128)S(1)} %collective-permute-done.20.a1, f32[32,640]{1,0:T(8,128)S(1)} %collective-permute-done.21.a2, f32[32,640]{1,0:T(8,128)S(1)} %collective-permute-done.22.a3), custom_call_target="tpu_custom_call" | custom-call | tf_op jit(solution)/shard_map/final/pallas_call | solution.py:386
  (52 shorter events, 6.6 us)
Async XLA Ops:
  1.5 1.3 %collective-permute-start = (bf16[16,576]{1,0:T(8,128)(2,1)S(1)}, bf16[16,576]{1,0:T(8,128)(2,1)S(1)}, u32[]{:S(2)}, u32[]{:S(2)}) collective-permute-start(bf16[16,576]{1,0:T(8,128)(2,1)S(1)} %get-tuple-element.107), channel_id=1, source_target_pairs={{0,8},{8,0},{1,9},{9,1},{2,10},{10,2},{3,11},{11,3},{4,12},{12,4},... | collective-permute-start | bytes 55304 | tf_op jit(solution)/shard_map/ppermute | solution.py:421
  2.9 8.2 %collective-permute-start.1 = (bf16[16,1152]{1,0:T(8,128)(2,1)S(1)}, bf16[16,1152]{1,0:T(8,128)(2,1)S(1)}, u32[]{:S(2)}, u32[]{:S(2)}) collective-permute-start(bf16[16,1152]{1,0:T(8,128)(2,1)S(1)} %maximum_select_fusion), channel_id=1, source_target_pairs={{0,16},{8,24},{1,17},{9,25},{2,18},{10,26},{3,19},{11,27},{4,20},{... | collective-permute-start | bytes 110600 | tf_op jit(solution)/shard_map/ppermute | solution.py:421
  11.1 6.7 %collective-permute-start.2 = (bf16[2,16,1152]{2,1,0:T(8,128)(2,1)S(1)}, bf16[2,16,1152]{2,1,0:T(8,128)(2,1)S(1)}, u32[]{:S(2)}, u32[]{:S(2)}) collective-permute-start(bf16[2,16,1152]{2,1,0:T(8,128)(2,1)S(1)} %pad_maximum_fusion.4), channel_id=1, source_target_pairs={{0,32},{8,40},{1,33},{9,41},{2,34},{10,42},{3,35},{11,43},{4,36},{... | collective-permute-start | bytes 221192 | tf_op jit(solution)/shard_map/ppermute | solution.py:421
  17.9 9.5 %copy-start.1 = (bf16[592,576]{1,0:T(8,128)(2,1)S(1)}, bf16[592,576]{1,0:T(8,128)(2,1)}, u32[]{:S(2)}) copy-start(bf16[592,576]{1,0:T(8,128)(2,1)} %constant.82.clone.f_ref) | copy-start | bytes 2045956
  17.9 8.5 %collective-permute-start.6 = (bf16[2,2,16,1152]{3,2,1,0:T(8,128)(2,1)S(1)}, bf16[2,2,16,1152]{3,2,1,0:T(8,128)(2,1)}, u32[]{:S(2)}, u32[]{:S(2)}) collective-permute-start(bf16[2,2,16,1152]{3,2,1,0:T(8,128)(2,1)S(1)} %pad_maximum_fusion.3), channel_id=1, source_target_pairs={{0,64},{8,72},{1,65},{9,73},{2,66},{10,74},{3,67},{11,75},{4,68},{... | collective-permute-start | bytes 442376 | tf_op jit(solution)/shard_map/ppermute | solution.py:421
  20.9 36.0 %copy-start = (bf16[16,576,128]{2,1,0:T(8,128)(2,1)S(1)}, bf16[16,576,128]{2,1,0:T(8,128)(2,1)}, u32[]{:S(2)}) copy-start(bf16[16,576,128]{2,1,0:T(8,128)(2,1)} %get-tuple-element.76.w_ref) | copy-start | bytes 7077892
  20.9 31.0 %collective-permute-start.3 = (bf16[128,2432]{1,0:T(8,128)(2,1)}, bf16[128,2432]{1,0:T(8,128)(2,1)S(1)}, u32[]{:S(2)}, u32[]{:S(2)}) collective-permute-start(bf16[128,2432]{1,0:T(8,128)(2,1)} %get-tuple-element.72), channel_id=1, source_target_pairs={{0,32},{8,40},{1,33},{9,41},{2,34},{10,42},{3,35},{11,43},{4,36},{... | collective-permute-start | bytes 1867784 | tf_op jit(solution)/shard_map/ppermute | solution.py:421
  27.8 8.4 %collective-permute-start.9 = (bf16[37,16,256]{2,1,0:T(8,128)(2,1)S(1)}, bf16[37,16,256]{2,1,0:T(8,128)(2,1)S(1)}, u32[]{:S(2)}, u32[]{:S(2)}) collective-permute-start(bf16[37,16,256]{2,1,0:T(8,128)(2,1)S(1)} %ref_spectra.1), channel_id=1, source_target_pairs={{0,3},{8,11},{1,0},{9,8},{2,1},{10,9},{3,2},{11,10},{4,7},{12,15},... | collective-permute-start | bytes 909320 | tf_op jit(solution)/shard_map/ppermute | solution.py:421
  31.9 6.9 %collective-permute-start.7 = (bf16[37,16,256]{2,1,0:T(8,128)(2,1)S(1)}, bf16[37,16,256]{2,1,0:T(8,128)(2,1)}, u32[]{:S(2)}, u32[]{:S(2)}) collective-permute-start(bf16[37,16,256]{2,1,0:T(8,128)(2,1)S(1)} %ref_spectra.1), channel_id=1, source_target_pairs={{0,4},{8,12},{1,5},{9,13},{2,6},{10,14},{3,7},{11,15},{4,0},{12,8}... | collective-permute-start | bytes 909320 | tf_op jit(solution)/shard_map/ppermute | solution.py:421
  32.5 29.2 %collective-permute-start.4 = (bf16[128,2432]{1,0:T(8,128)(2,1)}, bf16[128,2432]{1,0:T(8,128)(2,1)}, u32[]{:S(2)}, u32[]{:S(2)}) collective-permute-start(bf16[128,2432]{1,0:T(8,128)(2,1)} %get-tuple-element.73), channel_id=1, source_target_pairs={{0,64},{8,72},{1,65},{9,73},{2,66},{10,74},{3,67},{11,75},{4,68},{... | collective-permute-start | bytes 1867784 | tf_op jit(solution)/shard_map/ppermute | solution.py:421
  35.4 26.4 %collective-permute-start.5 = (bf16[128,2432]{1,0:T(8,128)(2,1)}, bf16[128,2432]{1,0:T(8,128)(2,1)}, u32[]{:S(2)}, u32[]{:S(2)}) collective-permute-start(bf16[128,2432]{1,0:T(8,128)(2,1)} %get-tuple-element.74), channel_id=1, source_target_pairs={{0,96},{8,104},{1,97},{9,105},{2,98},{10,106},{3,99},{11,107},{4,1... | collective-permute-start | bytes 1867784 | tf_op jit(solution)/shard_map/ppermute | solution.py:421
  36.2 15.7 %copy-start.7 = (bf16[37,16,256]{2,1,0:T(8,128)(2,1)}, bf16[37,16,256]{2,1,0:T(8,128)(2,1)S(1)}, u32[]{:S(2)}) copy-start(bf16[37,16,256]{2,1,0:T(8,128)(2,1)S(1)} %collective-permute-done.9) | copy-start | bytes 909316
  36.2 8.6 %collective-permute-start.8 = (bf16[37,16,256]{2,1,0:T(8,128)(2,1)S(1)}, bf16[37,16,256]{2,1,0:T(8,128)(2,1)}, u32[]{:S(2)}, u32[]{:S(2)}) collective-permute-start(bf16[37,16,256]{2,1,0:T(8,128)(2,1)S(1)} %ref_spectra.1), channel_id=1, source_target_pairs={{0,1},{8,9},{1,2},{9,10},{2,3},{10,11},{3,0},{11,8},{4,5},{12,13},... | collective-permute-start | bytes 909320 | tf_op jit(solution)/shard_map/ppermute | solution.py:421
  38.8 15.9 %collective-permute-start.11 = (bf16[37,16,256]{2,1,0:T(8,128)(2,1)}, bf16[37,16,256]{2,1,0:T(8,128)(2,1)}, u32[]{:S(2)}, u32[]{:S(2)}) collective-permute-start(bf16[37,16,256]{2,1,0:T(8,128)(2,1)} %collective-permute-done.7), channel_id=1, source_target_pairs={{0,3},{8,11},{1,0},{9,8},{2,1},{10,9},{3,2},{11,10},{4,7},{12,15},... | collective-permute-start | bytes 909320 | tf_op jit(solution)/shard_map/ppermute | solution.py:421
  44.8 17.0 %collective-permute-start.10 = (bf16[37,16,256]{2,1,0:T(8,128)(2,1)}, bf16[37,16,256]{2,1,0:T(8,128)(2,1)}, u32[]{:S(2)}, u32[]{:S(2)}) collective-permute-start(bf16[37,16,256]{2,1,0:T(8,128)(2,1)} %collective-permute-done.7), channel_id=1, source_target_pairs={{0,1},{8,9},{1,2},{9,10},{2,3},{10,11},{3,0},{11,8},{4,5},{12,13},... | collective-permute-start | bytes 909320 | tf_op jit(solution)/shard_map/ppermute | solution.py:421
  52.0 0.8 copy-start.4
  52.8 9.1 %collective-permute-start.12 = (bf16[37,16,256]{2,1,0:T(8,128)(2,1)}, bf16[37,16,256]{2,1,0:T(8,128)(2,1)}, u32[]{:S(2)}, u32[]{:S(2)}) collective-permute-start(bf16[37,16,256]{2,1,0:T(8,128)(2,1)} %collective-permute-done.8), channel_id=1, source_target_pairs={{0,1},{8,9},{1,2},{9,10},{2,3},{10,11},{3,0},{11,8},{4,5},{12,13},... | collective-permute-start | bytes 909320 | tf_op jit(solution)/shard_map/ppermute | solution.py:421
  54.7 7.2 %collective-permute-start.13 = (bf16[37,16,256]{2,1,0:T(8,128)(2,1)}, bf16[37,16,256]{2,1,0:T(8,128)(2,1)}, u32[]{:S(2)}, u32[]{:S(2)}) collective-permute-start(bf16[37,16,256]{2,1,0:T(8,128)(2,1)} %collective-permute-done.11), channel_id=1, source_target_pairs={{0,3},{8,11},{1,0},{9,8},{2,1},{10,9},{3,2},{11,10},{4,7},{12,15},... | collective-permute-start | bytes 909320 | tf_op jit(solution)/shard_map/ppermute | solution.py:421
  56.9 3.4 %copy-start.8 = (bf16[37,16,256]{2,1,0:T(8,128)(2,1)S(1)}, bf16[37,16,256]{2,1,0:T(8,128)(2,1)}, u32[]{:S(2)}) copy-start(bf16[37,16,256]{2,1,0:T(8,128)(2,1)} %copy-done.7) | copy-start | bytes 909316
  60.3 1.6 %copy-start.2 = (bf16[128,2432]{1,0:T(8,128)(2,1)S(1)}, bf16[128,2432]{1,0:T(8,128)(2,1)}, u32[]{:S(2)}) copy-start(bf16[128,2432]{1,0:T(8,128)(2,1)} %get-tuple-element.81.c0) | copy-start | bytes 1867780
  60.3 1.6 %copy-start.3 = (f32[256,64]{0,1:T(8,128)S(1)}, f32[256,64]{0,1:T(8,128)}, u32[]{:S(2)}) copy-start(f32[256,64]{0,1:T(8,128)} %param.19) | copy-start | bytes 196612
  60.4 1.6 %copy-start.5 = (bf16[128,2432]{1,0:T(8,128)(2,1)S(1)}, bf16[128,2432]{1,0:T(8,128)(2,1)}, u32[]{:S(2)}) copy-start(bf16[128,2432]{1,0:T(8,128)(2,1)} %copy-done.4) | copy-start | bytes 1867780
  61.7 10.5 %collective-permute-start.18 = (bf16[4,37,16,256]{3,2,1,0:T(8,128)(2,1)S(1)}, bf16[4,37,16,256]{3,2,1,0:T(8,128)(2,1)S(1)}, u32[]{:S(2)}, u32[]{:S(2)}) collective-permute-start(bf16[4,37,16,256]{3,2,1,0:T(8,128)(2,1)S(1)} %pad_maximum_fusion.refs_1_), channel_id=1, source_target_pairs={{0,8},{8,0},{1,9},{9,1},{2,10},{10,2},{3,11},{11,3},{4,12},{12,4},... | collective-permute-start | bytes 3637256 | tf_op jit(solution)/shard_map/ppermute | solution.py:421
  64.8 3.1 %collective-permute-start.14 = (f32[2,256,640]{2,1,0:T(8,128)S(1)}, f32[2,256,640]{2,1,0:T(8,128)S(1)}, u32[]{:S(2)}, u32[]{:S(2)}) collective-permute-start(f32[2,256,640]{2,1,0:T(8,128)S(1)} %get-tuple-element.86), channel_id=1, source_target_pairs={{0,8},{8,0},{1,9},{9,1},{2,10},{10,2},{3,11},{11,3},{4,12},{12,4},... | collective-permute-start | bytes 3932168 | tf_op jit(solution)/shard_map/ppermute | solution.py:421
  66.6 5.6 %collective-permute-start.19 = (bf16[4,37,16,256]{3,2,1,0:T(8,128)(2,1)S(1)}, bf16[4,37,16,256]{3,2,1,0:T(8,128)(2,1)S(1)}, u32[]{:S(2)}, u32[]{:S(2)}) collective-permute-start(bf16[4,37,16,256]{3,2,1,0:T(8,128)(2,1)S(1)} %pad_maximum_fusion.1.refs_3_), channel_id=1, source_target_pairs={{0,8},{8,0},{1,9},{9,1},{2,10},{10,2},{3,11},{11,3},{4,12},{12,4},... | collective-permute-start | bytes 3637256 | tf_op jit(solution)/shard_map/ppermute | solution.py:421
  67.9 4.3 %copy-start.6 = (bf16[576,640]{1,0:T(8,128)(2,1)S(1)}, bf16[576,640]{1,0:T(8,128)(2,1)}, u32[]{:S(2)}) copy-start(bf16[576,640]{1,0:T(8,128)(2,1)} %constant.83.clone.refs_5_) | copy-start | bytes 2211844
  68.6 11.6 %collective-permute-start.15 = (bf16[128,640]{1,0:T(8,128)(2,1)S(1)}, bf16[128,640]{1,0:T(8,128)(2,1)S(1)}, u32[]{:S(2)}, u32[]{:S(2)}) collective-permute-start(bf16[128,640]{1,0:T(8,128)(2,1)S(1)} %get-tuple-element.88), channel_id=1, source_target_pairs={{0,4},{8,12},{1,5},{9,13},{2,6},{10,14},{3,7},{11,15},{4,16},{12,2... | collective-permute-start | bytes 491528 | tf_op jit(solution)/shard_map/ppermute | solution.py:421
  69.3 10.9 %collective-permute-start.16 = (bf16[128,640]{1,0:T(8,128)(2,1)S(1)}, bf16[128,640]{1,0:T(8,128)(2,1)S(1)}, u32[]{:S(2)}, u32[]{:S(2)}) collective-permute-start(bf16[128,640]{1,0:T(8,128)(2,1)S(1)} %get-tuple-element.89), channel_id=1, source_target_pairs={{0,16},{8,24},{1,17},{9,25},{2,18},{10,26},{3,19},{11,27},{4,20},{... | collective-permute-start | bytes 491528 | tf_op jit(solution)/shard_map/ppermute | solution.py:421
  71.3 9.2 %collective-permute-start.17 = (bf16[128,640]{1,0:T(8,128)(2,1)S(1)}, bf16[128,640]{1,0:T(8,128)(2,1)S(1)}, u32[]{:S(2)}, u32[]{:S(2)}) collective-permute-start(bf16[128,640]{1,0:T(8,128)(2,1)S(1)} %get-tuple-element.90), channel_id=1, source_target_pairs={{0,20},{8,28},{1,21},{9,29},{2,22},{10,30},{3,23},{11,31},{4,0},{1... | collective-permute-start | bytes 491528 | tf_op jit(solution)/shard_map/ppermute | solution.py:421
  81.1 6.6 %collective-permute-start.20 = (f32[32,640]{1,0:T(8,128)S(1)}, f32[32,640]{1,0:T(8,128)S(1)}, u32[]{:S(2)}, u32[]{:S(2)}) collective-permute-start(f32[32,640]{1,0:T(8,128)S(1)} %get-tuple-element.97), channel_id=1, source_target_pairs={{0,1},{8,9},{1,2},{9,10},{2,3},{10,11},{3,0},{11,8},{4,5},{12,13},... | collective-permute-start | bytes 245768 | tf_op jit(solution)/shard_map/ppermute | solution.py:421
  82.8 6.4 %collective-permute-start.21 = (f32[32,640]{1,0:T(8,128)S(1)}, f32[32,640]{1,0:T(8,128)S(1)}, u32[]{:S(2)}, u32[]{:S(2)}) collective-permute-start(f32[32,640]{1,0:T(8,128)S(1)} %get-tuple-element.98), channel_id=1, source_target_pairs={{0,2},{8,10},{1,3},{9,11},{2,0},{10,8},{3,1},{11,9},{4,6},{12,14},... | collective-permute-start | bytes 245768 | tf_op jit(solution)/shard_map/ppermute | solution.py:421
  85.6 4.4 %collective-permute-start.22 = (f32[32,640]{1,0:T(8,128)S(1)}, f32[32,640]{1,0:T(8,128)S(1)}, u32[]{:S(2)}, u32[]{:S(2)}) collective-permute-start(f32[32,640]{1,0:T(8,128)S(1)} %get-tuple-element.99), channel_id=1, source_target_pairs={{0,3},{8,11},{1,0},{9,8},{2,1},{10,9},{3,2},{11,10},{4,7},{12,15},... | collective-permute-start | bytes 245768 | tf_op jit(solution)/shard_map/ppermute | solution.py:421

commit v7 on v6

--- a/solution.py
+++ b/solution.py
@@ -461,9 +461,10 @@
     quad = join(pair, near, y % 2)
     octet = join(quad, move(quad, Y_FAR), y // 2).reshape(4, 2, 16, 1152)
 
-    held = [sent[0]] + [move(sent[d], YS[d]) for d in (1, 2, 3)]
+    across = move(sent[2], YS[2])
     part = spectra(weighted, fwd_k)
-
+    one, three = after([sent[1], sent[3]], across, part)
+    held = [sent[0], move(one, YS[1]), across, move(three, YS[3])]
     own = ref_spectra(octet, fwd_k)
     up, down = move(own, ZS[1]), move(own, ZS[3])
     side = move(own, LOW)
@@ -471,8 +472,7 @@
     on_up, on_down = move(up, ZS[1]), move(side_down, ZS[3])
     early = jnp.stack([own, side, up, down])
     early_twin = move(early, CORE)
-    held = after(held, side, up, down, side_up, side_down, part)
-    held = after(held, on_up, on_down)
+    held = after(held, side, up, down, side_up, side_down)
     mine, other = class_sums(sc, held, table)
     cut = cut_x(sc, mine, move(other, CORE))
     late = jnp.stack([side_up, side_down, on_up, on_down])

time: 91.8 us -> 92 us (level)
  waiting for transfers between devices: 26.1 us -> 27.7 us
  other arithmetic: 4.75 us -> 3.76 us
    ppermute x23, waiting for transfers between devices: 26.1 us -> 27.7 us  [move(): return lax.ppermute(value, AXES, pairs)]
  transfers between devices with their start and end apart: 23 -> 23, of which waited for: 12 -> 12; matrix products, arithmetic and copies ran while one was open for 4% -> 3% of each run, Pallas kernels for 28% -> 27%
where the time goes in v7:
time: 92 us; the launch traced here: 91.5 us
  starting transfers between devices  31.3 us (34%)
  waiting for transfers between devices  27.7 us (30%)
  Pallas kernels  27.1 us (29%)
  other arithmetic  3.76 us (4%)
    ppermute x23, starting transfers between devices, move(): return lax.ppermute(value, AXES, pairs)  31.3 us
    ppermute x23, waiting for transfers between devices, move(): return lax.ppermute(value, AXES, pairs)  27.7 us
    pallas_call x2, Pallas kernels, prep(): pl.pallas_call(functools.partial(prep_kernel, first), grid=(n // 32,), in...  10.1 us
    pallas_call x1, Pallas kernels, scores_of(): pl.pallas_call(score_kernel, in_specs=[v] * 6, out_specs=v, out_shape=jax...  7.91 us
    pallas_call x1, Pallas kernels, spectra(): pl.pallas_call(spectra_kernel, in_specs=[v, v], out_specs=v, out_shape=ja...  3.39 us
    pallas_call x1, Pallas kernels, class_sums(): pl.pallas_call(sums_kernel, in_specs=[pl.BlockSpec(memory_space=pltpu.SME...  2.64 us
  transfers between devices with their start and end apart: 23, of which 12 were waited for; matrix products, arithmetic and copies ran while one was open for 3% of the time, Pallas kernels for 27%

profile of v7, /device:TPU:0, one launch (start us, length us, event | category | flops | bytes accessed | tf_op | source)
XLA Modules:
  0.0 91.5 jit_solution(7637006855251170401)
XLA Ops:
  0.6 0.8 broadcast_select_fusion.1
  1.6 1.2 %collective-permute-done = bf16[16,576]{1,0:T(8,128)(2,1)S(1)} collective-permute-done((bf16[16,576]{1,0:T(8,128)(2,1)S(1)}, bf16[16,576]{1,0:T(8,128)(2,1)S(1)}, u32[]{:S(2)}, u32[]{:S(2)}) %collective-permute-start) | collective-permute-done | bytes 18464 | tf_op jit(solution)/shard_map/ppermute | solution.py:421
  2.9 3.2 %collective-permute-start.1 = (bf16[16,1152]{1,0:T(8,128)(2,1)S(1)}, bf16[16,1152]{1,0:T(8,128)(2,1)S(1)}, u32[]{:S(2)}, u32[]{:S(2)}) collective-permute-start(bf16[16,1152]{1,0:T(8,128)(2,1)S(1)} %maximum_select_fusion), channel_id=1, source_target_pairs={{0,16},{8,24},{1,17},{9,25},{2,18},{10,26},{3,19},{11,27},{4,20},{... | collective-permute-start | bytes 110600 | tf_op jit(solution)/shard_map/ppermute | solution.py:421
  6.0 5.0 %prep.2 = (bf16[16,576,128]{2,1,0:T(8,128)(2,1)}, bf16[128,2432]{1,0:T(8,128)(2,1)}, bf16[128,2432]{1,0:T(8,128)(2,1)}, bf16[128,2432]{1,0:T(8,128)(2,1)}, bf16[128,2432]{1,0:T(8,128)(2,1)}) custom-call(bf16[128,9216]{1,0:T(8,128)(2,1)} %x_ref.3, s32[2,128]{1,0:T(2,128)} %bitcast.39, s32[1,128]{1,0:T(1,128)} %bitcast.41, s32[1,128]{1,0:T(1,128)} %bitcast.43, ...), custom_call_target="tpu_custom_call" | custom-call | flops 20000000 | bytes 4000000 | tf_op jit(solution)/shard_map/prep/pallas_call | solution.py:144
  11.1 1.7 %collective-permute-start.2 = (bf16[2,16,1152]{2,1,0:T(8,128)(2,1)S(1)}, bf16[2,16,1152]{2,1,0:T(8,128)(2,1)S(1)}, u32[]{:S(2)}, u32[]{:S(2)}) collective-permute-start(bf16[2,16,1152]{2,1,0:T(8,128)(2,1)S(1)} %pad_maximum_fusion.4), channel_id=1, source_target_pairs={{0,32},{8,40},{1,33},{9,41},{2,34},{10,42},{3,35},{11,43},{4,36},{... | collective-permute-start | bytes 221192 | tf_op jit(solution)/shard_map/ppermute | solution.py:421
  12.8 5.0 %prep.3 = (bf16[16,576,128]{2,1,0:T(8,128)(2,1)}, bf16[128,2432]{1,0:T(8,128)(2,1)}, bf16[128,2432]{1,0:T(8,128)(2,1)}, bf16[128,2432]{1,0:T(8,128)(2,1)}, bf16[128,2432]{1,0:T(8,128)(2,1)}) custom-call(bf16[128,9216]{1,0:T(8,128)(2,1)} %x_ref.3, s32[2,128]{1,0:T(2,128)} %bitcast.40, ...), custom_call_target="tpu_custom_call", output_to_operand_aliasing={{0}: (9, {}), {1}: (10, {}), {2}: (11, {}), {3}: (12, {}), ... | custom-call | flops 20000000 | bytes 4000000 | tf_op jit(solution)/shard_map/prep/pallas_call | solution.py:144
  17.9 3.0 %collective-permute-start.6 = (bf16[2,2,16,1152]{3,2,1,0:T(8,128)(2,1)S(1)}, bf16[2,2,16,1152]{3,2,1,0:T(8,128)(2,1)S(1)}, u32[]{:S(2)}, u32[]{:S(2)}) collective-permute-start(bf16[2,2,16,1152]{3,2,1,0:T(8,128)(2,1)S(1)} %pad_maximum_fusion.3), channel_id=1, source_target_pairs={{0,64},{8,72},{1,65},{9,73},{2,66},{10,74},{3,67},{11,75},{4,68},{... | collective-permute-start | bytes 442376 | tf_op jit(solution)/shard_map/ppermute | solution.py:421
  21.5 3.7 %collective-permute-done.6 = bf16[2,2,16,1152]{3,2,1,0:T(8,128)(2,1)S(1)} collective-permute-done((bf16[2,2,16,1152]{3,2,1,0:T(8,128)(2,1)S(1)}, bf16[2,2,16,1152]{3,2,1,0:T(8,128)(2,1)S(1)}, u32[]{:S(2)}, u32[]{:S(2)}) %collective-permute-start.6) | collective-permute-done | bytes 147488 | tf_op jit(solution)/shard_map/ppermute | solution.py:421
  26.3 3.4 %spectra.1.refs_0_ = bf16[37,128,256]{2,1,0:T(8,128)(2,1)S(1)} custom-call(bf16[16,576,128]{2,1,0:T(8,128)(2,1)S(1)} %copy-done, bf16[592,576]{1,0:T(8,128)(2,1)S(1)} %copy-done.1), custom_call_target="tpu_custom_call" | custom-call | flops 1000 | bytes 1000 | tf_op jit(solution)/shard_map/spectra/pallas_call | solution.py:194
  29.7 8.4 %collective-permute-done.3.c2 = bf16[128,2432]{1,0:T(8,128)(2,1)S(1)} collective-permute-done((bf16[128,2432]{1,0:T(8,128)(2,1)}, bf16[128,2432]{1,0:T(8,128)(2,1)S(1)}, u32[]{:S(2)}, u32[]{:S(2)}) %collective-permute-start.3) | collective-permute-done | bytes 622624 | tf_op jit(solution)/shard_map/ppermute | solution.py:421
  38.2 0.8 copy-done.4
  39.5 2.8 %collective-permute-start.5 = (bf16[128,2432]{1,0:T(8,128)(2,1)}, bf16[128,2432]{1,0:T(8,128)(2,1)}, u32[]{:S(2)}, u32[]{:S(2)}) collective-permute-start(bf16[128,2432]{1,0:T(8,128)(2,1)} %get-tuple-element.75), channel_id=1, source_target_pairs={{0,96},{8,104},{1,97},{9,105},{2,98},{10,106},{3,99},{11,107},{4,1... | collective-permute-start | bytes 1867784 | tf_op jit(solution)/shard_map/ppermute | solution.py:421
  42.2 1.9 %collective-permute-start.8 = (bf16[37,16,256]{2,1,0:T(8,128)(2,1)S(1)}, bf16[37,16,256]{2,1,0:T(8,128)(2,1)}, u32[]{:S(2)}, u32[]{:S(2)}) collective-permute-start(bf16[37,16,256]{2,1,0:T(8,128)(2,1)S(1)} %ref_spectra.1), channel_id=1, source_target_pairs={{0,1},{8,9},{1,2},{9,10},{2,3},{10,11},{3,0},{11,8},{4,5},{12,13},... | collective-permute-start | bytes 909320 | tf_op jit(solution)/shard_map/ppermute | solution.py:421
  44.2 2.1 %collective-permute-start.9 = (bf16[37,16,256]{2,1,0:T(8,128)(2,1)S(1)}, bf16[37,16,256]{2,1,0:T(8,128)(2,1)}, u32[]{:S(2)}, u32[]{:S(2)}) collective-permute-start(bf16[37,16,256]{2,1,0:T(8,128)(2,1)S(1)} %ref_spectra.1), channel_id=1, source_target_pairs={{0,3},{8,11},{1,0},{9,8},{2,1},{10,9},{3,2},{11,10},{4,7},{12,15},... | collective-permute-start | bytes 909320 | tf_op jit(solution)/shard_map/ppermute | solution.py:421
  46.3 2.0 %collective-permute-start.11 = (bf16[37,16,256]{2,1,0:T(8,128)(2,1)}, bf16[37,16,256]{2,1,0:T(8,128)(2,1)}, u32[]{:S(2)}, u32[]{:S(2)}) collective-permute-start(bf16[37,16,256]{2,1,0:T(8,128)(2,1)} %collective-permute-done.7), channel_id=1, source_target_pairs={{0,3},{8,11},{1,0},{9,8},{2,1},{10,9},{3,2},{11,10},{4,7},{12,15},... | collective-permute-start | bytes 909320 | tf_op jit(solution)/shard_map/ppermute | solution.py:421
  48.3 3.6 %collective-permute-done.8 = bf16[37,16,256]{2,1,0:T(8,128)(2,1)} collective-permute-done((bf16[37,16,256]{2,1,0:T(8,128)(2,1)S(1)}, bf16[37,16,256]{2,1,0:T(8,128)(2,1)}, u32[]{:S(2)}, u32[]{:S(2)}) %collective-permute-start.8) | collective-permute-done | bytes 303136 | tf_op jit(solution)/shard_map/ppermute | solution.py:421
  51.9 2.5 %collective-permute-done.9 = bf16[37,16,256]{2,1,0:T(8,128)(2,1)} collective-permute-done((bf16[37,16,256]{2,1,0:T(8,128)(2,1)S(1)}, bf16[37,16,256]{2,1,0:T(8,128)(2,1)}, u32[]{:S(2)}, u32[]{:S(2)}) %collective-permute-start.9) | collective-permute-done | bytes 303136 | tf_op jit(solution)/shard_map/ppermute | solution.py:421
  54.4 1.9 %collective-permute-start.17 = (bf16[37,16,256]{2,1,0:T(8,128)(2,1)}, bf16[37,16,256]{2,1,0:T(8,128)(2,1)S(1)}, u32[]{:S(2)}, u32[]{:S(2)}) collective-permute-start(bf16[37,16,256]{2,1,0:T(8,128)(2,1)} %collective-permute-done.8), channel_id=1, source_target_pairs={{0,1},{8,9},{1,2},{9,10},{2,3},{10,11},{3,0},{11,8},{4,5},{12,13},... | collective-permute-start | bytes 909320 | tf_op jit(solution)/shard_map/ppermute | solution.py:421
  56.3 1.6 %collective-permute-done.11 = bf16[37,16,256]{2,1,0:T(8,128)(2,1)} collective-permute-done((bf16[37,16,256]{2,1,0:T(8,128)(2,1)}, bf16[37,16,256]{2,1,0:T(8,128)(2,1)}, u32[]{:S(2)}, u32[]{:S(2)}) %collective-permute-start.11) | collective-permute-done | bytes 303136 | tf_op jit(solution)/shard_map/ppermute | solution.py:421
  57.9 3.4 %collective-permute-start.18 = (bf16[37,16,256]{2,1,0:T(8,128)(2,1)}, bf16[37,16,256]{2,1,0:T(8,128)(2,1)S(1)}, u32[]{:S(2)}, u32[]{:S(2)}) collective-permute-start(bf16[37,16,256]{2,1,0:T(8,128)(2,1)} %collective-permute-done.11), channel_id=1, source_target_pairs={{0,3},{8,11},{1,0},{9,8},{2,1},{10,9},{3,2},{11,10},{4,7},{12,15},... | collective-permute-start | bytes 909320 | tf_op jit(solution)/shard_map/ppermute | solution.py:421
  61.4 1.4 %pad_maximum_fusion.refs_1_ = bf16[4,37,16,256]{3,2,1,0:T(8,128)(2,1)S(1)} fusion(bf16[1,37,16,256]{3,2,1,0:T(8,128)(2,1)} %bitcast.20, bf16[1,37,16,256]{3,2,1,0:T(8,128)(2,1)} %bitcast.19, bf16[1,37,16,256]{3,2,1,0:T(8,128)(2,1)} %bitcast.18, bf16[1,37,16,256]{3,2,1,0:T(8,128)(2,1)S(1)} %bitcast.32), kind=kLoop, calls=%fused_computation | loop fusion | flops 1818624 | bytes 2424832 | tf_op jit(solution)/shard_map/stack | solution.py:473
  63.3 2.6 %class_sums.1 = (f32[2,256,640]{2,1,0:T(8,128)S(1)}, f32[2,256,640]{2,1,0:T(8,128)S(1)}) custom-call(s32[4]{0:T(128)S(1)} %pad_add_fusion.sc, bf16[128,2432]{1,0:T(8,128)(2,1)S(1)} %copy-done.2, bf16[128,2432]{1,0:T(8,128)(2,1)S(1)} %collective-permute-done.4.c1, bf16[128,2432]{1,0:T(8,128)(2,1)S(1)} %copy-done.5, ...), custom_call_target="tpu_custom_call" | custom-call | flops 700000000 | bytes 5000000 | tf_op jit(solution)/shard_map/class_sums/pallas_call | solution.py:314
  66.6 1.2 %pad_maximum_fusion.1.refs_3_ = bf16[4,37,16,256]{3,2,1,0:T(8,128)(2,1)S(1)} fusion(bf16[1,37,16,256]{3,2,1,0:T(8,128)(2,1)S(1)} %bitcast.38, bf16[1,37,16,256]{3,2,1,0:T(8,128)(2,1)S(1)} %bitcast.37, bf16[1,37,16,256]{3,2,1,0:T(8,128)(2,1)} %bitcast.22, bf16[1,37,16,256]{3,2,1,0:T(8,128)(2,1)} %bitcast.21), kind=kLoop, calls=%fused_computation.1 | loop fusion | flops 1818624 | bytes 2424832 | tf_op jit(solution)/shard_map/stack | solution.py:478
  67.9 1.3 %collective-permute-done.12.b_ref = f32[2,256,640]{2,1,0:T(8,128)S(1)} collective-permute-done((f32[2,256,640]{2,1,0:T(8,128)S(1)}, f32[2,256,640]{2,1,0:T(8,128)S(1)}, u32[]{:S(2)}, u32[]{:S(2)}) %collective-permute-start.12) | collective-permute-done | bytes 1310752 | tf_op jit(solution)/shard_map/ppermute | solution.py:421
  70.6 2.0 %collective-permute-start.14 = (bf16[128,640]{1,0:T(8,128)(2,1)S(1)}, bf16[128,640]{1,0:T(8,128)(2,1)S(1)}, u32[]{:S(2)}, u32[]{:S(2)}) collective-permute-start(bf16[128,640]{1,0:T(8,128)(2,1)S(1)} %get-tuple-element.85), channel_id=1, source_target_pairs={{0,16},{8,24},{1,17},{9,25},{2,18},{10,26},{3,19},{11,27},{4,20},{... | collective-permute-start | bytes 491528 | tf_op jit(solution)/shard_map/ppermute | solution.py:421
  72.6 0.8 collective-permute-start.15
  73.4 7.9 %scores.1 = f32[1,128]{1,0:T(1,128)} custom-call(bf16[37,128,256]{2,1,0:T(8,128)(2,1)S(1)} %spectra.1.refs_0_, bf16[4,37,16,256]{3,2,1,0:T(8,128)(2,1)S(1)} %pad_maximum_fusion.refs_1_, bf16[4,37,16,256]{3,2,1,0:T(8,128)(2,1)S(1)} %collective-permute-done.16.refs_2_, bf16[4,37,16,256]{3,2,1,0:T(8,128)(2,1)S(1)} %pad_maximum_fusion.1.refs_3_, ...), custom_call_target="tpu_custom_call" | custom-call | flops 6000000000 | bytes 8000000 | tf_op jit(solution)/shard_map/scores/pallas_call | solution.py:271
  82.5 3.2 %collective-permute-start.21 = (f32[32,640]{1,0:T(8,128)S(1)}, f32[32,640]{1,0:T(8,128)S(1)}, u32[]{:S(2)}, u32[]{:S(2)}) collective-permute-start(f32[32,640]{1,0:T(8,128)S(1)} %get-tuple-element.94), channel_id=1, source_target_pairs={{0,2},{8,10},{1,3},{9,11},{2,0},{10,8},{3,1},{11,9},{4,6},{12,14},... | collective-permute-start | bytes 245768 | tf_op jit(solution)/shard_map/ppermute | solution.py:421
  85.8 2.6 %collective-permute-done.20.a1 = f32[32,640]{1,0:T(8,128)S(1)} collective-permute-done((f32[32,640]{1,0:T(8,128)S(1)}, f32[32,640]{1,0:T(8,128)S(1)}, u32[]{:S(2)}, u32[]{:S(2)}) %collective-permute-start.20) | collective-permute-done | bytes 81952 | tf_op jit(solution)/shard_map/ppermute | solution.py:421
  88.3 0.9 collective-permute-done.21.a2
  89.2 1.0 %collective-permute-done.22.a3 = f32[32,640]{1,0:T(8,128)S(1)} collective-permute-done((f32[32,640]{1,0:T(8,128)S(1)}, f32[32,640]{1,0:T(8,128)S(1)}, u32[]{:S(2)}, u32[]{:S(2)}) %collective-permute-start.22) | collective-permute-done | bytes 81952 | tf_op jit(solution)/shard_map/ppermute | solution.py:421
  90.2 1.3 %final.1 = f32[25,576]{1,0:T(8,128)} custom-call(s32[4]{0:T(128)S(1)} %pad_add_fusion.sc, f32[32,640]{1,0:T(8,128)S(1)} %get-tuple-element.92.a0, f32[32,640]{1,0:T(8,128)S(1)} %collective-permute-done.20.a1, f32[32,640]{1,0:T(8,128)S(1)} %collective-permute-done.21.a2, f32[32,640]{1,0:T(8,128)S(1)} %collective-permute-done.22.a3), custom_call_target="tpu_custom_call" | custom-call | tf_op jit(solution)/shard_map/final/pallas_call | solution.py:386
  (48 shorter events, 6.3 us)
Async XLA Ops:
  1.5 1.3 %collective-permute-start = (bf16[16,576]{1,0:T(8,128)(2,1)S(1)}, bf16[16,576]{1,0:T(8,128)(2,1)S(1)}, u32[]{:S(2)}, u32[]{:S(2)}) collective-permute-start(bf16[16,576]{1,0:T(8,128)(2,1)S(1)} %get-tuple-element.103), channel_id=1, source_target_pairs={{0,8},{8,0},{1,9},{9,1},{2,10},{10,2},{3,11},{11,3},{4,12},{12,4},... | collective-permute-start | bytes 55304 | tf_op jit(solution)/shard_map/ppermute | solution.py:421
  2.9 8.2 %collective-permute-start.1 = (bf16[16,1152]{1,0:T(8,128)(2,1)S(1)}, bf16[16,1152]{1,0:T(8,128)(2,1)S(1)}, u32[]{:S(2)}, u32[]{:S(2)}) collective-permute-start(bf16[16,1152]{1,0:T(8,128)(2,1)S(1)} %maximum_select_fusion), channel_id=1, source_target_pairs={{0,16},{8,24},{1,17},{9,25},{2,18},{10,26},{3,19},{11,27},{4,20},{... | collective-permute-start | bytes 110600 | tf_op jit(solution)/shard_map/ppermute | solution.py:421
  11.1 6.7 %collective-permute-start.2 = (bf16[2,16,1152]{2,1,0:T(8,128)(2,1)S(1)}, bf16[2,16,1152]{2,1,0:T(8,128)(2,1)S(1)}, u32[]{:S(2)}, u32[]{:S(2)}) collective-permute-start(bf16[2,16,1152]{2,1,0:T(8,128)(2,1)S(1)} %pad_maximum_fusion.4), channel_id=1, source_target_pairs={{0,32},{8,40},{1,33},{9,41},{2,34},{10,42},{3,35},{11,43},{4,36},{... | collective-permute-start | bytes 221192 | tf_op jit(solution)/shard_map/ppermute | solution.py:421
  17.8 7.4 %copy-start.1 = (bf16[592,576]{1,0:T(8,128)(2,1)S(1)}, bf16[592,576]{1,0:T(8,128)(2,1)}, u32[]{:S(2)}) copy-start(bf16[592,576]{1,0:T(8,128)(2,1)} %constant.82.clone.f_ref) | copy-start | bytes 2045956
  17.9 7.3 %collective-permute-start.6 = (bf16[2,2,16,1152]{3,2,1,0:T(8,128)(2,1)S(1)}, bf16[2,2,16,1152]{3,2,1,0:T(8,128)(2,1)S(1)}, u32[]{:S(2)}, u32[]{:S(2)}) collective-permute-start(bf16[2,2,16,1152]{3,2,1,0:T(8,128)(2,1)S(1)} %pad_maximum_fusion.3), channel_id=1, source_target_pairs={{0,64},{8,72},{1,65},{9,73},{2,66},{10,74},{3,67},{11,75},{4,68},{... | collective-permute-start | bytes 442376 | tf_op jit(solution)/shard_map/ppermute | solution.py:421
  20.9 5.5 %copy-start = (bf16[16,576,128]{2,1,0:T(8,128)(2,1)S(1)}, bf16[16,576,128]{2,1,0:T(8,128)(2,1)}, u32[]{:S(2)}) copy-start(bf16[16,576,128]{2,1,0:T(8,128)(2,1)} %get-tuple-element.73.w_ref) | copy-start | bytes 7077892
  20.9 17.3 %collective-permute-start.3 = (bf16[128,2432]{1,0:T(8,128)(2,1)}, bf16[128,2432]{1,0:T(8,128)(2,1)S(1)}, u32[]{:S(2)}, u32[]{:S(2)}) collective-permute-start(bf16[128,2432]{1,0:T(8,128)(2,1)} %get-tuple-element.72), channel_id=1, source_target_pairs={{0,64},{8,72},{1,65},{9,73},{2,66},{10,74},{3,67},{11,75},{4,68},{... | collective-permute-start | bytes 1867784 | tf_op jit(solution)/shard_map/ppermute | solution.py:421
  25.7 20.6 %collective-permute-start.7 = (bf16[37,16,256]{2,1,0:T(8,128)(2,1)S(1)}, bf16[37,16,256]{2,1,0:T(8,128)(2,1)}, u32[]{:S(2)}, u32[]{:S(2)}) collective-permute-start(bf16[37,16,256]{2,1,0:T(8,128)(2,1)S(1)} %ref_spectra.1), channel_id=1, source_target_pairs={{0,4},{8,12},{1,5},{9,13},{2,6},{10,14},{3,7},{11,15},{4,0},{12,8}... | collective-permute-start | bytes 909320 | tf_op jit(solution)/shard_map/ppermute | solution.py:421
  38.2 0.8 copy-start.4
  39.0 24.3 %collective-permute-start.4 = (bf16[128,2432]{1,0:T(8,128)(2,1)}, bf16[128,2432]{1,0:T(8,128)(2,1)S(1)}, u32[]{:S(2)}, u32[]{:S(2)}) collective-permute-start(bf16[128,2432]{1,0:T(8,128)(2,1)} %get-tuple-element.74), channel_id=1, source_target_pairs={{0,32},{8,40},{1,33},{9,41},{2,34},{10,42},{3,35},{11,43},{4,36},{... | collective-permute-start | bytes 1867784 | tf_op jit(solution)/shard_map/ppermute | solution.py:421
  39.5 23.8 %collective-permute-start.5 = (bf16[128,2432]{1,0:T(8,128)(2,1)}, bf16[128,2432]{1,0:T(8,128)(2,1)}, u32[]{:S(2)}, u32[]{:S(2)}) collective-permute-start(bf16[128,2432]{1,0:T(8,128)(2,1)} %get-tuple-element.75), channel_id=1, source_target_pairs={{0,96},{8,104},{1,97},{9,105},{2,98},{10,106},{3,99},{11,107},{4,1... | collective-permute-start | bytes 1867784 | tf_op jit(solution)/shard_map/ppermute | solution.py:421
  42.2 9.7 %collective-permute-start.8 = (bf16[37,16,256]{2,1,0:T(8,128)(2,1)S(1)}, bf16[37,16,256]{2,1,0:T(8,128)(2,1)}, u32[]{:S(2)}, u32[]{:S(2)}) collective-permute-start(bf16[37,16,256]{2,1,0:T(8,128)(2,1)S(1)} %ref_spectra.1), channel_id=1, source_target_pairs={{0,1},{8,9},{1,2},{9,10},{2,3},{10,11},{3,0},{11,8},{4,5},{12,13},... | collective-permute-start | bytes 909320 | tf_op jit(solution)/shard_map/ppermute | solution.py:421
  44.2 10.2 %collective-permute-start.9 = (bf16[37,16,256]{2,1,0:T(8,128)(2,1)S(1)}, bf16[37,16,256]{2,1,0:T(8,128)(2,1)}, u32[]{:S(2)}, u32[]{:S(2)}) collective-permute-start(bf16[37,16,256]{2,1,0:T(8,128)(2,1)S(1)} %ref_spectra.1), channel_id=1, source_target_pairs={{0,3},{8,11},{1,0},{9,8},{2,1},{10,9},{3,2},{11,10},{4,7},{12,15},... | collective-permute-start | bytes 909320 | tf_op jit(solution)/shard_map/ppermute | solution.py:421
  46.3 11.6 %collective-permute-start.11 = (bf16[37,16,256]{2,1,0:T(8,128)(2,1)}, bf16[37,16,256]{2,1,0:T(8,128)(2,1)}, u32[]{:S(2)}, u32[]{:S(2)}) collective-permute-start(bf16[37,16,256]{2,1,0:T(8,128)(2,1)} %collective-permute-done.7), channel_id=1, source_target_pairs={{0,3},{8,11},{1,0},{9,8},{2,1},{10,9},{3,2},{11,10},{4,7},{12,15},... | collective-permute-start | bytes 909320 | tf_op jit(solution)/shard_map/ppermute | solution.py:421
  51.9 11.4 %collective-permute-start.10 = (bf16[37,16,256]{2,1,0:T(8,128)(2,1)}, bf16[37,16,256]{2,1,0:T(8,128)(2,1)}, u32[]{:S(2)}, u32[]{:S(2)}) collective-permute-start(bf16[37,16,256]{2,1,0:T(8,128)(2,1)} %collective-permute-done.7), channel_id=1, source_target_pairs={{0,1},{8,9},{1,2},{9,10},{2,3},{10,11},{3,0},{11,8},{4,5},{12,13},... | collective-permute-start | bytes 909320 | tf_op jit(solution)/shard_map/ppermute | solution.py:421
  54.4 12.2 %collective-permute-start.17 = (bf16[37,16,256]{2,1,0:T(8,128)(2,1)}, bf16[37,16,256]{2,1,0:T(8,128)(2,1)S(1)}, u32[]{:S(2)}, u32[]{:S(2)}) collective-permute-start(bf16[37,16,256]{2,1,0:T(8,128)(2,1)} %collective-permute-done.8), channel_id=1, source_target_pairs={{0,1},{8,9},{1,2},{9,10},{2,3},{10,11},{3,0},{11,8},{4,5},{12,13},... | collective-permute-start | bytes 909320 | tf_op jit(solution)/shard_map/ppermute | solution.py:421
  57.9 8.6 %collective-permute-start.18 = (bf16[37,16,256]{2,1,0:T(8,128)(2,1)}, bf16[37,16,256]{2,1,0:T(8,128)(2,1)S(1)}, u32[]{:S(2)}, u32[]{:S(2)}) collective-permute-start(bf16[37,16,256]{2,1,0:T(8,128)(2,1)} %collective-permute-done.11), channel_id=1, source_target_pairs={{0,3},{8,11},{1,0},{9,8},{2,1},{10,9},{3,2},{11,10},{4,7},{12,15},... | collective-permute-start | bytes 909320 | tf_op jit(solution)/shard_map/ppermute | solution.py:421
  61.4 1.9 %copy-start.2 = (bf16[128,2432]{1,0:T(8,128)(2,1)S(1)}, bf16[128,2432]{1,0:T(8,128)(2,1)}, u32[]{:S(2)}) copy-start(bf16[128,2432]{1,0:T(8,128)(2,1)} %get-tuple-element.77.c0) | copy-start | bytes 1867780
  61.4 1.9 %copy-start.3 = (f32[256,64]{0,1:T(8,128)S(1)}, f32[256,64]{0,1:T(8,128)}, u32[]{:S(2)}) copy-start(f32[256,64]{0,1:T(8,128)} %param.19) | copy-start | bytes 196612
  61.4 1.9 %copy-start.5 = (bf16[128,2432]{1,0:T(8,128)(2,1)S(1)}, bf16[128,2432]{1,0:T(8,128)(2,1)}, u32[]{:S(2)}) copy-start(bf16[128,2432]{1,0:T(8,128)(2,1)} %copy-done.4) | copy-start | bytes 1867780
  63.3 10.1 %collective-permute-start.16 = (bf16[4,37,16,256]{3,2,1,0:T(8,128)(2,1)S(1)}, bf16[4,37,16,256]{3,2,1,0:T(8,128)(2,1)S(1)}, u32[]{:S(2)}, u32[]{:S(2)}) collective-permute-start(bf16[4,37,16,256]{3,2,1,0:T(8,128)(2,1)S(1)} %pad_maximum_fusion.refs_1_), channel_id=1, source_target_pairs={{0,8},{8,0},{1,9},{9,1},{2,10},{10,2},{3,11},{11,3},{4,12},{12,4},... | collective-permute-start | bytes 3637256 | tf_op jit(solution)/shard_map/ppermute | solution.py:421
  66.0 3.2 %collective-permute-start.12 = (f32[2,256,640]{2,1,0:T(8,128)S(1)}, f32[2,256,640]{2,1,0:T(8,128)S(1)}, u32[]{:S(2)}, u32[]{:S(2)}) collective-permute-start(f32[2,256,640]{2,1,0:T(8,128)S(1)} %get-tuple-element.82), channel_id=1, source_target_pairs={{0,8},{8,0},{1,9},{9,1},{2,10},{10,2},{3,11},{11,3},{4,12},{12,4},... | collective-permute-start | bytes 3932168 | tf_op jit(solution)/shard_map/ppermute | solution.py:421
  67.8 5.6 %collective-permute-start.19 = (bf16[4,37,16,256]{3,2,1,0:T(8,128)(2,1)S(1)}, bf16[4,37,16,256]{3,2,1,0:T(8,128)(2,1)S(1)}, u32[]{:S(2)}, u32[]{:S(2)}) collective-permute-start(bf16[4,37,16,256]{3,2,1,0:T(8,128)(2,1)S(1)} %pad_maximum_fusion.1.refs_3_), channel_id=1, source_target_pairs={{0,8},{8,0},{1,9},{9,1},{2,10},{10,2},{3,11},{11,3},{4,12},{12,4},... | collective-permute-start | bytes 3637256 | tf_op jit(solution)/shard_map/ppermute | solution.py:421
  69.2 4.1 %copy-start.6 = (bf16[576,640]{1,0:T(8,128)(2,1)S(1)}, bf16[576,640]{1,0:T(8,128)(2,1)}, u32[]{:S(2)}) copy-start(bf16[576,640]{1,0:T(8,128)(2,1)} %constant.83.clone.refs_5_) | copy-start | bytes 2211844
  69.9 11.4 %collective-permute-start.13 = (bf16[128,640]{1,0:T(8,128)(2,1)S(1)}, bf16[128,640]{1,0:T(8,128)(2,1)S(1)}, u32[]{:S(2)}, u32[]{:S(2)}) collective-permute-start(bf16[128,640]{1,0:T(8,128)(2,1)S(1)} %get-tuple-element.84), channel_id=1, source_target_pairs={{0,4},{8,12},{1,5},{9,13},{2,6},{10,14},{3,7},{11,15},{4,16},{12,2... | collective-permute-start | bytes 491528 | tf_op jit(solution)/shard_map/ppermute | solution.py:421
  70.6 10.7 %collective-permute-start.14 = (bf16[128,640]{1,0:T(8,128)(2,1)S(1)}, bf16[128,640]{1,0:T(8,128)(2,1)S(1)}, u32[]{:S(2)}, u32[]{:S(2)}) collective-permute-start(bf16[128,640]{1,0:T(8,128)(2,1)S(1)} %get-tuple-element.85), channel_id=1, source_target_pairs={{0,16},{8,24},{1,17},{9,25},{2,18},{10,26},{3,19},{11,27},{4,20},{... | collective-permute-start | bytes 491528 | tf_op jit(solution)/shard_map/ppermute | solution.py:421
  72.6 9.2 %collective-permute-start.15 = (bf16[128,640]{1,0:T(8,128)(2,1)S(1)}, bf16[128,640]{1,0:T(8,128)(2,1)S(1)}, u32[]{:S(2)}, u32[]{:S(2)}) collective-permute-start(bf16[128,640]{1,0:T(8,128)(2,1)S(1)} %get-tuple-element.86), channel_id=1, source_target_pairs={{0,20},{8,28},{1,21},{9,29},{2,22},{10,30},{3,23},{11,31},{4,0},{1... | collective-permute-start | bytes 491528 | tf_op jit(solution)/shard_map/ppermute | solution.py:421
  82.4 5.9 %collective-permute-start.20 = (f32[32,640]{1,0:T(8,128)S(1)}, f32[32,640]{1,0:T(8,128)S(1)}, u32[]{:S(2)}, u32[]{:S(2)}) collective-permute-start(f32[32,640]{1,0:T(8,128)S(1)} %get-tuple-element.93), channel_id=1, source_target_pairs={{0,1},{8,9},{1,2},{9,10},{2,3},{10,11},{3,0},{11,8},{4,5},{12,13},... | collective-permute-start | bytes 245768 | tf_op jit(solution)/shard_map/ppermute | solution.py:421
  82.5 6.7 %collective-permute-start.21 = (f32[32,640]{1,0:T(8,128)S(1)}, f32[32,640]{1,0:T(8,128)S(1)}, u32[]{:S(2)}, u32[]{:S(2)}) collective-permute-start(f32[32,640]{1,0:T(8,128)S(1)} %get-tuple-element.94), channel_id=1, source_target_pairs={{0,2},{8,10},{1,3},{9,11},{2,0},{10,8},{3,1},{11,9},{4,6},{12,14},... | collective-permute-start | bytes 245768 | tf_op jit(solution)/shard_map/ppermute | solution.py:421
  85.8 4.4 %collective-permute-start.22 = (f32[32,640]{1,0:T(8,128)S(1)}, f32[32,640]{1,0:T(8,128)S(1)}, u32[]{:S(2)}, u32[]{:S(2)}) collective-permute-start(f32[32,640]{1,0:T(8,128)S(1)} %get-tuple-element.95), channel_id=1, source_target_pairs={{0,3},{8,11},{1,0},{9,8},{2,1},{10,9},{3,2},{11,10},{4,7},{12,15},... | collective-permute-start | bytes 245768 | tf_op jit(solution)/shard_map/ppermute | solution.py:421

commit v8 on v7

--- a/solution.py
+++ b/solution.py
@@ -463,16 +463,16 @@
 
     across = move(sent[2], YS[2])
     part = spectra(weighted, fwd_k)
-    one, three = after([sent[1], sent[3]], across, part)
-    held = [sent[0], move(one, YS[1]), across, move(three, YS[3])]
     own = ref_spectra(octet, fwd_k)
     up, down = move(own, ZS[1]), move(own, ZS[3])
     side = move(own, LOW)
     side_up, side_down = move(side, ZS[1]), move(side, ZS[3])
+    one, three = after([sent[1], sent[3]], across, part, up, down)
+    held = [sent[0], move(one, YS[1]), across, move(three, YS[3])]
     on_up, on_down = move(up, ZS[1]), move(side_down, ZS[3])
     early = jnp.stack([own, side, up, down])
     early_twin = move(early, CORE)
-    held = after(held, side, up, down, side_up, side_down)
+    held = after(held, side_up, side_down)
     mine, other = class_sums(sc, held, table)
     cut = cut_x(sc, mine, move(other, CORE))
     late = jnp.stack([side_up, side_down, on_up, on_down])

time: 92 us -> 86.6 us (0.941)
  waiting for transfers between devices: 27.7 us -> 21.4 us
    ppermute x23, waiting for transfers between devices: 27.7 us -> 21.4 us  [move(): return lax.ppermute(value, AXES, pairs)]
  transfers between devices with their start and end apart: 23 -> 23, of which waited for: 12 -> 10; matrix products, arithmetic and copies ran while one was open for 3% -> 3% of each run, Pallas kernels for 27% -> 29%
where the time goes in v8:
time: 86.6 us; the launch traced here: 85.9 us
  starting transfers between devices  31.9 us (37%)
  Pallas kernels  27.1 us (31%)
  waiting for transfers between devices  21.4 us (25%)
  other arithmetic  3.76 us (4%)
  local copies, waits for them, and re-layouts  0.88 us (1%)
    ppermute x23, starting transfers between devices, move(): return lax.ppermute(value, AXES, pairs)  31.9 us
    ppermute x23, waiting for transfers between devices, move(): return lax.ppermute(value, AXES, pairs)  21.4 us
    pallas_call x2, Pallas kernels, prep(): pl.pallas_call(functools.partial(prep_kernel, first), grid=(n // 32,), in...  10.1 us
    pallas_call x1, Pallas kernels, scores_of(): pl.pallas_call(score_kernel, in_specs=[v] * 6, out_specs=v, out_shape=jax...  7.94 us
    pallas_call x1, Pallas kernels, spectra(): pl.pallas_call(spectra_kernel, in_specs=[v, v], out_specs=v, out_shape=ja...  3.4 us
    pallas_call x1, Pallas kernels, class_sums(): pl.pallas_call(sums_kernel, in_specs=[pl.BlockSpec(memory_space=pltpu.SME...  2.64 us
  transfers between devices with their start and end apart: 23, of which 10 were waited for; matrix products, arithmetic and copies ran while one was open for 3% of the time, Pallas kernels for 29%

profile of v8, /device:TPU:0, one launch (start us, length us, event | category | flops | bytes accessed | tf_op | source)
XLA Modules:
  0.0 85.9 jit_solution(16905992058532287677)
XLA Ops:
  0.6 0.8 broadcast_select_fusion.1
  1.6 1.2 %collective-permute-done = bf16[16,576]{1,0:T(8,128)(2,1)S(1)} collective-permute-done((bf16[16,576]{1,0:T(8,128)(2,1)S(1)}, bf16[16,576]{1,0:T(8,128)(2,1)S(1)}, u32[]{:S(2)}, u32[]{:S(2)}) %collective-permute-start) | collective-permute-done | bytes 18464 | tf_op jit(solution)/shard_map/ppermute | solution.py:421
  2.9 3.2 %collective-permute-start.1 = (bf16[16,1152]{1,0:T(8,128)(2,1)S(1)}, bf16[16,1152]{1,0:T(8,128)(2,1)S(1)}, u32[]{:S(2)}, u32[]{:S(2)}) collective-permute-start(bf16[16,1152]{1,0:T(8,128)(2,1)S(1)} %maximum_select_fusion), channel_id=1, source_target_pairs={{0,16},{8,24},{1,17},{9,25},{2,18},{10,26},{3,19},{11,27},{4,20},{... | collective-permute-start | bytes 110600 | tf_op jit(solution)/shard_map/ppermute | solution.py:421
  6.0 5.0 %prep.2 = (bf16[16,576,128]{2,1,0:T(8,128)(2,1)}, bf16[128,2432]{1,0:T(8,128)(2,1)}, bf16[128,2432]{1,0:T(8,128)(2,1)}, bf16[128,2432]{1,0:T(8,128)(2,1)}, bf16[128,2432]{1,0:T(8,128)(2,1)}) custom-call(bf16[128,9216]{1,0:T(8,128)(2,1)} %x_ref.3, s32[2,128]{1,0:T(2,128)} %bitcast.41, s32[1,128]{1,0:T(1,128)} %bitcast.43, s32[1,128]{1,0:T(1,128)} %bitcast.45, ...), custom_call_target="tpu_custom_call" | custom-call | flops 20000000 | bytes 4000000 | tf_op jit(solution)/shard_map/prep/pallas_call | solution.py:144
  11.1 1.7 %collective-permute-start.2 = (bf16[2,16,1152]{2,1,0:T(8,128)(2,1)S(1)}, bf16[2,16,1152]{2,1,0:T(8,128)(2,1)S(1)}, u32[]{:S(2)}, u32[]{:S(2)}) collective-permute-start(bf16[2,16,1152]{2,1,0:T(8,128)(2,1)S(1)} %pad_maximum_fusion.4), channel_id=1, source_target_pairs={{0,32},{8,40},{1,33},{9,41},{2,34},{10,42},{3,35},{11,43},{4,36},{... | collective-permute-start | bytes 221192 | tf_op jit(solution)/shard_map/ppermute | solution.py:421
  12.8 5.0 %prep.3 = (bf16[16,576,128]{2,1,0:T(8,128)(2,1)}, bf16[128,2432]{1,0:T(8,128)(2,1)}, bf16[128,2432]{1,0:T(8,128)(2,1)}, bf16[128,2432]{1,0:T(8,128)(2,1)}, bf16[128,2432]{1,0:T(8,128)(2,1)}) custom-call(bf16[128,9216]{1,0:T(8,128)(2,1)} %x_ref.3, s32[2,128]{1,0:T(2,128)} %bitcast.42, ...), custom_call_target="tpu_custom_call", output_to_operand_aliasing={{0}: (9, {}), {1}: (10, {}), {2}: (11, {}), {3}: (12, {}), ... | custom-call | flops 20000000 | bytes 4000000 | tf_op jit(solution)/shard_map/prep/pallas_call | solution.py:144
  17.9 3.0 %collective-permute-start.4 = (bf16[2,2,16,1152]{3,2,1,0:T(8,128)(2,1)S(1)}, bf16[2,2,16,1152]{3,2,1,0:T(8,128)(2,1)S(1)}, u32[]{:S(2)}, u32[]{:S(2)}) collective-permute-start(bf16[2,2,16,1152]{3,2,1,0:T(8,128)(2,1)S(1)} %pad_maximum_fusion.3), channel_id=1, source_target_pairs={{0,64},{8,72},{1,65},{9,73},{2,66},{10,74},{3,67},{11,75},{4,68},{... | collective-permute-start | bytes 442376 | tf_op jit(solution)/shard_map/ppermute | solution.py:421
  21.5 3.7 %collective-permute-done.4 = bf16[2,2,16,1152]{3,2,1,0:T(8,128)(2,1)S(1)} collective-permute-done((bf16[2,2,16,1152]{3,2,1,0:T(8,128)(2,1)S(1)}, bf16[2,2,16,1152]{3,2,1,0:T(8,128)(2,1)S(1)}, u32[]{:S(2)}, u32[]{:S(2)}) %collective-permute-start.4) | collective-permute-done | bytes 147488 | tf_op jit(solution)/shard_map/ppermute | solution.py:421
  25.6 2.0 %collective-permute-start.5 = (bf16[37,16,256]{2,1,0:T(8,128)(2,1)S(1)}, bf16[37,16,256]{2,1,0:T(8,128)(2,1)S(1)}, u32[]{:S(2)}, u32[]{:S(2)}) collective-permute-start(bf16[37,16,256]{2,1,0:T(8,128)(2,1)S(1)} %ref_spectra.1), channel_id=1, source_target_pairs={{0,1},{8,9},{1,2},{9,10},{2,3},{10,11},{3,0},{11,8},{4,5},{12,13},... | collective-permute-start | bytes 909320 | tf_op jit(solution)/shard_map/ppermute | solution.py:421
  27.6 2.2 %collective-permute-start.6 = (bf16[37,16,256]{2,1,0:T(8,128)(2,1)S(1)}, bf16[37,16,256]{2,1,0:T(8,128)(2,1)S(1)}, u32[]{:S(2)}, u32[]{:S(2)}) collective-permute-start(bf16[37,16,256]{2,1,0:T(8,128)(2,1)S(1)} %ref_spectra.1), channel_id=1, source_target_pairs={{0,3},{8,11},{1,0},{9,8},{2,1},{10,9},{3,2},{11,10},{4,7},{12,15},... | collective-permute-start | bytes 909320 | tf_op jit(solution)/shard_map/ppermute | solution.py:421
  30.4 3.4 %spectra.1.refs_0_ = bf16[37,128,256]{2,1,0:T(8,128)(2,1)S(1)} custom-call(bf16[16,576,128]{2,1,0:T(8,128)(2,1)S(1)} %copy-done, bf16[592,576]{1,0:T(8,128)(2,1)S(1)} %copy-done.1), custom_call_target="tpu_custom_call" | custom-call | flops 1000 | bytes 1000 | tf_op jit(solution)/shard_map/spectra/pallas_call | solution.py:194
  33.8 1.6 %collective-permute-done.5 = bf16[37,16,256]{2,1,0:T(8,128)(2,1)S(1)} collective-permute-done((bf16[37,16,256]{2,1,0:T(8,128)(2,1)S(1)}, bf16[37,16,256]{2,1,0:T(8,128)(2,1)S(1)}, u32[]{:S(2)}, u32[]{:S(2)}) %collective-permute-start.5) | collective-permute-done | bytes 303136 | tf_op jit(solution)/shard_map/ppermute | solution.py:421
  35.5 2.7 %collective-permute-done.3.c2 = bf16[128,2432]{1,0:T(8,128)(2,1)S(1)} collective-permute-done((bf16[128,2432]{1,0:T(8,128)(2,1)}, bf16[128,2432]{1,0:T(8,128)(2,1)S(1)}, u32[]{:S(2)}, u32[]{:S(2)}) %collective-permute-start.3) | collective-permute-done | bytes 622624 | tf_op jit(solution)/shard_map/ppermute | solution.py:421
  38.2 0.9 copy-done.4
  39.5 2.8 %collective-permute-start.8 = (bf16[128,2432]{1,0:T(8,128)(2,1)}, bf16[128,2432]{1,0:T(8,128)(2,1)}, u32[]{:S(2)}, u32[]{:S(2)}) collective-permute-start(bf16[128,2432]{1,0:T(8,128)(2,1)} %get-tuple-element.76), channel_id=1, source_target_pairs={{0,96},{8,104},{1,97},{9,105},{2,98},{10,106},{3,99},{11,107},{4,1... | collective-permute-start | bytes 1867784 | tf_op jit(solution)/shard_map/ppermute | solution.py:421
  42.3 4.0 %collective-permute-start.11 = (bf16[37,16,256]{2,1,0:T(8,128)(2,1)}, bf16[37,16,256]{2,1,0:T(8,128)(2,1)}, u32[]{:S(2)}, u32[]{:S(2)}) collective-permute-start(bf16[37,16,256]{2,1,0:T(8,128)(2,1)} %collective-permute-done.9), channel_id=1, source_target_pairs={{0,3},{8,11},{1,0},{9,8},{2,1},{10,9},{3,2},{11,10},{4,7},{12,15},... | collective-permute-start | bytes 909320 | tf_op jit(solution)/shard_map/ppermute | solution.py:421
  46.3 5.1 %collective-permute-done.11 = bf16[37,16,256]{2,1,0:T(8,128)(2,1)} collective-permute-done((bf16[37,16,256]{2,1,0:T(8,128)(2,1)}, bf16[37,16,256]{2,1,0:T(8,128)(2,1)}, u32[]{:S(2)}, u32[]{:S(2)}) %collective-permute-start.11) | collective-permute-done | bytes 303136 | tf_op jit(solution)/shard_map/ppermute | solution.py:421
  51.4 3.7 %collective-permute-start.18 = (bf16[37,16,256]{2,1,0:T(8,128)(2,1)}, bf16[37,16,256]{2,1,0:T(8,128)(2,1)S(1)}, u32[]{:S(2)}, u32[]{:S(2)}) collective-permute-start(bf16[37,16,256]{2,1,0:T(8,128)(2,1)} %collective-permute-done.11), channel_id=1, source_target_pairs={{0,3},{8,11},{1,0},{9,8},{2,1},{10,9},{3,2},{11,10},{4,7},{12,15},... | collective-permute-start | bytes 909320 | tf_op jit(solution)/shard_map/ppermute | solution.py:421
  55.2 1.4 %pad_maximum_fusion.refs_1_ = bf16[4,37,16,256]{3,2,1,0:T(8,128)(2,1)S(1)} fusion(bf16[1,37,16,256]{3,2,1,0:T(8,128)(2,1)} %bitcast.38, bf16[1,37,16,256]{3,2,1,0:T(8,128)(2,1)} %bitcast.37, bf16[1,37,16,256]{3,2,1,0:T(8,128)(2,1)} %bitcast.18, bf16[1,37,16,256]{3,2,1,0:T(8,128)(2,1)S(1)} %bitcast.32), kind=kLoop, calls=%fused_computation | loop fusion | flops 1818624 | bytes 2424832 | tf_op jit(solution)/shard_map/stack | solution.py:473
  56.6 1.4 %collective-permute-done.10 = bf16[37,16,256]{2,1,0:T(8,128)(2,1)} collective-permute-done((bf16[37,16,256]{2,1,0:T(8,128)(2,1)}, bf16[37,16,256]{2,1,0:T(8,128)(2,1)}, u32[]{:S(2)}, u32[]{:S(2)}) %collective-permute-start.10) | collective-permute-done | bytes 303136 | tf_op jit(solution)/shard_map/ppermute | solution.py:421
  58.0 2.6 %class_sums.1 = (f32[2,256,640]{2,1,0:T(8,128)S(1)}, f32[2,256,640]{2,1,0:T(8,128)S(1)}) custom-call(s32[4]{0:T(128)S(1)} %pad_add_fusion.sc, bf16[128,2432]{1,0:T(8,128)(2,1)S(1)} %copy-done.2, bf16[128,2432]{1,0:T(8,128)(2,1)S(1)} %collective-permute-done.7.c1, bf16[128,2432]{1,0:T(8,128)(2,1)S(1)} %copy-done.5, ...), custom_call_target="tpu_custom_call" | custom-call | flops 700000000 | bytes 5000000 | tf_op jit(solution)/shard_map/class_sums/pallas_call | solution.py:314
  61.2 1.2 %pad_maximum_fusion.1.refs_3_ = bf16[4,37,16,256]{3,2,1,0:T(8,128)(2,1)S(1)} fusion(bf16[1,37,16,256]{3,2,1,0:T(8,128)(2,1)S(1)} %bitcast.40, bf16[1,37,16,256]{3,2,1,0:T(8,128)(2,1)S(1)} %bitcast.39, bf16[1,37,16,256]{3,2,1,0:T(8,128)(2,1)} %bitcast.22, bf16[1,37,16,256]{3,2,1,0:T(8,128)(2,1)} %bitcast.21), kind=kLoop, calls=%fused_computation.1 | loop fusion | flops 1818624 | bytes 2424832 | tf_op jit(solution)/shard_map/stack | solution.py:478
  62.5 1.3 %collective-permute-done.12.b_ref = f32[2,256,640]{2,1,0:T(8,128)S(1)} collective-permute-done((f32[2,256,640]{2,1,0:T(8,128)S(1)}, f32[2,256,640]{2,1,0:T(8,128)S(1)}, u32[]{:S(2)}, u32[]{:S(2)}) %collective-permute-start.12) | collective-permute-done | bytes 1310752 | tf_op jit(solution)/shard_map/ppermute | solution.py:421
  63.9 0.7 cut_x.1
  64.6 0.7 collective-permute-start.13
  65.2 2.0 %collective-permute-start.14 = (bf16[128,640]{1,0:T(8,128)(2,1)S(1)}, bf16[128,640]{1,0:T(8,128)(2,1)S(1)}, u32[]{:S(2)}, u32[]{:S(2)}) collective-permute-start(bf16[128,640]{1,0:T(8,128)(2,1)S(1)} %get-tuple-element.85), channel_id=1, source_target_pairs={{0,16},{8,24},{1,17},{9,25},{2,18},{10,26},{3,19},{11,27},{4,20},{... | collective-permute-start | bytes 491528 | tf_op jit(solution)/shard_map/ppermute | solution.py:421
  67.3 0.9 %collective-permute-start.15 = (bf16[128,640]{1,0:T(8,128)(2,1)S(1)}, bf16[128,640]{1,0:T(8,128)(2,1)S(1)}, u32[]{:S(2)}, u32[]{:S(2)}) collective-permute-start(bf16[128,640]{1,0:T(8,128)(2,1)S(1)} %get-tuple-element.86), channel_id=1, source_target_pairs={{0,20},{8,28},{1,21},{9,29},{2,22},{10,30},{3,23},{11,31},{4,0},{1... | collective-permute-start | bytes 491528 | tf_op jit(solution)/shard_map/ppermute | solution.py:421
  68.2 7.9 %scores.1 = f32[1,128]{1,0:T(1,128)} custom-call(bf16[37,128,256]{2,1,0:T(8,128)(2,1)S(1)} %spectra.1.refs_0_, bf16[4,37,16,256]{3,2,1,0:T(8,128)(2,1)S(1)} %pad_maximum_fusion.refs_1_, bf16[4,37,16,256]{3,2,1,0:T(8,128)(2,1)S(1)} %collective-permute-done.16.refs_2_, bf16[4,37,16,256]{3,2,1,0:T(8,128)(2,1)S(1)} %pad_maximum_fusion.1.refs_3_, ...), custom_call_target="tpu_custom_call" | custom-call | flops 6000000000 | bytes 8000000 | tf_op jit(solution)/shard_map/scores/pallas_call | solution.py:271
  77.2 2.3 %collective-permute-start.21 = (f32[32,640]{1,0:T(8,128)S(1)}, f32[32,640]{1,0:T(8,128)S(1)}, u32[]{:S(2)}, u32[]{:S(2)}) collective-permute-start(f32[32,640]{1,0:T(8,128)S(1)} %get-tuple-element.94), channel_id=1, source_target_pairs={{0,2},{8,10},{1,3},{9,11},{2,0},{10,8},{3,1},{11,9},{4,6},{12,14},... | collective-permute-start | bytes 245768 | tf_op jit(solution)/shard_map/ppermute | solution.py:421
  79.5 1.0 %collective-permute-start.22 = (f32[32,640]{1,0:T(8,128)S(1)}, f32[32,640]{1,0:T(8,128)S(1)}, u32[]{:S(2)}, u32[]{:S(2)}) collective-permute-start(f32[32,640]{1,0:T(8,128)S(1)} %get-tuple-element.95), channel_id=1, source_target_pairs={{0,3},{8,11},{1,0},{9,8},{2,1},{10,9},{3,2},{11,10},{4,7},{12,15},... | collective-permute-start | bytes 245768 | tf_op jit(solution)/shard_map/ppermute | solution.py:421
  80.4 3.5 %collective-permute-done.20.a1 = f32[32,640]{1,0:T(8,128)S(1)} collective-permute-done((f32[32,640]{1,0:T(8,128)S(1)}, f32[32,640]{1,0:T(8,128)S(1)}, u32[]{:S(2)}, u32[]{:S(2)}) %collective-permute-start.20) | collective-permute-done | bytes 81952 | tf_op jit(solution)/shard_map/ppermute | solution.py:421
  84.5 1.4 %final.1 = f32[25,576]{1,0:T(8,128)} custom-call(s32[4]{0:T(128)S(1)} %pad_add_fusion.sc, f32[32,640]{1,0:T(8,128)S(1)} %get-tuple-element.92.a0, f32[32,640]{1,0:T(8,128)S(1)} %collective-permute-done.20.a1, f32[32,640]{1,0:T(8,128)S(1)} %collective-permute-done.21.a2, f32[32,640]{1,0:T(8,128)S(1)} %collective-permute-done.22.a3), custom_call_target="tpu_custom_call" | custom-call | tf_op jit(solution)/shard_map/final/pallas_call | solution.py:386
  (52 shorter events, 4.8 us)
Async XLA Ops:
  1.5 1.3 %collective-permute-start = (bf16[16,576]{1,0:T(8,128)(2,1)S(1)}, bf16[16,576]{1,0:T(8,128)(2,1)S(1)}, u32[]{:S(2)}, u32[]{:S(2)}) collective-permute-start(bf16[16,576]{1,0:T(8,128)(2,1)S(1)} %get-tuple-element.103), channel_id=1, source_target_pairs={{0,8},{8,0},{1,9},{9,1},{2,10},{10,2},{3,11},{11,3},{4,12},{12,4},... | collective-permute-start | bytes 55304 | tf_op jit(solution)/shard_map/ppermute | solution.py:421
  2.9 8.2 %collective-permute-start.1 = (bf16[16,1152]{1,0:T(8,128)(2,1)S(1)}, bf16[16,1152]{1,0:T(8,128)(2,1)S(1)}, u32[]{:S(2)}, u32[]{:S(2)}) collective-permute-start(bf16[16,1152]{1,0:T(8,128)(2,1)S(1)} %maximum_select_fusion), channel_id=1, source_target_pairs={{0,16},{8,24},{1,17},{9,25},{2,18},{10,26},{3,19},{11,27},{4,20},{... | collective-permute-start | bytes 110600 | tf_op jit(solution)/shard_map/ppermute | solution.py:421
  11.1 6.7 %collective-permute-start.2 = (bf16[2,16,1152]{2,1,0:T(8,128)(2,1)S(1)}, bf16[2,16,1152]{2,1,0:T(8,128)(2,1)S(1)}, u32[]{:S(2)}, u32[]{:S(2)}) collective-permute-start(bf16[2,16,1152]{2,1,0:T(8,128)(2,1)S(1)} %pad_maximum_fusion.4), channel_id=1, source_target_pairs={{0,32},{8,40},{1,33},{9,41},{2,34},{10,42},{3,35},{11,43},{4,36},{... | collective-permute-start | bytes 221192 | tf_op jit(solution)/shard_map/ppermute | solution.py:421
  17.8 7.4 %copy-start.1 = (bf16[592,576]{1,0:T(8,128)(2,1)S(1)}, bf16[592,576]{1,0:T(8,128)(2,1)}, u32[]{:S(2)}) copy-start(bf16[592,576]{1,0:T(8,128)(2,1)} %constant.82.clone.f_ref) | copy-start | bytes 2045956
  17.9 7.3 %collective-permute-start.4 = (bf16[2,2,16,1152]{3,2,1,0:T(8,128)(2,1)S(1)}, bf16[2,2,16,1152]{3,2,1,0:T(8,128)(2,1)S(1)}, u32[]{:S(2)}, u32[]{:S(2)}) collective-permute-start(bf16[2,2,16,1152]{3,2,1,0:T(8,128)(2,1)S(1)} %pad_maximum_fusion.3), channel_id=1, source_target_pairs={{0,64},{8,72},{1,65},{9,73},{2,66},{10,74},{3,67},{11,75},{4,68},{... | collective-permute-start | bytes 442376 | tf_op jit(solution)/shard_map/ppermute | solution.py:421
  20.9 9.6 %copy-start = (bf16[16,576,128]{2,1,0:T(8,128)(2,1)S(1)}, bf16[16,576,128]{2,1,0:T(8,128)(2,1)}, u32[]{:S(2)}) copy-start(bf16[16,576,128]{2,1,0:T(8,128)(2,1)} %get-tuple-element.73.w_ref) | copy-start | bytes 7077892
  20.9 17.3 %collective-permute-start.3 = (bf16[128,2432]{1,0:T(8,128)(2,1)}, bf16[128,2432]{1,0:T(8,128)(2,1)S(1)}, u32[]{:S(2)}, u32[]{:S(2)}) collective-permute-start(bf16[128,2432]{1,0:T(8,128)(2,1)} %get-tuple-element.72), channel_id=1, source_target_pairs={{0,64},{8,72},{1,65},{9,73},{2,66},{10,74},{3,67},{11,75},{4,68},{... | collective-permute-start | bytes 1867784 | tf_op jit(solution)/shard_map/ppermute | solution.py:421
  25.6 9.8 %collective-permute-start.5 = (bf16[37,16,256]{2,1,0:T(8,128)(2,1)S(1)}, bf16[37,16,256]{2,1,0:T(8,128)(2,1)S(1)}, u32[]{:S(2)}, u32[]{:S(2)}) collective-permute-start(bf16[37,16,256]{2,1,0:T(8,128)(2,1)S(1)} %ref_spectra.1), channel_id=1, source_target_pairs={{0,1},{8,9},{1,2},{9,10},{2,3},{10,11},{3,0},{11,8},{4,5},{12,13},... | collective-permute-start | bytes 909320 | tf_op jit(solution)/shard_map/ppermute | solution.py:421
  27.6 7.8 %collective-permute-start.6 = (bf16[37,16,256]{2,1,0:T(8,128)(2,1)S(1)}, bf16[37,16,256]{2,1,0:T(8,128)(2,1)S(1)}, u32[]{:S(2)}, u32[]{:S(2)}) collective-permute-start(bf16[37,16,256]{2,1,0:T(8,128)(2,1)S(1)} %ref_spectra.1), channel_id=1, source_target_pairs={{0,3},{8,11},{1,0},{9,8},{2,1},{10,9},{3,2},{11,10},{4,7},{12,15},... | collective-permute-start | bytes 909320 | tf_op jit(solution)/shard_map/ppermute | solution.py:421
  29.8 12.4 %collective-permute-start.9 = (bf16[37,16,256]{2,1,0:T(8,128)(2,1)S(1)}, bf16[37,16,256]{2,1,0:T(8,128)(2,1)}, u32[]{:S(2)}, u32[]{:S(2)}) collective-permute-start(bf16[37,16,256]{2,1,0:T(8,128)(2,1)S(1)} %ref_spectra.1), channel_id=1, source_target_pairs={{0,4},{8,12},{1,5},{9,13},{2,6},{10,14},{3,7},{11,15},{4,0},{12,8}... | collective-permute-start | bytes 909320 | tf_op jit(solution)/shard_map/ppermute | solution.py:421
  35.5 6.8 %copy-start.7 = (bf16[37,16,256]{2,1,0:T(8,128)(2,1)}, bf16[37,16,256]{2,1,0:T(8,128)(2,1)S(1)}, u32[]{:S(2)}) copy-start(bf16[37,16,256]{2,1,0:T(8,128)(2,1)S(1)} %collective-permute-done.5) | copy-start | bytes 909316
  35.5 10.8 %copy-start.8 = (bf16[37,16,256]{2,1,0:T(8,128)(2,1)}, bf16[37,16,256]{2,1,0:T(8,128)(2,1)S(1)}, u32[]{:S(2)}) copy-start(bf16[37,16,256]{2,1,0:T(8,128)(2,1)S(1)} %collective-permute-done.6) | copy-start | bytes 909316
  38.2 0.9 copy-start.4
  39.0 18.9 %collective-permute-start.7 = (bf16[128,2432]{1,0:T(8,128)(2,1)}, bf16[128,2432]{1,0:T(8,128)(2,1)S(1)}, u32[]{:S(2)}, u32[]{:S(2)}) collective-permute-start(bf16[128,2432]{1,0:T(8,128)(2,1)} %get-tuple-element.75), channel_id=1, source_target_pairs={{0,32},{8,40},{1,33},{9,41},{2,34},{10,42},{3,35},{11,43},{4,36},{... | collective-permute-start | bytes 1867784 | tf_op jit(solution)/shard_map/ppermute | solution.py:421
  39.5 18.5 %collective-permute-start.8 = (bf16[128,2432]{1,0:T(8,128)(2,1)}, bf16[128,2432]{1,0:T(8,128)(2,1)}, u32[]{:S(2)}, u32[]{:S(2)}) collective-permute-start(bf16[128,2432]{1,0:T(8,128)(2,1)} %get-tuple-element.76), channel_id=1, source_target_pairs={{0,96},{8,104},{1,97},{9,105},{2,98},{10,106},{3,99},{11,107},{4,1... | collective-permute-start | bytes 1867784 | tf_op jit(solution)/shard_map/ppermute | solution.py:421
  42.3 9.1 %collective-permute-start.11 = (bf16[37,16,256]{2,1,0:T(8,128)(2,1)}, bf16[37,16,256]{2,1,0:T(8,128)(2,1)}, u32[]{:S(2)}, u32[]{:S(2)}) collective-permute-start(bf16[37,16,256]{2,1,0:T(8,128)(2,1)} %collective-permute-done.9), channel_id=1, source_target_pairs={{0,3},{8,11},{1,0},{9,8},{2,1},{10,9},{3,2},{11,10},{4,7},{12,15},... | collective-permute-start | bytes 909320 | tf_op jit(solution)/shard_map/ppermute | solution.py:421
  46.3 11.6 %collective-permute-start.10 = (bf16[37,16,256]{2,1,0:T(8,128)(2,1)}, bf16[37,16,256]{2,1,0:T(8,128)(2,1)}, u32[]{:S(2)}, u32[]{:S(2)}) collective-permute-start(bf16[37,16,256]{2,1,0:T(8,128)(2,1)} %collective-permute-done.9), channel_id=1, source_target_pairs={{0,1},{8,9},{1,2},{9,10},{2,3},{10,11},{3,0},{11,8},{4,5},{12,13},... | collective-permute-start | bytes 909320 | tf_op jit(solution)/shard_map/ppermute | solution.py:421
  46.3 14.9 %collective-permute-start.17 = (bf16[37,16,256]{2,1,0:T(8,128)(2,1)}, bf16[37,16,256]{2,1,0:T(8,128)(2,1)S(1)}, u32[]{:S(2)}, u32[]{:S(2)}) collective-permute-start(bf16[37,16,256]{2,1,0:T(8,128)(2,1)} %copy-done.7), channel_id=1, source_target_pairs={{0,1},{8,9},{1,2},{9,10},{2,3},{10,11},{3,0},{11,8},{4,5},{12,13},... | collective-permute-start | bytes 909320 | tf_op jit(solution)/shard_map/ppermute | solution.py:421
  51.4 9.8 %collective-permute-start.18 = (bf16[37,16,256]{2,1,0:T(8,128)(2,1)}, bf16[37,16,256]{2,1,0:T(8,128)(2,1)S(1)}, u32[]{:S(2)}, u32[]{:S(2)}) collective-permute-start(bf16[37,16,256]{2,1,0:T(8,128)(2,1)} %collective-permute-done.11), channel_id=1, source_target_pairs={{0,3},{8,11},{1,0},{9,8},{2,1},{10,9},{3,2},{11,10},{4,7},{12,15},... | collective-permute-start | bytes 909320 | tf_op jit(solution)/shard_map/ppermute | solution.py:421
  55.2 2.8 %copy-start.2 = (bf16[128,2432]{1,0:T(8,128)(2,1)S(1)}, bf16[128,2432]{1,0:T(8,128)(2,1)}, u32[]{:S(2)}) copy-start(bf16[128,2432]{1,0:T(8,128)(2,1)} %get-tuple-element.77.c0) | copy-start | bytes 1867780
  55.2 2.8 %copy-start.3 = (f32[256,64]{0,1:T(8,128)S(1)}, f32[256,64]{0,1:T(8,128)}, u32[]{:S(2)}) copy-start(f32[256,64]{0,1:T(8,128)} %param.19) | copy-start | bytes 196612
  55.2 2.8 %copy-start.5 = (bf16[128,2432]{1,0:T(8,128)(2,1)S(1)}, bf16[128,2432]{1,0:T(8,128)(2,1)}, u32[]{:S(2)}) copy-start(bf16[128,2432]{1,0:T(8,128)(2,1)} %copy-done.4) | copy-start | bytes 1867780
  57.9 10.2 %collective-permute-start.16 = (bf16[4,37,16,256]{3,2,1,0:T(8,128)(2,1)S(1)}, bf16[4,37,16,256]{3,2,1,0:T(8,128)(2,1)S(1)}, u32[]{:S(2)}, u32[]{:S(2)}) collective-permute-start(bf16[4,37,16,256]{3,2,1,0:T(8,128)(2,1)S(1)} %pad_maximum_fusion.refs_1_), channel_id=1, source_target_pairs={{0,8},{8,0},{1,9},{9,1},{2,10},{10,2},{3,11},{11,3},{4,12},{12,4},... | collective-permute-start | bytes 3637256 | tf_op jit(solution)/shard_map/ppermute | solution.py:421
  60.6 3.2 %collective-permute-start.12 = (f32[2,256,640]{2,1,0:T(8,128)S(1)}, f32[2,256,640]{2,1,0:T(8,128)S(1)}, u32[]{:S(2)}, u32[]{:S(2)}) collective-permute-start(f32[2,256,640]{2,1,0:T(8,128)S(1)} %get-tuple-element.82), channel_id=1, source_target_pairs={{0,8},{8,0},{1,9},{9,1},{2,10},{10,2},{3,11},{11,3},{4,12},{12,4},... | collective-permute-start | bytes 3932168 | tf_op jit(solution)/shard_map/ppermute | solution.py:421
  62.4 5.8 %collective-permute-start.19 = (bf16[4,37,16,256]{3,2,1,0:T(8,128)(2,1)S(1)}, bf16[4,37,16,256]{3,2,1,0:T(8,128)(2,1)S(1)}, u32[]{:S(2)}, u32[]{:S(2)}) collective-permute-start(bf16[4,37,16,256]{3,2,1,0:T(8,128)(2,1)S(1)} %pad_maximum_fusion.1.refs_3_), channel_id=1, source_target_pairs={{0,8},{8,0},{1,9},{9,1},{2,10},{10,2},{3,11},{11,3},{4,12},{12,4},... | collective-permute-start | bytes 3637256 | tf_op jit(solution)/shard_map/ppermute | solution.py:421
  63.9 4.3 %copy-start.6 = (bf16[576,640]{1,0:T(8,128)(2,1)S(1)}, bf16[576,640]{1,0:T(8,128)(2,1)}, u32[]{:S(2)}) copy-start(bf16[576,640]{1,0:T(8,128)(2,1)} %constant.83.clone.refs_5_) | copy-start | bytes 2211844
  64.6 11.6 %collective-permute-start.13 = (bf16[128,640]{1,0:T(8,128)(2,1)S(1)}, bf16[128,640]{1,0:T(8,128)(2,1)S(1)}, u32[]{:S(2)}, u32[]{:S(2)}) collective-permute-start(bf16[128,640]{1,0:T(8,128)(2,1)S(1)} %get-tuple-element.84), channel_id=1, source_target_pairs={{0,4},{8,12},{1,5},{9,13},{2,6},{10,14},{3,7},{11,15},{4,16},{12,2... | collective-permute-start | bytes 491528 | tf_op jit(solution)/shard_map/ppermute | solution.py:421
  65.2 10.9 %collective-permute-start.14 = (bf16[128,640]{1,0:T(8,128)(2,1)S(1)}, bf16[128,640]{1,0:T(8,128)(2,1)S(1)}, u32[]{:S(2)}, u32[]{:S(2)}) collective-permute-start(bf16[128,640]{1,0:T(8,128)(2,1)S(1)} %get-tuple-element.85), channel_id=1, source_target_pairs={{0,16},{8,24},{1,17},{9,25},{2,18},{10,26},{3,19},{11,27},{4,20},{... | collective-permute-start | bytes 491528 | tf_op jit(solution)/shard_map/ppermute | solution.py:421
  67.3 9.2 %collective-permute-start.15 = (bf16[128,640]{1,0:T(8,128)(2,1)S(1)}, bf16[128,640]{1,0:T(8,128)(2,1)S(1)}, u32[]{:S(2)}, u32[]{:S(2)}) collective-permute-start(bf16[128,640]{1,0:T(8,128)(2,1)S(1)} %get-tuple-element.86), channel_id=1, source_target_pairs={{0,20},{8,28},{1,21},{9,29},{2,22},{10,30},{3,23},{11,31},{4,0},{1... | collective-permute-start | bytes 491528 | tf_op jit(solution)/shard_map/ppermute | solution.py:421
  77.1 6.9 %collective-permute-start.20 = (f32[32,640]{1,0:T(8,128)S(1)}, f32[32,640]{1,0:T(8,128)S(1)}, u32[]{:S(2)}, u32[]{:S(2)}) collective-permute-start(f32[32,640]{1,0:T(8,128)S(1)} %get-tuple-element.93), channel_id=1, source_target_pairs={{0,1},{8,9},{1,2},{9,10},{2,3},{10,11},{3,0},{11,8},{4,5},{12,13},... | collective-permute-start | bytes 245768 | tf_op jit(solution)/shard_map/ppermute | solution.py:421
  77.2 6.8 %collective-permute-start.21 = (f32[32,640]{1,0:T(8,128)S(1)}, f32[32,640]{1,0:T(8,128)S(1)}, u32[]{:S(2)}, u32[]{:S(2)}) collective-permute-start(f32[32,640]{1,0:T(8,128)S(1)} %get-tuple-element.94), channel_id=1, source_target_pairs={{0,2},{8,10},{1,3},{9,11},{2,0},{10,8},{3,1},{11,9},{4,6},{12,14},... | collective-permute-start | bytes 245768 | tf_op jit(solution)/shard_map/ppermute | solution.py:421
  79.5 5.1 %collective-permute-start.22 = (f32[32,640]{1,0:T(8,128)S(1)}, f32[32,640]{1,0:T(8,128)S(1)}, u32[]{:S(2)}, u32[]{:S(2)}) collective-permute-start(f32[32,640]{1,0:T(8,128)S(1)} %get-tuple-element.95), channel_id=1, source_target_pairs={{0,3},{8,11},{1,0},{9,8},{2,1},{10,9},{3,2},{11,10},{4,7},{12,15},... | collective-permute-start | bytes 245768 | tf_op jit(solution)/shard_map/ppermute | solution.py:421

commit v9 on v8

--- a/solution.py
+++ b/solution.py
@@ -349,7 +349,7 @@
         z = lax.rem(sc[3] + dz, 4)
         rows = pl.ds(pl.multiple_of(z * 32, 32), 32)
         far = a1[rows, :].astype(F32) + a2[rows, :].astype(F32) + a3[rows, :].astype(F32)
-        o[...] = a0[rows, :] + far
+        o[...] = (a0[rows, :] + far).astype(o.dtype)
 
 
 def cut_z(sc, parts):
@@ -358,7 +358,7 @@
         cut_z_kernel,
         in_specs=[pl.BlockSpec(memory_space=pltpu.SMEM)] + [v] * 4,
         out_specs=[v] * 4,
-        out_shape=[jax.ShapeDtypeStruct((32, 640), F32)] * 4,
+        out_shape=[jax.ShapeDtypeStruct((32, 640), F32)] + [jax.ShapeDtypeStruct((32, 640), BF)] * 3,
         compiler_params=pltpu.CompilerParams(vmem_limit_bytes=VMEM_LIMIT),
         cost_estimate=pl.CostEstimate(flops=400_000, bytes_accessed=1_700_000, transcendentals=0),
         name="cut_z",
@@ -366,7 +366,7 @@
 
 
 def final_kernel(sc, a0, a1, a2, a3, o_ref):
-    s = (a0[...] + a1[...]) + (a2[...] + a3[...])
+    s = a0[...] + (a1[...].astype(F32) + a2[...].astype(F32) + a3[...].astype(F32))
     odd = sc[2] == 1
     left = lax.broadcasted_iota(jnp.int32, (32, 128), 1) < R
     tile = [s[:, 128 * t : 128 * t + 128] for t in range(5)]

time: 86.6 us -> 85.4 us (0.986)
  waiting for transfers between devices: 21.4 us -> 20.5 us
    ppermute x23, waiting for transfers between devices: 21.4 us -> 20.5 us  [move(): return lax.ppermute(value, AXES, pairs)]
  transfers between devices with their start and end apart: 23 -> 23, of which waited for: 10 -> 10; matrix products, arithmetic and copies ran while one was open for 3% -> 3% of each run, Pallas kernels for 29% -> 30%
where the time goes in v9:
time: 85.4 us; the launch traced here: 85 us
  starting transfers between devices  31.9 us (37%)
  Pallas kernels  27.1 us (32%)
  waiting for transfers between devices  20.5 us (24%)
  other arithmetic  3.76 us (4%)
  local copies, waits for them, and re-layouts  0.88 us (1%)
    ppermute x23, starting transfers between devices, move(): return lax.ppermute(value, AXES, pairs)  31.9 us
    ppermute x23, waiting for transfers between devices, move(): return lax.ppermute(value, AXES, pairs)  20.5 us
    pallas_call x2, Pallas kernels, prep(): pl.pallas_call(functools.partial(prep_kernel, first), grid=(n // 32,), in...  10.1 us
    pallas_call x1, Pallas kernels, scores_of(): pl.pallas_call(score_kernel, in_specs=[v] * 6, out_specs=v, out_shape=jax...  7.94 us
    pallas_call x1, Pallas kernels, spectra(): pl.pallas_call(spectra_kernel, in_specs=[v, v], out_specs=v, out_shape=ja...  3.4 us
    pallas_call x1, Pallas kernels, class_sums(): pl.pallas_call(sums_kernel, in_specs=[pl.BlockSpec(memory_space=pltpu.SME...  2.64 us
  transfers between devices with their start and end apart: 23, of which 10 were waited for; matrix products, arithmetic and copies ran while one was open for 3% of the time, Pallas kernels for 30%

profile of v9, /device:TPU:0, one launch (start us, length us, event | category | flops | bytes accessed | tf_op | source)
XLA Modules:
  0.0 85.0 jit_solution(15419981765841694923)
XLA Ops:
  0.6 0.8 broadcast_select_fusion.1
  1.6 1.2 %collective-permute-done = bf16[16,576]{1,0:T(8,128)(2,1)S(1)} collective-permute-done((bf16[16,576]{1,0:T(8,128)(2,1)S(1)}, bf16[16,576]{1,0:T(8,128)(2,1)S(1)}, u32[]{:S(2)}, u32[]{:S(2)}) %collective-permute-start) | collective-permute-done | bytes 18464 | tf_op jit(solution)/shard_map/ppermute | solution.py:421
  2.9 3.2 %collective-permute-start.1 = (bf16[16,1152]{1,0:T(8,128)(2,1)S(1)}, bf16[16,1152]{1,0:T(8,128)(2,1)S(1)}, u32[]{:S(2)}, u32[]{:S(2)}) collective-permute-start(bf16[16,1152]{1,0:T(8,128)(2,1)S(1)} %maximum_select_fusion), channel_id=1, source_target_pairs={{0,16},{8,24},{1,17},{9,25},{2,18},{10,26},{3,19},{11,27},{4,20},{... | collective-permute-start | bytes 110600 | tf_op jit(solution)/shard_map/ppermute | solution.py:421
  6.0 5.0 %prep.2 = (bf16[16,576,128]{2,1,0:T(8,128)(2,1)}, bf16[128,2432]{1,0:T(8,128)(2,1)}, bf16[128,2432]{1,0:T(8,128)(2,1)}, bf16[128,2432]{1,0:T(8,128)(2,1)}, bf16[128,2432]{1,0:T(8,128)(2,1)}) custom-call(bf16[128,9216]{1,0:T(8,128)(2,1)} %x_ref.3, s32[2,128]{1,0:T(2,128)} %bitcast.41, s32[1,128]{1,0:T(1,128)} %bitcast.43, s32[1,128]{1,0:T(1,128)} %bitcast.45, ...), custom_call_target="tpu_custom_call" | custom-call | flops 20000000 | bytes 4000000 | tf_op jit(solution)/shard_map/prep/pallas_call | solution.py:144
  11.1 1.7 %collective-permute-start.2 = (bf16[2,16,1152]{2,1,0:T(8,128)(2,1)S(1)}, bf16[2,16,1152]{2,1,0:T(8,128)(2,1)S(1)}, u32[]{:S(2)}, u32[]{:S(2)}) collective-permute-start(bf16[2,16,1152]{2,1,0:T(8,128)(2,1)S(1)} %pad_maximum_fusion.4), channel_id=1, source_target_pairs={{0,32},{8,40},{1,33},{9,41},{2,34},{10,42},{3,35},{11,43},{4,36},{... | collective-permute-start | bytes 221192 | tf_op jit(solution)/shard_map/ppermute | solution.py:421
  12.8 5.0 %prep.3 = (bf16[16,576,128]{2,1,0:T(8,128)(2,1)}, bf16[128,2432]{1,0:T(8,128)(2,1)}, bf16[128,2432]{1,0:T(8,128)(2,1)}, bf16[128,2432]{1,0:T(8,128)(2,1)}, bf16[128,2432]{1,0:T(8,128)(2,1)}) custom-call(bf16[128,9216]{1,0:T(8,128)(2,1)} %x_ref.3, s32[2,128]{1,0:T(2,128)} %bitcast.42, ...), custom_call_target="tpu_custom_call", output_to_operand_aliasing={{0}: (9, {}), {1}: (10, {}), {2}: (11, {}), {3}: (12, {}), ... | custom-call | flops 20000000 | bytes 4000000 | tf_op jit(solution)/shard_map/prep/pallas_call | solution.py:144
  17.9 3.0 %collective-permute-start.4 = (bf16[2,2,16,1152]{3,2,1,0:T(8,128)(2,1)S(1)}, bf16[2,2,16,1152]{3,2,1,0:T(8,128)(2,1)S(1)}, u32[]{:S(2)}, u32[]{:S(2)}) collective-permute-start(bf16[2,2,16,1152]{3,2,1,0:T(8,128)(2,1)S(1)} %pad_maximum_fusion.3), channel_id=1, source_target_pairs={{0,64},{8,72},{1,65},{9,73},{2,66},{10,74},{3,67},{11,75},{4,68},{... | collective-permute-start | bytes 442376 | tf_op jit(solution)/shard_map/ppermute | solution.py:421
  21.5 3.7 %collective-permute-done.4 = bf16[2,2,16,1152]{3,2,1,0:T(8,128)(2,1)S(1)} collective-permute-done((bf16[2,2,16,1152]{3,2,1,0:T(8,128)(2,1)S(1)}, bf16[2,2,16,1152]{3,2,1,0:T(8,128)(2,1)S(1)}, u32[]{:S(2)}, u32[]{:S(2)}) %collective-permute-start.4) | collective-permute-done | bytes 147488 | tf_op jit(solution)/shard_map/ppermute | solution.py:421
  25.6 2.0 %collective-permute-start.5 = (bf16[37,16,256]{2,1,0:T(8,128)(2,1)S(1)}, bf16[37,16,256]{2,1,0:T(8,128)(2,1)S(1)}, u32[]{:S(2)}, u32[]{:S(2)}) collective-permute-start(bf16[37,16,256]{2,1,0:T(8,128)(2,1)S(1)} %ref_spectra.1), channel_id=1, source_target_pairs={{0,1},{8,9},{1,2},{9,10},{2,3},{10,11},{3,0},{11,8},{4,5},{12,13},... | collective-permute-start | bytes 909320 | tf_op jit(solution)/shard_map/ppermute | solution.py:421
  27.6 2.2 %collective-permute-start.6 = (bf16[37,16,256]{2,1,0:T(8,128)(2,1)S(1)}, bf16[37,16,256]{2,1,0:T(8,128)(2,1)S(1)}, u32[]{:S(2)}, u32[]{:S(2)}) collective-permute-start(bf16[37,16,256]{2,1,0:T(8,128)(2,1)S(1)} %ref_spectra.1), channel_id=1, source_target_pairs={{0,3},{8,11},{1,0},{9,8},{2,1},{10,9},{3,2},{11,10},{4,7},{12,15},... | collective-permute-start | bytes 909320 | tf_op jit(solution)/shard_map/ppermute | solution.py:421
  30.4 3.4 %spectra.1.refs_0_ = bf16[37,128,256]{2,1,0:T(8,128)(2,1)S(1)} custom-call(bf16[16,576,128]{2,1,0:T(8,128)(2,1)S(1)} %copy-done, bf16[592,576]{1,0:T(8,128)(2,1)S(1)} %copy-done.1), custom_call_target="tpu_custom_call" | custom-call | flops 1000 | bytes 1000 | tf_op jit(solution)/shard_map/spectra/pallas_call | solution.py:194
  33.8 1.6 %collective-permute-done.5 = bf16[37,16,256]{2,1,0:T(8,128)(2,1)S(1)} collective-permute-done((bf16[37,16,256]{2,1,0:T(8,128)(2,1)S(1)}, bf16[37,16,256]{2,1,0:T(8,128)(2,1)S(1)}, u32[]{:S(2)}, u32[]{:S(2)}) %collective-permute-start.5) | collective-permute-done | bytes 303136 | tf_op jit(solution)/shard_map/ppermute | solution.py:421
  35.5 2.7 %collective-permute-done.3.c2 = bf16[128,2432]{1,0:T(8,128)(2,1)S(1)} collective-permute-done((bf16[128,2432]{1,0:T(8,128)(2,1)}, bf16[128,2432]{1,0:T(8,128)(2,1)S(1)}, u32[]{:S(2)}, u32[]{:S(2)}) %collective-permute-start.3) | collective-permute-done | bytes 622624 | tf_op jit(solution)/shard_map/ppermute | solution.py:421
  38.2 0.9 %copy-done.4 = bf16[128,2432]{1,0:T(8,128)(2,1)} copy-done((bf16[128,2432]{1,0:T(8,128)(2,1)}, bf16[128,2432]{1,0:T(8,128)(2,1)S(1)}, u32[]{:S(2)}) %copy-start.4) | copy-done | bytes 622616
  39.5 2.8 %collective-permute-start.8 = (bf16[128,2432]{1,0:T(8,128)(2,1)}, bf16[128,2432]{1,0:T(8,128)(2,1)}, u32[]{:S(2)}, u32[]{:S(2)}) collective-permute-start(bf16[128,2432]{1,0:T(8,128)(2,1)} %get-tuple-element.76), channel_id=1, source_target_pairs={{0,96},{8,104},{1,97},{9,105},{2,98},{10,106},{3,99},{11,107},{4,1... | collective-permute-start | bytes 1867784 | tf_op jit(solution)/shard_map/ppermute | solution.py:421
  42.3 4.0 %collective-permute-start.11 = (bf16[37,16,256]{2,1,0:T(8,128)(2,1)}, bf16[37,16,256]{2,1,0:T(8,128)(2,1)}, u32[]{:S(2)}, u32[]{:S(2)}) collective-permute-start(bf16[37,16,256]{2,1,0:T(8,128)(2,1)} %collective-permute-done.9), channel_id=1, source_target_pairs={{0,3},{8,11},{1,0},{9,8},{2,1},{10,9},{3,2},{11,10},{4,7},{12,15},... | collective-permute-start | bytes 909320 | tf_op jit(solution)/shard_map/ppermute | solution.py:421
  46.3 5.1 %collective-permute-done.11 = bf16[37,16,256]{2,1,0:T(8,128)(2,1)} collective-permute-done((bf16[37,16,256]{2,1,0:T(8,128)(2,1)}, bf16[37,16,256]{2,1,0:T(8,128)(2,1)}, u32[]{:S(2)}, u32[]{:S(2)}) %collective-permute-start.11) | collective-permute-done | bytes 303136 | tf_op jit(solution)/shard_map/ppermute | solution.py:421
  51.4 3.7 %collective-permute-start.18 = (bf16[37,16,256]{2,1,0:T(8,128)(2,1)}, bf16[37,16,256]{2,1,0:T(8,128)(2,1)S(1)}, u32[]{:S(2)}, u32[]{:S(2)}) collective-permute-start(bf16[37,16,256]{2,1,0:T(8,128)(2,1)} %collective-permute-done.11), channel_id=1, source_target_pairs={{0,3},{8,11},{1,0},{9,8},{2,1},{10,9},{3,2},{11,10},{4,7},{12,15},... | collective-permute-start | bytes 909320 | tf_op jit(solution)/shard_map/ppermute | solution.py:421
  55.2 1.4 %pad_maximum_fusion.refs_1_ = bf16[4,37,16,256]{3,2,1,0:T(8,128)(2,1)S(1)} fusion(bf16[1,37,16,256]{3,2,1,0:T(8,128)(2,1)} %bitcast.38, bf16[1,37,16,256]{3,2,1,0:T(8,128)(2,1)} %bitcast.37, bf16[1,37,16,256]{3,2,1,0:T(8,128)(2,1)} %bitcast.18, bf16[1,37,16,256]{3,2,1,0:T(8,128)(2,1)S(1)} %bitcast.32), kind=kLoop, calls=%fused_computation | loop fusion | flops 1818624 | bytes 2424832 | tf_op jit(solution)/shard_map/stack | solution.py:473
  56.6 1.4 %collective-permute-done.10 = bf16[37,16,256]{2,1,0:T(8,128)(2,1)} collective-permute-done((bf16[37,16,256]{2,1,0:T(8,128)(2,1)}, bf16[37,16,256]{2,1,0:T(8,128)(2,1)}, u32[]{:S(2)}, u32[]{:S(2)}) %collective-permute-start.10) | collective-permute-done | bytes 303136 | tf_op jit(solution)/shard_map/ppermute | solution.py:421
  58.0 2.6 %class_sums.1 = (f32[2,256,640]{2,1,0:T(8,128)S(1)}, f32[2,256,640]{2,1,0:T(8,128)S(1)}) custom-call(s32[4]{0:T(128)S(1)} %pad_add_fusion.sc, bf16[128,2432]{1,0:T(8,128)(2,1)S(1)} %copy-done.2, bf16[128,2432]{1,0:T(8,128)(2,1)S(1)} %collective-permute-done.7.c1, bf16[128,2432]{1,0:T(8,128)(2,1)S(1)} %copy-done.5, ...), custom_call_target="tpu_custom_call" | custom-call | flops 700000000 | bytes 5000000 | tf_op jit(solution)/shard_map/class_sums/pallas_call | solution.py:314
  61.2 1.2 %pad_maximum_fusion.1.refs_3_ = bf16[4,37,16,256]{3,2,1,0:T(8,128)(2,1)S(1)} fusion(bf16[1,37,16,256]{3,2,1,0:T(8,128)(2,1)S(1)} %bitcast.40, bf16[1,37,16,256]{3,2,1,0:T(8,128)(2,1)S(1)} %bitcast.39, bf16[1,37,16,256]{3,2,1,0:T(8,128)(2,1)} %bitcast.22, bf16[1,37,16,256]{3,2,1,0:T(8,128)(2,1)} %bitcast.21), kind=kLoop, calls=%fused_computation.1 | loop fusion | flops 1818624 | bytes 2424832 | tf_op jit(solution)/shard_map/stack | solution.py:478
  62.5 1.3 %collective-permute-done.12.b_ref = f32[2,256,640]{2,1,0:T(8,128)S(1)} collective-permute-done((f32[2,256,640]{2,1,0:T(8,128)S(1)}, f32[2,256,640]{2,1,0:T(8,128)S(1)}, u32[]{:S(2)}, u32[]{:S(2)}) %collective-permute-start.12) | collective-permute-done | bytes 1310752 | tf_op jit(solution)/shard_map/ppermute | solution.py:421
  63.9 0.7 cut_x.1
  65.2 2.0 %collective-permute-start.14 = (bf16[128,640]{1,0:T(8,128)(2,1)S(1)}, bf16[128,640]{1,0:T(8,128)(2,1)S(1)}, u32[]{:S(2)}, u32[]{:S(2)}) collective-permute-start(bf16[128,640]{1,0:T(8,128)(2,1)S(1)} %get-tuple-element.85), channel_id=1, source_target_pairs={{0,16},{8,24},{1,17},{9,25},{2,18},{10,26},{3,19},{11,27},{4,20},{... | collective-permute-start | bytes 491528 | tf_op jit(solution)/shard_map/ppermute | solution.py:421
  67.3 0.9 %collective-permute-start.15 = (bf16[128,640]{1,0:T(8,128)(2,1)S(1)}, bf16[128,640]{1,0:T(8,128)(2,1)S(1)}, u32[]{:S(2)}, u32[]{:S(2)}) collective-permute-start(bf16[128,640]{1,0:T(8,128)(2,1)S(1)} %get-tuple-element.86), channel_id=1, source_target_pairs={{0,20},{8,28},{1,21},{9,29},{2,22},{10,30},{3,23},{11,31},{4,0},{1... | collective-permute-start | bytes 491528 | tf_op jit(solution)/shard_map/ppermute | solution.py:421
  68.2 7.9 %scores.1 = f32[1,128]{1,0:T(1,128)} custom-call(bf16[37,128,256]{2,1,0:T(8,128)(2,1)S(1)} %spectra.1.refs_0_, bf16[4,37,16,256]{3,2,1,0:T(8,128)(2,1)S(1)} %pad_maximum_fusion.refs_1_, bf16[4,37,16,256]{3,2,1,0:T(8,128)(2,1)S(1)} %collective-permute-done.16.refs_2_, bf16[4,37,16,256]{3,2,1,0:T(8,128)(2,1)S(1)} %pad_maximum_fusion.1.refs_3_, ...), custom_call_target="tpu_custom_call" | custom-call | flops 6000000000 | bytes 8000000 | tf_op jit(solution)/shard_map/scores/pallas_call | solution.py:271
  77.2 2.3 %collective-permute-start.21 = (bf16[32,640]{1,0:T(8,128)(2,1)S(1)}, bf16[32,640]{1,0:T(8,128)(2,1)S(1)}, u32[]{:S(2)}, u32[]{:S(2)}) collective-permute-start(bf16[32,640]{1,0:T(8,128)(2,1)S(1)} %get-tuple-element.94), channel_id=1, source_target_pairs={{0,2},{8,10},{1,3},{9,11},{2,0},{10,8},{3,1},{11,9},{4,6},{12,14},... | collective-permute-start | bytes 122888 | tf_op jit(solution)/shard_map/ppermute | solution.py:421
  79.5 1.0 %collective-permute-start.22 = (bf16[32,640]{1,0:T(8,128)(2,1)S(1)}, bf16[32,640]{1,0:T(8,128)(2,1)S(1)}, u32[]{:S(2)}, u32[]{:S(2)}) collective-permute-start(bf16[32,640]{1,0:T(8,128)(2,1)S(1)} %get-tuple-element.95), channel_id=1, source_target_pairs={{0,3},{8,11},{1,0},{9,8},{2,1},{10,9},{3,2},{11,10},{4,7},{12,15},... | collective-permute-start | bytes 122888 | tf_op jit(solution)/shard_map/ppermute | solution.py:421
  80.4 2.4 %collective-permute-done.20.a1 = bf16[32,640]{1,0:T(8,128)(2,1)S(1)} collective-permute-done((bf16[32,640]{1,0:T(8,128)(2,1)S(1)}, bf16[32,640]{1,0:T(8,128)(2,1)S(1)}, u32[]{:S(2)}, u32[]{:S(2)}) %collective-permute-start.20) | collective-permute-done | bytes 40992 | tf_op jit(solution)/shard_map/ppermute | solution.py:421
  82.8 0.9 %collective-permute-done.22.a3 = bf16[32,640]{1,0:T(8,128)(2,1)S(1)} collective-permute-done((bf16[32,640]{1,0:T(8,128)(2,1)S(1)}, bf16[32,640]{1,0:T(8,128)(2,1)S(1)}, u32[]{:S(2)}, u32[]{:S(2)}) %collective-permute-start.22) | collective-permute-done | bytes 40992 | tf_op jit(solution)/shard_map/ppermute | solution.py:421
  83.7 1.4 %final.1 = f32[25,576]{1,0:T(8,128)} custom-call(s32[4]{0:T(128)S(1)} %pad_add_fusion.sc, f32[32,640]{1,0:T(8,128)S(1)} %get-tuple-element.92.a0, bf16[32,640]{1,0:T(8,128)(2,1)S(1)} %collective-permute-done.20.a1, bf16[32,640]{1,0:T(8,128)(2,1)S(1)} %collective-permute-done.21.a2, bf16[32,640]{1,0:T(8,128)(2,1)S(1)} %collective-permute-done.22.a3), custom_call_target="tpu_custom_call" | custom-call | tf_op jit(solution)/shard_map/final/pallas_call | solution.py:386
  (52 shorter events, 4.9 us)
Async XLA Ops:
  1.5 1.3 %collective-permute-start = (bf16[16,576]{1,0:T(8,128)(2,1)S(1)}, bf16[16,576]{1,0:T(8,128)(2,1)S(1)}, u32[]{:S(2)}, u32[]{:S(2)}) collective-permute-start(bf16[16,576]{1,0:T(8,128)(2,1)S(1)} %get-tuple-element.103), channel_id=1, source_target_pairs={{0,8},{8,0},{1,9},{9,1},{2,10},{10,2},{3,11},{11,3},{4,12},{12,4},... | collective-permute-start | bytes 55304 | tf_op jit(solution)/shard_map/ppermute | solution.py:421
  2.9 8.2 %collective-permute-start.1 = (bf16[16,1152]{1,0:T(8,128)(2,1)S(1)}, bf16[16,1152]{1,0:T(8,128)(2,1)S(1)}, u32[]{:S(2)}, u32[]{:S(2)}) collective-permute-start(bf16[16,1152]{1,0:T(8,128)(2,1)S(1)} %maximum_select_fusion), channel_id=1, source_target_pairs={{0,16},{8,24},{1,17},{9,25},{2,18},{10,26},{3,19},{11,27},{4,20},{... | collective-permute-start | bytes 110600 | tf_op jit(solution)/shard_map/ppermute | solution.py:421
  11.1 6.7 %collective-permute-start.2 = (bf16[2,16,1152]{2,1,0:T(8,128)(2,1)S(1)}, bf16[2,16,1152]{2,1,0:T(8,128)(2,1)S(1)}, u32[]{:S(2)}, u32[]{:S(2)}) collective-permute-start(bf16[2,16,1152]{2,1,0:T(8,128)(2,1)S(1)} %pad_maximum_fusion.4), channel_id=1, source_target_pairs={{0,32},{8,40},{1,33},{9,41},{2,34},{10,42},{3,35},{11,43},{4,36},{... | collective-permute-start | bytes 221192 | tf_op jit(solution)/shard_map/ppermute | solution.py:421
  17.8 7.4 %copy-start.1 = (bf16[592,576]{1,0:T(8,128)(2,1)S(1)}, bf16[592,576]{1,0:T(8,128)(2,1)}, u32[]{:S(2)}) copy-start(bf16[592,576]{1,0:T(8,128)(2,1)} %constant.82.clone.f_ref) | copy-start | bytes 2045956
  17.9 7.3 %collective-permute-start.4 = (bf16[2,2,16,1152]{3,2,1,0:T(8,128)(2,1)S(1)}, bf16[2,2,16,1152]{3,2,1,0:T(8,128)(2,1)S(1)}, u32[]{:S(2)}, u32[]{:S(2)}) collective-permute-start(bf16[2,2,16,1152]{3,2,1,0:T(8,128)(2,1)S(1)} %pad_maximum_fusion.3), channel_id=1, source_target_pairs={{0,64},{8,72},{1,65},{9,73},{2,66},{10,74},{3,67},{11,75},{4,68},{... | collective-permute-start | bytes 442376 | tf_op jit(solution)/shard_map/ppermute | solution.py:421
  20.9 9.6 %copy-start = (bf16[16,576,128]{2,1,0:T(8,128)(2,1)S(1)}, bf16[16,576,128]{2,1,0:T(8,128)(2,1)}, u32[]{:S(2)}) copy-start(bf16[16,576,128]{2,1,0:T(8,128)(2,1)} %get-tuple-element.73.w_ref) | copy-start | bytes 7077892
  20.9 17.3 %collective-permute-start.3 = (bf16[128,2432]{1,0:T(8,128)(2,1)}, bf16[128,2432]{1,0:T(8,128)(2,1)S(1)}, u32[]{:S(2)}, u32[]{:S(2)}) collective-permute-start(bf16[128,2432]{1,0:T(8,128)(2,1)} %get-tuple-element.72), channel_id=1, source_target_pairs={{0,64},{8,72},{1,65},{9,73},{2,66},{10,74},{3,67},{11,75},{4,68},{... | collective-permute-start | bytes 1867784 | tf_op jit(solution)/shard_map/ppermute | solution.py:421
  25.6 9.8 %collective-permute-start.5 = (bf16[37,16,256]{2,1,0:T(8,128)(2,1)S(1)}, bf16[37,16,256]{2,1,0:T(8,128)(2,1)S(1)}, u32[]{:S(2)}, u32[]{:S(2)}) collective-permute-start(bf16[37,16,256]{2,1,0:T(8,128)(2,1)S(1)} %ref_spectra.1), channel_id=1, source_target_pairs={{0,1},{8,9},{1,2},{9,10},{2,3},{10,11},{3,0},{11,8},{4,5},{12,13},... | collective-permute-start | bytes 909320 | tf_op jit(solution)/shard_map/ppermute | solution.py:421
  27.6 7.8 %collective-permute-start.6 = (bf16[37,16,256]{2,1,0:T(8,128)(2,1)S(1)}, bf16[37,16,256]{2,1,0:T(8,128)(2,1)S(1)}, u32[]{:S(2)}, u32[]{:S(2)}) collective-permute-start(bf16[37,16,256]{2,1,0:T(8,128)(2,1)S(1)} %ref_spectra.1), channel_id=1, source_target_pairs={{0,3},{8,11},{1,0},{9,8},{2,1},{10,9},{3,2},{11,10},{4,7},{12,15},... | collective-permute-start | bytes 909320 | tf_op jit(solution)/shard_map/ppermute | solution.py:421
  29.8 12.4 %collective-permute-start.9 = (bf16[37,16,256]{2,1,0:T(8,128)(2,1)S(1)}, bf16[37,16,256]{2,1,0:T(8,128)(2,1)}, u32[]{:S(2)}, u32[]{:S(2)}) collective-permute-start(bf16[37,16,256]{2,1,0:T(8,128)(2,1)S(1)} %ref_spectra.1), channel_id=1, source_target_pairs={{0,4},{8,12},{1,5},{9,13},{2,6},{10,14},{3,7},{11,15},{4,0},{12,8}... | collective-permute-start | bytes 909320 | tf_op jit(solution)/shard_map/ppermute | solution.py:421
  35.5 6.8 %copy-start.7 = (bf16[37,16,256]{2,1,0:T(8,128)(2,1)}, bf16[37,16,256]{2,1,0:T(8,128)(2,1)S(1)}, u32[]{:S(2)}) copy-start(bf16[37,16,256]{2,1,0:T(8,128)(2,1)S(1)} %collective-permute-done.5) | copy-start | bytes 909316
  35.5 10.8 %copy-start.8 = (bf16[37,16,256]{2,1,0:T(8,128)(2,1)}, bf16[37,16,256]{2,1,0:T(8,128)(2,1)S(1)}, u32[]{:S(2)}) copy-start(bf16[37,16,256]{2,1,0:T(8,128)(2,1)S(1)} %collective-permute-done.6) | copy-start | bytes 909316
  38.2 0.9 %copy-start.4 = (bf16[128,2432]{1,0:T(8,128)(2,1)}, bf16[128,2432]{1,0:T(8,128)(2,1)S(1)}, u32[]{:S(2)}) copy-start(bf16[128,2432]{1,0:T(8,128)(2,1)S(1)} %collective-permute-done.3.c2) | copy-start | bytes 1867780
  39.0 18.9 %collective-permute-start.7 = (bf16[128,2432]{1,0:T(8,128)(2,1)}, bf16[128,2432]{1,0:T(8,128)(2,1)S(1)}, u32[]{:S(2)}, u32[]{:S(2)}) collective-permute-start(bf16[128,2432]{1,0:T(8,128)(2,1)} %get-tuple-element.75), channel_id=1, source_target_pairs={{0,32},{8,40},{1,33},{9,41},{2,34},{10,42},{3,35},{11,43},{4,36},{... | collective-permute-start | bytes 1867784 | tf_op jit(solution)/shard_map/ppermute | solution.py:421
  39.5 18.5 %collective-permute-start.8 = (bf16[128,2432]{1,0:T(8,128)(2,1)}, bf16[128,2432]{1,0:T(8,128)(2,1)}, u32[]{:S(2)}, u32[]{:S(2)}) collective-permute-start(bf16[128,2432]{1,0:T(8,128)(2,1)} %get-tuple-element.76), channel_id=1, source_target_pairs={{0,96},{8,104},{1,97},{9,105},{2,98},{10,106},{3,99},{11,107},{4,1... | collective-permute-start | bytes 1867784 | tf_op jit(solution)/shard_map/ppermute | solution.py:421
  42.3 9.1 %collective-permute-start.11 = (bf16[37,16,256]{2,1,0:T(8,128)(2,1)}, bf16[37,16,256]{2,1,0:T(8,128)(2,1)}, u32[]{:S(2)}, u32[]{:S(2)}) collective-permute-start(bf16[37,16,256]{2,1,0:T(8,128)(2,1)} %collective-permute-done.9), channel_id=1, source_target_pairs={{0,3},{8,11},{1,0},{9,8},{2,1},{10,9},{3,2},{11,10},{4,7},{12,15},... | collective-permute-start | bytes 909320 | tf_op jit(solution)/shard_map/ppermute | solution.py:421
  46.3 11.6 %collective-permute-start.10 = (bf16[37,16,256]{2,1,0:T(8,128)(2,1)}, bf16[37,16,256]{2,1,0:T(8,128)(2,1)}, u32[]{:S(2)}, u32[]{:S(2)}) collective-permute-start(bf16[37,16,256]{2,1,0:T(8,128)(2,1)} %collective-permute-done.9), channel_id=1, source_target_pairs={{0,1},{8,9},{1,2},{9,10},{2,3},{10,11},{3,0},{11,8},{4,5},{12,13},... | collective-permute-start | bytes 909320 | tf_op jit(solution)/shard_map/ppermute | solution.py:421
  46.3 14.9 %collective-permute-start.17 = (bf16[37,16,256]{2,1,0:T(8,128)(2,1)}, bf16[37,16,256]{2,1,0:T(8,128)(2,1)S(1)}, u32[]{:S(2)}, u32[]{:S(2)}) collective-permute-start(bf16[37,16,256]{2,1,0:T(8,128)(2,1)} %copy-done.7), channel_id=1, source_target_pairs={{0,1},{8,9},{1,2},{9,10},{2,3},{10,11},{3,0},{11,8},{4,5},{12,13},... | collective-permute-start | bytes 909320 | tf_op jit(solution)/shard_map/ppermute | solution.py:421
  51.4 9.8 %collective-permute-start.18 = (bf16[37,16,256]{2,1,0:T(8,128)(2,1)}, bf16[37,16,256]{2,1,0:T(8,128)(2,1)S(1)}, u32[]{:S(2)}, u32[]{:S(2)}) collective-permute-start(bf16[37,16,256]{2,1,0:T(8,128)(2,1)} %collective-permute-done.11), channel_id=1, source_target_pairs={{0,3},{8,11},{1,0},{9,8},{2,1},{10,9},{3,2},{11,10},{4,7},{12,15},... | collective-permute-start | bytes 909320 | tf_op jit(solution)/shard_map/ppermute | solution.py:421
  55.2 2.8 %copy-start.2 = (bf16[128,2432]{1,0:T(8,128)(2,1)S(1)}, bf16[128,2432]{1,0:T(8,128)(2,1)}, u32[]{:S(2)}) copy-start(bf16[128,2432]{1,0:T(8,128)(2,1)} %get-tuple-element.77.c0) | copy-start | bytes 1867780
  55.2 2.8 %copy-start.3 = (f32[256,64]{0,1:T(8,128)S(1)}, f32[256,64]{0,1:T(8,128)}, u32[]{:S(2)}) copy-start(f32[256,64]{0,1:T(8,128)} %param.19) | copy-start | bytes 196612
  55.2 2.8 %copy-start.5 = (bf16[128,2432]{1,0:T(8,128)(2,1)S(1)}, bf16[128,2432]{1,0:T(8,128)(2,1)}, u32[]{:S(2)}) copy-start(bf16[128,2432]{1,0:T(8,128)(2,1)} %copy-done.4) | copy-start | bytes 1867780
  57.9 10.2 %collective-permute-start.16 = (bf16[4,37,16,256]{3,2,1,0:T(8,128)(2,1)S(1)}, bf16[4,37,16,256]{3,2,1,0:T(8,128)(2,1)S(1)}, u32[]{:S(2)}, u32[]{:S(2)}) collective-permute-start(bf16[4,37,16,256]{3,2,1,0:T(8,128)(2,1)S(1)} %pad_maximum_fusion.refs_1_), channel_id=1, source_target_pairs={{0,8},{8,0},{1,9},{9,1},{2,10},{10,2},{3,11},{11,3},{4,12},{12,4},... | collective-permute-start | bytes 3637256 | tf_op jit(solution)/shard_map/ppermute | solution.py:421
  60.6 3.2 %collective-permute-start.12 = (f32[2,256,640]{2,1,0:T(8,128)S(1)}, f32[2,256,640]{2,1,0:T(8,128)S(1)}, u32[]{:S(2)}, u32[]{:S(2)}) collective-permute-start(f32[2,256,640]{2,1,0:T(8,128)S(1)} %get-tuple-element.82), channel_id=1, source_target_pairs={{0,8},{8,0},{1,9},{9,1},{2,10},{10,2},{3,11},{11,3},{4,12},{12,4},... | collective-permute-start | bytes 3932168 | tf_op jit(solution)/shard_map/ppermute | solution.py:421
  62.4 5.8 %collective-permute-start.19 = (bf16[4,37,16,256]{3,2,1,0:T(8,128)(2,1)S(1)}, bf16[4,37,16,256]{3,2,1,0:T(8,128)(2,1)S(1)}, u32[]{:S(2)}, u32[]{:S(2)}) collective-permute-start(bf16[4,37,16,256]{3,2,1,0:T(8,128)(2,1)S(1)} %pad_maximum_fusion.1.refs_3_), channel_id=1, source_target_pairs={{0,8},{8,0},{1,9},{9,1},{2,10},{10,2},{3,11},{11,3},{4,12},{12,4},... | collective-permute-start | bytes 3637256 | tf_op jit(solution)/shard_map/ppermute | solution.py:421
  63.9 4.3 %copy-start.6 = (bf16[576,640]{1,0:T(8,128)(2,1)S(1)}, bf16[576,640]{1,0:T(8,128)(2,1)}, u32[]{:S(2)}) copy-start(bf16[576,640]{1,0:T(8,128)(2,1)} %constant.83.clone.refs_5_) | copy-start | bytes 2211844
  64.6 11.6 %collective-permute-start.13 = (bf16[128,640]{1,0:T(8,128)(2,1)S(1)}, bf16[128,640]{1,0:T(8,128)(2,1)S(1)}, u32[]{:S(2)}, u32[]{:S(2)}) collective-permute-start(bf16[128,640]{1,0:T(8,128)(2,1)S(1)} %get-tuple-element.84), channel_id=1, source_target_pairs={{0,4},{8,12},{1,5},{9,13},{2,6},{10,14},{3,7},{11,15},{4,16},{12,2... | collective-permute-start | bytes 491528 | tf_op jit(solution)/shard_map/ppermute | solution.py:421
  65.2 10.9 %collective-permute-start.14 = (bf16[128,640]{1,0:T(8,128)(2,1)S(1)}, bf16[128,640]{1,0:T(8,128)(2,1)S(1)}, u32[]{:S(2)}, u32[]{:S(2)}) collective-permute-start(bf16[128,640]{1,0:T(8,128)(2,1)S(1)} %get-tuple-element.85), channel_id=1, source_target_pairs={{0,16},{8,24},{1,17},{9,25},{2,18},{10,26},{3,19},{11,27},{4,20},{... | collective-permute-start | bytes 491528 | tf_op jit(solution)/shard_map/ppermute | solution.py:421
  67.3 9.2 %collective-permute-start.15 = (bf16[128,640]{1,0:T(8,128)(2,1)S(1)}, bf16[128,640]{1,0:T(8,128)(2,1)S(1)}, u32[]{:S(2)}, u32[]{:S(2)}) collective-permute-start(bf16[128,640]{1,0:T(8,128)(2,1)S(1)} %get-tuple-element.86), channel_id=1, source_target_pairs={{0,20},{8,28},{1,21},{9,29},{2,22},{10,30},{3,23},{11,31},{4,0},{1... | collective-permute-start | bytes 491528 | tf_op jit(solution)/shard_map/ppermute | solution.py:421
  77.1 5.7 %collective-permute-start.20 = (bf16[32,640]{1,0:T(8,128)(2,1)S(1)}, bf16[32,640]{1,0:T(8,128)(2,1)S(1)}, u32[]{:S(2)}, u32[]{:S(2)}) collective-permute-start(bf16[32,640]{1,0:T(8,128)(2,1)S(1)} %get-tuple-element.93), channel_id=1, source_target_pairs={{0,1},{8,9},{1,2},{9,10},{2,3},{10,11},{3,0},{11,8},{4,5},{12,13},... | collective-permute-start | bytes 122888 | tf_op jit(solution)/shard_map/ppermute | solution.py:421
  77.2 5.6 %collective-permute-start.21 = (bf16[32,640]{1,0:T(8,128)(2,1)S(1)}, bf16[32,640]{1,0:T(8,128)(2,1)S(1)}, u32[]{:S(2)}, u32[]{:S(2)}) collective-permute-start(bf16[32,640]{1,0:T(8,128)(2,1)S(1)} %get-tuple-element.94), channel_id=1, source_target_pairs={{0,2},{8,10},{1,3},{9,11},{2,0},{10,8},{3,1},{11,9},{4,6},{12,14},... | collective-permute-start | bytes 122888 | tf_op jit(solution)/shard_map/ppermute | solution.py:421
  79.5 4.2 %collective-permute-start.22 = (bf16[32,640]{1,0:T(8,128)(2,1)S(1)}, bf16[32,640]{1,0:T(8,128)(2,1)S(1)}, u32[]{:S(2)}, u32[]{:S(2)}) collective-permute-start(bf16[32,640]{1,0:T(8,128)(2,1)S(1)} %get-tuple-element.95), channel_id=1, source_target_pairs={{0,3},{8,11},{1,0},{9,8},{2,1},{10,9},{3,2},{11,10},{4,7},{12,15},... | collective-permute-start | bytes 122888 | tf_op jit(solution)/shard_map/ppermute | solution.py:421

commit v10 on v9

--- a/solution.py
+++ b/solution.py
@@ -78,61 +78,64 @@
         flipped = tab_ref[...].T
         tab[...] = jnp.concatenate([flipped, flipped], axis=1)
 
-    here = aux[pl.ds(pl.multiple_of((step + first) * 16, 16), 16), :]
-    lane = lax.broadcasted_iota(jnp.int32, (16, 128), 1)
-    left = lane < R
-    shift = jnp.where(left, 0.0, -0.25).astype(F32)
-    sxb = jnp.broadcast_to(here[:, 0:1], (16, 128))
-    syb = jnp.broadcast_to(here[:, 1:2], (16, 128))
-    ctf = jnp.where(here[:, 3:4] > 0.5, tab[pl.ds(mine + 1, 1), :], tab[pl.ds(mine, 1), :])
-    ctf_s = jnp.where(left, -ctf, ctf)
-    for b in range(A // 4):
-        done = []
-        for a in (2 * b, 2 * b + 1):
-            v = (sxb * fx_ref[a : a + 1, :] + syb * fy_ref[a : a + 1, :]) + shift
-            v = v - jnp.round(v)
-            q = v * v
-            e = jnp.full_like(q, COEF[-1])
-            for k in COEF[-2::-1]:
-                e = e * q + k
-            er = pltpu.roll(e, R, 1)
-            cc = jnp.where(left, e, er) * ctf
-            ss = jnp.where(left, er, e) * ctf_s
-            x0 = x_ref[:, a * 128 : (a + 1) * 128].astype(F32)
-            h = a + A // 2
-            x1 = x_ref[:, h * 128 : (h + 1) * 128].astype(F32)
-            w0 = x0 * cc + pltpu.roll(x0, R, 1) * ss
-            w1 = x1 * cc - pltpu.roll(x1, R, 1) * ss
-            ws[:, a * 128 : (a + 1) * 128] = w0
-            ws[:, h * 128 : (h + 1) * 128] = w1
-            done.append((w0, w1))
-        for half in (0, 1):
-            row = (2 * b + half * (A // 2)) * 8
-            for g in (0, 1):
-                w_ref[g, row : row + 16, :] = jnp.concatenate(
-                    [done[0][half][8 * g : 8 * g + 8], done[1][half][8 * g : 8 * g + 8]], axis=0
-                ).astype(BF)
-    rotb = jnp.broadcast_to(here[:, 2:3], (16, 128)).astype(jnp.int32)
-    bit = [(rotb & (1 << k)) != 0 for k in range(7)]
-    for r in range(8):
-        t = [ws[:, (r + 8 * n) * 128 : (r + 8 * n + 1) * 128] for n in range(9)]
-        for k in range(4):
-            t = [jnp.where(bit[3 + k], t[(n + (1 << k)) % 9], t[n]) for n in range(9)]
-        for n in range(9):
-            us[:, (r + 8 * n) * 128 : (r + 8 * n + 1) * 128] = t[n]
-    for j0 in range(0, A, 8):
-        t = [us[:, ((j0 + i) % A) * 128 : ((j0 + i) % A + 1) * 128] for i in range(15)]
-        t = [jnp.where(bit[0], t[i + 1], t[i]) for i in range(14)]
-        t = [jnp.where(bit[1], t[i + 2], t[i]) for i in range(12)]
-        for i in range(8):
-            ws[:, (j0 + i) * 128 : (j0 + i + 1) * 128] = jnp.where(bit[2], t[i + 4], t[i])
-    meta = jnp.where(lane == 0, here[:, 4:5], jnp.where(lane == 1, here[:, 5:6], 0.0)).astype(BF)
-    width = 18 * 128
-    for dy, c_ref in enumerate((c0, c1, c2, c3)):
-        dest = lax.rem(dom // 4 + dy, 4)
-        start = pl.multiple_of(dest * width, 128)
-        c_ref[:, 0:width] = ws[:, pl.ds(start, width)].astype(BF)
-        c_ref[:, width : width + 128] = meta
+    @pl.loop(0, 2)
+    def _(half):
+        span = pl.ds(pl.multiple_of(half * 16, 16), 16)
+        here = aux[pl.ds(pl.multiple_of((2 * (step + first) + half) * 16, 16), 16), :]
+        lane = lax.broadcasted_iota(jnp.int32, (16, 128), 1)
+        left = lane < R
+        shift = jnp.where(left, 0.0, -0.25).astype(F32)
+        sxb = jnp.broadcast_to(here[:, 0:1], (16, 128))
+        syb = jnp.broadcast_to(here[:, 1:2], (16, 128))
+        ctf = jnp.where(here[:, 3:4] > 0.5, tab[pl.ds(mine + 1, 1), :], tab[pl.ds(mine, 1), :])
+        ctf_s = jnp.where(left, -ctf, ctf)
+        for b in range(A // 4):
+            done = []
+            for a in (2 * b, 2 * b + 1):
+                v = (sxb * fx_ref[a : a + 1, :] + syb * fy_ref[a : a + 1, :]) + shift
+                v = v - jnp.round(v)
+                q = v * v
+                e = jnp.full_like(q, COEF[-1])
+                for k in COEF[-2::-1]:
+                    e = e * q + k
+                er = pltpu.roll(e, R, 1)
+                cc = jnp.where(left, e, er) * ctf
+                ss = jnp.where(left, er, e) * ctf_s
+                x0 = x_ref[span, a * 128 : (a + 1) * 128].astype(F32)
+                h = a + A // 2
+                x1 = x_ref[span, h * 128 : (h + 1) * 128].astype(F32)
+                w0 = x0 * cc + pltpu.roll(x0, R, 1) * ss
+                w1 = x1 * cc - pltpu.roll(x1, R, 1) * ss
+                ws[:, a * 128 : (a + 1) * 128] = w0
+                ws[:, h * 128 : (h + 1) * 128] = w1
+                done.append((w0, w1))
+            for turn in (0, 1):
+                row = (2 * b + turn * (A // 2)) * 8
+                for g in (0, 1):
+                    w_ref[2 * half + g, row : row + 16, :] = jnp.concatenate(
+                        [done[0][turn][8 * g : 8 * g + 8], done[1][turn][8 * g : 8 * g + 8]], axis=0
+                    ).astype(BF)
+        rotb = jnp.broadcast_to(here[:, 2:3], (16, 128)).astype(jnp.int32)
+        bit = [(rotb & (1 << k)) != 0 for k in range(7)]
+        for r in range(8):
+            t = [ws[:, (r + 8 * n) * 128 : (r + 8 * n + 1) * 128] for n in range(9)]
+            for k in range(4):
+                t = [jnp.where(bit[3 + k], t[(n + (1 << k)) % 9], t[n]) for n in range(9)]
+            for n in range(9):
+                us[:, (r + 8 * n) * 128 : (r + 8 * n + 1) * 128] = t[n]
+        for j0 in range(0, A, 8):
+            t = [us[:, ((j0 + i) % A) * 128 : ((j0 + i) % A + 1) * 128] for i in range(15)]
+            t = [jnp.where(bit[0], t[i + 1], t[i]) for i in range(14)]
+            t = [jnp.where(bit[1], t[i + 2], t[i]) for i in range(12)]
+            for i in range(8):
+                ws[:, (j0 + i) * 128 : (j0 + i + 1) * 128] = jnp.where(bit[2], t[i + 4], t[i])
+        meta = jnp.where(lane == 0, here[:, 4:5], jnp.where(lane == 1, here[:, 5:6], 0.0)).astype(BF)
+        width = 18 * 128
+        for dy, c_ref in enumerate((c0, c1, c2, c3)):
+            dest = lax.rem(dom // 4 + dy, 4)
+            start = pl.multiple_of(dest * width, 128)
+            c_ref[span, 0:width] = ws[:, pl.ds(start, width)].astype(BF)
+            c_ref[span, width : width + 128] = meta
 
 
 def prep(particles, rows, table, fx, fy, first, held=()):
@@ -143,12 +146,12 @@
     given = len(args)
     return pl.pallas_call(
         functools.partial(prep_kernel, first),
-        grid=(n // 32,),
-        in_specs=[pl.BlockSpec((16, A * 128), block)]
+        grid=(n // 64,),
+        in_specs=[pl.BlockSpec((32, A * 128), block)]
         + [whole(a) for a in args[1:]]
         + [pl.BlockSpec(memory_space=pltpu.HBM)] * len(held),
-        out_specs=[pl.BlockSpec((2, A * 8, 128), lambda i: (i + first, 0, 0))]
-        + [pl.BlockSpec((16, 19 * 128), block)] * 4,
+        out_specs=[pl.BlockSpec((4, A * 8, 128), lambda i: (i + first, 0, 0))]
+        + [pl.BlockSpec((32, 19 * 128), block)] * 4,
         scratch_shapes=[
             pltpu.VMEM((16, A * 128), F32),
             pltpu.VMEM((16, A * 128), F32),
@@ -203,14 +206,16 @@
     )(w, fwd_k)
 
 
-def ref_kernel(b_ref, f_ref, r_ref, s):
-    for y in range(4):
-        for xh in range(2):
-            for t in range(9):
-                v = b_ref[y, xh, :, t * 128 : (t + 1) * 128].astype(F32)
-                row = (y * 2 + xh) * 72 + 8 * t
-                s[row : row + 8, 0:128] = v[0:8]
-                s[row : row + 8, 128:256] = v[8:16]
+def ref_kernel(own_ref, far_ref, f_ref, r_ref, s):
+    upper = lax.rem(lax.axis_index("dom") // 8, 2)
+    for ref, place_of in ((own_ref, upper), (far_ref, 1 - upper)):
+        for y in range(2):
+            for xh in range(2):
+                for t in range(9):
+                    v = ref[y, xh, :, t * 128 : (t + 1) * 128].astype(F32)
+                    row = pl.multiple_of(place_of * 288 + (y * 2 + xh) * 72 + 8 * t, 8)
+                    s[pl.ds(row, 8), 0:128] = v[0:8]
+                    s[pl.ds(row, 8), 128:256] = v[8:16]
     out = jnp.dot(f_ref[...], s[...].astype(BF), preferred_element_type=F32)
     for m in range(M):
         for i in range(2):
@@ -220,18 +225,18 @@
             ).astype(BF)
 
 
-def ref_spectra(blocks, fwd_k):
+def ref_spectra(own, far, fwd_k):
     v = pl.BlockSpec(memory_space=pltpu.VMEM)
     return pl.pallas_call(
         ref_kernel,
-        in_specs=[v, v],
+        in_specs=[v, v, v],
         out_specs=v,
         out_shape=jax.ShapeDtypeStruct((M, 16, 256), BF),
         scratch_shapes=[pltpu.VMEM((A * 8, 256), F32)],
         compiler_params=pltpu.CompilerParams(vmem_limit_bytes=8 * MIB),
         cost_estimate=pl.CostEstimate(flops=1000, bytes_accessed=1000, transcendentals=0),
         name="ref_spectra",
-    )(blocks, fwd_k)
+    )(own, far, fwd_k)
 
 
 def score_kernel(*refs):
@@ -455,15 +460,15 @@
     far, *half = lax.optimization_barrier((far, *half))
     pair = join(block, far, xh)
     pair, rows[1] = lax.optimization_barrier((pair, rows[1]))
-    weighted, *sent = prep(particles, rows, table, fx, fy, 4, half)
+    weighted, *sent = prep(particles, rows, table, fx, fy, 2, half)
     near = move(pair, Y_NEAR)
     near, weighted, *sent = lax.optimization_barrier((near, weighted, *sent))
     quad = join(pair, near, y % 2)
-    octet = join(quad, move(quad, Y_FAR), y // 2).reshape(4, 2, 16, 1152)
+    opposite = move(quad, Y_FAR)
 
     across = move(sent[2], YS[2])
     part = spectra(weighted, fwd_k)
-    own = ref_spectra(octet, fwd_k)
+    own = ref_spectra(quad, opposite, fwd_k)
     up, down = move(own, ZS[1]), move(own, ZS[3])
     side = move(own, LOW)
     side_up, side_down = move(side, ZS[1]), move(side, ZS[3])

time: 85.4 us -> 93.6 us (1.096)
  waiting for transfers between devices: 20.5 us -> 28.7 us
    ppermute x23, waiting for transfers between devices: 20.5 us -> 28.7 us  [move(): return lax.ppermute(value, AXES, pairs)]
  transfers between devices with their start and end apart: 23 -> 23, of which waited for: 10 -> 9; matrix products, arithmetic and copies ran while one was open for 3% -> 3% of each run, Pallas kernels for 30% -> 27%
where the time goes in v10:
time: 93.6 us; the launch traced here: 93.3 us
  starting transfers between devices  31.2 us (33%)
  waiting for transfers between devices  28.7 us (31%)
  Pallas kernels  27.3 us (29%)
  other arithmetic  3.65 us (4%)
  local copies, waits for them, and re-layouts  1.69 us (2%)
    ppermute x23, starting transfers between devices, move(): return lax.ppermute(value, AXES, pairs)  31.2 us
    ppermute x23, waiting for transfers between devices, move(): return lax.ppermute(value, AXES, pairs)  28.7 us
    pallas_call x2, Pallas kernels, prep(): pl.pallas_call(functools.partial(prep_kernel, first), grid=(n // 64,), in...  9.99 us
    pallas_call x1, Pallas kernels, scores_of(): pl.pallas_call(score_kernel, in_specs=[v] * 6, out_specs=v, out_shape=jax...  7.93 us
    pallas_call x1, Pallas kernels, spectra(): pl.pallas_call(spectra_kernel, in_specs=[v, v], out_specs=v, out_shape=ja...  3.4 us
    pallas_call x1, Pallas kernels, class_sums(): pl.pallas_call(sums_kernel, in_specs=[pl.BlockSpec(memory_space=pltpu.SME...  2.82 us
  transfers between devices with their start and end apart: 23, of which 9 were waited for; matrix products, arithmetic and copies ran while one was open for 3% of the time, Pallas kernels for 27%

profile of v10, /device:TPU:0, one launch (start us, length us, event | category | flops | bytes accessed | tf_op | source)
XLA Modules:
  0.0 93.3 jit_solution(1149427760507679488)
XLA Ops:
  0.6 0.8 broadcast_select_fusion.1
  1.6 1.2 %collective-permute-done = bf16[16,576]{1,0:T(8,128)(2,1)S(1)} collective-permute-done((bf16[16,576]{1,0:T(8,128)(2,1)S(1)}, bf16[16,576]{1,0:T(8,128)(2,1)S(1)}, u32[]{:S(2)}, u32[]{:S(2)}) %collective-permute-start) | collective-permute-done | bytes 18464 | tf_op jit(solution)/shard_map/ppermute | solution.py:426
  2.9 3.2 %collective-permute-start.1 = (bf16[16,1152]{1,0:T(8,128)(2,1)S(1)}, bf16[16,1152]{1,0:T(8,128)(2,1)S(1)}, u32[]{:S(2)}, u32[]{:S(2)}) collective-permute-start(bf16[16,1152]{1,0:T(8,128)(2,1)S(1)} %maximum_select_fusion), channel_id=1, source_target_pairs={{0,16},{8,24},{1,17},{9,25},{2,18},{10,26},{3,19},{11,27},{4,20},{... | collective-permute-start | bytes 110600 | tf_op jit(solution)/shard_map/ppermute | solution.py:426
  6.0 5.0 %prep.2 = (bf16[16,576,128]{2,1,0:T(8,128)(2,1)}, bf16[128,2432]{1,0:T(8,128)(2,1)}, bf16[128,2432]{1,0:T(8,128)(2,1)}, bf16[128,2432]{1,0:T(8,128)(2,1)}, bf16[128,2432]{1,0:T(8,128)(2,1)}) custom-call(bf16[128,9216]{1,0:T(8,128)(2,1)} %x_ref.3, s32[2,128]{1,0:T(2,128)} %bitcast.35, s32[1,128]{1,0:T(1,128)} %bitcast.37, s32[1,128]{1,0:T(1,128)} %bitcast.39, ...), custom_call_target="tpu_custom_call" | custom-call | flops 20000000 | bytes 4000000 | tf_op jit(solution)/shard_map/prep/pallas_call | solution.py:147
  11.0 1.7 %collective-permute-start.2 = (bf16[2,16,1152]{2,1,0:T(8,128)(2,1)S(1)}, bf16[2,16,1152]{2,1,0:T(8,128)(2,1)S(1)}, u32[]{:S(2)}, u32[]{:S(2)}) collective-permute-start(bf16[2,16,1152]{2,1,0:T(8,128)(2,1)S(1)} %pad_maximum_fusion.3), channel_id=1, source_target_pairs={{0,32},{8,40},{1,33},{9,41},{2,34},{10,42},{3,35},{11,43},{4,36},{... | collective-permute-start | bytes 221192 | tf_op jit(solution)/shard_map/ppermute | solution.py:426
  12.7 5.0 %prep.3 = (bf16[16,576,128]{2,1,0:T(8,128)(2,1)}, bf16[128,2432]{1,0:T(8,128)(2,1)}, bf16[128,2432]{1,0:T(8,128)(2,1)}, bf16[128,2432]{1,0:T(8,128)(2,1)}, bf16[128,2432]{1,0:T(8,128)(2,1)}) custom-call(bf16[128,9216]{1,0:T(8,128)(2,1)} %x_ref.3, s32[2,128]{1,0:T(2,128)} %bitcast.36, ...), custom_call_target="tpu_custom_call", output_to_operand_aliasing={{0}: (9, {}), {1}: (10, {}), {2}: (11, {}), {3}: (12, {}), ... | custom-call | flops 20000000 | bytes 4000000 | tf_op jit(solution)/shard_map/prep/pallas_call | solution.py:147
  17.7 3.0 %collective-permute-start.3 = (bf16[128,2432]{1,0:T(8,128)(2,1)}, bf16[128,2432]{1,0:T(8,128)(2,1)S(1)}, u32[]{:S(2)}, u32[]{:S(2)}) collective-permute-start(bf16[128,2432]{1,0:T(8,128)(2,1)} %get-tuple-element.72), channel_id=1, source_target_pairs={{0,64},{8,72},{1,65},{9,73},{2,66},{10,74},{3,67},{11,75},{4,68},{... | collective-permute-start | bytes 1867784 | tf_op jit(solution)/shard_map/ppermute | solution.py:426
  20.8 0.7 collective-permute-start.4
  21.5 16.8 %collective-permute-done.4.far_ref = bf16[2,2,16,1152]{3,2,1,0:T(8,128)(2,1)S(1)} collective-permute-done((bf16[2,2,16,1152]{3,2,1,0:T(8,128)(2,1)S(1)}, bf16[2,2,16,1152]{3,2,1,0:T(8,128)(2,1)S(1)}, u32[]{:S(2)}, u32[]{:S(2)}) %collective-permute-start.4) | collective-permute-done | bytes 147488 | tf_op jit(solution)/shard_map/ppermute | solution.py:426
  38.8 2.0 %collective-permute-start.5 = (bf16[37,16,256]{2,1,0:T(8,128)(2,1)S(1)}, bf16[37,16,256]{2,1,0:T(8,128)(2,1)S(1)}, u32[]{:S(2)}, u32[]{:S(2)}) collective-permute-start(bf16[37,16,256]{2,1,0:T(8,128)(2,1)S(1)} %ref_spectra.1), channel_id=1, source_target_pairs={{0,1},{8,9},{1,2},{9,10},{2,3},{10,11},{3,0},{11,8},{4,5},{12,13},... | collective-permute-start | bytes 909320 | tf_op jit(solution)/shard_map/ppermute | solution.py:426
  40.8 2.2 %collective-permute-start.6 = (bf16[37,16,256]{2,1,0:T(8,128)(2,1)S(1)}, bf16[37,16,256]{2,1,0:T(8,128)(2,1)S(1)}, u32[]{:S(2)}, u32[]{:S(2)}) collective-permute-start(bf16[37,16,256]{2,1,0:T(8,128)(2,1)S(1)} %ref_spectra.1), channel_id=1, source_target_pairs={{0,3},{8,11},{1,0},{9,8},{2,1},{10,9},{3,2},{11,10},{4,7},{12,15},... | collective-permute-start | bytes 909320 | tf_op jit(solution)/shard_map/ppermute | solution.py:426
  43.5 1.7 %copy-done = bf16[16,576,128]{2,1,0:T(8,128)(2,1)S(1)} copy-done((bf16[16,576,128]{2,1,0:T(8,128)(2,1)S(1)}, bf16[16,576,128]{2,1,0:T(8,128)(2,1)}, u32[]{:S(2)}) %copy-start) | copy-done | bytes 2359320
  45.2 3.4 %spectra.1.refs_0_ = bf16[37,128,256]{2,1,0:T(8,128)(2,1)S(1)} custom-call(bf16[16,576,128]{2,1,0:T(8,128)(2,1)S(1)} %copy-done, bf16[592,576]{1,0:T(8,128)(2,1)S(1)} %copy-done.1), custom_call_target="tpu_custom_call" | custom-call | flops 1000 | bytes 1000 | tf_op jit(solution)/shard_map/spectra/pallas_call | solution.py:197
  49.5 2.8 %collective-permute-start.8 = (bf16[128,2432]{1,0:T(8,128)(2,1)}, bf16[128,2432]{1,0:T(8,128)(2,1)}, u32[]{:S(2)}, u32[]{:S(2)}) collective-permute-start(bf16[128,2432]{1,0:T(8,128)(2,1)} %get-tuple-element.76), channel_id=1, source_target_pairs={{0,96},{8,104},{1,97},{9,105},{2,98},{10,106},{3,99},{11,107},{4,1... | collective-permute-start | bytes 1867784 | tf_op jit(solution)/shard_map/ppermute | solution.py:426
  52.2 3.0 %collective-permute-start.11 = (bf16[37,16,256]{2,1,0:T(8,128)(2,1)}, bf16[37,16,256]{2,1,0:T(8,128)(2,1)}, u32[]{:S(2)}, u32[]{:S(2)}) collective-permute-start(bf16[37,16,256]{2,1,0:T(8,128)(2,1)} %collective-permute-done.9), channel_id=1, source_target_pairs={{0,3},{8,11},{1,0},{9,8},{2,1},{10,9},{3,2},{11,10},{4,7},{12,15},... | collective-permute-start | bytes 909320 | tf_op jit(solution)/shard_map/ppermute | solution.py:426
  55.5 4.4 %collective-permute-done.11 = bf16[37,16,256]{2,1,0:T(8,128)(2,1)} collective-permute-done((bf16[37,16,256]{2,1,0:T(8,128)(2,1)}, bf16[37,16,256]{2,1,0:T(8,128)(2,1)}, u32[]{:S(2)}, u32[]{:S(2)}) %collective-permute-start.11) | collective-permute-done | bytes 303136 | tf_op jit(solution)/shard_map/ppermute | solution.py:426
  59.9 3.7 %collective-permute-start.18 = (bf16[37,16,256]{2,1,0:T(8,128)(2,1)}, bf16[37,16,256]{2,1,0:T(8,128)(2,1)S(1)}, u32[]{:S(2)}, u32[]{:S(2)}) collective-permute-start(bf16[37,16,256]{2,1,0:T(8,128)(2,1)} %collective-permute-done.11), channel_id=1, source_target_pairs={{0,3},{8,11},{1,0},{9,8},{2,1},{10,9},{3,2},{11,10},{4,7},{12,15},... | collective-permute-start | bytes 909320 | tf_op jit(solution)/shard_map/ppermute | solution.py:426
  63.6 1.4 %pad_maximum_fusion.refs_1_ = bf16[4,37,16,256]{3,2,1,0:T(8,128)(2,1)S(1)} fusion(bf16[1,37,16,256]{3,2,1,0:T(8,128)(2,1)} %bitcast.32, bf16[1,37,16,256]{3,2,1,0:T(8,128)(2,1)} %bitcast.31, bf16[1,37,16,256]{3,2,1,0:T(8,128)(2,1)} %bitcast.15, bf16[1,37,16,256]{3,2,1,0:T(8,128)(2,1)S(1)} %bitcast.27), kind=kLoop, calls=%fused_computation | loop fusion | flops 1818624 | bytes 2424832 | tf_op jit(solution)/shard_map/stack | solution.py:478
  65.0 1.0 %collective-permute-done.10 = bf16[37,16,256]{2,1,0:T(8,128)(2,1)} collective-permute-done((bf16[37,16,256]{2,1,0:T(8,128)(2,1)}, bf16[37,16,256]{2,1,0:T(8,128)(2,1)}, u32[]{:S(2)}, u32[]{:S(2)}) %collective-permute-start.10) | collective-permute-done | bytes 303136 | tf_op jit(solution)/shard_map/ppermute | solution.py:426
  66.0 2.8 %class_sums.1 = (f32[2,256,640]{2,1,0:T(8,128)S(1)}, f32[2,256,640]{2,1,0:T(8,128)S(1)}) custom-call(s32[4]{0:T(128)S(1)} %pad_add_fusion.sc, bf16[128,2432]{1,0:T(8,128)(2,1)S(1)} %copy-done.2, bf16[128,2432]{1,0:T(8,128)(2,1)} %collective-permute-done.7.c1, bf16[128,2432]{1,0:T(8,128)(2,1)S(1)} %collective-permute-done.3.c2, ...), custom_call_target="tpu_custom_call" | custom-call | flops 700000000 | bytes 5000000 | tf_op jit(solution)/shard_map/class_sums/pallas_call | solution.py:319
  69.5 1.2 %pad_maximum_fusion.1.refs_3_ = bf16[4,37,16,256]{3,2,1,0:T(8,128)(2,1)S(1)} fusion(bf16[1,37,16,256]{3,2,1,0:T(8,128)(2,1)S(1)} %bitcast.34, bf16[1,37,16,256]{3,2,1,0:T(8,128)(2,1)S(1)} %bitcast.33, bf16[1,37,16,256]{3,2,1,0:T(8,128)(2,1)} %bitcast.19, bf16[1,37,16,256]{3,2,1,0:T(8,128)(2,1)} %bitcast.18), kind=kLoop, calls=%fused_computation.1 | loop fusion | flops 1818624 | bytes 2424832 | tf_op jit(solution)/shard_map/stack | solution.py:483
  70.8 1.3 %collective-permute-done.12.b_ref = f32[2,256,640]{2,1,0:T(8,128)S(1)} collective-permute-done((f32[2,256,640]{2,1,0:T(8,128)S(1)}, f32[2,256,640]{2,1,0:T(8,128)S(1)}, u32[]{:S(2)}, u32[]{:S(2)}) %collective-permute-start.12) | collective-permute-done | bytes 1310752 | tf_op jit(solution)/shard_map/ppermute | solution.py:426
  72.1 0.7 cut_x.1
  72.8 0.7 collective-permute-start.13
  73.5 2.0 %collective-permute-start.14 = (bf16[128,640]{1,0:T(8,128)(2,1)S(1)}, bf16[128,640]{1,0:T(8,128)(2,1)S(1)}, u32[]{:S(2)}, u32[]{:S(2)}) collective-permute-start(bf16[128,640]{1,0:T(8,128)(2,1)S(1)} %get-tuple-element.85), channel_id=1, source_target_pairs={{0,16},{8,24},{1,17},{9,25},{2,18},{10,26},{3,19},{11,27},{4,20},{... | collective-permute-start | bytes 491528 | tf_op jit(solution)/shard_map/ppermute | solution.py:426
  75.5 0.9 collective-permute-start.15
  76.4 7.9 %scores.1 = f32[1,128]{1,0:T(1,128)} custom-call(bf16[37,128,256]{2,1,0:T(8,128)(2,1)S(1)} %spectra.1.refs_0_, bf16[4,37,16,256]{3,2,1,0:T(8,128)(2,1)S(1)} %pad_maximum_fusion.refs_1_, bf16[4,37,16,256]{3,2,1,0:T(8,128)(2,1)S(1)} %collective-permute-done.16.refs_2_, bf16[4,37,16,256]{3,2,1,0:T(8,128)(2,1)S(1)} %pad_maximum_fusion.1.refs_3_, ...), custom_call_target="tpu_custom_call" | custom-call | flops 6000000000 | bytes 8000000 | tf_op jit(solution)/shard_map/scores/pallas_call | solution.py:276
  85.4 2.6 %collective-permute-start.21 = (bf16[32,640]{1,0:T(8,128)(2,1)S(1)}, bf16[32,640]{1,0:T(8,128)(2,1)S(1)}, u32[]{:S(2)}, u32[]{:S(2)}) collective-permute-start(bf16[32,640]{1,0:T(8,128)(2,1)S(1)} %get-tuple-element.94), channel_id=1, source_target_pairs={{0,2},{8,10},{1,3},{9,11},{2,0},{10,8},{3,1},{11,9},{4,6},{12,14},... | collective-permute-start | bytes 122888 | tf_op jit(solution)/shard_map/ppermute | solution.py:426
  88.0 0.7 collective-permute-start.22
  88.6 2.4 %collective-permute-done.20.a1 = bf16[32,640]{1,0:T(8,128)(2,1)S(1)} collective-permute-done((bf16[32,640]{1,0:T(8,128)(2,1)S(1)}, bf16[32,640]{1,0:T(8,128)(2,1)S(1)}, u32[]{:S(2)}, u32[]{:S(2)}) %collective-permute-start.20) | collective-permute-done | bytes 40992 | tf_op jit(solution)/shard_map/ppermute | solution.py:426
  91.0 0.9 collective-permute-done.22.a3
  92.0 1.4 %final.1 = f32[25,576]{1,0:T(8,128)} custom-call(s32[4]{0:T(128)S(1)} %pad_add_fusion.sc, f32[32,640]{1,0:T(8,128)S(1)} %get-tuple-element.92.a0, bf16[32,640]{1,0:T(8,128)(2,1)S(1)} %collective-permute-done.20.a1, bf16[32,640]{1,0:T(8,128)(2,1)S(1)} %collective-permute-done.21.a2, bf16[32,640]{1,0:T(8,128)(2,1)S(1)} %collective-permute-done.22.a3), custom_call_target="tpu_custom_call" | custom-call | tf_op jit(solution)/shard_map/final/pallas_call | solution.py:391
  (46 shorter events, 4.3 us)
Async XLA Ops:
  1.5 1.3 %collective-permute-start = (bf16[16,576]{1,0:T(8,128)(2,1)S(1)}, bf16[16,576]{1,0:T(8,128)(2,1)S(1)}, u32[]{:S(2)}, u32[]{:S(2)}) collective-permute-start(bf16[16,576]{1,0:T(8,128)(2,1)S(1)} %get-tuple-element.101), channel_id=1, source_target_pairs={{0,8},{8,0},{1,9},{9,1},{2,10},{10,2},{3,11},{11,3},{4,12},{12,4},... | collective-permute-start | bytes 55304 | tf_op jit(solution)/shard_map/ppermute | solution.py:426
  2.9 8.2 %collective-permute-start.1 = (bf16[16,1152]{1,0:T(8,128)(2,1)S(1)}, bf16[16,1152]{1,0:T(8,128)(2,1)S(1)}, u32[]{:S(2)}, u32[]{:S(2)}) collective-permute-start(bf16[16,1152]{1,0:T(8,128)(2,1)S(1)} %maximum_select_fusion), channel_id=1, source_target_pairs={{0,16},{8,24},{1,17},{9,25},{2,18},{10,26},{3,19},{11,27},{4,20},{... | collective-permute-start | bytes 110600 | tf_op jit(solution)/shard_map/ppermute | solution.py:426
  11.0 6.7 %collective-permute-start.2 = (bf16[2,16,1152]{2,1,0:T(8,128)(2,1)S(1)}, bf16[2,16,1152]{2,1,0:T(8,128)(2,1)S(1)}, u32[]{:S(2)}, u32[]{:S(2)}) collective-permute-start(bf16[2,16,1152]{2,1,0:T(8,128)(2,1)S(1)} %pad_maximum_fusion.3), channel_id=1, source_target_pairs={{0,32},{8,40},{1,33},{9,41},{2,34},{10,42},{3,35},{11,43},{4,36},{... | collective-permute-start | bytes 221192 | tf_op jit(solution)/shard_map/ppermute | solution.py:426
  12.7 25.5 %copy-start.1 = (bf16[592,576]{1,0:T(8,128)(2,1)S(1)}, bf16[592,576]{1,0:T(8,128)(2,1)}, u32[]{:S(2)}) copy-start(bf16[592,576]{1,0:T(8,128)(2,1)} %constant.75.clone.f_ref) | copy-start | bytes 2045956
  17.7 31.2 %collective-permute-start.3 = (bf16[128,2432]{1,0:T(8,128)(2,1)}, bf16[128,2432]{1,0:T(8,128)(2,1)S(1)}, u32[]{:S(2)}, u32[]{:S(2)}) collective-permute-start(bf16[128,2432]{1,0:T(8,128)(2,1)} %get-tuple-element.72), channel_id=1, source_target_pairs={{0,64},{8,72},{1,65},{9,73},{2,66},{10,74},{3,67},{11,75},{4,68},{... | collective-permute-start | bytes 1867784 | tf_op jit(solution)/shard_map/ppermute | solution.py:426
  20.8 17.5 %collective-permute-start.4 = (bf16[2,2,16,1152]{3,2,1,0:T(8,128)(2,1)S(1)}, bf16[2,2,16,1152]{3,2,1,0:T(8,128)(2,1)S(1)}, u32[]{:S(2)}, u32[]{:S(2)}) collective-permute-start(bf16[2,2,16,1152]{3,2,1,0:T(8,128)(2,1)S(1)} %pad_maximum_fusion.2.own_ref), channel_id=1, source_target_pairs={{0,64},{8,72},{1,65},{9,73},{2,66},{10,74},{3,67},{11,75},{4,68},{... | collective-permute-start | bytes 442376 | tf_op jit(solution)/shard_map/ppermute | solution.py:426
  38.8 10.2 %collective-permute-start.5 = (bf16[37,16,256]{2,1,0:T(8,128)(2,1)S(1)}, bf16[37,16,256]{2,1,0:T(8,128)(2,1)S(1)}, u32[]{:S(2)}, u32[]{:S(2)}) collective-permute-start(bf16[37,16,256]{2,1,0:T(8,128)(2,1)S(1)} %ref_spectra.1), channel_id=1, source_target_pairs={{0,1},{8,9},{1,2},{9,10},{2,3},{10,11},{3,0},{11,8},{4,5},{12,13},... | collective-permute-start | bytes 909320 | tf_op jit(solution)/shard_map/ppermute | solution.py:426
  40.8 8.2 %collective-permute-start.6 = (bf16[37,16,256]{2,1,0:T(8,128)(2,1)S(1)}, bf16[37,16,256]{2,1,0:T(8,128)(2,1)S(1)}, u32[]{:S(2)}, u32[]{:S(2)}) collective-permute-start(bf16[37,16,256]{2,1,0:T(8,128)(2,1)S(1)} %ref_spectra.1), channel_id=1, source_target_pairs={{0,3},{8,11},{1,0},{9,8},{2,1},{10,9},{3,2},{11,10},{4,7},{12,15},... | collective-permute-start | bytes 909320 | tf_op jit(solution)/shard_map/ppermute | solution.py:426
  43.0 9.3 %collective-permute-start.9 = (bf16[37,16,256]{2,1,0:T(8,128)(2,1)S(1)}, bf16[37,16,256]{2,1,0:T(8,128)(2,1)}, u32[]{:S(2)}, u32[]{:S(2)}) collective-permute-start(bf16[37,16,256]{2,1,0:T(8,128)(2,1)S(1)} %ref_spectra.1), channel_id=1, source_target_pairs={{0,4},{8,12},{1,5},{9,13},{2,6},{10,14},{3,7},{11,15},{4,0},{12,8}... | collective-permute-start | bytes 909320 | tf_op jit(solution)/shard_map/ppermute | solution.py:426
  43.5 1.7 %copy-start = (bf16[16,576,128]{2,1,0:T(8,128)(2,1)S(1)}, bf16[16,576,128]{2,1,0:T(8,128)(2,1)}, u32[]{:S(2)}) copy-start(bf16[16,576,128]{2,1,0:T(8,128)(2,1)} %get-tuple-element.73.w_ref) | copy-start | bytes 7077892
  48.9 3.3 %copy-start.5 = (bf16[37,16,256]{2,1,0:T(8,128)(2,1)}, bf16[37,16,256]{2,1,0:T(8,128)(2,1)S(1)}, u32[]{:S(2)}) copy-start(bf16[37,16,256]{2,1,0:T(8,128)(2,1)S(1)} %collective-permute-done.5) | copy-start | bytes 909316
  48.9 6.3 %copy-start.6 = (bf16[37,16,256]{2,1,0:T(8,128)(2,1)}, bf16[37,16,256]{2,1,0:T(8,128)(2,1)S(1)}, u32[]{:S(2)}) copy-start(bf16[37,16,256]{2,1,0:T(8,128)(2,1)S(1)} %collective-permute-done.6) | copy-start | bytes 909316
  48.9 17.1 %collective-permute-start.7 = (bf16[128,2432]{1,0:T(8,128)(2,1)}, bf16[128,2432]{1,0:T(8,128)(2,1)}, u32[]{:S(2)}, u32[]{:S(2)}) collective-permute-start(bf16[128,2432]{1,0:T(8,128)(2,1)} %get-tuple-element.75), channel_id=1, source_target_pairs={{0,32},{8,40},{1,33},{9,41},{2,34},{10,42},{3,35},{11,43},{4,36},{... | collective-permute-start | bytes 1867784 | tf_op jit(solution)/shard_map/ppermute | solution.py:426
  49.5 16.6 %collective-permute-start.8 = (bf16[128,2432]{1,0:T(8,128)(2,1)}, bf16[128,2432]{1,0:T(8,128)(2,1)}, u32[]{:S(2)}, u32[]{:S(2)}) collective-permute-start(bf16[128,2432]{1,0:T(8,128)(2,1)} %get-tuple-element.76), channel_id=1, source_target_pairs={{0,96},{8,104},{1,97},{9,105},{2,98},{10,106},{3,99},{11,107},{4,1... | collective-permute-start | bytes 1867784 | tf_op jit(solution)/shard_map/ppermute | solution.py:426
  52.2 7.6 %collective-permute-start.11 = (bf16[37,16,256]{2,1,0:T(8,128)(2,1)}, bf16[37,16,256]{2,1,0:T(8,128)(2,1)}, u32[]{:S(2)}, u32[]{:S(2)}) collective-permute-start(bf16[37,16,256]{2,1,0:T(8,128)(2,1)} %collective-permute-done.9), channel_id=1, source_target_pairs={{0,3},{8,11},{1,0},{9,8},{2,1},{10,9},{3,2},{11,10},{4,7},{12,15},... | collective-permute-start | bytes 909320 | tf_op jit(solution)/shard_map/ppermute | solution.py:426
  55.2 10.8 %collective-permute-start.10 = (bf16[37,16,256]{2,1,0:T(8,128)(2,1)}, bf16[37,16,256]{2,1,0:T(8,128)(2,1)}, u32[]{:S(2)}, u32[]{:S(2)}) collective-permute-start(bf16[37,16,256]{2,1,0:T(8,128)(2,1)} %collective-permute-done.9), channel_id=1, source_target_pairs={{0,1},{8,9},{1,2},{9,10},{2,3},{10,11},{3,0},{11,8},{4,5},{12,13},... | collective-permute-start | bytes 909320 | tf_op jit(solution)/shard_map/ppermute | solution.py:426
  55.2 14.2 %collective-permute-start.17 = (bf16[37,16,256]{2,1,0:T(8,128)(2,1)}, bf16[37,16,256]{2,1,0:T(8,128)(2,1)S(1)}, u32[]{:S(2)}, u32[]{:S(2)}) collective-permute-start(bf16[37,16,256]{2,1,0:T(8,128)(2,1)} %copy-done.5), channel_id=1, source_target_pairs={{0,1},{8,9},{1,2},{9,10},{2,3},{10,11},{3,0},{11,8},{4,5},{12,13},... | collective-permute-start | bytes 909320 | tf_op jit(solution)/shard_map/ppermute | solution.py:426
  59.9 9.6 %collective-permute-start.18 = (bf16[37,16,256]{2,1,0:T(8,128)(2,1)}, bf16[37,16,256]{2,1,0:T(8,128)(2,1)S(1)}, u32[]{:S(2)}, u32[]{:S(2)}) collective-permute-start(bf16[37,16,256]{2,1,0:T(8,128)(2,1)} %collective-permute-done.11), channel_id=1, source_target_pairs={{0,3},{8,11},{1,0},{9,8},{2,1},{10,9},{3,2},{11,10},{4,7},{12,15},... | collective-permute-start | bytes 909320 | tf_op jit(solution)/shard_map/ppermute | solution.py:426
  63.6 2.4 %copy-start.2 = (bf16[128,2432]{1,0:T(8,128)(2,1)S(1)}, bf16[128,2432]{1,0:T(8,128)(2,1)}, u32[]{:S(2)}) copy-start(bf16[128,2432]{1,0:T(8,128)(2,1)} %get-tuple-element.77.c0) | copy-start | bytes 1867780
  63.6 2.4 %copy-start.3 = (f32[256,64]{0,1:T(8,128)S(1)}, f32[256,64]{0,1:T(8,128)}, u32[]{:S(2)}) copy-start(f32[256,64]{0,1:T(8,128)} %param.19) | copy-start | bytes 196612
  66.0 10.4 %collective-permute-start.16 = (bf16[4,37,16,256]{3,2,1,0:T(8,128)(2,1)S(1)}, bf16[4,37,16,256]{3,2,1,0:T(8,128)(2,1)S(1)}, u32[]{:S(2)}, u32[]{:S(2)}) collective-permute-start(bf16[4,37,16,256]{3,2,1,0:T(8,128)(2,1)S(1)} %pad_maximum_fusion.refs_1_), channel_id=1, source_target_pairs={{0,8},{8,0},{1,9},{9,1},{2,10},{10,2},{3,11},{11,3},{4,12},{12,4},... | collective-permute-start | bytes 3637256 | tf_op jit(solution)/shard_map/ppermute | solution.py:426
  68.9 3.2 %collective-permute-start.12 = (f32[2,256,640]{2,1,0:T(8,128)S(1)}, f32[2,256,640]{2,1,0:T(8,128)S(1)}, u32[]{:S(2)}, u32[]{:S(2)}) collective-permute-start(f32[2,256,640]{2,1,0:T(8,128)S(1)} %get-tuple-element.82), channel_id=1, source_target_pairs={{0,8},{8,0},{1,9},{9,1},{2,10},{10,2},{3,11},{11,3},{4,12},{12,4},... | collective-permute-start | bytes 3932168 | tf_op jit(solution)/shard_map/ppermute | solution.py:426
  70.7 5.8 %collective-permute-start.19 = (bf16[4,37,16,256]{3,2,1,0:T(8,128)(2,1)S(1)}, bf16[4,37,16,256]{3,2,1,0:T(8,128)(2,1)S(1)}, u32[]{:S(2)}, u32[]{:S(2)}) collective-permute-start(bf16[4,37,16,256]{3,2,1,0:T(8,128)(2,1)S(1)} %pad_maximum_fusion.1.refs_3_), channel_id=1, source_target_pairs={{0,8},{8,0},{1,9},{9,1},{2,10},{10,2},{3,11},{11,3},{4,12},{12,4},... | collective-permute-start | bytes 3637256 | tf_op jit(solution)/shard_map/ppermute | solution.py:426
  72.1 4.3 %copy-start.4 = (bf16[576,640]{1,0:T(8,128)(2,1)S(1)}, bf16[576,640]{1,0:T(8,128)(2,1)}, u32[]{:S(2)}) copy-start(bf16[576,640]{1,0:T(8,128)(2,1)} %constant.76.clone.refs_5_) | copy-start | bytes 2211844
  72.8 11.6 %collective-permute-start.13 = (bf16[128,640]{1,0:T(8,128)(2,1)S(1)}, bf16[128,640]{1,0:T(8,128)(2,1)S(1)}, u32[]{:S(2)}, u32[]{:S(2)}) collective-permute-start(bf16[128,640]{1,0:T(8,128)(2,1)S(1)} %get-tuple-element.84), channel_id=1, source_target_pairs={{0,4},{8,12},{1,5},{9,13},{2,6},{10,14},{3,7},{11,15},{4,16},{12,2... | collective-permute-start | bytes 491528 | tf_op jit(solution)/shard_map/ppermute | solution.py:426
  73.5 10.9 %collective-permute-start.14 = (bf16[128,640]{1,0:T(8,128)(2,1)S(1)}, bf16[128,640]{1,0:T(8,128)(2,1)S(1)}, u32[]{:S(2)}, u32[]{:S(2)}) collective-permute-start(bf16[128,640]{1,0:T(8,128)(2,1)S(1)} %get-tuple-element.85), channel_id=1, source_target_pairs={{0,16},{8,24},{1,17},{9,25},{2,18},{10,26},{3,19},{11,27},{4,20},{... | collective-permute-start | bytes 491528 | tf_op jit(solution)/shard_map/ppermute | solution.py:426
  75.5 9.2 %collective-permute-start.15 = (bf16[128,640]{1,0:T(8,128)(2,1)S(1)}, bf16[128,640]{1,0:T(8,128)(2,1)S(1)}, u32[]{:S(2)}, u32[]{:S(2)}) collective-permute-start(bf16[128,640]{1,0:T(8,128)(2,1)S(1)} %get-tuple-element.86), channel_id=1, source_target_pairs={{0,20},{8,28},{1,21},{9,29},{2,22},{10,30},{3,23},{11,31},{4,0},{1... | collective-permute-start | bytes 491528 | tf_op jit(solution)/shard_map/ppermute | solution.py:426
  85.3 5.7 %collective-permute-start.20 = (bf16[32,640]{1,0:T(8,128)(2,1)S(1)}, bf16[32,640]{1,0:T(8,128)(2,1)S(1)}, u32[]{:S(2)}, u32[]{:S(2)}) collective-permute-start(bf16[32,640]{1,0:T(8,128)(2,1)S(1)} %get-tuple-element.93), channel_id=1, source_target_pairs={{0,1},{8,9},{1,2},{9,10},{2,3},{10,11},{3,0},{11,8},{4,5},{12,13},... | collective-permute-start | bytes 122888 | tf_op jit(solution)/shard_map/ppermute | solution.py:426
  85.4 5.6 %collective-permute-start.21 = (bf16[32,640]{1,0:T(8,128)(2,1)S(1)}, bf16[32,640]{1,0:T(8,128)(2,1)S(1)}, u32[]{:S(2)}, u32[]{:S(2)}) collective-permute-start(bf16[32,640]{1,0:T(8,128)(2,1)S(1)} %get-tuple-element.94), channel_id=1, source_target_pairs={{0,2},{8,10},{1,3},{9,11},{2,0},{10,8},{3,1},{11,9},{4,6},{12,14},... | collective-permute-start | bytes 122888 | tf_op jit(solution)/shard_map/ppermute | solution.py:426
  88.0 4.0 %collective-permute-start.22 = (bf16[32,640]{1,0:T(8,128)(2,1)S(1)}, bf16[32,640]{1,0:T(8,128)(2,1)S(1)}, u32[]{:S(2)}, u32[]{:S(2)}) collective-permute-start(bf16[32,640]{1,0:T(8,128)(2,1)S(1)} %get-tuple-element.95), channel_id=1, source_target_pairs={{0,3},{8,11},{1,0},{9,8},{2,1},{10,9},{3,2},{11,10},{4,7},{12,15},... | collective-permute-start | bytes 122888 | tf_op jit(solution)/shard_map/ppermute | solution.py:426

commit v11 on v10

--- a/solution.py
+++ b/solution.py
@@ -472,7 +472,7 @@
     up, down = move(own, ZS[1]), move(own, ZS[3])
     side = move(own, LOW)
     side_up, side_down = move(side, ZS[1]), move(side, ZS[3])
-    one, three = after([sent[1], sent[3]], across, part, up, down)
+    one, three = after([sent[1], sent[3]], part, up, down)
     held = [sent[0], move(one, YS[1]), across, move(three, YS[3])]
     on_up, on_down = move(up, ZS[1]), move(side_down, ZS[3])
     early = jnp.stack([own, side, up, down])

time: 93.6 us -> 86.8 us (0.927)
  waiting for transfers between devices: 28.7 us -> 21 us
    ppermute x23, waiting for transfers between devices: 28.7 us -> 21 us  [move(): return lax.ppermute(value, AXES, pairs)]
  transfers between devices with their start and end apart: 23 -> 23, of which waited for: 9 -> 10; matrix products, arithmetic and copies ran while one was open for 3% -> 3% of each run, Pallas kernels for 27% -> 29%
where the time goes in v11:
time: 86.8 us; the launch traced here: 86.4 us
  starting transfers between devices  32 us (37%)
  Pallas kernels  27.3 us (31%)
  waiting for transfers between devices  21 us (24%)
  other arithmetic  3.65 us (4%)
  local copies, waits for them, and re-layouts  1.69 us (2%)
    ppermute x23, starting transfers between devices, move(): return lax.ppermute(value, AXES, pairs)  32 us
    ppermute x23, waiting for transfers between devices, move(): return lax.ppermute(value, AXES, pairs)  21 us
    pallas_call x2, Pallas kernels, prep(): pl.pallas_call(functools.partial(prep_kernel, first), grid=(n // 64,), in...  9.99 us
    pallas_call x1, Pallas kernels, scores_of(): pl.pallas_call(score_kernel, in_specs=[v] * 6, out_specs=v, out_shape=jax...  7.93 us
    pallas_call x1, Pallas kernels, spectra(): pl.pallas_call(spectra_kernel, in_specs=[v, v], out_specs=v, out_shape=ja...  3.4 us
    pallas_call x1, Pallas kernels, class_sums(): pl.pallas_call(sums_kernel, in_specs=[pl.BlockSpec(memory_space=pltpu.SME...  2.82 us
  transfers between devices with their start and end apart: 23, of which 10 were waited for; matrix products, arithmetic and copies ran while one was open for 3% of the time, Pallas kernels for 29%

profile of v11, /device:TPU:0, one launch (start us, length us, event | category | flops | bytes accessed | tf_op | source)
XLA Modules:
  0.0 86.4 jit_solution(10834559210334252109)
XLA Ops:
  0.6 0.8 broadcast_select_fusion.1
  1.6 1.2 %collective-permute-done = bf16[16,576]{1,0:T(8,128)(2,1)S(1)} collective-permute-done((bf16[16,576]{1,0:T(8,128)(2,1)S(1)}, bf16[16,576]{1,0:T(8,128)(2,1)S(1)}, u32[]{:S(2)}, u32[]{:S(2)}) %collective-permute-start) | collective-permute-done | bytes 18464 | tf_op jit(solution)/shard_map/ppermute | solution.py:426
  2.9 3.2 %collective-permute-start.1 = (bf16[16,1152]{1,0:T(8,128)(2,1)S(1)}, bf16[16,1152]{1,0:T(8,128)(2,1)S(1)}, u32[]{:S(2)}, u32[]{:S(2)}) collective-permute-start(bf16[16,1152]{1,0:T(8,128)(2,1)S(1)} %maximum_select_fusion), channel_id=1, source_target_pairs={{0,16},{8,24},{1,17},{9,25},{2,18},{10,26},{3,19},{11,27},{4,20},{... | collective-permute-start | bytes 110600 | tf_op jit(solution)/shard_map/ppermute | solution.py:426
  6.0 5.0 %prep.2 = (bf16[16,576,128]{2,1,0:T(8,128)(2,1)}, bf16[128,2432]{1,0:T(8,128)(2,1)}, bf16[128,2432]{1,0:T(8,128)(2,1)}, bf16[128,2432]{1,0:T(8,128)(2,1)}, bf16[128,2432]{1,0:T(8,128)(2,1)}) custom-call(bf16[128,9216]{1,0:T(8,128)(2,1)} %x_ref.3, s32[2,128]{1,0:T(2,128)} %bitcast.35, s32[1,128]{1,0:T(1,128)} %bitcast.37, s32[1,128]{1,0:T(1,128)} %bitcast.39, ...), custom_call_target="tpu_custom_call" | custom-call | flops 20000000 | bytes 4000000 | tf_op jit(solution)/shard_map/prep/pallas_call | solution.py:147
  11.0 1.7 %collective-permute-start.2 = (bf16[2,16,1152]{2,1,0:T(8,128)(2,1)S(1)}, bf16[2,16,1152]{2,1,0:T(8,128)(2,1)S(1)}, u32[]{:S(2)}, u32[]{:S(2)}) collective-permute-start(bf16[2,16,1152]{2,1,0:T(8,128)(2,1)S(1)} %pad_maximum_fusion.3), channel_id=1, source_target_pairs={{0,32},{8,40},{1,33},{9,41},{2,34},{10,42},{3,35},{11,43},{4,36},{... | collective-permute-start | bytes 221192 | tf_op jit(solution)/shard_map/ppermute | solution.py:426
  12.7 5.0 %prep.3 = (bf16[16,576,128]{2,1,0:T(8,128)(2,1)}, bf16[128,2432]{1,0:T(8,128)(2,1)}, bf16[128,2432]{1,0:T(8,128)(2,1)}, bf16[128,2432]{1,0:T(8,128)(2,1)}, bf16[128,2432]{1,0:T(8,128)(2,1)}) custom-call(bf16[128,9216]{1,0:T(8,128)(2,1)} %x_ref.3, s32[2,128]{1,0:T(2,128)} %bitcast.36, ...), custom_call_target="tpu_custom_call", output_to_operand_aliasing={{0}: (9, {}), {1}: (10, {}), {2}: (11, {}), {3}: (12, {}), ... | custom-call | flops 20000000 | bytes 4000000 | tf_op jit(solution)/shard_map/prep/pallas_call | solution.py:147
  17.8 3.0 %collective-permute-start.3 = (bf16[2,2,16,1152]{3,2,1,0:T(8,128)(2,1)S(1)}, bf16[2,2,16,1152]{3,2,1,0:T(8,128)(2,1)S(1)}, u32[]{:S(2)}, u32[]{:S(2)}) collective-permute-start(bf16[2,2,16,1152]{3,2,1,0:T(8,128)(2,1)S(1)} %pad_maximum_fusion.2.own_ref), channel_id=1, source_target_pairs={{0,64},{8,72},{1,65},{9,73},{2,66},{10,74},{3,67},{11,75},{4,68},{... | collective-permute-start | bytes 442376 | tf_op jit(solution)/shard_map/ppermute | solution.py:426
  20.8 4.0 %collective-permute-done.3.far_ref = bf16[2,2,16,1152]{3,2,1,0:T(8,128)(2,1)S(1)} collective-permute-done((bf16[2,2,16,1152]{3,2,1,0:T(8,128)(2,1)S(1)}, bf16[2,2,16,1152]{3,2,1,0:T(8,128)(2,1)S(1)}, u32[]{:S(2)}, u32[]{:S(2)}) %collective-permute-start.3) | collective-permute-done | bytes 147488 | tf_op jit(solution)/shard_map/ppermute | solution.py:426
  25.3 2.0 %collective-permute-start.4 = (bf16[37,16,256]{2,1,0:T(8,128)(2,1)S(1)}, bf16[37,16,256]{2,1,0:T(8,128)(2,1)S(1)}, u32[]{:S(2)}, u32[]{:S(2)}) collective-permute-start(bf16[37,16,256]{2,1,0:T(8,128)(2,1)S(1)} %ref_spectra.1), channel_id=1, source_target_pairs={{0,1},{8,9},{1,2},{9,10},{2,3},{10,11},{3,0},{11,8},{4,5},{12,13},... | collective-permute-start | bytes 909320 | tf_op jit(solution)/shard_map/ppermute | solution.py:426
  27.3 2.2 %collective-permute-start.5 = (bf16[37,16,256]{2,1,0:T(8,128)(2,1)S(1)}, bf16[37,16,256]{2,1,0:T(8,128)(2,1)S(1)}, u32[]{:S(2)}, u32[]{:S(2)}) collective-permute-start(bf16[37,16,256]{2,1,0:T(8,128)(2,1)S(1)} %ref_spectra.1), channel_id=1, source_target_pairs={{0,3},{8,11},{1,0},{9,8},{2,1},{10,9},{3,2},{11,10},{4,7},{12,15},... | collective-permute-start | bytes 909320 | tf_op jit(solution)/shard_map/ppermute | solution.py:426
  29.5 2.9 %collective-permute-start.7 = (bf16[128,2432]{1,0:T(8,128)(2,1)}, bf16[128,2432]{1,0:T(8,128)(2,1)S(1)}, u32[]{:S(2)}, u32[]{:S(2)}) collective-permute-start(bf16[128,2432]{1,0:T(8,128)(2,1)} %get-tuple-element.75), channel_id=1, source_target_pairs={{0,64},{8,72},{1,65},{9,73},{2,66},{10,74},{3,67},{11,75},{4,68},{... | collective-permute-start | bytes 1867784 | tf_op jit(solution)/shard_map/ppermute | solution.py:426
  33.0 1.7 %copy-done = bf16[16,576,128]{2,1,0:T(8,128)(2,1)S(1)} copy-done((bf16[16,576,128]{2,1,0:T(8,128)(2,1)S(1)}, bf16[16,576,128]{2,1,0:T(8,128)(2,1)}, u32[]{:S(2)}) %copy-start) | copy-done | bytes 2359320
  34.6 3.4 %spectra.1.refs_0_ = bf16[37,128,256]{2,1,0:T(8,128)(2,1)S(1)} custom-call(bf16[16,576,128]{2,1,0:T(8,128)(2,1)S(1)} %copy-done, bf16[592,576]{1,0:T(8,128)(2,1)S(1)} %copy-done.1), custom_call_target="tpu_custom_call" | custom-call | flops 1000 | bytes 1000 | tf_op jit(solution)/shard_map/spectra/pallas_call | solution.py:197
  38.3 3.1 %collective-permute-start.8 = (bf16[128,2432]{1,0:T(8,128)(2,1)}, bf16[128,2432]{1,0:T(8,128)(2,1)}, u32[]{:S(2)}, u32[]{:S(2)}) collective-permute-start(bf16[128,2432]{1,0:T(8,128)(2,1)} %get-tuple-element.76), channel_id=1, source_target_pairs={{0,96},{8,104},{1,97},{9,105},{2,98},{10,106},{3,99},{11,107},{4,1... | collective-permute-start | bytes 1867784 | tf_op jit(solution)/shard_map/ppermute | solution.py:426
  41.4 2.0 %collective-permute-start.11 = (bf16[37,16,256]{2,1,0:T(8,128)(2,1)}, bf16[37,16,256]{2,1,0:T(8,128)(2,1)}, u32[]{:S(2)}, u32[]{:S(2)}) collective-permute-start(bf16[37,16,256]{2,1,0:T(8,128)(2,1)} %collective-permute-done.9), channel_id=1, source_target_pairs={{0,3},{8,11},{1,0},{9,8},{2,1},{10,9},{3,2},{11,10},{4,7},{12,15},... | collective-permute-start | bytes 909320 | tf_op jit(solution)/shard_map/ppermute | solution.py:426
  43.4 4.8 %collective-permute-done.7.c2 = bf16[128,2432]{1,0:T(8,128)(2,1)S(1)} collective-permute-done((bf16[128,2432]{1,0:T(8,128)(2,1)}, bf16[128,2432]{1,0:T(8,128)(2,1)S(1)}, u32[]{:S(2)}, u32[]{:S(2)}) %collective-permute-start.7) | collective-permute-done | bytes 622624 | tf_op jit(solution)/shard_map/ppermute | solution.py:426
  48.2 0.9 %collective-permute-done.11 = bf16[37,16,256]{2,1,0:T(8,128)(2,1)} collective-permute-done((bf16[37,16,256]{2,1,0:T(8,128)(2,1)}, bf16[37,16,256]{2,1,0:T(8,128)(2,1)}, u32[]{:S(2)}, u32[]{:S(2)}) %collective-permute-start.11) | collective-permute-done | bytes 303136 | tf_op jit(solution)/shard_map/ppermute | solution.py:426
  49.1 2.6 %collective-permute-start.18 = (bf16[37,16,256]{2,1,0:T(8,128)(2,1)}, bf16[37,16,256]{2,1,0:T(8,128)(2,1)S(1)}, u32[]{:S(2)}, u32[]{:S(2)}) collective-permute-start(bf16[37,16,256]{2,1,0:T(8,128)(2,1)} %collective-permute-done.11), channel_id=1, source_target_pairs={{0,3},{8,11},{1,0},{9,8},{2,1},{10,9},{3,2},{11,10},{4,7},{12,15},... | collective-permute-start | bytes 909320 | tf_op jit(solution)/shard_map/ppermute | solution.py:426
  51.8 1.4 %pad_maximum_fusion.refs_1_ = bf16[4,37,16,256]{3,2,1,0:T(8,128)(2,1)S(1)} fusion(bf16[1,37,16,256]{3,2,1,0:T(8,128)(2,1)} %bitcast.32, bf16[1,37,16,256]{3,2,1,0:T(8,128)(2,1)} %bitcast.31, bf16[1,37,16,256]{3,2,1,0:T(8,128)(2,1)} %bitcast.15, bf16[1,37,16,256]{3,2,1,0:T(8,128)(2,1)S(1)} %bitcast.27), kind=kLoop, calls=%fused_computation | loop fusion | flops 1818624 | bytes 2424832 | tf_op jit(solution)/shard_map/stack | solution.py:478
  53.1 0.8 collective-permute-done.10
  53.9 5.0 %collective-permute-done.6.c1 = bf16[128,2432]{1,0:T(8,128)(2,1)} collective-permute-done((bf16[128,2432]{1,0:T(8,128)(2,1)}, bf16[128,2432]{1,0:T(8,128)(2,1)}, u32[]{:S(2)}, u32[]{:S(2)}) %collective-permute-start.6) | collective-permute-done | bytes 622624 | tf_op jit(solution)/shard_map/ppermute | solution.py:426
  59.0 2.8 %class_sums.1 = (f32[2,256,640]{2,1,0:T(8,128)S(1)}, f32[2,256,640]{2,1,0:T(8,128)S(1)}) custom-call(s32[4]{0:T(128)S(1)} %pad_add_fusion.sc, bf16[128,2432]{1,0:T(8,128)(2,1)S(1)} %copy-done.2, bf16[128,2432]{1,0:T(8,128)(2,1)} %collective-permute-done.6.c1, bf16[128,2432]{1,0:T(8,128)(2,1)S(1)} %collective-permute-done.7.c2, ...), custom_call_target="tpu_custom_call" | custom-call | flops 700000000 | bytes 5000000 | tf_op jit(solution)/shard_map/class_sums/pallas_call | solution.py:319
  61.9 1.2 %pad_maximum_fusion.1.refs_3_ = bf16[4,37,16,256]{3,2,1,0:T(8,128)(2,1)S(1)} fusion(bf16[1,37,16,256]{3,2,1,0:T(8,128)(2,1)S(1)} %bitcast.34, bf16[1,37,16,256]{3,2,1,0:T(8,128)(2,1)S(1)} %bitcast.33, bf16[1,37,16,256]{3,2,1,0:T(8,128)(2,1)} %bitcast.19, bf16[1,37,16,256]{3,2,1,0:T(8,128)(2,1)} %bitcast.18), kind=kLoop, calls=%fused_computation.1 | loop fusion | flops 1818624 | bytes 2424832 | tf_op jit(solution)/shard_map/stack | solution.py:483
  63.7 1.2 %collective-permute-done.12.b_ref = f32[2,256,640]{2,1,0:T(8,128)S(1)} collective-permute-done((f32[2,256,640]{2,1,0:T(8,128)S(1)}, f32[2,256,640]{2,1,0:T(8,128)S(1)}, u32[]{:S(2)}, u32[]{:S(2)}) %collective-permute-start.12) | collective-permute-done | bytes 1310752 | tf_op jit(solution)/shard_map/ppermute | solution.py:426
  66.3 2.0 %collective-permute-start.14 = (bf16[128,640]{1,0:T(8,128)(2,1)S(1)}, bf16[128,640]{1,0:T(8,128)(2,1)S(1)}, u32[]{:S(2)}, u32[]{:S(2)}) collective-permute-start(bf16[128,640]{1,0:T(8,128)(2,1)S(1)} %get-tuple-element.85), channel_id=1, source_target_pairs={{0,16},{8,24},{1,17},{9,25},{2,18},{10,26},{3,19},{11,27},{4,20},{... | collective-permute-start | bytes 491528 | tf_op jit(solution)/shard_map/ppermute | solution.py:426
  68.3 0.9 %collective-permute-start.15 = (bf16[128,640]{1,0:T(8,128)(2,1)S(1)}, bf16[128,640]{1,0:T(8,128)(2,1)S(1)}, u32[]{:S(2)}, u32[]{:S(2)}) collective-permute-start(bf16[128,640]{1,0:T(8,128)(2,1)S(1)} %get-tuple-element.86), channel_id=1, source_target_pairs={{0,20},{8,28},{1,21},{9,29},{2,22},{10,30},{3,23},{11,31},{4,0},{1... | collective-permute-start | bytes 491528 | tf_op jit(solution)/shard_map/ppermute | solution.py:426
  69.2 7.9 %scores.1 = f32[1,128]{1,0:T(1,128)} custom-call(bf16[37,128,256]{2,1,0:T(8,128)(2,1)S(1)} %spectra.1.refs_0_, bf16[4,37,16,256]{3,2,1,0:T(8,128)(2,1)S(1)} %pad_maximum_fusion.refs_1_, bf16[4,37,16,256]{3,2,1,0:T(8,128)(2,1)S(1)} %collective-permute-done.16.refs_2_, bf16[4,37,16,256]{3,2,1,0:T(8,128)(2,1)S(1)} %pad_maximum_fusion.1.refs_3_, ...), custom_call_target="tpu_custom_call" | custom-call | flops 6000000000 | bytes 8000000 | tf_op jit(solution)/shard_map/scores/pallas_call | solution.py:276
  78.0 3.1 %collective-permute-start.21 = (bf16[32,640]{1,0:T(8,128)(2,1)S(1)}, bf16[32,640]{1,0:T(8,128)(2,1)S(1)}, u32[]{:S(2)}, u32[]{:S(2)}) collective-permute-start(bf16[32,640]{1,0:T(8,128)(2,1)S(1)} %get-tuple-element.94), channel_id=1, source_target_pairs={{0,2},{8,10},{1,3},{9,11},{2,0},{10,8},{3,1},{11,9},{4,6},{12,14},... | collective-permute-start | bytes 122888 | tf_op jit(solution)/shard_map/ppermute | solution.py:426
  81.1 1.0 %collective-permute-start.22 = (bf16[32,640]{1,0:T(8,128)(2,1)S(1)}, bf16[32,640]{1,0:T(8,128)(2,1)S(1)}, u32[]{:S(2)}, u32[]{:S(2)}) collective-permute-start(bf16[32,640]{1,0:T(8,128)(2,1)S(1)} %get-tuple-element.95), channel_id=1, source_target_pairs={{0,3},{8,11},{1,0},{9,8},{2,1},{10,9},{3,2},{11,10},{4,7},{12,15},... | collective-permute-start | bytes 122888 | tf_op jit(solution)/shard_map/ppermute | solution.py:426
  82.1 1.5 %collective-permute-done.20.a1 = bf16[32,640]{1,0:T(8,128)(2,1)S(1)} collective-permute-done((bf16[32,640]{1,0:T(8,128)(2,1)S(1)}, bf16[32,640]{1,0:T(8,128)(2,1)S(1)}, u32[]{:S(2)}, u32[]{:S(2)}) %collective-permute-start.20) | collective-permute-done | bytes 40992 | tf_op jit(solution)/shard_map/ppermute | solution.py:426
  83.6 1.5 %collective-permute-done.22.a3 = bf16[32,640]{1,0:T(8,128)(2,1)S(1)} collective-permute-done((bf16[32,640]{1,0:T(8,128)(2,1)S(1)}, bf16[32,640]{1,0:T(8,128)(2,1)S(1)}, u32[]{:S(2)}, u32[]{:S(2)}) %collective-permute-start.22) | collective-permute-done | bytes 40992 | tf_op jit(solution)/shard_map/ppermute | solution.py:426
  85.1 1.4 %final.1 = f32[25,576]{1,0:T(8,128)} custom-call(s32[4]{0:T(128)S(1)} %pad_add_fusion.sc, f32[32,640]{1,0:T(8,128)S(1)} %get-tuple-element.92.a0, bf16[32,640]{1,0:T(8,128)(2,1)S(1)} %collective-permute-done.20.a1, bf16[32,640]{1,0:T(8,128)(2,1)S(1)} %collective-permute-done.21.a2, bf16[32,640]{1,0:T(8,128)(2,1)S(1)} %collective-permute-done.22.a3), custom_call_target="tpu_custom_call" | custom-call | tf_op jit(solution)/shard_map/final/pallas_call | solution.py:391
  (46 shorter events, 4.6 us)
Async XLA Ops:
  1.5 1.3 %collective-permute-start = (bf16[16,576]{1,0:T(8,128)(2,1)S(1)}, bf16[16,576]{1,0:T(8,128)(2,1)S(1)}, u32[]{:S(2)}, u32[]{:S(2)}) collective-permute-start(bf16[16,576]{1,0:T(8,128)(2,1)S(1)} %get-tuple-element.101), channel_id=1, source_target_pairs={{0,8},{8,0},{1,9},{9,1},{2,10},{10,2},{3,11},{11,3},{4,12},{12,4},... | collective-permute-start | bytes 55304 | tf_op jit(solution)/shard_map/ppermute | solution.py:426
  2.9 8.2 %collective-permute-start.1 = (bf16[16,1152]{1,0:T(8,128)(2,1)S(1)}, bf16[16,1152]{1,0:T(8,128)(2,1)S(1)}, u32[]{:S(2)}, u32[]{:S(2)}) collective-permute-start(bf16[16,1152]{1,0:T(8,128)(2,1)S(1)} %maximum_select_fusion), channel_id=1, source_target_pairs={{0,16},{8,24},{1,17},{9,25},{2,18},{10,26},{3,19},{11,27},{4,20},{... | collective-permute-start | bytes 110600 | tf_op jit(solution)/shard_map/ppermute | solution.py:426
  11.0 6.7 %collective-permute-start.2 = (bf16[2,16,1152]{2,1,0:T(8,128)(2,1)S(1)}, bf16[2,16,1152]{2,1,0:T(8,128)(2,1)S(1)}, u32[]{:S(2)}, u32[]{:S(2)}) collective-permute-start(bf16[2,16,1152]{2,1,0:T(8,128)(2,1)S(1)} %pad_maximum_fusion.3), channel_id=1, source_target_pairs={{0,32},{8,40},{1,33},{9,41},{2,34},{10,42},{3,35},{11,43},{4,36},{... | collective-permute-start | bytes 221192 | tf_op jit(solution)/shard_map/ppermute | solution.py:426
  12.7 12.0 %copy-start.1 = (bf16[592,576]{1,0:T(8,128)(2,1)S(1)}, bf16[592,576]{1,0:T(8,128)(2,1)}, u32[]{:S(2)}) copy-start(bf16[592,576]{1,0:T(8,128)(2,1)} %constant.75.clone.f_ref) | copy-start | bytes 2045956
  17.8 6.9 %collective-permute-start.3 = (bf16[2,2,16,1152]{3,2,1,0:T(8,128)(2,1)S(1)}, bf16[2,2,16,1152]{3,2,1,0:T(8,128)(2,1)S(1)}, u32[]{:S(2)}, u32[]{:S(2)}) collective-permute-start(bf16[2,2,16,1152]{3,2,1,0:T(8,128)(2,1)S(1)} %pad_maximum_fusion.2.own_ref), channel_id=1, source_target_pairs={{0,64},{8,72},{1,65},{9,73},{2,66},{10,74},{3,67},{11,75},{4,68},{... | collective-permute-start | bytes 442376 | tf_op jit(solution)/shard_map/ppermute | solution.py:426
  25.3 12.8 %collective-permute-start.4 = (bf16[37,16,256]{2,1,0:T(8,128)(2,1)S(1)}, bf16[37,16,256]{2,1,0:T(8,128)(2,1)S(1)}, u32[]{:S(2)}, u32[]{:S(2)}) collective-permute-start(bf16[37,16,256]{2,1,0:T(8,128)(2,1)S(1)} %ref_spectra.1), channel_id=1, source_target_pairs={{0,1},{8,9},{1,2},{9,10},{2,3},{10,11},{3,0},{11,8},{4,5},{12,13},... | collective-permute-start | bytes 909320 | tf_op jit(solution)/shard_map/ppermute | solution.py:426
  27.3 10.8 %collective-permute-start.5 = (bf16[37,16,256]{2,1,0:T(8,128)(2,1)S(1)}, bf16[37,16,256]{2,1,0:T(8,128)(2,1)S(1)}, u32[]{:S(2)}, u32[]{:S(2)}) collective-permute-start(bf16[37,16,256]{2,1,0:T(8,128)(2,1)S(1)} %ref_spectra.1), channel_id=1, source_target_pairs={{0,3},{8,11},{1,0},{9,8},{2,1},{10,9},{3,2},{11,10},{4,7},{12,15},... | collective-permute-start | bytes 909320 | tf_op jit(solution)/shard_map/ppermute | solution.py:426
  29.5 18.7 %collective-permute-start.7 = (bf16[128,2432]{1,0:T(8,128)(2,1)}, bf16[128,2432]{1,0:T(8,128)(2,1)S(1)}, u32[]{:S(2)}, u32[]{:S(2)}) collective-permute-start(bf16[128,2432]{1,0:T(8,128)(2,1)} %get-tuple-element.75), channel_id=1, source_target_pairs={{0,64},{8,72},{1,65},{9,73},{2,66},{10,74},{3,67},{11,75},{4,68},{... | collective-permute-start | bytes 1867784 | tf_op jit(solution)/shard_map/ppermute | solution.py:426
  32.4 9.0 %collective-permute-start.9 = (bf16[37,16,256]{2,1,0:T(8,128)(2,1)S(1)}, bf16[37,16,256]{2,1,0:T(8,128)(2,1)}, u32[]{:S(2)}, u32[]{:S(2)}) collective-permute-start(bf16[37,16,256]{2,1,0:T(8,128)(2,1)S(1)} %ref_spectra.1), channel_id=1, source_target_pairs={{0,4},{8,12},{1,5},{9,13},{2,6},{10,14},{3,7},{11,15},{4,0},{12,8}... | collective-permute-start | bytes 909320 | tf_op jit(solution)/shard_map/ppermute | solution.py:426
  33.0 1.7 %copy-start = (bf16[16,576,128]{2,1,0:T(8,128)(2,1)S(1)}, bf16[16,576,128]{2,1,0:T(8,128)(2,1)}, u32[]{:S(2)}) copy-start(bf16[16,576,128]{2,1,0:T(8,128)(2,1)} %get-tuple-element.72.w_ref) | copy-start | bytes 7077892
  38.0 3.3 %copy-start.5 = (bf16[37,16,256]{2,1,0:T(8,128)(2,1)}, bf16[37,16,256]{2,1,0:T(8,128)(2,1)S(1)}, u32[]{:S(2)}) copy-start(bf16[37,16,256]{2,1,0:T(8,128)(2,1)S(1)} %collective-permute-done.4) | copy-start | bytes 909316
  38.1 5.3 %copy-start.6 = (bf16[37,16,256]{2,1,0:T(8,128)(2,1)}, bf16[37,16,256]{2,1,0:T(8,128)(2,1)S(1)}, u32[]{:S(2)}) copy-start(bf16[37,16,256]{2,1,0:T(8,128)(2,1)S(1)} %collective-permute-done.5) | copy-start | bytes 909316
  38.1 20.9 %collective-permute-start.6 = (bf16[128,2432]{1,0:T(8,128)(2,1)}, bf16[128,2432]{1,0:T(8,128)(2,1)}, u32[]{:S(2)}, u32[]{:S(2)}) collective-permute-start(bf16[128,2432]{1,0:T(8,128)(2,1)} %get-tuple-element.74), channel_id=1, source_target_pairs={{0,32},{8,40},{1,33},{9,41},{2,34},{10,42},{3,35},{11,43},{4,36},{... | collective-permute-start | bytes 1867784 | tf_op jit(solution)/shard_map/ppermute | solution.py:426
  38.3 20.7 %collective-permute-start.8 = (bf16[128,2432]{1,0:T(8,128)(2,1)}, bf16[128,2432]{1,0:T(8,128)(2,1)}, u32[]{:S(2)}, u32[]{:S(2)}) collective-permute-start(bf16[128,2432]{1,0:T(8,128)(2,1)} %get-tuple-element.76), channel_id=1, source_target_pairs={{0,96},{8,104},{1,97},{9,105},{2,98},{10,106},{3,99},{11,107},{4,1... | collective-permute-start | bytes 1867784 | tf_op jit(solution)/shard_map/ppermute | solution.py:426
  41.4 7.7 %collective-permute-start.11 = (bf16[37,16,256]{2,1,0:T(8,128)(2,1)}, bf16[37,16,256]{2,1,0:T(8,128)(2,1)}, u32[]{:S(2)}, u32[]{:S(2)}) collective-permute-start(bf16[37,16,256]{2,1,0:T(8,128)(2,1)} %collective-permute-done.9), channel_id=1, source_target_pairs={{0,3},{8,11},{1,0},{9,8},{2,1},{10,9},{3,2},{11,10},{4,7},{12,15},... | collective-permute-start | bytes 909320 | tf_op jit(solution)/shard_map/ppermute | solution.py:426
  43.3 10.6 %collective-permute-start.10 = (bf16[37,16,256]{2,1,0:T(8,128)(2,1)}, bf16[37,16,256]{2,1,0:T(8,128)(2,1)}, u32[]{:S(2)}, u32[]{:S(2)}) collective-permute-start(bf16[37,16,256]{2,1,0:T(8,128)(2,1)} %collective-permute-done.9), channel_id=1, source_target_pairs={{0,1},{8,9},{1,2},{9,10},{2,3},{10,11},{3,0},{11,8},{4,5},{12,13},... | collective-permute-start | bytes 909320 | tf_op jit(solution)/shard_map/ppermute | solution.py:426
  48.2 13.7 %collective-permute-start.17 = (bf16[37,16,256]{2,1,0:T(8,128)(2,1)}, bf16[37,16,256]{2,1,0:T(8,128)(2,1)S(1)}, u32[]{:S(2)}, u32[]{:S(2)}) collective-permute-start(bf16[37,16,256]{2,1,0:T(8,128)(2,1)} %copy-done.5), channel_id=1, source_target_pairs={{0,1},{8,9},{1,2},{9,10},{2,3},{10,11},{3,0},{11,8},{4,5},{12,13},... | collective-permute-start | bytes 909320 | tf_op jit(solution)/shard_map/ppermute | solution.py:426
  49.1 12.8 %collective-permute-start.18 = (bf16[37,16,256]{2,1,0:T(8,128)(2,1)}, bf16[37,16,256]{2,1,0:T(8,128)(2,1)S(1)}, u32[]{:S(2)}, u32[]{:S(2)}) collective-permute-start(bf16[37,16,256]{2,1,0:T(8,128)(2,1)} %collective-permute-done.11), channel_id=1, source_target_pairs={{0,3},{8,11},{1,0},{9,8},{2,1},{10,9},{3,2},{11,10},{4,7},{12,15},... | collective-permute-start | bytes 909320 | tf_op jit(solution)/shard_map/ppermute | solution.py:426
  51.8 7.2 %copy-start.2 = (bf16[128,2432]{1,0:T(8,128)(2,1)S(1)}, bf16[128,2432]{1,0:T(8,128)(2,1)}, u32[]{:S(2)}) copy-start(bf16[128,2432]{1,0:T(8,128)(2,1)} %get-tuple-element.77.c0) | copy-start | bytes 1867780
  51.8 7.2 %copy-start.3 = (f32[256,64]{0,1:T(8,128)S(1)}, f32[256,64]{0,1:T(8,128)}, u32[]{:S(2)}) copy-start(f32[256,64]{0,1:T(8,128)} %param.19) | copy-start | bytes 196612
  53.9 15.3 %collective-permute-start.16 = (bf16[4,37,16,256]{3,2,1,0:T(8,128)(2,1)S(1)}, bf16[4,37,16,256]{3,2,1,0:T(8,128)(2,1)S(1)}, u32[]{:S(2)}, u32[]{:S(2)}) collective-permute-start(bf16[4,37,16,256]{3,2,1,0:T(8,128)(2,1)S(1)} %pad_maximum_fusion.refs_1_), channel_id=1, source_target_pairs={{0,8},{8,0},{1,9},{9,1},{2,10},{10,2},{3,11},{11,3},{4,12},{12,4},... | collective-permute-start | bytes 3637256 | tf_op jit(solution)/shard_map/ppermute | solution.py:426
  61.8 3.1 %collective-permute-start.12 = (f32[2,256,640]{2,1,0:T(8,128)S(1)}, f32[2,256,640]{2,1,0:T(8,128)S(1)}, u32[]{:S(2)}, u32[]{:S(2)}) collective-permute-start(f32[2,256,640]{2,1,0:T(8,128)S(1)} %get-tuple-element.82), channel_id=1, source_target_pairs={{0,8},{8,0},{1,9},{9,1},{2,10},{10,2},{3,11},{11,3},{4,12},{12,4},... | collective-permute-start | bytes 3932168 | tf_op jit(solution)/shard_map/ppermute | solution.py:426
  63.1 6.1 %collective-permute-start.19 = (bf16[4,37,16,256]{3,2,1,0:T(8,128)(2,1)S(1)}, bf16[4,37,16,256]{3,2,1,0:T(8,128)(2,1)S(1)}, u32[]{:S(2)}, u32[]{:S(2)}) collective-permute-start(bf16[4,37,16,256]{3,2,1,0:T(8,128)(2,1)S(1)} %pad_maximum_fusion.1.refs_3_), channel_id=1, source_target_pairs={{0,8},{8,0},{1,9},{9,1},{2,10},{10,2},{3,11},{11,3},{4,12},{12,4},... | collective-permute-start | bytes 3637256 | tf_op jit(solution)/shard_map/ppermute | solution.py:426
  64.9 4.3 %copy-start.4 = (bf16[576,640]{1,0:T(8,128)(2,1)S(1)}, bf16[576,640]{1,0:T(8,128)(2,1)}, u32[]{:S(2)}) copy-start(bf16[576,640]{1,0:T(8,128)(2,1)} %constant.76.clone.refs_5_) | copy-start | bytes 2211844
  65.6 11.6 %collective-permute-start.13 = (bf16[128,640]{1,0:T(8,128)(2,1)S(1)}, bf16[128,640]{1,0:T(8,128)(2,1)S(1)}, u32[]{:S(2)}, u32[]{:S(2)}) collective-permute-start(bf16[128,640]{1,0:T(8,128)(2,1)S(1)} %get-tuple-element.84), channel_id=1, source_target_pairs={{0,4},{8,12},{1,5},{9,13},{2,6},{10,14},{3,7},{11,15},{4,16},{12,2... | collective-permute-start | bytes 491528 | tf_op jit(solution)/shard_map/ppermute | solution.py:426
  66.3 10.9 %collective-permute-start.14 = (bf16[128,640]{1,0:T(8,128)(2,1)S(1)}, bf16[128,640]{1,0:T(8,128)(2,1)S(1)}, u32[]{:S(2)}, u32[]{:S(2)}) collective-permute-start(bf16[128,640]{1,0:T(8,128)(2,1)S(1)} %get-tuple-element.85), channel_id=1, source_target_pairs={{0,16},{8,24},{1,17},{9,25},{2,18},{10,26},{3,19},{11,27},{4,20},{... | collective-permute-start | bytes 491528 | tf_op jit(solution)/shard_map/ppermute | solution.py:426
  68.3 9.0 %collective-permute-start.15 = (bf16[128,640]{1,0:T(8,128)(2,1)S(1)}, bf16[128,640]{1,0:T(8,128)(2,1)S(1)}, u32[]{:S(2)}, u32[]{:S(2)}) collective-permute-start(bf16[128,640]{1,0:T(8,128)(2,1)S(1)} %get-tuple-element.86), channel_id=1, source_target_pairs={{0,20},{8,28},{1,21},{9,29},{2,22},{10,30},{3,23},{11,31},{4,0},{1... | collective-permute-start | bytes 491528 | tf_op jit(solution)/shard_map/ppermute | solution.py:426
  77.9 5.7 %collective-permute-start.20 = (bf16[32,640]{1,0:T(8,128)(2,1)S(1)}, bf16[32,640]{1,0:T(8,128)(2,1)S(1)}, u32[]{:S(2)}, u32[]{:S(2)}) collective-permute-start(bf16[32,640]{1,0:T(8,128)(2,1)S(1)} %get-tuple-element.93), channel_id=1, source_target_pairs={{0,1},{8,9},{1,2},{9,10},{2,3},{10,11},{3,0},{11,8},{4,5},{12,13},... | collective-permute-start | bytes 122888 | tf_op jit(solution)/shard_map/ppermute | solution.py:426
  78.0 5.6 %collective-permute-start.21 = (bf16[32,640]{1,0:T(8,128)(2,1)S(1)}, bf16[32,640]{1,0:T(8,128)(2,1)S(1)}, u32[]{:S(2)}, u32[]{:S(2)}) collective-permute-start(bf16[32,640]{1,0:T(8,128)(2,1)S(1)} %get-tuple-element.94), channel_id=1, source_target_pairs={{0,2},{8,10},{1,3},{9,11},{2,0},{10,8},{3,1},{11,9},{4,6},{12,14},... | collective-permute-start | bytes 122888 | tf_op jit(solution)/shard_map/ppermute | solution.py:426
  81.1 4.0 %collective-permute-start.22 = (bf16[32,640]{1,0:T(8,128)(2,1)S(1)}, bf16[32,640]{1,0:T(8,128)(2,1)S(1)}, u32[]{:S(2)}, u32[]{:S(2)}) collective-permute-start(bf16[32,640]{1,0:T(8,128)(2,1)S(1)} %get-tuple-element.95), channel_id=1, source_target_pairs={{0,3},{8,11},{1,0},{9,8},{2,1},{10,9},{3,2},{11,10},{4,7},{12,15},... | collective-permute-start | bytes 122888 | tf_op jit(solution)/shard_map/ppermute | solution.py:426

commit v12 on v9

--- a/solution.py
+++ b/solution.py
@@ -466,8 +466,9 @@
     own = ref_spectra(octet, fwd_k)
     up, down = move(own, ZS[1]), move(own, ZS[3])
     side = move(own, LOW)
-    side_up, side_down = move(side, ZS[1]), move(side, ZS[3])
-    one, three = after([sent[1], sent[3]], across, part, up, down)
+    (ready,) = after([side], across)
+    side_up, side_down = move(ready, ZS[1]), move(ready, ZS[3])
+    one, three = after([sent[1], sent[3]], part, up, down)
     held = [sent[0], move(one, YS[1]), across, move(three, YS[3])]
     on_up, on_down = move(up, ZS[1]), move(side_down, ZS[3])
     early = jnp.stack([own, side, up, down])

time: 85.4 us -> 82.9 us (0.971)
  waiting for transfers between devices: 20.5 us -> 17.9 us
    ppermute x23, waiting for transfers between devices: 20.5 us -> 17.9 us  [move(): return lax.ppermute(value, AXES, pairs)]
where the time goes in v12:
time: 82.9 us; the launch traced here: 82.5 us
  starting transfers between devices  32.1 us (39%)
  Pallas kernels  27.1 us (33%)
  waiting for transfers between devices  17.9 us (22%)
  other arithmetic  3.76 us (5%)
  local copies, waits for them, and re-layouts  0.88 us (1%)
  between operations  0.84 us (1%)
    ppermute x23, starting transfers between devices, move(): return lax.ppermute(value, AXES, pairs)  32.1 us
    ppermute x23, waiting for transfers between devices, move(): return lax.ppermute(value, AXES, pairs)  17.9 us
    pallas_call x2, Pallas kernels, prep(): pl.pallas_call(functools.partial(prep_kernel, first), grid=(n // 32,), in...  10.1 us
    pallas_call x1, Pallas kernels, scores_of(): pl.pallas_call(score_kernel, in_specs=[v] * 6, out_specs=v, out_shape=jax...  7.93 us
    pallas_call x1, Pallas kernels, spectra(): pl.pallas_call(spectra_kernel, in_specs=[v, v], out_specs=v, out_shape=ja...  3.4 us
    pallas_call x1, Pallas kernels, class_sums(): pl.pallas_call(sums_kernel, in_specs=[pl.BlockSpec(memory_space=pltpu.SME...  2.64 us
  transfers between devices with their start and end apart: 23, of which 10 were waited for; matrix products, arithmetic and copies ran while one was open for 3% of the time, Pallas kernels for 30%

profile of v12, /device:TPU:0, one launch (start us, length us, event | category | flops | bytes accessed | tf_op | source)
XLA Modules:
  0.0 82.5 jit_solution(6598783020532888672)
XLA Ops:
  0.6 0.8 %broadcast_select_fusion.1 = (bf16[16,576]{1,0:T(8,128)(2,1)S(1)}, bf16[16,576]{1,0:T(8,128)(2,1)S(1)}) fusion(pred[]{:T(512)S(6)} %eq.18, bf16[25,576]{1,0:T(8,128)(2,1)} %param.13), kind=kLoop, calls=%fused_computation.13 | loop fusion | flops 18432 | bytes 73729 | tf_op jit(solution)/shard_map/jit(_where)/select_n | solution.py:444
  1.6 1.2 %collective-permute-done = bf16[16,576]{1,0:T(8,128)(2,1)S(1)} collective-permute-done((bf16[16,576]{1,0:T(8,128)(2,1)S(1)}, bf16[16,576]{1,0:T(8,128)(2,1)S(1)}, u32[]{:S(2)}, u32[]{:S(2)}) %collective-permute-start) | collective-permute-done | bytes 18464 | tf_op jit(solution)/shard_map/ppermute | solution.py:421
  2.9 3.2 %collective-permute-start.1 = (bf16[16,1152]{1,0:T(8,128)(2,1)S(1)}, bf16[16,1152]{1,0:T(8,128)(2,1)S(1)}, u32[]{:S(2)}, u32[]{:S(2)}) collective-permute-start(bf16[16,1152]{1,0:T(8,128)(2,1)S(1)} %maximum_select_fusion), channel_id=1, source_target_pairs={{0,16},{8,24},{1,17},{9,25},{2,18},{10,26},{3,19},{11,27},{4,20},{... | collective-permute-start | bytes 110600 | tf_op jit(solution)/shard_map/ppermute | solution.py:421
  6.0 5.0 %prep.2 = (bf16[16,576,128]{2,1,0:T(8,128)(2,1)}, bf16[128,2432]{1,0:T(8,128)(2,1)}, bf16[128,2432]{1,0:T(8,128)(2,1)}, bf16[128,2432]{1,0:T(8,128)(2,1)}, bf16[128,2432]{1,0:T(8,128)(2,1)}) custom-call(bf16[128,9216]{1,0:T(8,128)(2,1)} %x_ref.3, s32[2,128]{1,0:T(2,128)} %bitcast.41, s32[1,128]{1,0:T(1,128)} %bitcast.43, s32[1,128]{1,0:T(1,128)} %bitcast.45, ...), custom_call_target="tpu_custom_call" | custom-call | flops 20000000 | bytes 4000000 | tf_op jit(solution)/shard_map/prep/pallas_call | solution.py:144
  11.1 1.7 %collective-permute-start.2 = (bf16[2,16,1152]{2,1,0:T(8,128)(2,1)S(1)}, bf16[2,16,1152]{2,1,0:T(8,128)(2,1)S(1)}, u32[]{:S(2)}, u32[]{:S(2)}) collective-permute-start(bf16[2,16,1152]{2,1,0:T(8,128)(2,1)S(1)} %pad_maximum_fusion.4), channel_id=1, source_target_pairs={{0,32},{8,40},{1,33},{9,41},{2,34},{10,42},{3,35},{11,43},{4,36},{... | collective-permute-start | bytes 221192 | tf_op jit(solution)/shard_map/ppermute | solution.py:421
  12.8 5.0 %prep.3 = (bf16[16,576,128]{2,1,0:T(8,128)(2,1)}, bf16[128,2432]{1,0:T(8,128)(2,1)}, bf16[128,2432]{1,0:T(8,128)(2,1)}, bf16[128,2432]{1,0:T(8,128)(2,1)}, bf16[128,2432]{1,0:T(8,128)(2,1)}) custom-call(bf16[128,9216]{1,0:T(8,128)(2,1)} %x_ref.3, s32[2,128]{1,0:T(2,128)} %bitcast.42, ...), custom_call_target="tpu_custom_call", output_to_operand_aliasing={{0}: (9, {}), {1}: (10, {}), {2}: (11, {}), {3}: (12, {}), ... | custom-call | flops 20000000 | bytes 4000000 | tf_op jit(solution)/shard_map/prep/pallas_call | solution.py:144
  17.9 3.0 %collective-permute-start.3 = (bf16[2,2,16,1152]{3,2,1,0:T(8,128)(2,1)S(1)}, bf16[2,2,16,1152]{3,2,1,0:T(8,128)(2,1)S(1)}, u32[]{:S(2)}, u32[]{:S(2)}) collective-permute-start(bf16[2,2,16,1152]{3,2,1,0:T(8,128)(2,1)S(1)} %pad_maximum_fusion.3), channel_id=1, source_target_pairs={{0,64},{8,72},{1,65},{9,73},{2,66},{10,74},{3,67},{11,75},{4,68},{... | collective-permute-start | bytes 442376 | tf_op jit(solution)/shard_map/ppermute | solution.py:421
  21.5 3.7 %collective-permute-done.3 = bf16[2,2,16,1152]{3,2,1,0:T(8,128)(2,1)S(1)} collective-permute-done((bf16[2,2,16,1152]{3,2,1,0:T(8,128)(2,1)S(1)}, bf16[2,2,16,1152]{3,2,1,0:T(8,128)(2,1)S(1)}, u32[]{:S(2)}, u32[]{:S(2)}) %collective-permute-start.3) | collective-permute-done | bytes 147488 | tf_op jit(solution)/shard_map/ppermute | solution.py:421
  25.6 2.0 %collective-permute-start.4 = (bf16[37,16,256]{2,1,0:T(8,128)(2,1)S(1)}, bf16[37,16,256]{2,1,0:T(8,128)(2,1)S(1)}, u32[]{:S(2)}, u32[]{:S(2)}) collective-permute-start(bf16[37,16,256]{2,1,0:T(8,128)(2,1)S(1)} %ref_spectra.1), channel_id=1, source_target_pairs={{0,1},{8,9},{1,2},{9,10},{2,3},{10,11},{3,0},{11,8},{4,5},{12,13},... | collective-permute-start | bytes 909320 | tf_op jit(solution)/shard_map/ppermute | solution.py:421
  27.6 2.2 %collective-permute-start.5 = (bf16[37,16,256]{2,1,0:T(8,128)(2,1)S(1)}, bf16[37,16,256]{2,1,0:T(8,128)(2,1)S(1)}, u32[]{:S(2)}, u32[]{:S(2)}) collective-permute-start(bf16[37,16,256]{2,1,0:T(8,128)(2,1)S(1)} %ref_spectra.1), channel_id=1, source_target_pairs={{0,3},{8,11},{1,0},{9,8},{2,1},{10,9},{3,2},{11,10},{4,7},{12,15},... | collective-permute-start | bytes 909320 | tf_op jit(solution)/shard_map/ppermute | solution.py:421
  30.4 3.4 %spectra.1.refs_0_ = bf16[37,128,256]{2,1,0:T(8,128)(2,1)S(1)} custom-call(bf16[16,576,128]{2,1,0:T(8,128)(2,1)S(1)} %copy-done, bf16[592,576]{1,0:T(8,128)(2,1)S(1)} %copy-done.1), custom_call_target="tpu_custom_call" | custom-call | flops 1000 | bytes 1000 | tf_op jit(solution)/shard_map/spectra/pallas_call | solution.py:194
  33.8 1.6 %collective-permute-done.4 = bf16[37,16,256]{2,1,0:T(8,128)(2,1)S(1)} collective-permute-done((bf16[37,16,256]{2,1,0:T(8,128)(2,1)S(1)}, bf16[37,16,256]{2,1,0:T(8,128)(2,1)S(1)}, u32[]{:S(2)}, u32[]{:S(2)}) %collective-permute-start.4) | collective-permute-done | bytes 303136 | tf_op jit(solution)/shard_map/ppermute | solution.py:421
  36.0 2.8 %collective-permute-start.8 = (bf16[128,2432]{1,0:T(8,128)(2,1)}, bf16[128,2432]{1,0:T(8,128)(2,1)}, u32[]{:S(2)}, u32[]{:S(2)}) collective-permute-start(bf16[128,2432]{1,0:T(8,128)(2,1)} %get-tuple-element.77), channel_id=1, source_target_pairs={{0,96},{8,104},{1,97},{9,105},{2,98},{10,106},{3,99},{11,107},{4,1... | collective-permute-start | bytes 1867784 | tf_op jit(solution)/shard_map/ppermute | solution.py:421
  39.4 0.9 %copy-done.4 = bf16[128,2432]{1,0:T(8,128)(2,1)} copy-done((bf16[128,2432]{1,0:T(8,128)(2,1)}, bf16[128,2432]{1,0:T(8,128)(2,1)S(1)}, u32[]{:S(2)}) %copy-start.4) | copy-done | bytes 622616
  40.3 4.2 %collective-permute-start.11 = (bf16[37,16,256]{2,1,0:T(8,128)(2,1)}, bf16[37,16,256]{2,1,0:T(8,128)(2,1)}, u32[]{:S(2)}, u32[]{:S(2)}) collective-permute-start(bf16[37,16,256]{2,1,0:T(8,128)(2,1)} %collective-permute-done.9), channel_id=1, source_target_pairs={{0,3},{8,11},{1,0},{9,8},{2,1},{10,9},{3,2},{11,10},{4,7},{12,15},... | collective-permute-start | bytes 909320 | tf_op jit(solution)/shard_map/ppermute | solution.py:421
  44.4 4.6 %collective-permute-done.11 = bf16[37,16,256]{2,1,0:T(8,128)(2,1)} collective-permute-done((bf16[37,16,256]{2,1,0:T(8,128)(2,1)}, bf16[37,16,256]{2,1,0:T(8,128)(2,1)}, u32[]{:S(2)}, u32[]{:S(2)}) %collective-permute-start.11) | collective-permute-done | bytes 303136 | tf_op jit(solution)/shard_map/ppermute | solution.py:421
  49.1 3.7 %collective-permute-start.18 = (bf16[37,16,256]{2,1,0:T(8,128)(2,1)}, bf16[37,16,256]{2,1,0:T(8,128)(2,1)S(1)}, u32[]{:S(2)}, u32[]{:S(2)}) collective-permute-start(bf16[37,16,256]{2,1,0:T(8,128)(2,1)} %collective-permute-done.11), channel_id=1, source_target_pairs={{0,3},{8,11},{1,0},{9,8},{2,1},{10,9},{3,2},{11,10},{4,7},{12,15},... | collective-permute-start | bytes 909320 | tf_op jit(solution)/shard_map/ppermute | solution.py:421
  52.9 1.4 %pad_maximum_fusion.refs_1_ = bf16[4,37,16,256]{3,2,1,0:T(8,128)(2,1)S(1)} fusion(bf16[1,37,16,256]{3,2,1,0:T(8,128)(2,1)} %bitcast.38, bf16[1,37,16,256]{3,2,1,0:T(8,128)(2,1)} %bitcast.37, bf16[1,37,16,256]{3,2,1,0:T(8,128)(2,1)} %bitcast.18, bf16[1,37,16,256]{3,2,1,0:T(8,128)(2,1)S(1)} %bitcast.32), kind=kLoop, calls=%fused_computation | loop fusion | flops 1818624 | bytes 2424832 | tf_op jit(solution)/shard_map/stack | solution.py:474
  54.3 1.1 %collective-permute-done.10 = bf16[37,16,256]{2,1,0:T(8,128)(2,1)} collective-permute-done((bf16[37,16,256]{2,1,0:T(8,128)(2,1)}, bf16[37,16,256]{2,1,0:T(8,128)(2,1)}, u32[]{:S(2)}, u32[]{:S(2)}) %collective-permute-start.10) | collective-permute-done | bytes 303136 | tf_op jit(solution)/shard_map/ppermute | solution.py:421
  55.4 2.6 %class_sums.1 = (f32[2,256,640]{2,1,0:T(8,128)S(1)}, f32[2,256,640]{2,1,0:T(8,128)S(1)}) custom-call(s32[4]{0:T(128)S(1)} %pad_add_fusion.sc, bf16[128,2432]{1,0:T(8,128)(2,1)S(1)} %copy-done.2, bf16[128,2432]{1,0:T(8,128)(2,1)S(1)} %collective-permute-done.6.c1, bf16[128,2432]{1,0:T(8,128)(2,1)S(1)} %copy-done.5, ...), custom_call_target="tpu_custom_call" | custom-call | flops 700000000 | bytes 5000000 | tf_op jit(solution)/shard_map/class_sums/pallas_call | solution.py:314
  58.6 1.2 %pad_maximum_fusion.1.refs_3_ = bf16[4,37,16,256]{3,2,1,0:T(8,128)(2,1)S(1)} fusion(bf16[1,37,16,256]{3,2,1,0:T(8,128)(2,1)S(1)} %bitcast.40, bf16[1,37,16,256]{3,2,1,0:T(8,128)(2,1)S(1)} %bitcast.39, bf16[1,37,16,256]{3,2,1,0:T(8,128)(2,1)} %bitcast.22, bf16[1,37,16,256]{3,2,1,0:T(8,128)(2,1)} %bitcast.21), kind=kLoop, calls=%fused_computation.1 | loop fusion | flops 1818624 | bytes 2424832 | tf_op jit(solution)/shard_map/stack | solution.py:479
  60.0 1.3 %collective-permute-done.12.b_ref = f32[2,256,640]{2,1,0:T(8,128)S(1)} collective-permute-done((f32[2,256,640]{2,1,0:T(8,128)S(1)}, f32[2,256,640]{2,1,0:T(8,128)S(1)}, u32[]{:S(2)}, u32[]{:S(2)}) %collective-permute-start.12) | collective-permute-done | bytes 1310752 | tf_op jit(solution)/shard_map/ppermute | solution.py:421
  61.3 0.7 cut_x.1
  62.0 0.7 collective-permute-start.13
  62.7 2.0 %collective-permute-start.14 = (bf16[128,640]{1,0:T(8,128)(2,1)S(1)}, bf16[128,640]{1,0:T(8,128)(2,1)S(1)}, u32[]{:S(2)}, u32[]{:S(2)}) collective-permute-start(bf16[128,640]{1,0:T(8,128)(2,1)S(1)} %get-tuple-element.87), channel_id=1, source_target_pairs={{0,16},{8,24},{1,17},{9,25},{2,18},{10,26},{3,19},{11,27},{4,20},{... | collective-permute-start | bytes 491528 | tf_op jit(solution)/shard_map/ppermute | solution.py:421
  64.7 0.9 %collective-permute-start.15 = (bf16[128,640]{1,0:T(8,128)(2,1)S(1)}, bf16[128,640]{1,0:T(8,128)(2,1)S(1)}, u32[]{:S(2)}, u32[]{:S(2)}) collective-permute-start(bf16[128,640]{1,0:T(8,128)(2,1)S(1)} %get-tuple-element.88), channel_id=1, source_target_pairs={{0,20},{8,28},{1,21},{9,29},{2,22},{10,30},{3,23},{11,31},{4,0},{1... | collective-permute-start | bytes 491528 | tf_op jit(solution)/shard_map/ppermute | solution.py:421
  65.6 7.9 %scores.1 = f32[1,128]{1,0:T(1,128)} custom-call(bf16[37,128,256]{2,1,0:T(8,128)(2,1)S(1)} %spectra.1.refs_0_, bf16[4,37,16,256]{3,2,1,0:T(8,128)(2,1)S(1)} %pad_maximum_fusion.refs_1_, bf16[4,37,16,256]{3,2,1,0:T(8,128)(2,1)S(1)} %collective-permute-done.16.refs_2_, bf16[4,37,16,256]{3,2,1,0:T(8,128)(2,1)S(1)} %pad_maximum_fusion.1.refs_3_, ...), custom_call_target="tpu_custom_call" | custom-call | flops 6000000000 | bytes 8000000 | tf_op jit(solution)/shard_map/scores/pallas_call | solution.py:271
  74.6 2.6 %collective-permute-start.21 = (bf16[32,640]{1,0:T(8,128)(2,1)S(1)}, bf16[32,640]{1,0:T(8,128)(2,1)S(1)}, u32[]{:S(2)}, u32[]{:S(2)}) collective-permute-start(bf16[32,640]{1,0:T(8,128)(2,1)S(1)} %get-tuple-element.96), channel_id=1, source_target_pairs={{0,2},{8,10},{1,3},{9,11},{2,0},{10,8},{3,1},{11,9},{4,6},{12,14},... | collective-permute-start | bytes 122888 | tf_op jit(solution)/shard_map/ppermute | solution.py:421
  77.2 0.6 collective-permute-start.22
  77.8 2.4 %collective-permute-done.20.a1 = bf16[32,640]{1,0:T(8,128)(2,1)S(1)} collective-permute-done((bf16[32,640]{1,0:T(8,128)(2,1)S(1)}, bf16[32,640]{1,0:T(8,128)(2,1)S(1)}, u32[]{:S(2)}, u32[]{:S(2)}) %collective-permute-start.20) | collective-permute-done | bytes 40992 | tf_op jit(solution)/shard_map/ppermute | solution.py:421
  80.2 0.9 %collective-permute-done.22.a3 = bf16[32,640]{1,0:T(8,128)(2,1)S(1)} collective-permute-done((bf16[32,640]{1,0:T(8,128)(2,1)S(1)}, bf16[32,640]{1,0:T(8,128)(2,1)S(1)}, u32[]{:S(2)}, u32[]{:S(2)}) %collective-permute-start.22) | collective-permute-done | bytes 40992 | tf_op jit(solution)/shard_map/ppermute | solution.py:421
  81.2 1.4 %final.1 = f32[25,576]{1,0:T(8,128)} custom-call(s32[4]{0:T(128)S(1)} %pad_add_fusion.sc, f32[32,640]{1,0:T(8,128)S(1)} %get-tuple-element.94.a0, bf16[32,640]{1,0:T(8,128)(2,1)S(1)} %collective-permute-done.20.a1, bf16[32,640]{1,0:T(8,128)(2,1)S(1)} %collective-permute-done.21.a2, bf16[32,640]{1,0:T(8,128)(2,1)S(1)} %collective-permute-done.22.a3), custom_call_target="tpu_custom_call" | custom-call | tf_op jit(solution)/shard_map/final/pallas_call | solution.py:386
  (52 shorter events, 4.9 us)
Async XLA Ops:
  1.5 1.3 %collective-permute-start = (bf16[16,576]{1,0:T(8,128)(2,1)S(1)}, bf16[16,576]{1,0:T(8,128)(2,1)S(1)}, u32[]{:S(2)}, u32[]{:S(2)}) collective-permute-start(bf16[16,576]{1,0:T(8,128)(2,1)S(1)} %get-tuple-element.105), channel_id=1, source_target_pairs={{0,8},{8,0},{1,9},{9,1},{2,10},{10,2},{3,11},{11,3},{4,12},{12,4},... | collective-permute-start | bytes 55304 | tf_op jit(solution)/shard_map/ppermute | solution.py:421
  2.9 8.2 %collective-permute-start.1 = (bf16[16,1152]{1,0:T(8,128)(2,1)S(1)}, bf16[16,1152]{1,0:T(8,128)(2,1)S(1)}, u32[]{:S(2)}, u32[]{:S(2)}) collective-permute-start(bf16[16,1152]{1,0:T(8,128)(2,1)S(1)} %maximum_select_fusion), channel_id=1, source_target_pairs={{0,16},{8,24},{1,17},{9,25},{2,18},{10,26},{3,19},{11,27},{4,20},{... | collective-permute-start | bytes 110600 | tf_op jit(solution)/shard_map/ppermute | solution.py:421
  11.1 6.7 %collective-permute-start.2 = (bf16[2,16,1152]{2,1,0:T(8,128)(2,1)S(1)}, bf16[2,16,1152]{2,1,0:T(8,128)(2,1)S(1)}, u32[]{:S(2)}, u32[]{:S(2)}) collective-permute-start(bf16[2,16,1152]{2,1,0:T(8,128)(2,1)S(1)} %pad_maximum_fusion.4), channel_id=1, source_target_pairs={{0,32},{8,40},{1,33},{9,41},{2,34},{10,42},{3,35},{11,43},{4,36},{... | collective-permute-start | bytes 221192 | tf_op jit(solution)/shard_map/ppermute | solution.py:421
  17.8 7.4 %copy-start.1 = (bf16[592,576]{1,0:T(8,128)(2,1)S(1)}, bf16[592,576]{1,0:T(8,128)(2,1)}, u32[]{:S(2)}) copy-start(bf16[592,576]{1,0:T(8,128)(2,1)} %constant.82.clone.f_ref) | copy-start | bytes 2045956
  17.9 7.3 %collective-permute-start.3 = (bf16[2,2,16,1152]{3,2,1,0:T(8,128)(2,1)S(1)}, bf16[2,2,16,1152]{3,2,1,0:T(8,128)(2,1)S(1)}, u32[]{:S(2)}, u32[]{:S(2)}) collective-permute-start(bf16[2,2,16,1152]{3,2,1,0:T(8,128)(2,1)S(1)} %pad_maximum_fusion.3), channel_id=1, source_target_pairs={{0,64},{8,72},{1,65},{9,73},{2,66},{10,74},{3,67},{11,75},{4,68},{... | collective-permute-start | bytes 442376 | tf_op jit(solution)/shard_map/ppermute | solution.py:421
  20.9 9.6 %copy-start = (bf16[16,576,128]{2,1,0:T(8,128)(2,1)S(1)}, bf16[16,576,128]{2,1,0:T(8,128)(2,1)}, u32[]{:S(2)}) copy-start(bf16[16,576,128]{2,1,0:T(8,128)(2,1)} %get-tuple-element.73.w_ref) | copy-start | bytes 7077892
  20.9 18.6 %collective-permute-start.7 = (bf16[128,2432]{1,0:T(8,128)(2,1)}, bf16[128,2432]{1,0:T(8,128)(2,1)S(1)}, u32[]{:S(2)}, u32[]{:S(2)}) collective-permute-start(bf16[128,2432]{1,0:T(8,128)(2,1)} %get-tuple-element.76), channel_id=1, source_target_pairs={{0,64},{8,72},{1,65},{9,73},{2,66},{10,74},{3,67},{11,75},{4,68},{... | collective-permute-start | bytes 1867784 | tf_op jit(solution)/shard_map/ppermute | solution.py:421
  25.6 9.8 %collective-permute-start.4 = (bf16[37,16,256]{2,1,0:T(8,128)(2,1)S(1)}, bf16[37,16,256]{2,1,0:T(8,128)(2,1)S(1)}, u32[]{:S(2)}, u32[]{:S(2)}) collective-permute-start(bf16[37,16,256]{2,1,0:T(8,128)(2,1)S(1)} %ref_spectra.1), channel_id=1, source_target_pairs={{0,1},{8,9},{1,2},{9,10},{2,3},{10,11},{3,0},{11,8},{4,5},{12,13},... | collective-permute-start | bytes 909320 | tf_op jit(solution)/shard_map/ppermute | solution.py:421
  27.6 7.8 %collective-permute-start.5 = (bf16[37,16,256]{2,1,0:T(8,128)(2,1)S(1)}, bf16[37,16,256]{2,1,0:T(8,128)(2,1)S(1)}, u32[]{:S(2)}, u32[]{:S(2)}) collective-permute-start(bf16[37,16,256]{2,1,0:T(8,128)(2,1)S(1)} %ref_spectra.1), channel_id=1, source_target_pairs={{0,3},{8,11},{1,0},{9,8},{2,1},{10,9},{3,2},{11,10},{4,7},{12,15},... | collective-permute-start | bytes 909320 | tf_op jit(solution)/shard_map/ppermute | solution.py:421
  29.8 9.0 %collective-permute-start.9 = (bf16[37,16,256]{2,1,0:T(8,128)(2,1)S(1)}, bf16[37,16,256]{2,1,0:T(8,128)(2,1)}, u32[]{:S(2)}, u32[]{:S(2)}) collective-permute-start(bf16[37,16,256]{2,1,0:T(8,128)(2,1)S(1)} %ref_spectra.1), channel_id=1, source_target_pairs={{0,4},{8,12},{1,5},{9,13},{2,6},{10,14},{3,7},{11,15},{4,0},{12,8}... | collective-permute-start | bytes 909320 | tf_op jit(solution)/shard_map/ppermute | solution.py:421
  35.5 3.9 %copy-start.7 = (bf16[37,16,256]{2,1,0:T(8,128)(2,1)}, bf16[37,16,256]{2,1,0:T(8,128)(2,1)S(1)}, u32[]{:S(2)}) copy-start(bf16[37,16,256]{2,1,0:T(8,128)(2,1)S(1)} %collective-permute-done.4) | copy-start | bytes 909316
  35.5 9.0 %copy-start.8 = (bf16[37,16,256]{2,1,0:T(8,128)(2,1)}, bf16[37,16,256]{2,1,0:T(8,128)(2,1)S(1)}, u32[]{:S(2)}) copy-start(bf16[37,16,256]{2,1,0:T(8,128)(2,1)S(1)} %collective-permute-done.5) | copy-start | bytes 909316
  35.5 19.9 %collective-permute-start.6 = (bf16[128,2432]{1,0:T(8,128)(2,1)}, bf16[128,2432]{1,0:T(8,128)(2,1)S(1)}, u32[]{:S(2)}, u32[]{:S(2)}) collective-permute-start(bf16[128,2432]{1,0:T(8,128)(2,1)} %get-tuple-element.75), channel_id=1, source_target_pairs={{0,32},{8,40},{1,33},{9,41},{2,34},{10,42},{3,35},{11,43},{4,36},{... | collective-permute-start | bytes 1867784 | tf_op jit(solution)/shard_map/ppermute | solution.py:421
  36.0 19.4 %collective-permute-start.8 = (bf16[128,2432]{1,0:T(8,128)(2,1)}, bf16[128,2432]{1,0:T(8,128)(2,1)}, u32[]{:S(2)}, u32[]{:S(2)}) collective-permute-start(bf16[128,2432]{1,0:T(8,128)(2,1)} %get-tuple-element.77), channel_id=1, source_target_pairs={{0,96},{8,104},{1,97},{9,105},{2,98},{10,106},{3,99},{11,107},{4,1... | collective-permute-start | bytes 1867784 | tf_op jit(solution)/shard_map/ppermute | solution.py:421
  39.4 0.9 %copy-start.4 = (bf16[128,2432]{1,0:T(8,128)(2,1)}, bf16[128,2432]{1,0:T(8,128)(2,1)S(1)}, u32[]{:S(2)}) copy-start(bf16[128,2432]{1,0:T(8,128)(2,1)S(1)} %collective-permute-done.7.c2) | copy-start | bytes 1867780
  40.3 8.8 %collective-permute-start.11 = (bf16[37,16,256]{2,1,0:T(8,128)(2,1)}, bf16[37,16,256]{2,1,0:T(8,128)(2,1)}, u32[]{:S(2)}, u32[]{:S(2)}) collective-permute-start(bf16[37,16,256]{2,1,0:T(8,128)(2,1)} %collective-permute-done.9), channel_id=1, source_target_pairs={{0,3},{8,11},{1,0},{9,8},{2,1},{10,9},{3,2},{11,10},{4,7},{12,15},... | collective-permute-start | bytes 909320 | tf_op jit(solution)/shard_map/ppermute | solution.py:421
  44.4 10.9 %collective-permute-start.10 = (bf16[37,16,256]{2,1,0:T(8,128)(2,1)}, bf16[37,16,256]{2,1,0:T(8,128)(2,1)}, u32[]{:S(2)}, u32[]{:S(2)}) collective-permute-start(bf16[37,16,256]{2,1,0:T(8,128)(2,1)} %collective-permute-done.9), channel_id=1, source_target_pairs={{0,1},{8,9},{1,2},{9,10},{2,3},{10,11},{3,0},{11,8},{4,5},{12,13},... | collective-permute-start | bytes 909320 | tf_op jit(solution)/shard_map/ppermute | solution.py:421
  44.4 14.2 %collective-permute-start.17 = (bf16[37,16,256]{2,1,0:T(8,128)(2,1)}, bf16[37,16,256]{2,1,0:T(8,128)(2,1)S(1)}, u32[]{:S(2)}, u32[]{:S(2)}) collective-permute-start(bf16[37,16,256]{2,1,0:T(8,128)(2,1)} %copy-done.7), channel_id=1, source_target_pairs={{0,1},{8,9},{1,2},{9,10},{2,3},{10,11},{3,0},{11,8},{4,5},{12,13},... | collective-permute-start | bytes 909320 | tf_op jit(solution)/shard_map/ppermute | solution.py:421
  49.1 9.6 %collective-permute-start.18 = (bf16[37,16,256]{2,1,0:T(8,128)(2,1)}, bf16[37,16,256]{2,1,0:T(8,128)(2,1)S(1)}, u32[]{:S(2)}, u32[]{:S(2)}) collective-permute-start(bf16[37,16,256]{2,1,0:T(8,128)(2,1)} %collective-permute-done.11), channel_id=1, source_target_pairs={{0,3},{8,11},{1,0},{9,8},{2,1},{10,9},{3,2},{11,10},{4,7},{12,15},... | collective-permute-start | bytes 909320 | tf_op jit(solution)/shard_map/ppermute | solution.py:421
  52.9 2.5 %copy-start.2 = (bf16[128,2432]{1,0:T(8,128)(2,1)S(1)}, bf16[128,2432]{1,0:T(8,128)(2,1)}, u32[]{:S(2)}) copy-start(bf16[128,2432]{1,0:T(8,128)(2,1)} %get-tuple-element.79.c0) | copy-start | bytes 1867780
  52.9 2.5 %copy-start.3 = (f32[256,64]{0,1:T(8,128)S(1)}, f32[256,64]{0,1:T(8,128)}, u32[]{:S(2)}) copy-start(f32[256,64]{0,1:T(8,128)} %param.19) | copy-start | bytes 196612
  52.9 2.5 %copy-start.5 = (bf16[128,2432]{1,0:T(8,128)(2,1)S(1)}, bf16[128,2432]{1,0:T(8,128)(2,1)}, u32[]{:S(2)}) copy-start(bf16[128,2432]{1,0:T(8,128)(2,1)} %copy-done.4) | copy-start | bytes 1867780
  55.4 10.2 %collective-permute-start.16 = (bf16[4,37,16,256]{3,2,1,0:T(8,128)(2,1)S(1)}, bf16[4,37,16,256]{3,2,1,0:T(8,128)(2,1)S(1)}, u32[]{:S(2)}, u32[]{:S(2)}) collective-permute-start(bf16[4,37,16,256]{3,2,1,0:T(8,128)(2,1)S(1)} %pad_maximum_fusion.refs_1_), channel_id=1, source_target_pairs={{0,8},{8,0},{1,9},{9,1},{2,10},{10,2},{3,11},{11,3},{4,12},{12,4},... | collective-permute-start | bytes 3637256 | tf_op jit(solution)/shard_map/ppermute | solution.py:421
  58.1 3.2 %collective-permute-start.12 = (f32[2,256,640]{2,1,0:T(8,128)S(1)}, f32[2,256,640]{2,1,0:T(8,128)S(1)}, u32[]{:S(2)}, u32[]{:S(2)}) collective-permute-start(f32[2,256,640]{2,1,0:T(8,128)S(1)} %get-tuple-element.84), channel_id=1, source_target_pairs={{0,8},{8,0},{1,9},{9,1},{2,10},{10,2},{3,11},{11,3},{4,12},{12,4},... | collective-permute-start | bytes 3932168 | tf_op jit(solution)/shard_map/ppermute | solution.py:421
  59.9 5.8 %collective-permute-start.19 = (bf16[4,37,16,256]{3,2,1,0:T(8,128)(2,1)S(1)}, bf16[4,37,16,256]{3,2,1,0:T(8,128)(2,1)S(1)}, u32[]{:S(2)}, u32[]{:S(2)}) collective-permute-start(bf16[4,37,16,256]{3,2,1,0:T(8,128)(2,1)S(1)} %pad_maximum_fusion.1.refs_3_), channel_id=1, source_target_pairs={{0,8},{8,0},{1,9},{9,1},{2,10},{10,2},{3,11},{11,3},{4,12},{12,4},... | collective-permute-start | bytes 3637256 | tf_op jit(solution)/shard_map/ppermute | solution.py:421
  61.3 4.3 %copy-start.6 = (bf16[576,640]{1,0:T(8,128)(2,1)S(1)}, bf16[576,640]{1,0:T(8,128)(2,1)}, u32[]{:S(2)}) copy-start(bf16[576,640]{1,0:T(8,128)(2,1)} %constant.83.clone.refs_5_) | copy-start | bytes 2211844
  62.0 11.6 %collective-permute-start.13 = (bf16[128,640]{1,0:T(8,128)(2,1)S(1)}, bf16[128,640]{1,0:T(8,128)(2,1)S(1)}, u32[]{:S(2)}, u32[]{:S(2)}) collective-permute-start(bf16[128,640]{1,0:T(8,128)(2,1)S(1)} %get-tuple-element.86), channel_id=1, source_target_pairs={{0,4},{8,12},{1,5},{9,13},{2,6},{10,14},{3,7},{11,15},{4,16},{12,2... | collective-permute-start | bytes 491528 | tf_op jit(solution)/shard_map/ppermute | solution.py:421
  62.7 10.9 %collective-permute-start.14 = (bf16[128,640]{1,0:T(8,128)(2,1)S(1)}, bf16[128,640]{1,0:T(8,128)(2,1)S(1)}, u32[]{:S(2)}, u32[]{:S(2)}) collective-permute-start(bf16[128,640]{1,0:T(8,128)(2,1)S(1)} %get-tuple-element.87), channel_id=1, source_target_pairs={{0,16},{8,24},{1,17},{9,25},{2,18},{10,26},{3,19},{11,27},{4,20},{... | collective-permute-start | bytes 491528 | tf_op jit(solution)/shard_map/ppermute | solution.py:421
  64.7 9.2 %collective-permute-start.15 = (bf16[128,640]{1,0:T(8,128)(2,1)S(1)}, bf16[128,640]{1,0:T(8,128)(2,1)S(1)}, u32[]{:S(2)}, u32[]{:S(2)}) collective-permute-start(bf16[128,640]{1,0:T(8,128)(2,1)S(1)} %get-tuple-element.88), channel_id=1, source_target_pairs={{0,20},{8,28},{1,21},{9,29},{2,22},{10,30},{3,23},{11,31},{4,0},{1... | collective-permute-start | bytes 491528 | tf_op jit(solution)/shard_map/ppermute | solution.py:421
  74.5 5.7 %collective-permute-start.20 = (bf16[32,640]{1,0:T(8,128)(2,1)S(1)}, bf16[32,640]{1,0:T(8,128)(2,1)S(1)}, u32[]{:S(2)}, u32[]{:S(2)}) collective-permute-start(bf16[32,640]{1,0:T(8,128)(2,1)S(1)} %get-tuple-element.95), channel_id=1, source_target_pairs={{0,1},{8,9},{1,2},{9,10},{2,3},{10,11},{3,0},{11,8},{4,5},{12,13},... | collective-permute-start | bytes 122888 | tf_op jit(solution)/shard_map/ppermute | solution.py:421
  74.6 5.6 %collective-permute-start.21 = (bf16[32,640]{1,0:T(8,128)(2,1)S(1)}, bf16[32,640]{1,0:T(8,128)(2,1)S(1)}, u32[]{:S(2)}, u32[]{:S(2)}) collective-permute-start(bf16[32,640]{1,0:T(8,128)(2,1)S(1)} %get-tuple-element.96), channel_id=1, source_target_pairs={{0,2},{8,10},{1,3},{9,11},{2,0},{10,8},{3,1},{11,9},{4,6},{12,14},... | collective-permute-start | bytes 122888 | tf_op jit(solution)/shard_map/ppermute | solution.py:421
  77.2 4.0 %collective-permute-start.22 = (bf16[32,640]{1,0:T(8,128)(2,1)S(1)}, bf16[32,640]{1,0:T(8,128)(2,1)S(1)}, u32[]{:S(2)}, u32[]{:S(2)}) collective-permute-start(bf16[32,640]{1,0:T(8,128)(2,1)S(1)} %get-tuple-element.97), channel_id=1, source_target_pairs={{0,3},{8,11},{1,0},{9,8},{2,1},{10,9},{3,2},{11,10},{4,7},{12,15},... | collective-permute-start | bytes 122888 | tf_op jit(solution)/shard_map/ppermute | solution.py:421
